TPU v7x, 32 devices: a whole 2x2x4 slice. The times are simulated.
32 devices in a mesh: ctx: 8 (over y, x, core), wsh: 4 (over z).
Axes of the slice: x: 2, y: 2, z: 4, core: 2. Of those that a mesh axis runs over, the one named last changes fastest.
Arguments:
- tokens: bfloat16 [4, 2048, 1024], P('wsh', 'ctx'), may hold values from -6 to 6
- cotangent: bfloat16 [4, 2048, 1024], P('wsh', 'ctx'), may hold values from -6 to 6
- doc_starts: int32 [4, 2], P('wsh'), may hold values from 0 to 1848, as said below
- doc_lengths: int32 [4, 2], P('wsh'), may hold values from 200 to 1848, as said below
- query_weight: float32 [2, 1024, 1024], P(None, 'wsh'), may hold values from -0.1875 to 0.1875
- key_weight: float32 [2, 1024, 1024], P(None, 'wsh'), may hold values from -0.1875 to 0.1875
- value_weight: float32 [2, 1024, 1024], P(None, 'wsh'), may hold values from -0.1875 to 0.1875
- out_weight: float32 [2, 1024, 1024], P(None, 'wsh'), may hold values from -0.75 to 0.75
- inner_weight: float32 [2, 1024, 4096], P(None, 'wsh'), may hold values from -0.1875 to 0.1875
- outer_weight: float32 [2, 4096, 1024], P(None, None, 'wsh'), may hold values from -0.09375 to 0.09375
- query_bias: float32 [2, 1024], P(None, 'wsh'), may hold values from -1.8 to 1.8
- value_bias: float32 [2, 1024], P(None, 'wsh'), may hold values from -1.8 to 1.8
- out_bias: float32 [2, 1024], P(None, 'wsh'), may hold values from -1.8 to 1.8
- inner_bias: float32 [2, 4096], P(None, 'wsh'), may hold values from -1.8 to 1.8
- outer_bias: float32 [2, 1024], P(None, 'wsh'), may hold values from -1.8 to 1.8
- first_gain: float32 [2, 1024], P(None, 'wsh'), may hold values from 0.5 to 1.5
- first_shift: float32 [2, 1024], P(None, 'wsh'), may hold values from -1.8 to 1.8
- second_gain: float32 [2, 1024], P(None, 'wsh'), may hold values from 0.5 to 1.5
- second_shift: float32 [2, 1024], P(None, 'wsh'), may hold values from -1.8 to 1.8
Outputs:
- out_first: bfloat16 [4, 2048, 1024], P('wsh', 'ctx')
- out_second: bfloat16 [4, 2048, 1024], P('wsh', 'ctx')
- grad_tokens: bfloat16 [4, 2048, 1024], P('wsh', 'ctx')
- grad_query_weight: float32 [2, 1024, 1024], P(None, 'wsh')
- grad_key_weight: float32 [2, 1024, 1024], P(None, 'wsh')
- grad_value_weight: float32 [2, 1024, 1024], P(None, 'wsh')
- grad_out_weight: float32 [2, 1024, 1024], P(None, 'wsh')
- grad_inner_weight: float32 [2, 1024, 4096], P(None, 'wsh')
- grad_outer_weight: float32 [2, 4096, 1024], P(None, None, 'wsh')
- grad_query_bias: float32 [2, 1024], P(None, 'wsh')
- grad_value_bias: float32 [2, 1024], P(None, 'wsh')
- grad_out_bias: float32 [2, 1024], P(None, 'wsh')
- grad_inner_bias: float32 [2, 4096], P(None, 'wsh')
- grad_outer_bias: float32 [2, 1024], P(None, 'wsh')
- grad_first_gain: float32 [2, 1024], P(None, 'wsh')
- grad_first_shift: float32 [2, 1024], P(None, 'wsh')
- grad_second_gain: float32 [2, 1024], P(None, 'wsh')
- grad_second_shift: float32 [2, 1024], P(None, 'wsh')
Inputs may be any that keep to these rules, and one draw needn't show every extreme that they name: The documents of a sequence lie one after another in order from position 0 and cover all 2048 positions; doc_starts is 0 for the first and each start is the previous start plus the previous length. `doc_lengths`: each document has 200 to 1848 tokens, never more than 2000; in every sequence one has exactly 1848.
All inputs are finite; a program needn't handle non-finite values.
Results may differ from a plain program's by a relative error of at most 0.023.
Values may be sent and summed in bfloat16 or wider, within the bound.
No kernel may reach another device: no remote copies, remote signals or barrier semaphores. Data moves between devices by JAX's collectives and lax.ppermute only.
A program may use at most 384 MiB of HBM per device.

v0:
```python
import jax
import jax.numpy as jnp
from jax import lax
from jax.sharding import PartitionSpec as P

HEADS = 16
HDIM = 64
LAYERS = 2
DOC_CAP = 2000


epsilon = 1e-05
neg_fill = -1e30
head_pair = 2


def from_behind(block, axis, distance):
    devices = range(lax.axis_size(axis))
    route = [(i - distance, i) for i in devices if i - distance in devices]
    return lax.ppermute(block, axis, route)


def normalize(values_in, gain_row, shift_row):
    centre = values_in - jnp.mean(values_in, axis=-1, keepdims=True)
    spread = jnp.mean(centre * centre, axis=-1, keepdims=True)
    return centre * lax.rsqrt(spread + epsilon) * gain_row + shift_row


def exact_gelu(values_in):
    return jax.nn.gelu(values_in, approximate=False)


def product(form, left, right):
    return jnp.einsum(form, left, right, preferred_element_type=jnp.float32)


def doc_labels(positions, starts, lengths):
    inside = (positions[:, None] >= starts[None, :]) & (
        positions[:, None] < (starts + lengths)[None, :]
    )
    labels = jnp.arange(1, starts.shape[0] + 1, dtype=jnp.int32)
    return jnp.sum(jnp.where(inside, labels[None, :], 0), axis=1)


def extend_rows(rows_in, dim, reach, mover):
    pieces = []
    for offset in range(-reach, reach + 1):
        if offset == 0:
            pieces.append(rows_in)
        else:
            pieces.append(mover(rows_in, -offset))
    return jnp.concatenate(pieces, axis=dim)


def move_keys_fwd(rows_in, steps):
    return from_behind(rows_in, "ctx", steps)


def move_keys_back(rows_in, steps):
    return from_behind(rows_in, "ctx", steps)


def fetch_forward(params, layer_index):
    shards = [piece[layer_index].astype(jnp.bfloat16) for piece in params]
    return (
        lax.all_gather(shards[0], "wsh", axis=0, tiled=True),
        lax.all_gather(shards[1], "wsh", axis=0, tiled=True),
        lax.all_gather(shards[2], "wsh", axis=0, tiled=True),
        lax.all_gather(shards[3], "wsh", axis=0, tiled=True),
        lax.all_gather(shards[4], "wsh", axis=0, tiled=True),
        lax.all_gather(shards[5], "wsh", axis=1, tiled=True),
        lax.all_gather(shards[6], "wsh", axis=0, tiled=True),
        lax.all_gather(shards[7], "wsh", axis=0, tiled=True),
        lax.all_gather(shards[8], "wsh", axis=0, tiled=True),
        lax.all_gather(shards[9], "wsh", axis=0, tiled=True),
        lax.all_gather(shards[10], "wsh", axis=0, tiled=True),
        lax.all_gather(shards[11], "wsh", axis=0, tiled=True),
        lax.all_gather(shards[12], "wsh", axis=0, tiled=True),
        lax.all_gather(shards[13], "wsh", axis=0, tiled=True),
        lax.all_gather(shards[14], "wsh", axis=0, tiled=True),
    )


def fetch_backward(params, layer_index):
    shards = [piece[layer_index].astype(jnp.bfloat16) for piece in params]
    return (
        lax.all_gather(shards[0], "wsh", axis=0, tiled=True),
        lax.all_gather(shards[1], "wsh", axis=0, tiled=True),
        lax.all_gather(shards[2], "wsh", axis=0, tiled=True),
        lax.all_gather(shards[3], "wsh", axis=0, tiled=True),
        lax.all_gather(shards[4], "wsh", axis=0, tiled=True),
        lax.all_gather(shards[5], "wsh", axis=1, tiled=True),
        lax.all_gather(shards[6], "wsh", axis=0, tiled=True),
        lax.all_gather(shards[7], "wsh", axis=0, tiled=True),
        lax.all_gather(shards[8], "wsh", axis=0, tiled=True),
        lax.all_gather(shards[9], "wsh", axis=0, tiled=True),
        lax.all_gather(shards[10], "wsh", axis=0, tiled=True),
        lax.all_gather(shards[11], "wsh", axis=0, tiled=True),
        lax.all_gather(shards[12], "wsh", axis=0, tiled=True),
        lax.all_gather(shards[13], "wsh", axis=0, tiled=True),
        lax.all_gather(shards[14], "wsh", axis=0, tiled=True),
    )


def reduce_grads(local_grads):
    shares = (
        lax.psum_scatter(
            local_grads[0].astype(jnp.bfloat16), "wsh", scatter_dimension=0, tiled=True
        ).astype(jnp.float32),
        lax.psum_scatter(
            local_grads[1].astype(jnp.bfloat16), "wsh", scatter_dimension=0, tiled=True
        ).astype(jnp.float32),
        lax.psum_scatter(
            local_grads[2].astype(jnp.bfloat16), "wsh", scatter_dimension=0, tiled=True
        ).astype(jnp.float32),
        lax.psum_scatter(
            local_grads[3].astype(jnp.bfloat16), "wsh", scatter_dimension=0, tiled=True
        ).astype(jnp.float32),
        lax.psum_scatter(
            local_grads[4].astype(jnp.bfloat16), "wsh", scatter_dimension=0, tiled=True
        ).astype(jnp.float32),
        lax.psum_scatter(
            local_grads[5].astype(jnp.bfloat16), "wsh", scatter_dimension=1, tiled=True
        ).astype(jnp.float32),
        lax.psum_scatter(
            local_grads[6].astype(jnp.bfloat16), "wsh", scatter_dimension=0, tiled=True
        ).astype(jnp.float32),
        lax.psum_scatter(
            local_grads[7].astype(jnp.bfloat16), "wsh", scatter_dimension=0, tiled=True
        ).astype(jnp.float32),
        lax.psum_scatter(
            local_grads[8].astype(jnp.bfloat16), "wsh", scatter_dimension=0, tiled=True
        ).astype(jnp.float32),
        lax.psum_scatter(
            local_grads[9].astype(jnp.bfloat16), "wsh", scatter_dimension=0, tiled=True
        ).astype(jnp.float32),
        lax.psum_scatter(
            local_grads[10].astype(jnp.bfloat16), "wsh", scatter_dimension=0, tiled=True
        ).astype(jnp.float32),
        lax.psum_scatter(
            local_grads[11].astype(jnp.bfloat16), "wsh", scatter_dimension=0, tiled=True
        ).astype(jnp.float32),
        lax.psum_scatter(
            local_grads[12].astype(jnp.bfloat16), "wsh", scatter_dimension=0, tiled=True
        ).astype(jnp.float32),
        lax.psum_scatter(
            local_grads[13].astype(jnp.bfloat16), "wsh", scatter_dimension=0, tiled=True
        ).astype(jnp.float32),
        lax.psum_scatter(
            local_grads[14].astype(jnp.bfloat16), "wsh", scatter_dimension=0, tiled=True
        ).astype(jnp.float32),
    )
    return (
        lax.psum(shares[0].astype(jnp.bfloat16), "ctx").astype(jnp.float32),
        lax.psum(shares[1].astype(jnp.bfloat16), "ctx").astype(jnp.float32),
        lax.psum(shares[2].astype(jnp.bfloat16), "ctx").astype(jnp.float32),
        lax.psum(shares[3].astype(jnp.bfloat16), "ctx").astype(jnp.float32),
        lax.psum(shares[4].astype(jnp.bfloat16), "ctx").astype(jnp.float32),
        lax.psum(shares[5].astype(jnp.bfloat16), "ctx").astype(jnp.float32),
        lax.psum(shares[6].astype(jnp.bfloat16), "ctx").astype(jnp.float32),
        lax.psum(shares[7].astype(jnp.bfloat16), "ctx").astype(jnp.float32),
        lax.psum(shares[8].astype(jnp.bfloat16), "ctx").astype(jnp.float32),
        lax.psum(shares[9].astype(jnp.bfloat16), "ctx").astype(jnp.float32),
        lax.psum(shares[10].astype(jnp.bfloat16), "ctx").astype(jnp.float32),
        lax.psum(shares[11].astype(jnp.bfloat16), "ctx").astype(jnp.float32),
        lax.psum(shares[12].astype(jnp.bfloat16), "ctx").astype(jnp.float32),
        lax.psum(shares[13].astype(jnp.bfloat16), "ctx").astype(jnp.float32),
        lax.psum(shares[14].astype(jnp.bfloat16), "ctx").astype(jnp.float32),
    )


def attend(queries, key_ext, value_ext, allowed, score_scale):
    rows_local = queries.shape[0]
    rows_keys = key_ext.shape[0]
    groups = HEADS // head_pair
    span = head_pair * HDIM
    query_groups = queries.reshape(rows_local, groups, span)
    key_groups = key_ext.reshape(rows_keys, groups, span)
    value_groups = value_ext.reshape(rows_keys, groups, span)

    def one_group(group_index, carry):
        mixed_all, log_all = carry
        query_part = lax.dynamic_index_in_dim(query_groups, group_index, 1, keepdims=False).reshape(
            rows_local, head_pair, HDIM
        )
        key_part = lax.dynamic_index_in_dim(key_groups, group_index, 1, keepdims=False).reshape(
            rows_keys, head_pair, HDIM
        )
        value_part = lax.dynamic_index_in_dim(value_groups, group_index, 1, keepdims=False).reshape(
            rows_keys, head_pair, HDIM
        )
        raw_scores = product("qhd,khd->hqk", query_part, key_part)
        scores = jnp.where(allowed[None], raw_scores * score_scale, neg_fill)
        row_peak = jnp.max(scores, axis=2, keepdims=True)
        exponent = jnp.exp(scores - row_peak)
        row_total = jnp.sum(exponent, axis=2, keepdims=True)
        probability = (exponent / row_total).astype(jnp.bfloat16)
        mixed_part = product("hqk,khd->qhd", probability, value_part)
        mixed_all = lax.dynamic_update_index_in_dim(
            mixed_all, mixed_part.reshape(rows_local, span), group_index, 1
        )
        log_all = lax.dynamic_update_index_in_dim(
            log_all, (row_peak + jnp.log(row_total))[:, :, 0], group_index, 0
        )
        return (mixed_all, log_all)

    start_carry = (
        jnp.zeros((rows_local, groups, span), jnp.float32),
        jnp.zeros((groups, head_pair, rows_local), jnp.float32),
    )
    mixed_all, log_all = lax.fori_loop(0, groups, one_group, start_carry)
    return (mixed_all.reshape(rows_local, groups * span), log_all)


def attend_back(queries, key_ext, value_ext, grad_mixed, log_all, allowed, score_scale):
    rows_local = queries.shape[0]
    rows_keys = key_ext.shape[0]
    groups = HEADS // head_pair
    span = head_pair * HDIM
    query_groups = queries.reshape(rows_local, groups, span)
    key_groups = key_ext.reshape(rows_keys, groups, span)
    value_groups = value_ext.reshape(rows_keys, groups, span)
    grad_groups = grad_mixed.reshape(rows_local, groups, span)

    def one_group(group_index, carry):
        query_part = lax.dynamic_index_in_dim(query_groups, group_index, 1, keepdims=False).reshape(
            rows_local, head_pair, HDIM
        )
        key_part = lax.dynamic_index_in_dim(key_groups, group_index, 1, keepdims=False).reshape(
            rows_keys, head_pair, HDIM
        )
        value_part = lax.dynamic_index_in_dim(value_groups, group_index, 1, keepdims=False).reshape(
            rows_keys, head_pair, HDIM
        )
        grad_part = lax.dynamic_index_in_dim(grad_groups, group_index, 1, keepdims=False).reshape(
            rows_local, head_pair, HDIM
        )
        log_part = lax.dynamic_index_in_dim(log_all, group_index, 0, keepdims=False)
        raw_scores = product("qhd,khd->hqk", query_part, key_part)
        scores = jnp.where(allowed[None], raw_scores * score_scale, neg_fill)
        probability = jnp.exp(scores - log_part[:, :, None])
        grad_prob = product("qhd,khd->hqk", grad_part, value_part)
        row_delta = jnp.sum(probability * grad_prob, axis=2, keepdims=True)
        grad_scores = (probability * (grad_prob - row_delta) * score_scale).astype(jnp.bfloat16)
        query_term = product("hqk,khd->qhd", grad_scores, key_part)
        grad_query = lax.dynamic_update_index_in_dim(
            carry[0], query_term.reshape(rows_local, span), group_index, 1
        )
        delta_all = lax.dynamic_update_index_in_dim(carry[1], row_delta[:, :, 0], group_index, 0)
        key_term = product("hqk,qhd->khd", grad_scores, query_part)
        value_term = product("hqk,qhd->khd", probability.astype(jnp.bfloat16), grad_part)
        grad_key = lax.dynamic_update_index_in_dim(
            carry[2], key_term.reshape(rows_keys, span), group_index, 1
        )
        grad_value = lax.dynamic_update_index_in_dim(
            carry[3], value_term.reshape(rows_keys, span), group_index, 1
        )
        return (grad_query, delta_all, grad_key, grad_value)

    start_carry = (
        jnp.zeros((rows_local, groups, span), jnp.float32),
        jnp.zeros((groups, head_pair, rows_local), jnp.float32),
    )
    start_carry = start_carry + (
        jnp.zeros((rows_keys, groups, span), jnp.float32),
        jnp.zeros((rows_keys, groups, span), jnp.float32),
    )
    finals = lax.fori_loop(0, groups, one_group, start_carry)
    grad_query = finals[0].reshape(rows_local, groups * span)
    return (
        grad_query,
        finals[2].reshape(rows_keys, groups * span),
        finals[3].reshape(rows_keys, groups * span),
    )


def layer_forward(activation, gathered, allowed, halo_rows, score_scale):
    (
        query_weight,
        key_weight,
        value_weight,
        out_weight,
        inner_weight,
        outer_weight,
        query_bias,
        value_bias,
        out_bias,
        inner_bias,
        outer_bias,
        first_gain,
        first_shift,
        second_gain,
        second_shift,
    ) = gathered
    rows_local = activation.shape[0]
    queries = (product("td,de->te", activation, query_weight) + query_bias).astype(jnp.bfloat16)
    key_rows = product("td,de->te", activation, key_weight).astype(jnp.bfloat16)
    value_rows = (product("td,de->te", activation, value_weight) + value_bias).astype(jnp.bfloat16)
    stacked = jnp.stack([key_rows, value_rows])
    extended = extend_rows(stacked, 1, halo_rows // rows_local, move_keys_fwd)
    mixed_heads, log_all = attend(queries, extended[0], extended[1], allowed, score_scale)
    mixed_low = mixed_heads.astype(jnp.bfloat16)
    first_pre = activation.astype(jnp.float32) + (
        product("td,de->te", mixed_low, out_weight) + out_bias
    )
    hidden = normalize(first_pre, first_gain.astype(jnp.float32), first_shift.astype(jnp.float32))
    hidden_low = hidden.astype(jnp.bfloat16)
    inner_pre = product("td,df->tf", hidden_low, inner_weight) + inner_bias
    active_low = exact_gelu(inner_pre).astype(jnp.bfloat16)
    second_pre = hidden + (product("tf,fd->td", active_low, outer_weight) + outer_bias)
    result_rows = normalize(
        second_pre, second_gain.astype(jnp.float32), second_shift.astype(jnp.float32)
    )
    saved = (
        activation,
        queries,
        extended,
        log_all,
        mixed_low,
        first_pre,
        hidden_low,
        inner_pre,
        active_low,
        second_pre,
    )
    return (saved, result_rows)


def return_rows(grad_ext, halo_rows, rows_local):
    reach = halo_rows // rows_local
    total = grad_ext[:, halo_rows : halo_rows + rows_local]
    for offset in range(-reach, reach + 1):
        if offset != 0:
            begin = halo_rows + offset * rows_local
            block_rows = grad_ext[:, begin : begin + rows_local]
            total = total + from_behind(block_rows.astype(jnp.bfloat16), "ctx", offset).astype(
                block_rows.dtype
            )
    return total


def layer_backward(gradient, saved, weights, allowed, halo_rows, score_scale):
    (
        query_weight,
        key_weight,
        value_weight,
        out_weight,
        inner_weight,
        outer_weight,
        query_bias,
        value_bias,
        out_bias,
        inner_bias,
        outer_bias,
        first_gain,
        first_shift,
        second_gain,
        second_shift,
    ) = weights
    (
        activation,
        queries,
        extended,
        log_all,
        mixed_low,
        first_pre,
        hidden_low,
        inner_pre,
        active_low,
        second_pre,
    ) = saved
    rows_local = activation.shape[0]
    reach = halo_rows // rows_local
    _, second_pull = jax.vjp(
        normalize, second_pre, second_gain.astype(jnp.float32), second_shift.astype(jnp.float32)
    )
    grad_second, grad_second_gain, grad_second_shift = second_pull(gradient)
    grad_outer = grad_second.astype(jnp.bfloat16)
    grad_outer_weight = product("tf,td->fd", active_low, grad_outer)
    grad_outer_bias = jnp.sum(grad_outer.astype(jnp.float32), axis=0)
    grad_active = product("td,fd->tf", grad_outer, outer_weight)
    _, gelu_pull = jax.vjp(exact_gelu, inner_pre)
    (grad_inner,) = gelu_pull(grad_active)
    grad_inner_low = grad_inner.astype(jnp.bfloat16)
    grad_inner_weight = product("td,tf->df", hidden_low, grad_inner_low)
    grad_inner_bias = jnp.sum(grad_inner_low.astype(jnp.float32), axis=0)
    grad_hidden = grad_second + product("tf,df->td", grad_inner_low, inner_weight)
    _, first_pull = jax.vjp(
        normalize, first_pre, first_gain.astype(jnp.float32), first_shift.astype(jnp.float32)
    )
    grad_first, grad_first_gain, grad_first_shift = first_pull(grad_hidden)
    grad_branch = grad_first.astype(jnp.bfloat16)
    grad_out_weight = product("te,td->ed", mixed_low, grad_branch)
    grad_out_bias = jnp.sum(grad_branch.astype(jnp.float32), axis=0)
    grad_mixed = product("td,ed->te", grad_branch, out_weight).astype(jnp.bfloat16)
    own_rows = extended[:, halo_rows : halo_rows + rows_local]
    key_ext = extend_rows(own_rows, 1, reach, move_keys_back)
    query_sum, key_win, value_win = attend_back(
        queries, key_ext[0], key_ext[1], grad_mixed, log_all, allowed, score_scale
    )
    owned = return_rows(jnp.stack([key_win, value_win]), halo_rows, rows_local)
    key_sum = owned[0]
    value_sum = owned[1]
    grad_query = query_sum.astype(jnp.bfloat16)
    grad_key = key_sum.astype(jnp.bfloat16)
    grad_value = value_sum.astype(jnp.bfloat16)
    grad_query_weight = product("te,td->ed", activation, grad_query)
    grad_key_weight = product("te,td->ed", activation, grad_key)
    grad_value_weight = product("te,td->ed", activation, grad_value)
    grad_query_bias = jnp.sum(grad_query.astype(jnp.float32), axis=0)
    grad_value_bias = jnp.sum(grad_value.astype(jnp.float32), axis=0)
    grad_activation = (
        grad_first
        + product("td,ed->te", grad_query, query_weight)
        + product("td,ed->te", grad_key, key_weight)
        + product("td,ed->te", grad_value, value_weight)
    )
    local_grads = (
        grad_query_weight,
        grad_key_weight,
        grad_value_weight,
        grad_out_weight,
        grad_inner_weight,
        grad_outer_weight,
        grad_query_bias,
        grad_value_bias,
        grad_out_bias,
        grad_inner_bias,
        grad_outer_bias,
        grad_first_gain,
        grad_first_shift,
        grad_second_gain,
        grad_second_shift,
    )
    return (grad_activation, local_grads)


def body(
    tokens,
    cotangent,
    doc_starts,
    doc_lengths,
    query_weight,
    key_weight,
    value_weight,
    out_weight,
    inner_weight,
    outer_weight,
    query_bias,
    value_bias,
    out_bias,
    inner_bias,
    outer_bias,
    first_gain,
    first_shift,
    second_gain,
    second_shift,
):
    params = (
        query_weight,
        key_weight,
        value_weight,
        out_weight,
        inner_weight,
        outer_weight,
        query_bias,
        value_bias,
        out_bias,
        inner_bias,
        outer_bias,
        first_gain,
        first_shift,
        second_gain,
        second_shift,
    )
    rows_local = tokens.shape[1]
    ctx_count = lax.axis_size("ctx")
    reach = min(-(-(DOC_CAP - 1) // rows_local), ctx_count - 1)
    halo_rows = reach * rows_local
    window = rows_local + 2 * halo_rows
    row_start = lax.axis_index("ctx") * rows_local
    local_positions = row_start + jnp.arange(rows_local, dtype=jnp.int32)
    window_positions = row_start - halo_rows + jnp.arange(window, dtype=jnp.int32)
    local_labels = doc_labels(local_positions, doc_starts[0], doc_lengths[0])
    window_labels = doc_labels(window_positions, doc_starts[0], doc_lengths[0])
    allowed = (local_labels[:, None] == window_labels[None, :]) & (local_labels[:, None] > 0)
    score_scale = HDIM ** (-0.5)
    activation = tokens[0]
    stashed = []
    outputs = []
    for layer_index in range(LAYERS):
        gathered = fetch_forward(params, layer_index)
        saved, result_rows = layer_forward(activation, gathered, allowed, halo_rows, score_scale)
        stashed.append((saved, gathered))
        outputs.append(result_rows)
        activation = result_rows.astype(jnp.bfloat16)
    gradient = cotangent[0].astype(jnp.float32)
    reduced = [None] * LAYERS
    for layer_index in reversed(range(LAYERS)):
        saved, gathered = stashed[layer_index]
        weights_now = fetch_backward(params, layer_index)
        gradient, local_grads = layer_backward(
            gradient, saved, weights_now, allowed, halo_rows, score_scale
        )
        reduced[layer_index] = reduce_grads(local_grads)
    stacked_grads = [
        jnp.stack([reduced[layer_index][member] for layer_index in range(LAYERS)])
        for member in range(15)
    ]
    heads_out = [
        outputs[0].astype(jnp.bfloat16)[None],
        outputs[LAYERS - 1].astype(jnp.bfloat16)[None],
        gradient.astype(jnp.bfloat16)[None],
    ]
    return tuple(heads_out + stacked_grads)


def solution(mesh):
    in_specs = (
        P("wsh", "ctx", None),
        P("wsh", "ctx", None),
        P("wsh", None),
        P("wsh", None),
        P(None, "wsh", None),
        P(None, "wsh", None),
        P(None, "wsh", None),
        P(None, "wsh", None),
        P(None, "wsh", None),
        P(None, None, "wsh"),
        P(None, "wsh"),
        P(None, "wsh"),
        P(None, "wsh"),
        P(None, "wsh"),
        P(None, "wsh"),
        P(None, "wsh"),
        P(None, "wsh"),
        P(None, "wsh"),
        P(None, "wsh"),
    )
    out_specs = (
        P("wsh", "ctx", None),
        P("wsh", "ctx", None),
        P("wsh", "ctx", None),
        P(None, "wsh", None),
        P(None, "wsh", None),
        P(None, "wsh", None),
        P(None, "wsh", None),
        P(None, "wsh", None),
        P(None, None, "wsh"),
        P(None, "wsh"),
        P(None, "wsh"),
        P(None, "wsh"),
        P(None, "wsh"),
        P(None, "wsh"),
        P(None, "wsh"),
        P(None, "wsh"),
        P(None, "wsh"),
        P(None, "wsh"),
    )
    return jax.shard_map(body, mesh=mesh, in_specs=in_specs, out_specs=out_specs, check_vma=False)
```

profile of v0, /device:TPU:9, one launch (start us, length us, event | category | flops | bytes accessed | tf_op | source)
XLA Modules:
  0.0 3108.7 jit_solution(11300263557744322337)
XLA Ops:
  58.0 44.5 %all-gather.45.cloned.1.call-done = bf16[1,1024,1024]{2,1,0:T(8,128)(2,1)} async-done(((bf16[1,256,1024]{2,1,0:T(8,128)(2,1)}), bf16[1,1024,1024]{2,1,0:T(8,128)(2,1)}) %all-gather.45.cloned.1.call-update) | async-done | bytes 2097168 | tf_op jit(solution)/shard_map/all_gather | solution.py:68
  262.3 55.2 %collective-permute-done.9 = bf16[2,256,1024]{2,1,0:T(8,128)(2,1)S(1)} collective-permute-done((bf16[2,256,1024]{2,1,0:T(8,128)(2,1)S(1)}, bf16[2,256,1024]{2,1,0:T(8,128)(2,1)S(1)}, u32[]{:S(2)}, u32[]{:S(2)}) %collective-permute-start.9) | collective-permute-done | bytes 1048608 | tf_op jit(solution)/shard_map/ppermute | solution.py:20
  349.9 86.9 %while.68 = (s32[]{:T(128)}, bf16[256,8,128]{0,2,1:T(8,128)(2,1)S(1)}, f32[8,2,256]{2,1,0:T(2,128)}, bf16[3840,8,128]{0,2,1:T(8,128)(2,1)}, bf16[256,8,128]{0,2,...) while((s32[]{:T(128)}, ...), condition=%wide.region_5.6_spmd.clone, body=%wide.region_2.5_spmd.clone.sunk | while | flops 528875008 | bytes 33849724 | solution.py:211
  456.3 38.5 %all-gather.53.cloned.1.call-done = bf16[1,4096,1024]{2,1,0:T(8,128)(2,1)} async-done(((bf16[1,4096,256]{2,1,0:T(8,128)(2,1)}), bf16[1,4096,1024]{2,1,0:T(8,128)(2,1)}) %all-gather.53.cloned.1.call-update) | async-done | bytes 8388624 | tf_op jit(solution)/shard_map/all_gather | solution.py:71
  502.7 39.5 %all-gather.55.cloned.1.call-done = bf16[1,1024,1024]{2,1,0:T(8,128)(2,1)} async-done(((bf16[1,256,1024]{2,1,0:T(8,128)(2,1)}), bf16[1,1024,1024]{2,1,0:T(8,128)(2,1)}) %all-gather.55.cloned.1.call-update) | async-done | bytes 2097168 | tf_op jit(solution)/shard_map/all_gather | solution.py:67
  544.5 44.4 %all-gather.57.cloned.1.call-done = bf16[1,1024,1024]{2,1,0:T(8,128)(2,1)} async-done(((bf16[1,256,1024]{2,1,0:T(8,128)(2,1)}), bf16[1,1024,1024]{2,1,0:T(8,128)(2,1)}) %all-gather.57.cloned.1.call-update) | async-done | bytes 2097168 | tf_op jit(solution)/shard_map/all_gather | solution.py:68
  737.4 57.2 %collective-permute-done.23 = bf16[2,256,1024]{2,1,0:T(8,128)(2,1)S(1)} collective-permute-done((bf16[2,256,1024]{2,1,0:T(8,128)(2,1)S(1)}, bf16[2,256,1024]{2,1,0:T(8,128)(2,1)S(1)}, u32[]{:S(2)}, u32[]{:S(2)}) %collective-permute-start.23) | collective-permute-done | bytes 1048608 | tf_op jit(solution)/shard_map/ppermute | solution.py:20
  826.5 82.4 %while.69 = (s32[]{:T(128)}, bf16[256,8,128]{0,2,1:T(8,128)(2,1)S(1)}, f32[8,2,256]{2,1,0:T(2,128)S(1)}, bf16[3840,8,128]{0,2,1:T(8,128)(2,1)}, bf16[256,8,128]{...) while((s32[]{:T(128)}, ...), condition=%wide.region_13.14_spmd.clone, body=%wide.region_10.13_spmd.clone.sunk | while | flops 528875008 | bytes 33849724 | solution.py:211
  928.0 52.9 %all-gather.65.cloned.1.call-done = bf16[1,4096,1024]{2,1,0:T(8,128)(2,1)} async-done(((bf16[1,4096,256]{2,1,0:T(8,128)(2,1)}), bf16[1,4096,1024]{2,1,0:T(8,128)(2,1)}) %all-gather.65.cloned.1.call-update) | async-done | bytes 8388624 | tf_op jit(solution)/shard_map/all_gather | solution.py:71
  1028.0 358.6 %while.70 = (s32[]{:T(128)}, bf16[256,8,128]{0,2,1:T(8,128)(2,1)S(1)}, f32[3840,8,128]{0,2,1:T(8,128)}, f32[3840,8,128]{0,2,1:T(8,128)}, bf16[3840,8,128]{0,2,1:...) while((s32[]{:T(128)}, ...), condition=%wide.region_24.25_spmd.clone, body=%wide.region_22.24_spmd.clone.sunk | while | flops 1287791104 | bytes 108288520 | solution.py:268
  1455.9 27.8 collective-permute-start.34
  1532.0 39.0 %collective-permute-done.31 = bf16[2,256,1024]{1,2,0:T(8,128)(2,1)} collective-permute-done((bf16[2,256,1024]{1,2,0:T(8,128)(2,1)}, bf16[2,256,1024]{1,2,0:T(8,128)(2,1)}, u32[]{:S(2)}, u32[]{:S(2)}) %collective-permute-start.31) | collective-permute-done | bytes 1048608 | tf_op jit(solution)/shard_map/ppermute | solution.py:20
  1623.8 363.6 %while.71 = (s32[]{:T(128)}, bf16[256,8,128]{0,2,1:T(8,128)(2,1)S(1)}, f32[3840,8,128]{0,2,1:T(8,128)}, f32[3840,8,128]{0,2,1:T(8,128)}, bf16[3840,8,128]{0,2,1:...) while((s32[]{:T(128)}, ...), condition=%wide.region_31.32_spmd.clone, body=%wide.region_29.31_spmd.clone.sunk | while | flops 1287791104 | bytes 108157392 | solution.py:268
  2006.7 26.2 collective-permute-start.54
  2077.6 25.5 collective-permute-start.48
  2131.7 56.0 %collective-permute-done.46 = bf16[2,256,1024]{1,2,0:T(8,128)(2,1)S(1)} collective-permute-done((bf16[2,256,1024]{1,2,0:T(8,128)(2,1)}, bf16[2,256,1024]{1,2,0:T(8,128)(2,1)S(1)}, u32[]{:S(2)}, u32[]{:S(2)}) %collective-permute-start.46) | collective-permute-done | bytes 1048608 | tf_op jit(solution)/shard_map/ppermute | solution.py:20
  2230.6 26.8 reduce-scatter.21.cloned.1.call-done
  2257.5 45.5 %reduce-scatter.17.cloned.1.call-done = bf16[256,1024]{0,1:T(8,128)(2,1)} async-done(((bf16[1024,1024]{0,1:T(8,128)(2,1)}), bf16[256,1024]{0,1:T(8,128)(2,1)}) %reduce-scatter.17.cloned.1.call-update) | async-done | bytes 524304 | tf_op jit(solution)/shard_map/reduce_scatter | solution.py:110
  2302.9 148.9 %reduce-scatter.31.cloned.1.call-done = bf16[256,4096]{1,0:T(8,128)(2,1)} async-done(((bf16[1024,4096]{1,0:T(8,128)(2,1)}), bf16[256,4096]{1,0:T(8,128)(2,1)}) %reduce-scatter.31.cloned.1.call-update) | async-done | bytes 2097168 | tf_op jit(solution)/shard_map/reduce_scatter | solution.py:119
  2451.8 147.6 %reduce-scatter.35.cloned.1.call-done = bf16[4096,256]{1,0:T(8,128)(2,1)} async-done(((bf16[4096,1024]{1,0:T(8,128)(2,1)}), bf16[4096,256]{1,0:T(8,128)(2,1)}) %reduce-scatter.35.cloned.1.call-update) | async-done | bytes 2097168 | tf_op jit(solution)/shard_map/reduce_scatter | solution.py:122
  2599.4 148.2 %reduce-scatter.29.cloned.1.call-done = bf16[256,4096]{1,0:T(8,128)(2,1)} async-done(((bf16[1024,4096]{1,0:T(8,128)(2,1)}), bf16[256,4096]{1,0:T(8,128)(2,1)}) %reduce-scatter.29.cloned.1.call-update) | async-done | bytes 2097168 | tf_op jit(solution)/shard_map/reduce_scatter | solution.py:119
  2747.6 147.4 %reduce-scatter.33.cloned.1.call-done = bf16[4096,256]{1,0:T(8,128)(2,1)} async-done(((bf16[4096,1024]{1,0:T(8,128)(2,1)}), bf16[4096,256]{1,0:T(8,128)(2,1)}) %reduce-scatter.33.cloned.1.call-update) | async-done | bytes 2097168 | tf_op jit(solution)/shard_map/reduce_scatter | solution.py:122
  2920.5 24.3 all-reduce.18
  2951.9 127.0 %all-reduce.23.cloned.1.call-done = (bf16[1,256,1024]{1,2,0:T(8,128)(2,1)}, bf16[1,256,1024]{1,2,0:T(8,128)(2,1)}, bf16[1,256,1024]{1,2,0:T(8,128)(2,1)}, bf16[1...) async-done(((bf16[1,256,1024]{1,2,0:T(8,128)(2,1)}, ...) | async-done | bytes 12582928 | tf_op jit(solution)/shard_map/psum | solution.py:154
  (1114 shorter events, 1766.5 us)
Async XLA Ops:
  11.5 229.4 %all-gather.47.cloned.1.call-start = ((), (), s32[]{:S(2)}) async-start(), calls=%async_computation.26 | async-start | bytes 2621440 | tf_op jit(solution)/shard_map/all_gather | solution.py:66
  14.3 422.5 %all-gather.49.cloned.1.call-start = ((), (), s32[]{:S(2)}) async-start(), calls=%async_computation.27 | async-start | bytes 2621440 | tf_op jit(solution)/shard_map/all_gather | solution.py:69
  15.6 424.2 %all-gather.51.cloned.1.call-start = ((), (), s32[]{:S(2)}) async-start(), calls=%async_computation.28 | async-start | bytes 10485760 | tf_op jit(solution)/shard_map/all_gather | solution.py:70
  22.1 472.8 %all-gather.53.cloned.1.call-start = ((), (), s32[]{:S(2)}) async-start(), calls=%async_computation.29 | async-start | bytes 10485760 | tf_op jit(solution)/shard_map/all_gather | solution.py:71
  28.3 513.8 %all-gather.55.cloned.1.call-start = ((), (), s32[]{:S(2)}) async-start(), calls=%async_computation.30 | async-start | bytes 2621440 | tf_op jit(solution)/shard_map/all_gather | solution.py:67
  29.0 559.9 %all-gather.57.cloned.1.call-start = ((), (), s32[]{:S(2)}) async-start(), calls=%async_computation.31 | async-start | bytes 2621440 | tf_op jit(solution)/shard_map/all_gather | solution.py:68
  29.8 688.5 %all-gather.59.cloned.1.call-start = ((), (), s32[]{:S(2)}) async-start(), calls=%async_computation.32 | async-start | bytes 2621440 | tf_op jit(solution)/shard_map/all_gather | solution.py:66
  30.5 878.4 %all-gather.61.cloned.1.call-start = ((), (), s32[]{:S(2)}) async-start(), calls=%async_computation.33 | async-start | bytes 2621440 | tf_op jit(solution)/shard_map/all_gather | solution.py:69
  31.1 880.6 %all-gather.63.cloned.1.call-start = ((), (), s32[]{:S(2)}) async-start(), calls=%async_computation.34 | async-start | bytes 10485760 | tf_op jit(solution)/shard_map/all_gather | solution.py:70
  31.8 949.0 %all-gather.65.cloned.1.call-start = ((), (), s32[]{:S(2)}) async-start(), calls=%async_computation.35 | async-start | bytes 10485760 | tf_op jit(solution)/shard_map/all_gather | solution.py:71
  120.7 126.2 %collective-permute-start.2 = (bf16[2,256,1024]{2,1,0:T(8,128)(2,1)S(1)}, bf16[2,256,1024]{2,1,0:T(8,128)(2,1)}, u32[]{:S(2)}, u32[]{:S(2)}) collective-permute-start(bf16[2,256,1024]{2,1,0:T(8,128)(2,1)S(1)} %pad_maximum_fusion.2), channel_id=1, source_target_pairs={{0,20},{4,24},{8,28},{1,21},{5,25},{9,29},{2,22},{6,26},{10,30},{3... | collective-permute-start | bytes 3145736 | tf_op jit(solution)/shard_map/ppermute | solution.py:20
  602.6 121.6 %collective-permute-start.16 = (bf16[2,256,1024]{2,1,0:T(8,128)(2,1)S(1)}, bf16[2,256,1024]{2,1,0:T(8,128)(2,1)}, u32[]{:S(2)}, u32[]{:S(2)}) collective-permute-start(bf16[2,256,1024]{2,1,0:T(8,128)(2,1)S(1)} %pad_maximum_fusion.3), channel_id=1, source_target_pairs={{0,20},{4,24},{8,28},{1,21},{5,25},{9,29},{2,22},{6,26},{10,30},{3... | collective-permute-start | bytes 3145736 | tf_op jit(solution)/shard_map/ppermute | solution.py:20
  636.4 1594.1 %reduce-scatter.27.cloned.1.call-start = ((), (), s32[]{:S(2)}) async-start(), calls=%async_computation.19 | async-start | bytes 2621440 | tf_op jit(solution)/shard_map/reduce_scatter | solution.py:116
  1014.3 1216.2 %reduce-scatter.15.cloned.1.call-start = ((), (), s32[]{:S(2)}) async-start(), calls=%async_computation.13 | async-start | bytes 2621440 | tf_op jit(solution)/shard_map/reduce_scatter | solution.py:107
  1512.8 717.8 %reduce-scatter.25.cloned.1.call-start = ((), (), s32[]{:S(2)}) async-start(), calls=%async_computation.18 | async-start | bytes 2621440 | tf_op jit(solution)/shard_map/reduce_scatter | solution.py:116
  1602.3 628.3 %reduce-scatter.23.cloned.1.call-start = ((), (), s32[]{:S(2)}) async-start(), calls=%async_computation.17 | async-start | bytes 2621440 | tf_op jit(solution)/shard_map/reduce_scatter | solution.py:113
  1604.4 626.2 %reduce-scatter.19.cloned.1.call-start = ((), (), s32[]{:S(2)}) async-start(), calls=%async_computation.15 | async-start | bytes 2621440 | tf_op jit(solution)/shard_map/reduce_scatter | solution.py:110
  1609.9 620.7 %reduce-scatter.13.cloned.1.call-start = ((), (), s32[]{:S(2)}) async-start(), calls=%async_computation.12 | async-start | bytes 2621440 | tf_op jit(solution)/shard_map/reduce_scatter | solution.py:107
  2037.5 220.0 %reduce-scatter.21.cloned.1.call-start = ((), (), s32[]{:S(2)}) async-start(), calls=%async_computation.16 | async-start | bytes 2621440 | tf_op jit(solution)/shard_map/reduce_scatter | solution.py:113
  2197.2 254.7 %reduce-scatter.31.cloned.1.call-start = ((), (), s32[]{:S(2)}) async-start(), calls=%async_computation.21 | async-start | bytes 10485760 | tf_op jit(solution)/shard_map/reduce_scatter | solution.py:119
  2204.8 394.6 %reduce-scatter.35.cloned.1.call-start = ((), (), s32[]{:S(2)}) async-start(), calls=%async_computation.23 | async-start | bytes 10485760 | tf_op jit(solution)/shard_map/reduce_scatter | solution.py:122
  2213.2 534.4 %reduce-scatter.29.cloned.1.call-start = ((), (), s32[]{:S(2)}) async-start(), calls=%async_computation.20 | async-start | bytes 10485760 | tf_op jit(solution)/shard_map/reduce_scatter | solution.py:119
  2221.9 673.1 %reduce-scatter.33.cloned.1.call-start = ((), (), s32[]{:S(2)}) async-start(), calls=%async_computation.22 | async-start | bytes 10485760 | tf_op jit(solution)/shard_map/reduce_scatter | solution.py:122
  2230.4 848.5 %all-reduce.23.cloned.1.call-start = ((), (), s32[]{:S(2)}) async-start(), calls=%async_computation.36 | async-start | bytes 25165824 | tf_op jit(solution)/shard_map/psum | solution.py:154
  (234 other events, 9257.8 us)
Sparse Core Ops, SparseCore 0:
  10.3 45.2 all-gather.42
  57.8 44.6 all-gather.44
  104.6 44.6 all-gather.46
  150.8 45.0 all-gather.48
  197.8 147.7 all-gather.50
  347.6 147.1 all-gather.52
  497.0 45.0 all-gather.54
  544.2 44.6 all-gather.56
  590.5 44.6 all-gather.58
  636.6 45.0 all-gather.60
  683.9 147.5 all-gather.62
  833.5 147.3 all-gather.64
  1014.4 42.4 reduce-scatter.26
  1512.9 50.3 reduce-scatter.14
  1602.4 60.5 reduce-scatter.24
  1665.3 43.0 reduce-scatter.22
  1710.5 43.3 reduce-scatter.18
  2195.2 62.2 reduce-scatter.20
  2259.7 43.1 reduce-scatter.16
  2305.9 145.9 reduce-scatter.30
  2454.2 145.1 reduce-scatter.34
  2602.4 145.1 reduce-scatter.28
  2749.8 145.1 reduce-scatter.32
  2901.0 177.8 all-reduce.22
  (1 shorter events, 41.3 us)
where the time goes:
time: 3130 us; the launch traced here: 3110 us
  waiting for transfers between devices  1410 us (45%)
  matrix products  752 us (24%)
  local copies, waits for them, and re-layouts  360 us (12%)
  starting transfers between devices  232 us (7%)
  blocking collectives  169 us (5%)
  other arithmetic  168 us (5%)
    dot_general x148, matrix products, product(): return jnp.einsum(form, left, right, preferred_element_type=jnp.float32)  752 us
    ppermute x56, waiting for transfers between devices, from_behind(): return lax.ppermute(block, axis, route)  378 us
    reduce_scatter x2, waiting for transfers between devices, reduce_grads(): lax.psum_scatter(local_grads[4].astype(jnp.bfloat16), 'wsh', scatter_dime...  297 us
    reduce_scatter x2, waiting for transfers between devices, reduce_grads(): lax.psum_scatter(local_grads[5].astype(jnp.bfloat16), 'wsh', scatter_dime...  295 us
    ppermute x56, starting transfers between devices, from_behind(): return lax.ppermute(block, axis, route)  230 us
    psum x1, waiting for transfers between devices, reduce_grads(): lax.psum(shares[0].astype(jnp.bfloat16), 'ctx').astype(jnp.float32)  127 us
    all_gather x2, waiting for transfers between devices, fetch_forward(): lax.all_gather(shards[5], 'wsh', axis=1, tiled=True)  91.4 us
    all_gather x2, waiting for transfers between devices, fetch_forward(): lax.all_gather(shards[2], 'wsh', axis=0, tiled=True)  89 us
  transfers between devices with their start and end apart: 81, of which 32 were waited for; matrix products, arithmetic and copies ran while one was open for 38% of the time, Pallas kernels for 0%

commit v1 on v0

--- a/solution.py
+++ b/solution.py
@@ -1,6 +1,10 @@
+import functools
+
 import jax
 import jax.numpy as jnp
 from jax import lax
+from jax.experimental import pallas as pl
+from jax.experimental.pallas import tpu as pltpu
 from jax.sharding import PartitionSpec as P
 
 HEADS = 16
@@ -435,7 +439,7 @@
     return (grad_activation, local_grads)
 
 
-def body(
+def window_body(
     tokens,
     cotangent,
     doc_starts,
@@ -515,6 +519,654 @@
     return tuple(heads_out + stacked_grads)
 
 
+NN = (((1,), (0,)), ((), ()))
+NT = (((1,), (1,)), ((), ()))
+TN = (((0,), (0,)), ((), ()))
+LANES = 128
+QUERY_BLOCK = 256
+CORE, ALONG_X, ALONG_Y = 1, 2, 4
+
+
+def mm(left, right, dims=NN):
+    return lax.dot_general(left, right, dims, preferred_element_type=jnp.float32)
+
+
+def swap(block, mask):
+    devices = range(lax.axis_size("ctx"))
+    return lax.ppermute(block, "ctx", [(i, i ^ mask) for i in devices])
+
+
+def turn(block, distance):
+    count = lax.axis_size("wsh")
+    return lax.ppermute(block, "wsh", [(i, (i + distance) % count) for i in range(count)])
+
+
+def low(values_in):
+    return values_in.astype(jnp.bfloat16)
+
+
+def wide(values_in):
+    return values_in.astype(jnp.float32)
+
+
+def mask_features(label_col):
+    rows = label_col.shape[0]
+    lane = lax.broadcasted_iota(jnp.int32, (rows, LANES), 1)
+    hit = lax.rem(lane, HDIM) == jnp.broadcast_to(label_col, (rows, LANES))
+    return (
+        jnp.where(hit, neg_fill, 0.0).astype(jnp.bfloat16),
+        jnp.where(hit, 0.0, 1.0).astype(jnp.bfloat16),
+    )
+
+
+def fill_key_scratch(key_rows, label_col, key_mask):
+    lane = lax.broadcasted_iota(jnp.int32, key_rows.shape, 1)
+    _, key_features = mask_features(label_col)
+    key_mask[0] = jnp.where(lane < HDIM, key_rows, key_features)
+    key_mask[1] = jnp.where(lane < HDIM, key_features, key_rows)
+
+
+def attention_forward_kernel(
+    query_ref, key_ref, value_ref, label_ref, query_label_ref, mixed_ref, log_ref, key_mask, value_t
+):
+    @pl.when(pl.program_id(0) == 0)
+    def _():
+        fill_key_scratch(key_ref[...], label_ref[...], key_mask)
+        value_t[...] = value_ref[...].T
+
+    scaled = low(wide(query_ref[...]) * HDIM ** (-0.5))
+    lane = lax.broadcasted_iota(jnp.int32, scaled.shape, 1)
+    features, _ = mask_features(query_label_ref[...])
+    parts = []
+    for head in range(2):
+        mine = (lane < HDIM) if head == 0 else (lane >= HDIM)
+        scores = mm(key_mask[head], jnp.where(mine, scaled, features), NT)
+        peak = jnp.max(scores, axis=0, keepdims=True)
+        exponent = jnp.exp(scores - peak)
+        total = jnp.sum(exponent, axis=0, keepdims=True)
+        mixed = mm(value_t[pl.ds(HDIM * head, HDIM), :], low(exponent))
+        parts.append(mixed / total)
+        log_ref[pl.ds(head, 1), :] = peak + jnp.log(total)
+    mixed_ref[...] = low(jnp.concatenate(parts, axis=0).T)
+
+
+def attention_forward(packed, labels):
+    rows = packed.shape[0]
+    mine = pl.BlockSpec((QUERY_BLOCK, LANES), lambda i: (i, 0))
+    return pl.pallas_call(
+        attention_forward_kernel,
+        grid=(rows // QUERY_BLOCK,),
+        in_specs=[
+            mine,
+            pl.BlockSpec((rows, LANES), lambda i: (0, 1)),
+            pl.BlockSpec((rows, LANES), lambda i: (0, 2)),
+            pl.BlockSpec((rows, 1), lambda i: (0, 0)),
+            pl.BlockSpec((QUERY_BLOCK, 1), lambda i: (i, 0)),
+        ],
+        out_specs=[mine, pl.BlockSpec((2, QUERY_BLOCK), lambda i: (0, i))],
+        out_shape=[
+            jax.ShapeDtypeStruct((rows, LANES), jnp.bfloat16),
+            jax.ShapeDtypeStruct((2, rows), jnp.float32),
+        ],
+        scratch_shapes=[
+            pltpu.VMEM((2, rows, LANES), jnp.bfloat16),
+            pltpu.VMEM((LANES, rows), jnp.bfloat16),
+        ],
+        cost_estimate=pl.CostEstimate(
+            flops=16 * rows * rows * LANES, bytes_accessed=rows * 1024, transcendentals=2 * rows * rows
+        ),
+        name="attention_forward",
+    )(packed, packed, packed, labels, labels)
+
+
+def attention_backward_kernel(
+    query_ref,
+    key_ref,
+    value_ref,
+    label_ref,
+    query_label_ref,
+    grad_ref,
+    log_ref,
+    out_query_ref,
+    out_key_ref,
+    out_value_ref,
+    key_mask,
+    key_t,
+    key_sum,
+    value_sum,
+):
+    step = pl.program_id(0)
+
+    @pl.when(step == 0)
+    def _():
+        fill_key_scratch(key_ref[...], label_ref[...], key_mask)
+        key_t[...] = key_ref[...].T
+        key_sum[...] = jnp.zeros_like(key_sum)
+        value_sum[...] = jnp.zeros_like(value_sum)
+
+    scaled = low(wide(query_ref[...]) * HDIM ** (-0.5))
+    grad = grad_ref[...]
+    value_rows = value_ref[...]
+    lane = lax.broadcasted_iota(jnp.int32, scaled.shape, 1)
+    features, _ = mask_features(query_label_ref[...])
+    zero = jnp.zeros(scaled.shape, jnp.bfloat16)
+    parts = []
+    for head in range(2):
+        mine = (lane < HDIM) if head == 0 else (lane >= HDIM)
+        query_own = jnp.where(mine, scaled, zero)
+        grad_own = jnp.where(mine, grad, zero)
+        scores = mm(key_mask[head], jnp.where(mine, scaled, features), NT)
+        probability = jnp.exp(scores - log_ref[pl.ds(head, 1), :])
+        grad_prob = mm(value_rows, grad_own, NT)
+        delta = jnp.sum(probability * grad_prob, axis=0, keepdims=True)
+        grad_scores = low(probability * (grad_prob - delta))
+        key_sum[...] += mm(grad_scores, query_own)
+        value_sum[...] += mm(low(probability), grad_own)
+        parts.append(mm(key_t[pl.ds(HDIM * head, HDIM), :], grad_scores) * HDIM ** (-0.5))
+    out_query_ref[...] = low(jnp.concatenate(parts, axis=0).T)
+
+    @pl.when(step == pl.num_programs(0) - 1)
+    def _():
+        out_key_ref[...] = low(key_sum[...])
+        out_value_ref[...] = low(value_sum[...])
+
+
+def attention_backward(packed, labels, grad, log_all):
+    rows = packed.shape[0]
+    mine = pl.BlockSpec((QUERY_BLOCK, LANES), lambda i: (i, 0))
+    whole = pl.BlockSpec((rows, LANES), lambda i: (0, 0))
+    return pl.pallas_call(
+        attention_backward_kernel,
+        grid=(rows // QUERY_BLOCK,),
+        in_specs=[
+            mine,
+            pl.BlockSpec((rows, LANES), lambda i: (0, 1)),
+            pl.BlockSpec((rows, LANES), lambda i: (0, 2)),
+            pl.BlockSpec((rows, 1), lambda i: (0, 0)),
+            pl.BlockSpec((QUERY_BLOCK, 1), lambda i: (i, 0)),
+            mine,
+            pl.BlockSpec((2, QUERY_BLOCK), lambda i: (0, i)),
+        ],
+        out_specs=[mine, whole, whole],
+        out_shape=[jax.ShapeDtypeStruct((rows, LANES), jnp.bfloat16)] * 3,
+        scratch_shapes=[
+            pltpu.VMEM((2, rows, LANES), jnp.bfloat16),
+            pltpu.VMEM((LANES, rows), jnp.bfloat16),
+            pltpu.VMEM((rows, LANES), jnp.float32),
+            pltpu.VMEM((rows, LANES), jnp.float32),
+        ],
+        cost_estimate=pl.CostEstimate(
+            flops=16 * rows * rows * LANES, bytes_accessed=rows * 2048, transcendentals=2 * rows * rows
+        ),
+        name="attention_backward",
+    )(packed, packed, packed, labels, labels, grad, log_all)
+
+
+def cast_blocks(weight, order, block, dim):
+    layers = weight.shape[0]
+    count = order.shape[0]
+    shape = [weight.shape[1], weight.shape[2]]
+    shape[dim] = block
+
+    def read(layer, index, order_ref):
+        place = [0, 0]
+        place[dim] = order_ref[index]
+        return (layer, *place)
+
+    def kernel(order_ref, in_ref, out_ref):
+        out_ref[0] = low(in_ref[...])
+
+    return pl.pallas_call(
+        kernel,
+        grid_spec=pltpu.PrefetchScalarGridSpec(
+            num_scalar_prefetch=1,
+            grid=(layers, count),
+            in_specs=[pl.BlockSpec((1, *shape), read)],
+            out_specs=pl.BlockSpec((1, 1, *shape), lambda layer, index, order_ref: (layer, index, 0, 0)),
+        ),
+        out_shape=jax.ShapeDtypeStruct((layers, count, *shape), jnp.bfloat16),
+        cost_estimate=pl.CostEstimate(
+            flops=0, bytes_accessed=layers * count * shape[0] * shape[1] * 6, transcendentals=0
+        ),
+        name="cast_blocks",
+    )(order, weight)
+
+
+def place_blocks(near, far, order, layer, dim, widths, previous):
+    count = near.shape[0]
+    rows, columns = near.shape[1:]
+    parts = len(widths)
+    outs, specs = [], []
+    for width in widths:
+        shape = [rows, width]
+        full = list(shape)
+        full[dim] *= 2 * count
+
+        def where(index, order_ref, dim=dim):
+            place = [0, 0]
+            place[dim] = order_ref[index]
+            return (layer, *place)
+
+        outs.append(jax.ShapeDtypeStruct((LAYERS, *full), jnp.float32))
+        specs.append(pl.BlockSpec((1, *shape), where))
+
+    def kernel(order_ref, near_ref, far_ref, *refs):
+        out_refs = refs[-parts:]
+
+        def write(source):
+            begin = 0
+            for out_ref, width in zip(out_refs, widths):
+                out_ref[0] = wide(source[0, :, begin : begin + width])
+                begin += width
+
+        @pl.when(pl.program_id(0) < count)
+        def _():
+            write(near_ref)
+
+        @pl.when(pl.program_id(0) >= count)
+        def _():
+            write(far_ref)
+
+    held = [] if previous is None else list(previous)
+    return pl.pallas_call(
+        kernel,
+        grid_spec=pltpu.PrefetchScalarGridSpec(
+            num_scalar_prefetch=1,
+            grid=(2 * count,),
+            in_specs=[
+                pl.BlockSpec((1, rows, columns), lambda i, order_ref: (jnp.minimum(i, count - 1), 0, 0)),
+                pl.BlockSpec((1, rows, columns), lambda i, order_ref: (jnp.maximum(i - count, 0), 0, 0)),
+            ]
+            + [pl.BlockSpec(memory_space=pl.ANY)] * len(held),
+            out_specs=specs,
+        ),
+        out_shape=outs,
+        input_output_aliases={3 + i: i for i in range(len(held))},
+        cost_estimate=pl.CostEstimate(
+            flops=0, bytes_accessed=12 * count * rows * columns, transcendentals=0
+        ),
+        name="place_blocks",
+    )(order, near, far, *held)
+
+
+def block_columns(values_in, order, width):
+    return jnp.concatenate(
+        [lax.dynamic_slice_in_dim(values_in, block * width, width, 1) for block in order], axis=1
+    )
+
+
+def norm_forward(values_in, gain_row, shift_row):
+    centre = values_in - jnp.mean(values_in, axis=-1, keepdims=True)
+    spread = jnp.mean(centre * centre, axis=-1, keepdims=True)
+    inverse = lax.rsqrt(spread + epsilon)
+    unit = centre * inverse
+    return (unit * gain_row + shift_row, unit, inverse)
+
+
+def norm_backward(grad, unit, inverse, gain_row):
+    grad_unit = grad * gain_row
+    back = inverse * (
+        grad_unit
+        - jnp.mean(grad_unit, axis=-1, keepdims=True)
+        - unit * jnp.mean(grad_unit * unit, axis=-1, keepdims=True)
+    )
+    return (back, jnp.sum(grad * unit, axis=0), jnp.sum(grad, axis=0))
+
+
+def spread_tokens(rows_in):
+    half = rows_in.shape[1] // 2
+    left, right = rows_in[:, :half], rows_in[:, half:]
+    left_pair = jnp.stack([left, swap(left, ALONG_X)])
+    right_pair = jnp.stack([right, swap(right, ALONG_Y)])
+    left_far = swap(left_pair, ALONG_Y)
+    right_far = swap(right_pair, ALONG_X)
+    left_all = jnp.concatenate([left_pair, left_far])
+    right_all = jnp.stack([right_pair[0], right_far[0], right_pair[1], right_far[1]])
+    near = jnp.concatenate([left_all, right_all], axis=2)
+    far = swap(near, CORE)
+    both = jnp.stack([near, far], axis=1)
+    return both.reshape(8 * rows_in.shape[0], rows_in.shape[1])
+
+
+def collect_tokens(partial):
+    rows = partial.shape[0] // 8
+    width = partial.shape[1]
+    blocks = partial.reshape(4, 2, rows, width)
+    near = blocks[:, 0] + wide(swap(low(blocks[:, 1]), CORE))
+    half = width // 2
+    left, right = near[:, :, :half], near[:, :, half:]
+    left_sent = swap(low(jnp.stack([left[1], left[3]])), ALONG_X)
+    right_sent = swap(low(right[2:]), ALONG_Y)
+    left = jnp.stack([left[0], left[2]]) + wide(left_sent)
+    right = right[:2] + wide(right_sent)
+    left = left[0] + wide(swap(low(left[1]), ALONG_Y))
+    right = right[0] + wide(swap(low(right[1]), ALONG_X))
+    return jnp.concatenate([left, right], axis=1)
+
+
+def plane_pieces(piece, first, second):
+    pair = jnp.stack([piece, swap(piece, first)])
+    near = jnp.concatenate([pair, swap(pair, second)])
+    return (near, swap(near, CORE))
+
+
+def exchange_heads(blocks, rows):
+    parts = [blocks[k * rows : (k + 1) * rows] for k in range(8)]
+    return [parts[0]] + [swap(parts[k], k) for k in range(1, 8)]
+
+
+def head_split_body(
+    tokens,
+    cotangent,
+    doc_starts,
+    doc_lengths,
+    query_weight,
+    key_weight,
+    value_weight,
+    out_weight,
+    inner_weight,
+    outer_weight,
+    query_bias,
+    value_bias,
+    out_bias,
+    inner_bias,
+    outer_bias,
+    first_gain,
+    first_shift,
+    second_gain,
+    second_shift,
+):
+    rows = tokens.shape[1]
+    width = tokens.shape[2]
+    here = lax.axis_index("ctx")
+    plane = lax.axis_index("wsh")
+    planes = lax.axis_size("wsh")
+    shard = width // planes
+    hidden = inner_weight.shape[2]
+    piece = hidden // 8
+    core = here % 2
+    chip = here // 2
+    relative = jnp.arange(8, dtype=jnp.int32)
+    turned = [(plane - r) % planes for r in range(planes)]
+    unturned = turned
+    positions = ((here ^ relative)[:, None] * rows + jnp.arange(rows, dtype=jnp.int32)).reshape(-1)
+    labels = doc_labels(positions, doc_starts[0], doc_lengths[0])[:, None]
+
+    inner_order = core * 4 + (chip ^ jnp.arange(4, dtype=jnp.int32))
+    inner_own = cast_blocks(inner_weight, inner_order, piece, 1)
+    outer_own = cast_blocks(outer_weight, inner_order, piece, 0)
+    joint_own = jnp.concatenate(
+        [
+            low(lax.dynamic_slice_in_dim(weight, here * LANES, LANES, 2))
+            for weight in (query_weight, key_weight, value_weight)
+        ],
+        axis=2,
+    )
+    small_own = low(
+        jnp.concatenate(
+            [
+                query_bias,
+                value_bias,
+                out_bias,
+                outer_bias,
+                first_gain,
+                first_shift,
+                second_gain,
+                second_shift,
+                inner_bias,
+            ],
+            axis=1,
+        )
+    )
+    small_turned = jnp.stack([small_own] + [turn(small_own, r) for r in range(1, planes)])
+    small_all = jnp.stack(
+        [lax.dynamic_index_in_dim(small_turned, unturned[i], 0, keepdims=False) for i in range(planes)], axis=1
+    )
+
+    def small(layer, index):
+        return small_all[layer, :, index * shard : (index + 1) * shard].reshape(width)
+
+    inner_bias_all = small_all[:, :, 8 * shard :].reshape(LAYERS, hidden)
+
+    def gather_joint(layer):
+        own = joint_own[layer]
+        stack = jnp.stack([own] + [turn(own, r) for r in range(1, planes)])
+        return jnp.concatenate(
+            [lax.dynamic_index_in_dim(stack, unturned[i], 0, keepdims=False) for i in range(planes)], axis=0
+        )
+
+    def gather_inner(layer):
+        own = inner_own[layer]
+        others = jnp.concatenate([turn(own[0], r) for r in range(1, planes)], axis=0)
+        by_x = swap(others, ALONG_X)
+        near_y = swap(others, ALONG_Y)
+        far_y = swap(by_x, ALONG_Y)
+        return jnp.concatenate(
+            [jnp.concatenate([own[j], part], axis=0) for j, part in enumerate((others, by_x, near_y, far_y))],
+            axis=1,
+        )
+
+    def gather_outer(layer):
+        own = outer_own[layer]
+        others = jnp.concatenate([turn(own[0], r) for r in range(1, planes)], axis=1)
+        by_y = swap(others, ALONG_Y)
+        near_x = swap(others, ALONG_X)
+        far_x = swap(by_y, ALONG_X)
+        return jnp.concatenate(
+            [jnp.concatenate([own[j], part], axis=1) for j, part in enumerate((others, near_x, by_y, far_x))],
+            axis=0,
+        )
+
+    activation = tokens[0]
+    stashed = []
+    outputs = []
+    for layer in range(LAYERS):
+        joint = gather_joint(layer)
+        out_full = lax.all_gather(low(out_weight[layer]), "wsh", axis=0, tiled=True)
+        inner_full = gather_inner(layer)
+        outer_full = gather_outer(layer)
+        first_gain_row, first_shift_row = wide(small(layer, 4)), wide(small(layer, 5))
+        second_gain_row, second_shift_row = wide(small(layer, 6)), wide(small(layer, 7))
+
+        everyone = spread_tokens(activation)
+        query_bias_own = lax.dynamic_slice_in_dim(small(layer, 0), here * LANES, LANES, 0)
+        value_bias_own = lax.dynamic_slice_in_dim(small(layer, 1), here * LANES, LANES, 0)
+        joint_bias = jnp.concatenate([query_bias_own, jnp.zeros_like(query_bias_own), value_bias_own])
+        packed = low(mm(everyone, joint) + wide(joint_bias))
+        mixed, log_all = attention_forward(packed, labels)
+        mixed_heads = jnp.concatenate(exchange_heads(mixed, rows), axis=1)
+        mixed_tokens = block_columns(mixed_heads, [here ^ k for k in range(8)], LANES)
+        first_pre = wide(activation) + (mm(mixed_tokens, out_full) + wide(small(layer, 2)))
+        hidden_rows, first_unit, first_inverse = norm_forward(first_pre, first_gain_row, first_shift_row)
+        hidden_turned = block_columns(low(hidden_rows), turned, shard)
+        hidden_pair = jnp.concatenate([hidden_turned, swap(hidden_turned, CORE)], axis=0)
+        inner_bias_own = jnp.concatenate(
+            [lax.dynamic_slice_in_dim(inner_bias_all[layer], inner_order[j] * piece, piece, 0) for j in range(4)]
+        )
+        inner_pre = mm(hidden_pair, inner_full) + wide(inner_bias_own)
+        below = 0.5 * (1.0 + lax.erf(inner_pre * (2.0**-0.5)))
+        active = low(inner_pre * below)
+        slope = low(below + inner_pre * jnp.exp(-0.5 * inner_pre * inner_pre) * ((2.0 * jnp.pi) ** -0.5))
+        outer_pair = mm(active, outer_full)
+        outer_turned = outer_pair[:rows] + wide(swap(low(outer_pair[rows:]), CORE))
+        outer_out = block_columns(outer_turned, unturned, shard)
+        second_pre = hidden_rows + (outer_out + wide(small(layer, 3)))
+        result, second_unit, second_inverse = norm_forward(second_pre, second_gain_row, second_shift_row)
+        stashed.append(
+            (
+                everyone,
+                packed,
+                log_all,
+                mixed_tokens,
+                first_unit,
+                first_inverse,
+                hidden_pair,
+                active,
+                slope,
+                second_unit,
+                second_inverse,
+                joint,
+                out_full,
+                inner_full,
+                outer_full,
+                first_gain_row,
+                second_gain_row,
+            )
+        )
+        activation = low(result)
+        outputs.append(activation)
+
+    joint_order = here ^ jnp.array([0, 2, 4, 6, 1, 3, 5, 7], jnp.int32)
+    swapped_order = here ^ jnp.array([0, 4, 2, 6, 1, 5, 3, 7], jnp.int32)
+    inner_place = (joint_order % 2) * 4 + joint_order // 2
+    outer_place = (swapped_order % 2) * 4 + swapped_order // 2
+    gradient = wide(cotangent[0])
+    small_grads = [None] * LAYERS
+    out_grads = [None] * LAYERS
+    joint_out = inner_out = outer_out = None
+    for layer in reversed(range(LAYERS)):
+        (
+            everyone,
+            packed,
+            log_all,
+            mixed_tokens,
+            first_unit,
+            first_inverse,
+            hidden_pair,
+            active,
+            slope,
+            second_unit,
+            second_inverse,
+            joint,
+            out_full,
+            inner_full,
+            outer_full,
+            first_gain_row,
+            second_gain_row,
+        ) = stashed[layer]
+        grad_second, grad_second_gain, grad_second_shift = norm_backward(
+            gradient, second_unit, second_inverse, second_gain_row
+        )
+        grad_outer = low(grad_second)
+        grad_outer_bias = jnp.sum(wide(grad_outer), axis=0)
+        grad_turned = block_columns(grad_outer, turned, shard)
+        grad_pair = jnp.concatenate([grad_turned, swap(grad_turned, CORE)], axis=0)
+        grad_inner = low(mm(grad_pair, outer_full, NT) * wide(slope))
+        hidden_back = mm(grad_inner, inner_full, NT)
+        hidden_back = hidden_back[:rows] + wide(swap(low(hidden_back[rows:]), CORE))
+        grad_hidden = grad_second + block_columns(hidden_back, unturned, shard)
+        grad_outer_weight = low(mm(active, grad_pair, TN))
+        grad_inner_weight = low(mm(hidden_pair, grad_inner, TN))
+        grad_inner_bias = jnp.sum(wide(grad_inner), axis=0)
+        grad_first, grad_first_gain, grad_first_shift = norm_backward(
+            grad_hidden, first_unit, first_inverse, first_gain_row
+        )
+        grad_branch = low(grad_first)
+        grad_out_bias = jnp.sum(wide(grad_branch), axis=0)
+        grad_mixed_tokens = low(mm(grad_branch, out_full, NT))
+        grad_mixed = jnp.concatenate(
+            [
+                part if k == 0 else swap(part, k)
+                for k, part in enumerate(
+                    lax.dynamic_slice_in_dim(grad_mixed_tokens, (here ^ k) * LANES, LANES, 1) for k in range(8)
+                )
+            ],
+            axis=0,
+        )
+        grad_out_weight = low(mm(mixed_tokens, grad_branch, TN))
+        grad_query, grad_key, grad_value = attention_backward(packed, labels, grad_mixed, log_all)
+        grad_packed = jnp.concatenate([grad_query, grad_key, grad_value], axis=1)
+        gradient = grad_first + collect_tokens(mm(grad_packed, joint, NT))
+        grad_joint = mm(everyone, grad_packed, TN)
+        joint_bias_grad = jnp.sum(wide(grad_packed), axis=0)
+
+        joint_parts = [
+            lax.dynamic_slice_in_dim(grad_joint, ((plane + s) % planes) * shard, shard, 0) for s in range(planes)
+        ]
+        joint_sum = joint_parts[0]
+        for s in range(1, planes):
+            joint_sum = joint_sum + wide(turn(low(joint_parts[s]), s))
+        blocks = [grad_inner_weight[:, j * piece : (j + 1) * piece] for j in range(4)]
+        came = swap(jnp.stack([blocks[1], blocks[3]]), ALONG_X)
+        kept = (wide(blocks[0]) + wide(came[0]), low(wide(blocks[2]) + wide(came[1])))
+        inner_sum = low(kept[0] + wide(swap(kept[1], ALONG_Y)))
+        inner_total = wide(inner_sum[:shard])
+        for r in range(1, planes):
+            inner_total = inner_total + wide(turn(inner_sum[r * shard : (r + 1) * shard], planes - r))
+        blocks = [grad_outer_weight[j * piece : (j + 1) * piece] for j in range(4)]
+        came = swap(jnp.stack([blocks[2], blocks[3]]), ALONG_Y)
+        kept = (wide(blocks[0]) + wide(came[0]), low(wide(blocks[1]) + wide(came[1])))
+        outer_sum = low(kept[0] + wide(swap(kept[1], ALONG_X)))
+        outer_total = wide(outer_sum[:, :shard])
+        for r in range(1, planes):
+            outer_total = outer_total + wide(turn(outer_sum[:, r * shard : (r + 1) * shard], planes - r))
+        joint_near, joint_far = plane_pieces(low(joint_sum), ALONG_X, ALONG_Y)
+        inner_near, inner_far = plane_pieces(low(inner_total), ALONG_X, ALONG_Y)
+        outer_near, outer_far = plane_pieces(low(outer_total), ALONG_Y, ALONG_X)
+        joint_out = place_blocks(joint_near, joint_far, joint_order, layer, 1, (LANES,) * 3, joint_out)
+        inner_out = place_blocks(inner_near, inner_far, inner_place, layer, 1, (piece,), inner_out)
+        outer_out = place_blocks(outer_near, outer_far, outer_place, layer, 0, (shard,), outer_out)
+        out_share = lax.psum_scatter(grad_out_weight, "wsh", scatter_dimension=0, tiled=True)
+        out_grads[layer] = wide(lax.psum(out_share, "ctx"))
+
+        placed_query = lax.dynamic_update_slice(
+            jnp.zeros((width,), jnp.float32), joint_bias_grad[:LANES], (here * LANES,)
+        )
+        placed_value = lax.dynamic_update_slice(
+            jnp.zeros((width,), jnp.float32), joint_bias_grad[2 * LANES :], (here * LANES,)
+        )
+        placed_inner = jnp.zeros((hidden,), jnp.float32)
+        for j in range(4):
+            placed_inner = lax.dynamic_update_slice(
+                placed_inner, grad_inner_bias[j * piece : (j + 1) * piece], (inner_order[j] * piece,)
+            )
+        small_grads[layer] = jnp.concatenate(
+            [
+                row.reshape(planes, -1)
+                for row in (
+                    placed_query,
+                    placed_value,
+                    grad_out_bias,
+                    grad_outer_bias,
+                    grad_first_gain,
+                    grad_first_shift,
+                    grad_second_gain,
+                    grad_second_shift,
+                    placed_inner,
+                )
+            ],
+            axis=1,
+        )
+    small_sum = lax.psum(jnp.stack(small_grads), ("ctx", "wsh"))
+    small_mine = lax.dynamic_index_in_dim(small_sum, plane, 1, keepdims=False)
+    small_outs = [small_mine[:, i * shard : (i + 1) * shard] for i in range(8)]
+    inner_bias_out = small_mine[:, 8 * shard :]
+    return (
+        outputs[0][None],
+        outputs[1][None],
+        low(gradient)[None],
+        *joint_out,
+        jnp.stack(out_grads),
+        inner_out[0],
+        outer_out[0],
+        small_outs[0],
+        small_outs[1],
+        small_outs[2],
+        inner_bias_out,
+        small_outs[3],
+        small_outs[4],
+        small_outs[5],
+        small_outs[6],
+        small_outs[7],
+    )
+
+
+def choose_body(mesh):
+    if mesh.shape["ctx"] == 8 and HEADS // 8 == 2:
+        return head_split_body
+    return window_body
+
+
 def solution(mesh):
     in_specs = (
         P("wsh", "ctx", None),
@@ -557,4 +1209,4 @@
         P(None, "wsh"),
         P(None, "wsh"),
     )
-    return jax.shard_map(body, mesh=mesh, in_specs=in_specs, out_specs=out_specs, check_vma=False)
+    return jax.shard_map(choose_body(mesh), mesh=mesh, in_specs=in_specs, out_specs=out_specs, check_vma=False)

time: 3130 us -> 1310 us (0.42)
  waiting for transfers between devices: 1410 us -> 575 us
  matrix products: 752 us -> 120 us
  local copies, waits for them, and re-layouts: 360 us -> 101 us
  Pallas kernels: 0 us -> 170 us
  blocking collectives: 169 us -> 0 us
  starting transfers between devices: 232 us -> 181 us
  other arithmetic: 168 us -> 129 us
    reduce_scatter x12 -> x2, waiting for transfers between devices: 665 us -> 0.01 us  [head_split_body(): lax.psum_scatter(grad_out_weight, 'wsh', scatter_dimension=0, tiled=True)]
    dot_general x148 -> x24, matrix products: 752 us -> 120 us  [mm(): lax.dot_general(left, right, dims, preferred_element_type=jnp.float32)]
    all_gather x12 -> x2, waiting for transfers between devices: 234 us -> 0.04 us  [head_split_body(): out_full = lax.all_gather(low(out_weight[layer]), 'wsh', axis=0, tiled=True)]
    pallas_call x0 -> x12, Pallas kernels: none -> 170 us  [the longest x2 65.9 us: attention_backward(): pl.pallas_call(attention_backward_kernel, grid=(rows // QUERY_BLOCK,), in...]
    all_gather x18 -> x0, blocking collectives: 132 us -> none  [the longest x2 17.8 us: fetch_forward(): lax.all_gather(shards[9], 'wsh', axis=0, tiled=True)]
    dynamic_slice x96 -> x15, local copies, waits for them, and re-layouts: 108 us -> 2.69 us  [the longest x2 0.94 us: head_split_body(): lax.dynamic_slice_in_dim(grad_mixed_tokens, (here ^ k) * LANES, LANES, 1)]
    ppermute x56 -> x133, waiting for transfers between devices: 378 us -> 476 us  [the longest x94 262 us: swap(): return lax.ppermute(block, 'ctx', [(i, i ^ mask) for i in devices])]
    concatenate x0 -> x17, other arithmetic: none -> 54.9 us  [the longest x2 42.2 us: gather_inner(): jnp.concatenate([jnp.concatenate([own[j], part], axis=0) for j, part in e...]
  transfers between devices with their start and end apart: 81 -> 139, of which waited for: 32 -> 67; matrix products, arithmetic and copies ran while one was open for 38% -> 20% of each run, Pallas kernels for 0% -> 13%
where the time goes in v1:
time: 1310 us; the launch traced here: 1300 us
  waiting for transfers between devices  575 us (44%)
  starting transfers between devices  181 us (14%)
  Pallas kernels  170 us (13%)
  other arithmetic  129 us (10%)
  matrix products  120 us (9%)
  local copies, waits for them, and re-layouts  101 us (8%)
  between operations  20.7 us (2%)
    ppermute x94, waiting for transfers between devices, swap(): return lax.ppermute(block, 'ctx', [(i, i ^ mask) for i in devices])  262 us
    ppermute x39, waiting for transfers between devices, turn(): lax.ppermute(block, 'wsh', [(i, (i + distance) % count) for i in range(co...  213 us
    ppermute x94, starting transfers between devices, swap(): return lax.ppermute(block, 'ctx', [(i, i ^ mask) for i in devices])  126 us
    dot_general x24, matrix products, mm(): lax.dot_general(left, right, dims, preferred_element_type=jnp.float32)  120 us
    pallas_call x2, Pallas kernels, attention_backward(): pl.pallas_call(attention_backward_kernel, grid=(rows // QUERY_BLOCK,), in...  65.9 us
    psum x1, waiting for transfers between devices, head_split_body(): out_grads[layer] = wide(lax.psum(out_share, 'ctx'))  54.1 us
    ppermute x39, starting transfers between devices, turn(): lax.ppermute(block, 'wsh', [(i, (i + distance) % count) for i in range(co...  53.7 us
    pallas_call x2, Pallas kernels, attention_forward(): pl.pallas_call(attention_forward_kernel, grid=(rows // QUERY_BLOCK,), in_...  49 us
  transfers between devices with their start and end apart: 139, of which 67 were waited for; matrix products, arithmetic and copies ran while one was open for 20% of the time, Pallas kernels for 13%

profile of v1, /device:TPU:9, one launch (start us, length us, event | category | flops | bytes accessed | tf_op | source)
XLA Modules:
  0.0 1296.4 jit_solution(6091506452497818843)
XLA Ops:
  57.7 10.7 collective-permute-done.3
  108.4 15.8 %collective-permute-done.19 = bf16[256,512]{1,0:T(8,128)(2,1)S(1)} collective-permute-done((bf16[256,512]{1,0:T(8,128)(2,1)S(1)}, bf16[256,512]{1,0:T(8,128)(2,1)S(1)}, u32[]{:S(2)}, u32[]{:S(2)}) %collective-permute-start.19) | collective-permute-done | bytes 262176 | tf_op jit(solution)/shard_map/ppermute | solution.py:541
  152.5 24.5 %attention_forward.2 = (bf16[2048,128]{1,0:T(8,128)(2,1)}, f32[2,2048]{1,0:T(2,128)}) custom-call(bf16[2048,384]{1,0:T(8,128)(2,1)} %add_convert_fusion.1.query_ref.key_ref.value_ref, bf16[2048,384]{1,0:T(8,128)(2,1)} %add_convert_fusion.1.query_ref.key_ref.value_ref, bf16[2048,384]{1,0:T(8,128)(2,1)} %add_convert_fusion.1.query_ref.key_ref.value_ref, ...), custom_call_target="tpu_custom_call" | custom-call | flops 8589934592 | bytes 2097152 | tf_op jit(solution)/shard_map/attention_forward/pallas_call | solution.py:596
  184.2 33.4 %collective-permute-done.12 = bf16[256,128]{1,0:T(8,128)(2,1)S(1)} collective-permute-done((bf16[256,128]{1,0:T(8,128)(2,1)S(1)}, bf16[256,128]{1,0:T(8,128)(2,1)S(1)}, u32[]{:S(2)}, u32[]{:S(2)}) %collective-permute-start.12) | collective-permute-done | bytes 65568 | tf_op jit(solution)/shard_map/ppermute | solution.py:536
  245.2 27.8 %maximum_maximum_fusion = bf16[1024,2048]{1,0:T(8,128)(2,1)S(1)} fusion(bf16[768,512]{1,0:T(8,128)(2,1)} %collective-permute-done.24, bf16[256,512]{1,0:T(8,128)(2,1)S(1)} %get-tuple-element.121, bf16[768,512]{1,0:T(8,128)(2,1)S(1)} %collective-permute-done.23, bf16[256,512]{1,0:T(8,128)(2,1)S(1)} %copy-done.41, ...), kind=kLoop, calls=%fused_computation.19 | loop fusion | flops 41943040 | bytes 8388608 | tf_op jit(solution)/shard_map/concatenate | solution.py:944
  280.2 17.0 %fusion.103 = f32[512,1024]{1,0:T(8,128)S(1)} fusion(bf16[512,2048]{1,0:T(8,128)(2,1)S(1)} %get-tuple-element.280, bf16[512,768]{1,0:T(8,128)(2,1)} %collective-permute-done.30, bf16[512,256]{1,0:T(8,128)(2,1)S(1)} %copy-done.105, bf16[512,768]{1,0:T(8,128)(2,1)} %collective-permute-done.29, bf16[512,256]{1,0:T(8,128)(2,1)S(1)} %copy-done.106, ...), kind=kOutput, calls=%fused_computation.510 | convolution fusion | flops 2189426688 | bytes 8388608 | tf_op jit(solution)/shard_map/dot_general | solution.py:531
  310.4 10.7 collective-permute-done.35
  338.7 27.3 %collective-permute-done.49 = bf16[256,512]{1,0:T(8,128)(2,1)} collective-permute-done((bf16[256,512]{1,0:T(8,128)(2,1)}, bf16[256,512]{1,0:T(8,128)(2,1)}, u32[]{:S(2)}, u32[]{:S(2)}) %collective-permute-start.49) | collective-permute-done | bytes 262176 | tf_op jit(solution)/shard_map/ppermute | solution.py:541
  370.8 14.8 %collective-permute-done.50 = bf16[256,512]{1,0:T(8,128)(2,1)} collective-permute-done((bf16[256,512]{1,0:T(8,128)(2,1)}, bf16[256,512]{1,0:T(8,128)(2,1)}, u32[]{:S(2)}, u32[]{:S(2)}) %collective-permute-start.50) | collective-permute-done | bytes 262176 | tf_op jit(solution)/shard_map/ppermute | solution.py:541
  390.2 13.7 %collective-permute-done.55 = bf16[512,256]{1,0:T(8,128)(2,1)S(1)} collective-permute-done((bf16[512,256]{1,0:T(8,128)(2,1)}, bf16[512,256]{1,0:T(8,128)(2,1)S(1)}, u32[]{:S(2)}, u32[]{:S(2)}) %collective-permute-start.55) | collective-permute-done | bytes 262176 | tf_op jit(solution)/shard_map/ppermute | solution.py:541
  415.7 24.5 %attention_forward.3 = (bf16[2048,128]{1,0:T(8,128)(2,1)}, f32[2,2048]{1,0:T(2,128)}) custom-call(bf16[2048,384]{1,0:T(8,128)(2,1)} %add_convert_fusion.query_ref.key_ref.value_ref, bf16[2048,384]{1,0:T(8,128)(2,1)} %add_convert_fusion.query_ref.key_ref.value_ref, bf16[2048,384]{1,0:T(8,128)(2,1)} %add_convert_fusion.query_ref.key_ref.value_ref, ...), custom_call_target="tpu_custom_call" | custom-call | flops 8589934592 | bytes 2097152 | tf_op jit(solution)/shard_map/attention_forward/pallas_call | solution.py:596
  447.1 34.6 %collective-permute-done.41 = bf16[256,128]{1,0:T(8,128)(2,1)S(1)} collective-permute-done((bf16[256,128]{1,0:T(8,128)(2,1)S(1)}, bf16[256,128]{1,0:T(8,128)(2,1)S(1)}, u32[]{:S(2)}, u32[]{:S(2)}) %collective-permute-start.41) | collective-permute-done | bytes 65568 | tf_op jit(solution)/shard_map/ppermute | solution.py:536
  509.7 14.3 %maximum_maximum_fusion.2 = bf16[1024,2048]{1,0:T(8,128)(2,1)S(1)} fusion(bf16[768,512]{1,0:T(8,128)(2,1)} %collective-permute-done.53, bf16[256,512]{1,0:T(8,128)(2,1)S(1)} %copy-done.39, bf16[768,512]{1,0:T(8,128)(2,1)} %collective-permute-done.52, bf16[256,512]{1,0:T(8,128)(2,1)S(1)} %copy-done.40, bf16[768,512]{1,0:T(8,128)(2,1)} %collective-permute-done.51, ...), kind=kLoop, calls=%fused_computation.22 | loop fusion | flops 41943040 | bytes 8388608 | tf_op jit(solution)/shard_map/concatenate | solution.py:944
  531.1 16.7 %fusion.102 = f32[512,1024]{1,0:T(8,128)S(1)} fusion(bf16[512,2048]{1,0:T(8,128)(2,1)S(1)} %get-tuple-element.284, bf16[512,768]{1,0:T(8,128)(2,1)} %collective-permute-done.59, bf16[512,256]{1,0:T(8,128)(2,1)S(1)} %copy-done.111, bf16[512,768]{1,0:T(8,128)(2,1)} %collective-permute-done.58, bf16[512,256]{1,0:T(8,128)(2,1)S(1)} %copy-done.112, ...), kind=kOutput, calls=%fused_computation.509 | convolution fusion | flops 2189426688 | bytes 8388608 | tf_op jit(solution)/shard_map/dot_general | solution.py:531
  612.5 33.4 %collective-permute-done.64 = bf16[256,128]{1,0:T(8,128)(2,1)S(1)} collective-permute-done((bf16[256,128]{1,0:T(8,128)(2,1)S(1)}, bf16[256,128]{1,0:T(8,128)(2,1)S(1)}, u32[]{:S(2)}, u32[]{:S(2)}) %collective-permute-start.64) | collective-permute-done | bytes 65568 | tf_op jit(solution)/shard_map/ppermute | solution.py:536
  664.7 33.0 %attention_backward.2 = (bf16[2048,128]{1,0:T(8,128)(2,1)}, bf16[2048,128]{1,0:T(8,128)(2,1)}, bf16[2048,128]{1,0:T(8,128)(2,1)}) custom-call(bf16[2048,384]{1,0:T(8,128)(2,1)} %add_convert_fusion.query_ref.key_ref.value_ref, bf16[2048,384]{1,0:T(8,128)(2,1)} %add_convert_fusion.query_ref.key_ref.value_ref, ...), custom_call_target="tpu_custom_call" | custom-call | flops 8589934592 | bytes 4194304 | tf_op jit(solution)/shard_map/attention_backward/pallas_call | solution.py:678
  752.2 15.9 %collective-permute-done.110 = bf16[1024,512]{1,0:T(8,128)(2,1)S(1)} collective-permute-done((bf16[1024,512]{1,0:T(8,128)(2,1)S(1)}, bf16[1024,512]{1,0:T(8,128)(2,1)S(1)}, u32[]{:S(2)}, u32[]{:S(2)}) %collective-permute-start.110) | collective-permute-done | bytes 1048608 | tf_op jit(solution)/shard_map/ppermute | solution.py:536
  876.8 32.9 %attention_backward.3 = (bf16[2048,128]{1,0:T(8,128)(2,1)}, bf16[2048,128]{1,0:T(8,128)(2,1)}, bf16[2048,128]{1,0:T(8,128)(2,1)}) custom-call(bf16[2048,384]{1,0:T(8,128)(2,1)} %add_convert_fusion.1.query_ref.key_ref.value_ref, bf16[2048,384]{1,0:T(8,128)(2,1)} %add_convert_fusion.1.query_ref.key_ref.value_ref, ...), custom_call_target="tpu_custom_call" | custom-call | flops 8589934592 | bytes 4194304 | tf_op jit(solution)/shard_map/attention_backward/pallas_call | solution.py:678
  984.1 12.0 collective-permute-done.131
  1003.5 44.9 %all-reduce.4.cloned.1.call-done = f32[2,4,3072]{2,0,1:T(2,128)} async-done(((f32[2,4,3072]{2,0,1:T(2,128)}), f32[2,4,3072]{2,0,1:T(2,128)}) %all-reduce.4.cloned.1.call-update) | async-done | bytes 98320 | tf_op jit(solution)/shard_map/psum | solution.py:1140
  1062.3 13.4 %collective-permute-done.102 = bf16[1024,512]{1,0:T(8,128)(2,1)S(1)} collective-permute-done((bf16[1024,512]{1,0:T(8,128)(2,1)S(1)}, bf16[1024,512]{1,0:T(8,128)(2,1)S(1)}, u32[]{:S(2)}, u32[]{:S(2)}) %collective-permute-start.102) | collective-permute-done | bytes 1048608 | tf_op jit(solution)/shard_map/ppermute | solution.py:536
  1105.1 19.0 %collective-permute-done.104 = bf16[256,512]{1,0:T(8,128)(2,1)S(1)} collective-permute-done((bf16[256,512]{1,0:T(8,128)(2,1)S(1)}, bf16[256,512]{1,0:T(8,128)(2,1)S(1)}, u32[]{:S(2)}, u32[]{:S(2)}) %collective-permute-start.104) | collective-permute-done | bytes 262176 | tf_op jit(solution)/shard_map/ppermute | solution.py:541
  1133.7 10.6 collective-permute-done.119
  1218.4 54.1 %all-reduce.6.cloned.1.call-done = (bf16[1,256,1024]{2,1,0:T(8,128)(2,1)}, bf16[1,256,1024]{2,1,0:T(8,128)(2,1)}) async-done(((bf16[1,256,1024]{2,1,0:T(8,128)(2,1)}, bf16[1,256,1024]{2,1,0:T(8,128)(2,1)}), (bf16[1,256,1024]{2,1,0:T(8,128)(2,1)}, bf16[1,256,1024]{2,1,0:T(8,128)(2,1)})) %all-reduce.6.cloned.1.call-update) | async-done | bytes 1048592 | tf_op jit(solution)/shard_map/psum | solution.py:1110
  (1020 shorter events, 720.4 us)
Async XLA Ops:
  7.2 233.5 %all-gather.5.cloned.1.call-start = ((), (), s32[]{:S(2)}) async-start(), calls=%async_computation.5 | async-start | bytes 2621440 | tf_op jit(solution)/shard_map/all_gather | solution.py:965
  22.7 480.7 %all-gather.7.cloned.1.call-start = ((), (), s32[]{:S(2)}) async-start(), calls=%async_computation.6 | async-start | bytes 2621440 | tf_op jit(solution)/shard_map/all_gather | solution.py:965
  68.8 77.2 %collective-permute-start.4 = (bf16[4,256,1024]{2,1,0:T(8,128)(2,1)S(1)}, bf16[4,256,1024]{2,1,0:T(8,128)(2,1)S(1)}, u32[]{:S(2)}, u32[]{:S(2)}) collective-permute-start(bf16[4,256,1024]{2,1,0:T(8,128)(2,1)S(1)} %maximum_maximum_fusion.4), channel_id=1, source_target_pairs={{0,4},{4,0},{8,12},{12,8},{16,20},{20,16},{24,28},{28,24},{1,5},{5... | collective-permute-start | bytes 6291464 | tf_op jit(solution)/shard_map/ppermute | solution.py:536
  180.2 99.9 %collective-permute-start.28 = (bf16[512,768]{1,0:T(8,128)(2,1)}, bf16[512,768]{1,0:T(8,128)(2,1)}, u32[]{:S(2)}, u32[]{:S(2)}) collective-permute-start(bf16[512,768]{1,0:T(8,128)(2,1)} %constant_dynamic-update-slice_fusion.37), channel_id=1, source_target_pairs={{0,8},{4,12},{8,0},{12,4},{16,24},{20,28},{24,16},{28,20},{1,9},{5... | collective-permute-start | bytes 2359304 | tf_op jit(solution)/shard_map/ppermute | solution.py:536
  182.7 97.4 %collective-permute-start.30 = (bf16[512,768]{1,0:T(8,128)(2,1)}, bf16[512,768]{1,0:T(8,128)(2,1)}, u32[]{:S(2)}, u32[]{:S(2)}) collective-permute-start(bf16[512,768]{1,0:T(8,128)(2,1)} %collective-permute-done.29), channel_id=1, source_target_pairs={{0,8},{4,12},{8,0},{12,4},{16,24},{20,28},{24,16},{28,20},{1,9},{5... | collective-permute-start | bytes 2359304 | tf_op jit(solution)/shard_map/ppermute | solution.py:536
  324.2 83.5 %collective-permute-start.36 = (bf16[4,256,1024]{2,1,0:T(8,128)(2,1)}, bf16[4,256,1024]{2,1,0:T(8,128)(2,1)}, u32[]{:S(2)}, u32[]{:S(2)}) collective-permute-start(bf16[4,256,1024]{2,1,0:T(8,128)(2,1)} %maximum_maximum_fusion.5), channel_id=1, source_target_pairs={{0,4},{4,0},{8,12},{12,8},{16,20},{20,16},{24,28},{28,24},{1,5},{5... | collective-permute-start | bytes 6291464 | tf_op jit(solution)/shard_map/ppermute | solution.py:536
  330.9 717.4 %all-reduce.4.cloned.1.call-start = ((), (), s32[]{:S(2)}) async-start(), calls=%async_computation.4 | async-start | bytes 196608 | tf_op jit(solution)/shard_map/psum | solution.py:1140
  331.0 73.8 %collective-permute-start.56 = (bf16[512,256]{1,0:T(8,128)(2,1)}, bf16[512,256]{1,0:T(8,128)(2,1)S(1)}, u32[]{:S(2)}, u32[]{:S(2)}) collective-permute-start(bf16[512,256]{1,0:T(8,128)(2,1)} %get-tuple-element.112), channel_id=1, source_target_pairs={{0,3},{1,0},{2,1},{3,2},{4,7},{5,4},{6,5},{7,6},{8,11},{9,8},{10,9... | collective-permute-start | bytes 786440 | tf_op jit(solution)/shard_map/ppermute | solution.py:541
  444.3 86.7 %collective-permute-start.57 = (bf16[512,768]{1,0:T(8,128)(2,1)}, bf16[512,768]{1,0:T(8,128)(2,1)}, u32[]{:S(2)}, u32[]{:S(2)}) collective-permute-start(bf16[512,768]{1,0:T(8,128)(2,1)} %constant_dynamic-update-slice_fusion.59), channel_id=1, source_target_pairs={{0,8},{4,12},{8,0},{12,4},{16,24},{20,28},{24,16},{28,20},{1,9},{5... | collective-permute-start | bytes 2359304 | tf_op jit(solution)/shard_map/ppermute | solution.py:536
  445.6 85.4 %collective-permute-start.59 = (bf16[512,768]{1,0:T(8,128)(2,1)}, bf16[512,768]{1,0:T(8,128)(2,1)}, u32[]{:S(2)}, u32[]{:S(2)}) collective-permute-start(bf16[512,768]{1,0:T(8,128)(2,1)} %collective-permute-done.58), channel_id=1, source_target_pairs={{0,8},{4,12},{8,0},{12,4},{16,24},{20,28},{24,16},{28,20},{1,9},{5... | collective-permute-start | bytes 2359304 | tf_op jit(solution)/shard_map/ppermute | solution.py:536
  594.1 148.2 %collective-permute-start.109 = (bf16[2,1024,512]{2,1,0:T(8,128)(2,1)}, bf16[2,1024,512]{2,1,0:T(8,128)(2,1)}, u32[]{:S(2)}, u32[]{:S(2)}) collective-permute-start(bf16[2,1024,512]{2,1,0:T(8,128)(2,1)} %pad_maximum_fusion.3), channel_id=1, source_target_pairs={{0,8},{4,12},{8,0},{12,4},{16,24},{20,28},{24,16},{28,20},{1,9},{5... | collective-permute-start | bytes 6291464 | tf_op jit(solution)/shard_map/ppermute | solution.py:536
  608.0 137.1 %collective-permute-start.125 = (bf16[2,512,1024]{2,1,0:T(8,128)(2,1)}, bf16[2,512,1024]{2,1,0:T(8,128)(2,1)}, u32[]{:S(2)}, u32[]{:S(2)}) collective-permute-start(bf16[2,512,1024]{2,1,0:T(8,128)(2,1)} %pad_maximum_fusion.5), channel_id=1, source_target_pairs={{0,16},{4,20},{8,24},{12,28},{16,0},{20,4},{24,8},{28,12},{1,17},{... | collective-permute-start | bytes 6291464 | tf_op jit(solution)/shard_map/ppermute | solution.py:536
  808.1 114.5 %collective-permute-start.99 = (bf16[2,256,384]{2,1,0:T(8,128)(2,1)}, bf16[2,256,384]{2,1,0:T(8,128)(2,1)}, u32[]{:S(2)}, u32[]{:S(2)}) collective-permute-start(bf16[2,256,384]{2,1,0:T(8,128)(2,1)} %pad_maximum_fusion.36), channel_id=1, source_target_pairs={{0,16},{4,20},{8,24},{12,28},{16,0},{20,4},{24,8},{28,12},{1,17},{... | collective-permute-start | bytes 1179656 | tf_op jit(solution)/shard_map/ppermute | solution.py:536
  819.0 106.8 %collective-permute-start.114 = (bf16[256,512]{1,0:T(8,128)(2,1)S(1)}, bf16[256,512]{1,0:T(8,128)(2,1)}, u32[]{:S(2)}, u32[]{:S(2)}) collective-permute-start(bf16[256,512]{1,0:T(8,128)(2,1)S(1)} %add_convert_fusion.6), channel_id=1, source_target_pairs={{0,8},{4,12},{8,0},{12,4},{16,24},{20,28},{24,16},{28,20},{1,9},{5... | collective-permute-start | bytes 786440 | tf_op jit(solution)/shard_map/ppermute | solution.py:536
  824.0 104.2 %collective-permute-start.130 = (bf16[512,256]{1,0:T(8,128)(2,1)}, bf16[512,256]{1,0:T(8,128)(2,1)}, u32[]{:S(2)}, u32[]{:S(2)}) collective-permute-start(bf16[512,256]{1,0:T(8,128)(2,1)} %add_convert_fusion.4), channel_id=1, source_target_pairs={{0,16},{4,20},{8,24},{12,28},{16,0},{20,4},{24,8},{28,12},{1,17},{... | collective-permute-start | bytes 786440 | tf_op jit(solution)/shard_map/ppermute | solution.py:536
  919.1 297.0 %reduce-scatter.5.cloned.1.call-start = ((), (), s32[]{:S(2)}) async-start(), calls=%async_computation.3 | async-start | bytes 2621440 | tf_op jit(solution)/shard_map/reduce_scatter | solution.py:1109
  922.3 293.8 %reduce-scatter.3.cloned.1.call-start = ((), (), s32[]{:S(2)}) async-start(), calls=%async_computation.2 | async-start | bytes 2621440 | tf_op jit(solution)/shard_map/reduce_scatter | solution.py:1109
  937.5 114.0 %collective-permute-start.101 = (bf16[2,1024,512]{2,1,0:T(8,128)(2,1)}, bf16[2,1024,512]{2,1,0:T(8,128)(2,1)}, u32[]{:S(2)}, u32[]{:S(2)}) collective-permute-start(bf16[2,1024,512]{2,1,0:T(8,128)(2,1)} %pad_maximum_fusion.2), channel_id=1, source_target_pairs={{0,8},{4,12},{8,0},{12,4},{16,24},{20,28},{24,16},{28,20},{1,9},{5... | collective-permute-start | bytes 6291464 | tf_op jit(solution)/shard_map/ppermute | solution.py:536
  945.0 109.6 %collective-permute-start.117 = (bf16[2,512,1024]{2,1,0:T(8,128)(2,1)}, bf16[2,512,1024]{2,1,0:T(8,128)(2,1)}, u32[]{:S(2)}, u32[]{:S(2)}) collective-permute-start(bf16[2,512,1024]{2,1,0:T(8,128)(2,1)} %pad_maximum_fusion.4), channel_id=1, source_target_pairs={{0,16},{4,20},{8,24},{12,28},{16,0},{20,4},{24,8},{28,12},{1,17},{... | collective-permute-start | bytes 6291464 | tf_op jit(solution)/shard_map/ppermute | solution.py:536
  972.6 84.4 %collective-permute-start.84 = (bf16[4,256,1024]{2,1,0:T(8,128)(2,1)}, bf16[4,256,1024]{2,1,0:T(8,128)(2,1)}, u32[]{:S(2)}, u32[]{:S(2)}) collective-permute-start(bf16[4,256,1024]{2,1,0:T(8,128)(2,1)} %fusion.13), channel_id=1, source_target_pairs={{0,4},{4,0},{8,12},{12,8},{16,20},{20,16},{24,28},{28,24},{1,5},{5... | collective-permute-start | bytes 6291464 | tf_op jit(solution)/shard_map/ppermute | solution.py:536
  1003.4 269.1 %all-reduce.6.cloned.1.call-start = ((), (), s32[]{:S(2)}) async-start(), calls=%async_computation.7 | async-start | bytes 2097152 | tf_op jit(solution)/shard_map/psum | solution.py:1110
  1061.3 106.8 %collective-permute-start.85 = (bf16[2,256,512]{2,1,0:T(8,128)(2,1)S(1)}, bf16[2,256,512]{2,1,0:T(8,128)(2,1)S(1)}, u32[]{:S(2)}, u32[]{:S(2)}) collective-permute-start(bf16[2,256,512]{2,1,0:T(8,128)(2,1)S(1)} %pad_maximum_fusion.29), channel_id=1, source_target_pairs={{0,8},{4,12},{8,0},{12,4},{16,24},{20,28},{24,16},{28,20},{1,9},{5... | collective-permute-start | bytes 1572872 | tf_op jit(solution)/shard_map/ppermute | solution.py:536
  1188.7 93.3 %collective-permute-start.108 = (bf16[4,256,512]{2,1,0:T(8,128)(2,1)S(1)}, bf16[4,256,512]{2,1,0:T(8,128)(2,1)}, u32[]{:S(2)}, u32[]{:S(2)}) collective-permute-start(bf16[4,256,512]{2,1,0:T(8,128)(2,1)S(1)} %pad_maximum_fusion.10.near_ref), channel_id=1, source_target_pairs={{0,4},{4,0},{8,12},{12,8},{16,20},{20,16},{24,28},{28,24},{1,5},{5... | collective-permute-start | bytes 3145736 | tf_op jit(solution)/shard_map/ppermute | solution.py:536
  1193.4 81.8 %collective-permute-start.124 = (bf16[4,512,256]{2,1,0:T(8,128)(2,1)}, bf16[4,512,256]{2,1,0:T(8,128)(2,1)}, u32[]{:S(2)}, u32[]{:S(2)}) collective-permute-start(bf16[4,512,256]{2,1,0:T(8,128)(2,1)} %pad_maximum_fusion.12.near_ref), channel_id=1, source_target_pairs={{0,4},{4,0},{8,12},{12,8},{16,20},{20,16},{24,28},{28,24},{1,5},{5... | collective-permute-start | bytes 3145736 | tf_op jit(solution)/shard_map/ppermute | solution.py:536
  (313 other events, 6063.8 us)
Sparse Core Ops, SparseCore 0:
  22.8 64.6 all-gather.4
  331.0 74.7 all-gather.6
  919.3 129.0 all-reduce.3
  1050.5 51.1 reduce-scatter.4
  1103.9 69.1 reduce-scatter.2
  1216.3 56.2 all-reduce.5

commit v2 on v1

--- a/solution.py
+++ b/solution.py
@@ -567,7 +567,7 @@
 
 
 def attention_forward_kernel(
-    query_ref, key_ref, value_ref, label_ref, query_label_ref, mixed_ref, log_ref, key_mask, value_t
+    order_ref, query_ref, key_ref, value_ref, label_ref, query_label_ref, mixed_ref, log_ref, key_mask, value_t
 ):
     @pl.when(pl.program_id(0) == 0)
     def _():
@@ -590,36 +590,43 @@
     mixed_ref[...] = low(jnp.concatenate(parts, axis=0).T)
 
 
-def attention_forward(packed, labels):
+def attention_forward(packed, labels, order):
     rows = packed.shape[0]
-    mine = pl.BlockSpec((QUERY_BLOCK, LANES), lambda i: (i, 0))
+    mine = pl.BlockSpec((QUERY_BLOCK, LANES), lambda i, order_ref: (i, 0))
     return pl.pallas_call(
         attention_forward_kernel,
-        grid=(rows // QUERY_BLOCK,),
-        in_specs=[
-            mine,
-            pl.BlockSpec((rows, LANES), lambda i: (0, 1)),
-            pl.BlockSpec((rows, LANES), lambda i: (0, 2)),
-            pl.BlockSpec((rows, 1), lambda i: (0, 0)),
-            pl.BlockSpec((QUERY_BLOCK, 1), lambda i: (i, 0)),
-        ],
-        out_specs=[mine, pl.BlockSpec((2, QUERY_BLOCK), lambda i: (0, i))],
+        grid_spec=pltpu.PrefetchScalarGridSpec(
+            num_scalar_prefetch=1,
+            grid=(rows // QUERY_BLOCK,),
+            in_specs=[
+                mine,
+                pl.BlockSpec((rows, LANES), lambda i, order_ref: (0, 1)),
+                pl.BlockSpec((rows, LANES), lambda i, order_ref: (0, 2)),
+                pl.BlockSpec((rows, 1), lambda i, order_ref: (0, 0)),
+                pl.BlockSpec((QUERY_BLOCK, 1), lambda i, order_ref: (i, 0)),
+            ],
+            out_specs=[
+                pl.BlockSpec((QUERY_BLOCK, LANES), lambda i, order_ref: (order_ref[i], 0)),
+                pl.BlockSpec((2, QUERY_BLOCK), lambda i, order_ref: (0, i)),
+            ],
+            scratch_shapes=[
+                pltpu.VMEM((2, rows, LANES), jnp.bfloat16),
+                pltpu.VMEM((LANES, rows), jnp.bfloat16),
+            ],
+        ),
         out_shape=[
             jax.ShapeDtypeStruct((rows, LANES), jnp.bfloat16),
             jax.ShapeDtypeStruct((2, rows), jnp.float32),
-        ],
-        scratch_shapes=[
-            pltpu.VMEM((2, rows, LANES), jnp.bfloat16),
-            pltpu.VMEM((LANES, rows), jnp.bfloat16),
         ],
         cost_estimate=pl.CostEstimate(
             flops=16 * rows * rows * LANES, bytes_accessed=rows * 1024, transcendentals=2 * rows * rows
         ),
         name="attention_forward",
-    )(packed, packed, packed, labels, labels)
+    )(order, packed, packed, packed, labels, labels)
 
 
 def attention_backward_kernel(
+    order_ref,
     query_ref,
     key_ref,
     value_ref,
@@ -671,93 +678,158 @@
         out_value_ref[...] = low(value_sum[...])
 
 
-def attention_backward(packed, labels, grad, log_all):
+def attention_backward(packed, labels, grad, log_all, order):
     rows = packed.shape[0]
-    mine = pl.BlockSpec((QUERY_BLOCK, LANES), lambda i: (i, 0))
-    whole = pl.BlockSpec((rows, LANES), lambda i: (0, 0))
+    mine = pl.BlockSpec((QUERY_BLOCK, LANES), lambda i, order_ref: (i, 0))
+    whole = pl.BlockSpec((rows, LANES), lambda i, order_ref: (0, 0))
     return pl.pallas_call(
         attention_backward_kernel,
-        grid=(rows // QUERY_BLOCK,),
-        in_specs=[
-            mine,
-            pl.BlockSpec((rows, LANES), lambda i: (0, 1)),
-            pl.BlockSpec((rows, LANES), lambda i: (0, 2)),
-            pl.BlockSpec((rows, 1), lambda i: (0, 0)),
-            pl.BlockSpec((QUERY_BLOCK, 1), lambda i: (i, 0)),
-            mine,
-            pl.BlockSpec((2, QUERY_BLOCK), lambda i: (0, i)),
-        ],
-        out_specs=[mine, whole, whole],
+        grid_spec=pltpu.PrefetchScalarGridSpec(
+            num_scalar_prefetch=1,
+            grid=(rows // QUERY_BLOCK,),
+            in_specs=[
+                mine,
+                pl.BlockSpec((rows, LANES), lambda i, order_ref: (0, 1)),
+                pl.BlockSpec((rows, LANES), lambda i, order_ref: (0, 2)),
+                pl.BlockSpec((rows, 1), lambda i, order_ref: (0, 0)),
+                pl.BlockSpec((QUERY_BLOCK, 1), lambda i, order_ref: (i, 0)),
+                pl.BlockSpec((QUERY_BLOCK, LANES), lambda i, order_ref: (order_ref[i], 0)),
+                pl.BlockSpec((2, QUERY_BLOCK), lambda i, order_ref: (0, i)),
+            ],
+            out_specs=[mine, whole, whole],
+            scratch_shapes=[
+                pltpu.VMEM((2, rows, LANES), jnp.bfloat16),
+                pltpu.VMEM((LANES, rows), jnp.bfloat16),
+                pltpu.VMEM((rows, LANES), jnp.float32),
+                pltpu.VMEM((rows, LANES), jnp.float32),
+            ],
+        ),
         out_shape=[jax.ShapeDtypeStruct((rows, LANES), jnp.bfloat16)] * 3,
-        scratch_shapes=[
-            pltpu.VMEM((2, rows, LANES), jnp.bfloat16),
-            pltpu.VMEM((LANES, rows), jnp.bfloat16),
-            pltpu.VMEM((rows, LANES), jnp.float32),
-            pltpu.VMEM((rows, LANES), jnp.float32),
-        ],
         cost_estimate=pl.CostEstimate(
             flops=16 * rows * rows * LANES, bytes_accessed=rows * 2048, transcendentals=2 * rows * rows
         ),
         name="attention_backward",
-    )(packed, packed, packed, labels, labels, grad, log_all)
-
-
-def cast_blocks(weight, order, block, dim):
-    layers = weight.shape[0]
-    count = order.shape[0]
-    shape = [weight.shape[1], weight.shape[2]]
-    shape[dim] = block
-
-    def read(layer, index, order_ref):
-        place = [0, 0]
-        place[dim] = order_ref[index]
-        return (layer, *place)
-
-    def kernel(order_ref, in_ref, out_ref):
-        out_ref[0] = low(in_ref[...])
-
+    )(order, packed, packed, packed, labels, labels, grad, log_all)
+
+
+def own_pieces(inner_weight, outer_weight, out_weight, joint_weights, here, first_block):
+    layers, shard, hidden = inner_weight.shape
+    piece = hidden // 8
+    total = 2 * piece + LANES
+
+    def kernel(place_ref, inner_ref, outer_ref, out_ref, query_ref, key_ref, value_ref, wide_ref, joint_ref):
+        wide_ref[0, :, :piece] = low(inner_ref[0])
+        wide_ref[0, :, piece : 2 * piece] = low(outer_ref[0]).T
+        wide_ref[0, :, 2 * piece :] = low(out_ref[0])
+        for at, ref in enumerate((query_ref, key_ref, value_ref)):
+            joint_ref[0, :, at * LANES : (at + 1) * LANES] = low(ref[0])
+
+    column = pl.BlockSpec((1, shard, LANES), lambda layer, place_ref: (layer, 0, place_ref[0]))
     return pl.pallas_call(
         kernel,
         grid_spec=pltpu.PrefetchScalarGridSpec(
             num_scalar_prefetch=1,
-            grid=(layers, count),
-            in_specs=[pl.BlockSpec((1, *shape), read)],
-            out_specs=pl.BlockSpec((1, 1, *shape), lambda layer, index, order_ref: (layer, index, 0, 0)),
+            grid=(layers,),
+            in_specs=[
+                pl.BlockSpec((1, shard, piece), lambda layer, place_ref: (layer, 0, place_ref[1])),
+                pl.BlockSpec((1, piece, shard), lambda layer, place_ref: (layer, place_ref[1], 0)),
+                column,
+                column,
+                column,
+                column,
+            ],
+            out_specs=[
+                pl.BlockSpec((1, shard, total), lambda layer, place_ref: (layer, 0, 0)),
+                pl.BlockSpec((1, shard, 3 * LANES), lambda layer, place_ref: (layer, 0, 0)),
+            ],
         ),
-        out_shape=jax.ShapeDtypeStruct((layers, count, *shape), jnp.bfloat16),
+        out_shape=[
+            jax.ShapeDtypeStruct((layers, shard, total), jnp.bfloat16),
+            jax.ShapeDtypeStruct((layers, shard, 3 * LANES), jnp.bfloat16),
+        ],
         cost_estimate=pl.CostEstimate(
-            flops=0, bytes_accessed=layers * count * shape[0] * shape[1] * 6, transcendentals=0
+            flops=0, bytes_accessed=layers * shard * (total + 3 * LANES) * 6, transcendentals=0
         ),
-        name="cast_blocks",
-    )(order, weight)
-
-
-def place_blocks(near, far, order, layer, dim, widths, previous):
-    count = near.shape[0]
-    rows, columns = near.shape[1:]
-    parts = len(widths)
-    outs, specs = [], []
-    for width in widths:
-        shape = [rows, width]
-        full = list(shape)
-        full[dim] *= 2 * count
-
-        def where(index, order_ref, dim=dim):
-            place = [0, 0]
-            place[dim] = order_ref[index]
-            return (layer, *place)
-
-        outs.append(jax.ShapeDtypeStruct((LAYERS, *full), jnp.float32))
-        specs.append(pl.BlockSpec((1, *shape), where))
+        name="own_pieces",
+    )(jnp.stack([here, first_block]).astype(jnp.int32), inner_weight, outer_weight, out_weight, *joint_weights)
+
+
+def own_blocks(inner_weight, outer_weight, out_weight, inner_order, out_order):
+    layers, shard, hidden = inner_weight.shape
+    piece = hidden // 8
+
+    def kernel(inner_order_ref, out_order_ref, *refs):
+        ins, (inner_out, outer_out, out_out) = refs[:-3], refs[-3:]
+        for j in range(4):
+            inner_out[0, j] = low(ins[j][0])
+            outer_out[0, j] = low(ins[4 + j][0]).T
+        for j in range(8):
+            out_out[0, :, j * LANES : (j + 1) * LANES] = low(ins[8 + j][0])
+
+    def inner_at(j):
+        return pl.BlockSpec((1, shard, piece), lambda layer, inner_ref, out_ref: (layer, 0, inner_ref[layer * 4 + j]))
+
+    def outer_at(j):
+        return pl.BlockSpec((1, piece, shard), lambda layer, inner_ref, out_ref: (layer, inner_ref[layer * 4 + j], 0))
+
+    def out_at(j):
+        return pl.BlockSpec((1, shard, LANES), lambda layer, inner_ref, out_ref: (layer, 0, out_ref[layer * 8 + j]))
+
+    block = pl.BlockSpec((1, 4, shard, piece), lambda layer, *_: (layer, 0, 0, 0))
+    return pl.pallas_call(
+        kernel,
+        grid_spec=pltpu.PrefetchScalarGridSpec(
+            num_scalar_prefetch=2,
+            grid=(layers,),
+            in_specs=[inner_at(j) for j in range(4)]
+            + [outer_at(j) for j in range(4)]
+            + [out_at(j) for j in range(8)],
+            out_specs=[block, block, pl.BlockSpec((1, shard, 8 * LANES), lambda layer, *_: (layer, 0, 0))],
+        ),
+        out_shape=[
+            jax.ShapeDtypeStruct((layers, 4, shard, piece), jnp.bfloat16),
+            jax.ShapeDtypeStruct((layers, 4, shard, piece), jnp.bfloat16),
+            jax.ShapeDtypeStruct((layers, shard, 8 * LANES), jnp.bfloat16),
+        ],
+        cost_estimate=pl.CostEstimate(
+            flops=0, bytes_accessed=layers * 8 * shard * (piece + LANES) * 6, transcendentals=0
+        ),
+        name="own_blocks",
+    )(inner_order, out_order, *[inner_weight] * 4, *[outer_weight] * 4, *[out_weight] * 8)
+
+
+def place_pieces(near, far, order, layer, previous):
+    count = 4
+    shard, columns = near.shape[1:]
+    piece = (columns - 4 * LANES) // 2
+    width = 8 * LANES
+    offset = far.shape[0] - count
+
+    def column(index, order_ref):
+        return (layer, 0, order_ref[index])
+
+    def inner_place(index, order_ref):
+        return (order_ref[index] % 2) * 4 + order_ref[index] // 2
+
+    square = jax.ShapeDtypeStruct((LAYERS, shard, width), jnp.float32)
+    outs = [square] * 4 + [
+        jax.ShapeDtypeStruct((LAYERS, shard, 8 * piece), jnp.float32),
+        jax.ShapeDtypeStruct((LAYERS, 8 * piece, shard), jnp.float32),
+    ]
+    specs = [pl.BlockSpec((1, shard, LANES), column)] * 4 + [
+        pl.BlockSpec((1, shard, piece), lambda i, order_ref: (layer, 0, inner_place(i, order_ref))),
+        pl.BlockSpec((1, piece, shard), lambda i, order_ref: (layer, inner_place(i, order_ref), 0)),
+    ]
 
     def kernel(order_ref, near_ref, far_ref, *refs):
-        out_refs = refs[-parts:]
+        query_out, key_out, value_out, out_out, inner_out, outer_out = refs[-6:]
 
         def write(source):
-            begin = 0
-            for out_ref, width in zip(out_refs, widths):
-                out_ref[0] = wide(source[0, :, begin : begin + width])
-                begin += width
+            inner_out[0] = wide(source[0, :, :piece])
+            outer_out[0] = wide(source[0, :, piece : 2 * piece].T)
+            for at, ref in enumerate((out_out, query_out, key_out, value_out)):
+                begin = 2 * piece + at * LANES
+                ref[0] = wide(source[0, :, begin : begin + LANES])
 
         @pl.when(pl.program_id(0) < count)
         def _():
@@ -774,8 +846,10 @@
             num_scalar_prefetch=1,
             grid=(2 * count,),
             in_specs=[
-                pl.BlockSpec((1, rows, columns), lambda i, order_ref: (jnp.minimum(i, count - 1), 0, 0)),
-                pl.BlockSpec((1, rows, columns), lambda i, order_ref: (jnp.maximum(i - count, 0), 0, 0)),
+                pl.BlockSpec((1, shard, columns), lambda i, order_ref: (jnp.minimum(i, count - 1), 0, 0)),
+                pl.BlockSpec(
+                    (1, shard, columns), lambda i, order_ref: (jnp.maximum(i - count, 0) + offset, 0, 0)
+                ),
             ]
             + [pl.BlockSpec(memory_space=pl.ANY)] * len(held),
             out_specs=specs,
@@ -783,10 +857,265 @@
         out_shape=outs,
         input_output_aliases={3 + i: i for i in range(len(held))},
         cost_estimate=pl.CostEstimate(
-            flops=0, bytes_accessed=12 * count * rows * columns, transcendentals=0
+            flops=0, bytes_accessed=12 * count * shard * columns, transcendentals=0
         ),
-        name="place_blocks",
+        name="place_pieces",
     )(order, near, far, *held)
+
+
+def half_erfc(values_in):
+    scaled = values_in * (2.0**-0.5)
+    part = 1.0 / (1.0 + 0.5 * scaled)
+    series = 0.17087277
+    for coefficient in (
+        -0.82215223,
+        1.48851587,
+        -1.13520398,
+        0.27886807,
+        -0.18628806,
+        0.09678418,
+        0.37409196,
+        1.00002368,
+        -1.26551223,
+    ):
+        series = coefficient + part * series
+    return 0.5 * part * jnp.exp(series - scaled * scaled)
+
+
+def load_weights(step, own_inner, own_outer, inner_refs, outer_refs, inner_now, outer_now):
+    shard = own_inner.shape[2]
+    inner_now[:shard] = own_inner[0, 0]
+    outer_now[:shard] = own_outer[0, 0]
+    if len(inner_refs) == 1:
+        inner_now[shard:] = inner_refs[0][0]
+        outer_now[shard:] = outer_refs[0][0]
+        return
+    for j in range(len(inner_refs)):
+
+        @pl.when(step == j)
+        def _(j=j):
+            inner_now[shard:] = inner_refs[j][...]
+            outer_now[shard:] = outer_refs[j][...]
+
+
+def weight_operands(weights, layer):
+    own_inner, own_outer, inner_parts, outer_parts = weights
+    shard, piece = own_inner.shape[2:]
+    own = pl.BlockSpec((1, 1, shard, piece), lambda i: (layer, i, 0, 0))
+    rest = 3 * shard
+    if inner_parts is outer_parts:
+        specs = [
+            pl.BlockSpec((1, rest, piece), lambda i: (i, 0, 0)),
+            pl.BlockSpec((1, rest, piece), lambda i: (i, 0, 1)),
+        ]
+        return ([own_inner, own_outer, inner_parts, outer_parts], [own, own] + specs, 1)
+    fixed = pl.BlockSpec((rest, piece), lambda i: (0, 0), pipeline_mode=pl.Buffered(1))
+    return (
+        [own_inner, own_outer, *inner_parts, *outer_parts],
+        [own, own] + [fixed] * (2 * len(inner_parts)),
+        len(inner_parts),
+    )
+
+
+def accumulate(step, total, part):
+    @pl.when(step == 0)
+    def _():
+        total[...] = part
+
+    @pl.when(step > 0)
+    def _():
+        total[...] += part
+
+
+def finish_pair(step, total, near_ref, far_ref):
+    rows = near_ref.shape[0]
+
+    @pl.when(step == pl.num_programs(0) - 1)
+    def _():
+        near_ref[...] = total[:rows]
+        far_ref[...] = low(total[rows:])
+
+
+def feed_forward_kernel(count, hidden_ref, bias_ref, own_inner, own_outer, *refs):
+    inner_refs, outer_refs = refs[:count], refs[count : 2 * count]
+    near_ref, far_ref, active_ref, slope_ref, total, inner_now, outer_now = refs[2 * count :]
+    step = pl.program_id(0)
+    load_weights(step, own_inner, own_outer, inner_refs, outer_refs, inner_now, outer_now)
+    pre = mm(hidden_ref[...], inner_now[...]) + bias_ref[...]
+    tail = half_erfc(jnp.abs(pre))
+    below = jnp.where(pre < 0.0, tail, 1.0 - tail)
+    active = low(pre * below)
+    active_ref[...] = active
+    slope_ref[...] = low(below + pre * (jnp.exp(-0.5 * pre * pre) * 0.3989422804014327))
+    accumulate(step, total, mm(active, outer_now[...], NT))
+    finish_pair(step, total, near_ref, far_ref)
+
+
+def feed_forward(hidden_pair, bias_row, weights, layer):
+    rows, width = hidden_pair.shape
+    hidden = bias_row.shape[1]
+    block = hidden // 4
+    arrays, specs, count = weight_operands(weights, layer)
+    column = pl.BlockSpec((rows, block), lambda i: (0, i))
+    half = pl.BlockSpec((rows // 2, width), lambda i: (0, 0))
+    return pl.pallas_call(
+        functools.partial(feed_forward_kernel, count),
+        grid=(4,),
+        in_specs=[
+            pl.BlockSpec((rows, width), lambda i: (0, 0)),
+            pl.BlockSpec((1, block), lambda i: (0, i)),
+            *specs,
+        ],
+        out_specs=[half, half, column, column],
+        out_shape=[
+            jax.ShapeDtypeStruct((rows // 2, width), jnp.float32),
+            jax.ShapeDtypeStruct((rows // 2, width), jnp.bfloat16),
+            jax.ShapeDtypeStruct((rows, hidden), jnp.bfloat16),
+            jax.ShapeDtypeStruct((rows, hidden), jnp.bfloat16),
+        ],
+        scratch_shapes=[
+            pltpu.VMEM((rows, width), jnp.float32),
+            pltpu.VMEM((width, block), jnp.bfloat16),
+            pltpu.VMEM((width, block), jnp.bfloat16),
+        ],
+        cost_estimate=pl.CostEstimate(
+            flops=4 * rows * width * hidden, bytes_accessed=4 * width * hidden, transcendentals=2 * rows * hidden
+        ),
+        name="feed_forward",
+    )(hidden_pair, bias_row, *arrays)
+
+
+def feed_backward_kernel(count, grad_ref, slope_ref, own_inner, own_outer, *refs):
+    inner_refs, outer_refs = refs[:count], refs[count : 2 * count]
+    near_ref, far_ref, inner_grad_ref, bias_ref, total, inner_now, outer_now = refs[2 * count :]
+    step = pl.program_id(0)
+    load_weights(step, own_inner, own_outer, inner_refs, outer_refs, inner_now, outer_now)
+    inner_grad = low(mm(grad_ref[...], outer_now[...]) * wide(slope_ref[...]))
+    inner_grad_ref[...] = inner_grad
+    bias_ref[...] = jnp.sum(wide(inner_grad), axis=0, keepdims=True)
+    accumulate(step, total, mm(inner_grad, inner_now[...], NT))
+    finish_pair(step, total, near_ref, far_ref)
+
+
+def feed_backward(grad_pair, slope, weights, layer):
+    rows, width = grad_pair.shape
+    hidden = slope.shape[1]
+    block = hidden // 4
+    arrays, specs, count = weight_operands(weights, layer)
+    column = pl.BlockSpec((rows, block), lambda i: (0, i))
+    half = pl.BlockSpec((rows // 2, width), lambda i: (0, 0))
+    return pl.pallas_call(
+        functools.partial(feed_backward_kernel, count),
+        grid=(4,),
+        in_specs=[pl.BlockSpec((rows, width), lambda i: (0, 0)), column, *specs],
+        out_specs=[half, half, column, pl.BlockSpec((1, block), lambda i: (0, i))],
+        out_shape=[
+            jax.ShapeDtypeStruct((rows // 2, width), jnp.float32),
+            jax.ShapeDtypeStruct((rows // 2, width), jnp.bfloat16),
+            jax.ShapeDtypeStruct((rows, hidden), jnp.bfloat16),
+            jax.ShapeDtypeStruct((1, hidden), jnp.float32),
+        ],
+        scratch_shapes=[
+            pltpu.VMEM((rows, width), jnp.float32),
+            pltpu.VMEM((width, block), jnp.bfloat16),
+            pltpu.VMEM((width, block), jnp.bfloat16),
+        ],
+        cost_estimate=pl.CostEstimate(
+            flops=4 * rows * width * hidden, bytes_accessed=4 * width * hidden, transcendentals=0
+        ),
+        name="feed_backward",
+    )(grad_pair, slope, *arrays)
+
+
+def weight_gradient_kernel(
+    split,
+    rows_ref,
+    hidden_ref,
+    grad_ref,
+    mixed_ref,
+    inner_grad_ref,
+    active_ref,
+    branch_ref,
+    *refs,
+):
+    outs, (hidden_t, grad_t, mixed_t) = refs[:-3], refs[-3:]
+    step = pl.program_id(0)
+    piece = active_ref.shape[1]
+
+    @pl.when(step == 0)
+    def _():
+        hidden_t[...] = hidden_ref[...].T
+        grad_t[...] = grad_ref[...].T
+        mixed_t[...] = mixed_ref[...].T
+
+    def write(store):
+        store(0, piece, low(mm(hidden_t[...], inner_grad_ref[...])))
+        store(piece, 2 * piece, low(mm(grad_t[...], active_ref[...])))
+        store(2 * piece, 2 * piece + LANES, low(mm(mixed_t[...], branch_ref[...])))
+
+    if not split:
+        (out_ref,) = outs
+
+        def store(begin, end, value):
+            shard = value.shape[0] // 4
+            for r in range(4):
+                place = pl.multiple_of(rows_ref[r] * shard, shard)
+                out_ref[0, pl.ds(place, shard), begin:end] = value[r * shard : (r + 1) * shard]
+
+        write(store)
+        return
+    first_keep, first_send, second_keep, second_send = outs
+    for j in range(4):
+
+        @pl.when(step == j)
+        def _(j=j):
+            first = (first_send if j % 2 else first_keep, j // 2)
+            second = (second_send if j // 2 else second_keep, j % 2)
+
+            def store(begin, end, value):
+                half = value.shape[0] // 2
+                first[0][first[1], :, begin:end] = value[:half]
+                second[0][second[1], :, begin:end] = value[half:]
+
+            write(store)
+
+
+def weight_gradients(hidden_pair, grad_pair, mixed_pair, inner_grad, active, branch_pair, plane_rows, split):
+    rows, width = hidden_pair.shape
+    hidden = active.shape[1]
+    piece = hidden // 4
+    total = 2 * piece + LANES
+    whole = pl.BlockSpec((rows, width), lambda i, rows_ref: (0, 0))
+    column = pl.BlockSpec((rows, piece), lambda i, rows_ref: (0, i))
+    if split:
+        shape = (2, width // 2, total)
+        out_specs = [pl.BlockSpec(shape, lambda i, rows_ref: (0, 0, 0), pipeline_mode=pl.Buffered(1))] * 4
+        out_shape = [jax.ShapeDtypeStruct(shape, jnp.bfloat16)] * 4
+    else:
+        out_specs = [pl.BlockSpec((1, width, total), lambda i, rows_ref: (i, 0, 0))]
+        out_shape = [jax.ShapeDtypeStruct((4, width, total), jnp.bfloat16)]
+    return pl.pallas_call(
+        functools.partial(weight_gradient_kernel, split),
+        grid_spec=pltpu.PrefetchScalarGridSpec(
+            num_scalar_prefetch=1,
+            grid=(4,),
+            in_specs=[
+                whole,
+                whole,
+                whole,
+                column,
+                column,
+                pl.BlockSpec((rows, LANES), lambda i, rows_ref: (0, i)),
+            ],
+            out_specs=out_specs,
+            scratch_shapes=[pltpu.VMEM((width, rows), jnp.bfloat16)] * 3,
+        ),
+        out_shape=out_shape,
+        cost_estimate=pl.CostEstimate(
+            flops=4 * rows * width * hidden, bytes_accessed=8 * width * hidden, transcendentals=0
+        ),
+        name="weight_gradients",
+    )(plane_rows, hidden_pair, grad_pair, mixed_pair, inner_grad, active, branch_pair)
 
 
 def block_columns(values_in, order, width):
@@ -828,31 +1157,36 @@
     return both.reshape(8 * rows_in.shape[0], rows_in.shape[1])
 
 
-def collect_tokens(partial):
+def plane_groups():
+    count = lax.axis_size("ctx")
+    return [list(range(0, count, 2)), list(range(1, count, 2))]
+
+
+def collect_tokens(partial, chip):
     rows = partial.shape[0] // 8
     width = partial.shape[1]
     blocks = partial.reshape(4, 2, rows, width)
-    near = blocks[:, 0] + wide(swap(low(blocks[:, 1]), CORE))
-    half = width // 2
-    left, right = near[:, :, :half], near[:, :, half:]
-    left_sent = swap(low(jnp.stack([left[1], left[3]])), ALONG_X)
-    right_sent = swap(low(right[2:]), ALONG_Y)
-    left = jnp.stack([left[0], left[2]]) + wide(left_sent)
-    right = right[:2] + wide(right_sent)
-    left = left[0] + wide(swap(low(left[1]), ALONG_Y))
-    right = right[0] + wide(swap(low(right[1]), ALONG_X))
-    return jnp.concatenate([left, right], axis=1)
-
-
-def plane_pieces(piece, first, second):
-    pair = jnp.stack([piece, swap(piece, first)])
-    near = jnp.concatenate([pair, swap(pair, second)])
+    near = low(blocks[:, 0] + wide(swap(low(blocks[:, 1]), CORE)))
+    sent = jnp.stack([lax.dynamic_index_in_dim(near, chip ^ j, 0, keepdims=False) for j in range(4)])
+    came = lax.all_to_all(sent, "ctx", 0, 0, axis_index_groups=plane_groups(), tiled=True)
+    return jnp.sum(wide(came), axis=0)
+
+
+def plane_pieces(piece):
+    half = piece.shape[1] // 2
+    left, right = piece[:, :half], piece[:, half:]
+    left_pair = jnp.stack([left, swap(left, ALONG_X)])
+    right_pair = jnp.stack([right, swap(right, ALONG_Y)])
+    left_far = swap(left_pair, ALONG_Y)
+    right_far = swap(right_pair, ALONG_X)
+    left_all = jnp.concatenate([left_pair, left_far])
+    right_all = jnp.stack([right_pair[0], right_far[0], right_pair[1], right_far[1]])
+    near = jnp.concatenate([left_all, right_all], axis=2)
     return (near, swap(near, CORE))
 
 
-def exchange_heads(blocks, rows):
-    parts = [blocks[k * rows : (k + 1) * rows] for k in range(8)]
-    return [parts[0]] + [swap(parts[k], k) for k in range(1, 8)]
+def exchange(blocks):
+    return lax.all_to_all(blocks, "ctx", 0, 0, tiled=True)
 
 
 def head_split_body(
@@ -892,15 +1226,22 @@
     positions = ((here ^ relative)[:, None] * rows + jnp.arange(rows, dtype=jnp.int32)).reshape(-1)
     labels = doc_labels(positions, doc_starts[0], doc_lengths[0])[:, None]
 
-    inner_order = core * 4 + (chip ^ jnp.arange(4, dtype=jnp.int32))
-    inner_own = cast_blocks(inner_weight, inner_order, piece, 1)
-    outer_own = cast_blocks(outer_weight, inner_order, piece, 0)
-    joint_own = jnp.concatenate(
-        [
-            low(lax.dynamic_slice_in_dim(weight, here * LANES, LANES, 2))
-            for weight in (query_weight, key_weight, value_weight)
-        ],
-        axis=2,
+    four = jnp.arange(4, dtype=jnp.int32)
+    chip_order = [chip ^ four, four]
+    inner_order = [core * 4 + order for order in chip_order]
+    out_order = [jnp.concatenate([2 * order + core, 2 * order + 1 - core]) for order in chip_order]
+    block_order = here ^ relative
+    plane_rows = jnp.stack(turned).astype(jnp.int32)
+    wide_own, joint_own = own_pieces(
+        inner_weight,
+        outer_weight,
+        out_weight,
+        (query_weight, key_weight, value_weight),
+        here,
+        core * 4 + chip,
+    )
+    inner_own, outer_own, out_own = own_blocks(
+        inner_weight, outer_weight, out_weight, jnp.concatenate(inner_order), jnp.concatenate(out_order)
     )
     small_own = low(
         jnp.concatenate(
@@ -918,53 +1259,60 @@
             axis=1,
         )
     )
-    small_turned = jnp.stack([small_own] + [turn(small_own, r) for r in range(1, planes)])
-    small_all = jnp.stack(
-        [lax.dynamic_index_in_dim(small_turned, unturned[i], 0, keepdims=False) for i in range(planes)], axis=1
-    )
+    wide_piece = 2 * piece + LANES
+    joint_width = 3 * LANES
+    small_rows = small_own.size // joint_width
+    first_joint = jnp.concatenate([joint_own[0], small_own.reshape(small_rows, joint_width)], axis=0)
+    joint_turned = jnp.stack([first_joint] + [turn(first_joint, r) for r in range(1, planes)])
+    joint_plain = jnp.stack([lax.dynamic_index_in_dim(joint_turned, i, 0, keepdims=False) for i in unturned])
+    small_all = joint_plain[:, shard:].reshape(planes, LAYERS, -1)
 
     def small(layer, index):
-        return small_all[layer, :, index * shard : (index + 1) * shard].reshape(width)
-
-    inner_bias_all = small_all[:, :, 8 * shard :].reshape(LAYERS, hidden)
-
-    def gather_joint(layer):
-        own = joint_own[layer]
-        stack = jnp.stack([own] + [turn(own, r) for r in range(1, planes)])
-        return jnp.concatenate(
-            [lax.dynamic_index_in_dim(stack, unturned[i], 0, keepdims=False) for i in range(planes)], axis=0
-        )
-
-    def gather_inner(layer):
-        own = inner_own[layer]
-        others = jnp.concatenate([turn(own[0], r) for r in range(1, planes)], axis=0)
-        by_x = swap(others, ALONG_X)
-        near_y = swap(others, ALONG_Y)
-        far_y = swap(by_x, ALONG_Y)
-        return jnp.concatenate(
-            [jnp.concatenate([own[j], part], axis=0) for j, part in enumerate((others, by_x, near_y, far_y))],
-            axis=1,
-        )
-
-    def gather_outer(layer):
-        own = outer_own[layer]
-        others = jnp.concatenate([turn(own[0], r) for r in range(1, planes)], axis=1)
-        by_y = swap(others, ALONG_Y)
-        near_x = swap(others, ALONG_X)
-        far_x = swap(by_y, ALONG_X)
-        return jnp.concatenate(
-            [jnp.concatenate([own[j], part], axis=1) for j, part in enumerate((others, near_x, by_y, far_x))],
-            axis=0,
-        )
+        return small_all[:, layer, index * shard : (index + 1) * shard].reshape(width)
+
+    inner_bias_all = small_all[:, :, 8 * shard :].swapaxes(0, 1).reshape(LAYERS, hidden)
+
+    def ordered(stack, order):
+        return jnp.concatenate([lax.dynamic_index_in_dim(stack, i, 0, keepdims=False) for i in order], axis=0)
+
+    joint_first = joint_plain[:, :shard].reshape(width, joint_width)
+    wide_first, _ = lax.optimization_barrier((wide_own[0], joint_first))
+    others_first = jnp.concatenate([turn(wide_first, r) for r in range(1, planes)], axis=0)
+    second_own, _ = lax.optimization_barrier(
+        (jnp.concatenate([wide_own[1], joint_own[1]], axis=1), others_first)
+    )
+    second_stack = lax.all_gather(second_own, "wsh", axis=0)
+    joint_second = second_stack[:, :, wide_piece:].reshape(width, joint_width)
+    others_second = ordered(second_stack[:, :, :wide_piece], turned[1:])
+    second_parts = lax.all_gather(others_second, "ctx", axis=0, axis_index_groups=plane_groups())
+
+    def layer_weights(layer):
+        if layer == 0:
+            first = jnp.concatenate([others_first[:, :piece], others_first[:, 2 * piece :]], axis=1)
+            second = others_first[:, piece : 2 * piece]
+            first_x = swap(first, ALONG_X)
+            second_y = swap(second, ALONG_Y)
+            firsts = (first, first_x, swap(first, ALONG_Y), swap(first_x, ALONG_Y))
+            seconds = (second, swap(second, ALONG_X), second_y, swap(second_y, ALONG_X))
+            near = jnp.concatenate([part[:, piece:] for part in firsts], axis=1)
+            weights = (inner_own, outer_own, firsts, seconds)
+        else:
+            near = jnp.concatenate([second_parts[j, :, 2 * piece :] for j in range(4)], axis=1)
+            weights = (inner_own, outer_own, second_parts, second_parts)
+        out_full = jnp.concatenate(
+            [out_own[layer], jnp.concatenate([near, swap(near, CORE)], axis=1)], axis=0
+        )
+        return (joint_first if layer == 0 else joint_second, weights, out_full)
+
+    def out_place(layer, block):
+        at = (block // 2) ^ chip if layer == 0 else block // 2
+        return at + 4 * ((block % 2) ^ core)
 
     activation = tokens[0]
     stashed = []
     outputs = []
     for layer in range(LAYERS):
-        joint = gather_joint(layer)
-        out_full = lax.all_gather(low(out_weight[layer]), "wsh", axis=0, tiled=True)
-        inner_full = gather_inner(layer)
-        outer_full = gather_outer(layer)
+        joint, weights, out_full = layer_weights(layer)
         first_gain_row, first_shift_row = wide(small(layer, 4)), wide(small(layer, 5))
         second_gain_row, second_shift_row = wide(small(layer, 6)), wide(small(layer, 7))
 
@@ -973,22 +1321,29 @@
         value_bias_own = lax.dynamic_slice_in_dim(small(layer, 1), here * LANES, LANES, 0)
         joint_bias = jnp.concatenate([query_bias_own, jnp.zeros_like(query_bias_own), value_bias_own])
         packed = low(mm(everyone, joint) + wide(joint_bias))
-        mixed, log_all = attention_forward(packed, labels)
-        mixed_heads = jnp.concatenate(exchange_heads(mixed, rows), axis=1)
-        mixed_tokens = block_columns(mixed_heads, [here ^ k for k in range(8)], LANES)
-        first_pre = wide(activation) + (mm(mixed_tokens, out_full) + wide(small(layer, 2)))
+        mixed, log_all = attention_forward(packed, labels, block_order)
+        mixed_heads = exchange(mixed.reshape(8, rows, LANES))
+        mixed_turned = jnp.concatenate(
+            [
+                lax.dynamic_index_in_dim(mixed_heads, 2 * turned[r] + i, 0, keepdims=False)
+                for r in range(planes)
+                for i in range(2)
+            ],
+            axis=1,
+        )
+        mixed_pair = jnp.concatenate([mixed_turned, swap(mixed_turned, CORE)], axis=0)
+        attended = block_columns(mm(mixed_turned, out_full), [out_place(layer, b) for b in range(8)], LANES)
+        first_pre = wide(activation) + (attended + wide(small(layer, 2)))
         hidden_rows, first_unit, first_inverse = norm_forward(first_pre, first_gain_row, first_shift_row)
         hidden_turned = block_columns(low(hidden_rows), turned, shard)
         hidden_pair = jnp.concatenate([hidden_turned, swap(hidden_turned, CORE)], axis=0)
         inner_bias_own = jnp.concatenate(
-            [lax.dynamic_slice_in_dim(inner_bias_all[layer], inner_order[j] * piece, piece, 0) for j in range(4)]
-        )
-        inner_pre = mm(hidden_pair, inner_full) + wide(inner_bias_own)
-        below = 0.5 * (1.0 + lax.erf(inner_pre * (2.0**-0.5)))
-        active = low(inner_pre * below)
-        slope = low(below + inner_pre * jnp.exp(-0.5 * inner_pre * inner_pre) * ((2.0 * jnp.pi) ** -0.5))
-        outer_pair = mm(active, outer_full)
-        outer_turned = outer_pair[:rows] + wide(swap(low(outer_pair[rows:]), CORE))
+            [lax.dynamic_slice_in_dim(inner_bias_all[layer], inner_order[layer][j] * piece, piece, 0) for j in range(4)]
+        )
+        outer_near, outer_far, active, slope = feed_forward(
+            hidden_pair, wide(inner_bias_own)[None], weights, layer
+        )
+        outer_turned = outer_near + wide(swap(outer_far, CORE))
         outer_out = block_columns(outer_turned, unturned, shard)
         second_pre = hidden_rows + (outer_out + wide(small(layer, 3)))
         result, second_unit, second_inverse = norm_forward(second_pre, second_gain_row, second_shift_row)
@@ -997,7 +1352,7 @@
                 everyone,
                 packed,
                 log_all,
-                mixed_tokens,
+                mixed_pair,
                 first_unit,
                 first_inverse,
                 hidden_pair,
@@ -1007,8 +1362,7 @@
                 second_inverse,
                 joint,
                 out_full,
-                inner_full,
-                outer_full,
+                weights,
                 first_gain_row,
                 second_gain_row,
             )
@@ -1016,20 +1370,15 @@
         activation = low(result)
         outputs.append(activation)
 
-    joint_order = here ^ jnp.array([0, 2, 4, 6, 1, 3, 5, 7], jnp.int32)
-    swapped_order = here ^ jnp.array([0, 4, 2, 6, 1, 5, 3, 7], jnp.int32)
-    inner_place = (joint_order % 2) * 4 + joint_order // 2
-    outer_place = (swapped_order % 2) * 4 + swapped_order // 2
     gradient = wide(cotangent[0])
     small_grads = [None] * LAYERS
-    out_grads = [None] * LAYERS
-    joint_out = inner_out = outer_out = None
+    placed = None
     for layer in reversed(range(LAYERS)):
         (
             everyone,
             packed,
             log_all,
-            mixed_tokens,
+            mixed_pair,
             first_unit,
             first_inverse,
             hidden_pair,
@@ -1039,8 +1388,7 @@
             second_inverse,
             joint,
             out_full,
-            inner_full,
-            outer_full,
+            weights,
             first_gain_row,
             second_gain_row,
         ) = stashed[layer]
@@ -1051,74 +1399,82 @@
         grad_outer_bias = jnp.sum(wide(grad_outer), axis=0)
         grad_turned = block_columns(grad_outer, turned, shard)
         grad_pair = jnp.concatenate([grad_turned, swap(grad_turned, CORE)], axis=0)
-        grad_inner = low(mm(grad_pair, outer_full, NT) * wide(slope))
-        hidden_back = mm(grad_inner, inner_full, NT)
-        hidden_back = hidden_back[:rows] + wide(swap(low(hidden_back[rows:]), CORE))
+        hidden_near, hidden_far, grad_inner, grad_inner_bias = feed_backward(grad_pair, slope, weights, layer)
+        hidden_back = hidden_near + wide(swap(hidden_far, CORE))
         grad_hidden = grad_second + block_columns(hidden_back, unturned, shard)
-        grad_outer_weight = low(mm(active, grad_pair, TN))
-        grad_inner_weight = low(mm(hidden_pair, grad_inner, TN))
-        grad_inner_bias = jnp.sum(wide(grad_inner), axis=0)
         grad_first, grad_first_gain, grad_first_shift = norm_backward(
             grad_hidden, first_unit, first_inverse, first_gain_row
         )
         grad_branch = low(grad_first)
         grad_out_bias = jnp.sum(wide(grad_branch), axis=0)
-        grad_mixed_tokens = low(mm(grad_branch, out_full, NT))
-        grad_mixed = jnp.concatenate(
-            [
-                part if k == 0 else swap(part, k)
-                for k, part in enumerate(
-                    lax.dynamic_slice_in_dim(grad_mixed_tokens, (here ^ k) * LANES, LANES, 1) for k in range(8)
-                )
-            ],
-            axis=0,
-        )
-        grad_out_weight = low(mm(mixed_tokens, grad_branch, TN))
-        grad_query, grad_key, grad_value = attention_backward(packed, labels, grad_mixed, log_all)
+        branch_spread = block_columns(grad_branch, [out_order[layer][p] for p in range(8)], LANES)
+        grad_mixed_turned = low(mm(branch_spread, out_full, NT))
+        grad_mixed = exchange(
+            jnp.stack(
+                [
+                    lax.dynamic_slice_in_dim(grad_mixed_turned, unturned[i // 2] * shard + (i % 2) * LANES, LANES, 1)
+                    for i in range(8)
+                ]
+            )
+        ).reshape(8 * rows, LANES)
+        branch_half = 4 * LANES
+        branch_pair = jnp.concatenate(
+            [branch_spread[:, :branch_half], swap(branch_spread[:, branch_half:], CORE)], axis=0
+        )
+        summed = weight_gradients(
+            hidden_pair, grad_pair, mixed_pair, grad_inner, active, branch_pair, plane_rows, layer == 0
+        )
+        grad_query, grad_key, grad_value = attention_backward(packed, labels, grad_mixed, log_all, block_order)
         grad_packed = jnp.concatenate([grad_query, grad_key, grad_value], axis=1)
-        gradient = grad_first + collect_tokens(mm(grad_packed, joint, NT))
-        grad_joint = mm(everyone, grad_packed, TN)
+        gradient = grad_first + collect_tokens(mm(grad_packed, joint, NT), chip)
+        grad_joint = low(mm(everyone, grad_packed, TN))
         joint_bias_grad = jnp.sum(wide(grad_packed), axis=0)
 
-        joint_parts = [
-            lax.dynamic_slice_in_dim(grad_joint, ((plane + s) % planes) * shard, shard, 0) for s in range(planes)
+        if layer == 0:
+            first_keep, first_send, second_keep, second_send = summed
+            came = swap(first_send, ALONG_X)
+            first_sum = (
+                wide(first_keep[0])
+                + wide(came[0])
+                + wide(swap(low(wide(first_keep[1]) + wide(came[1])), ALONG_Y))
+            )
+            came = swap(second_send, ALONG_Y)
+            second_sum = (
+                wide(second_keep[0])
+                + wide(came[0])
+                + wide(swap(low(wide(second_keep[1]) + wide(came[1])), ALONG_X))
+            )
+            total = first_sum[:shard]
+            for r, rows_sent in enumerate((first_sum[shard:], second_sum[:shard], second_sum[shard:]), 1):
+                total = total + wide(turn(low(rows_sent), planes - r))
+            joint_total = wide(lax.dynamic_slice_in_dim(grad_joint, plane * shard, shard, 0))
+            for r in range(1, planes):
+                part = lax.dynamic_slice_in_dim(grad_joint, turned[r] * shard, shard, 0)
+                joint_total = joint_total + wide(turn(part, planes - r))
+            near, far = plane_pieces(low(jnp.concatenate([total, joint_total], axis=1)))
+            near_first = here ^ (2 * four)
+            placed = place_pieces(near, far, jnp.concatenate([near_first, near_first ^ 1]), layer, placed)
+        else:
+            plane_sum = lax.psum_scatter(
+                summed[0].reshape(4 * width, wide_piece),
+                "ctx",
+                scatter_dimension=0,
+                axis_index_groups=plane_groups(),
+                tiled=True,
+            )
+            total = lax.psum_scatter(plane_sum, "wsh", scatter_dimension=0, tiled=True)
+            joint_total = lax.psum_scatter(grad_joint, "wsh", scatter_dimension=0, tiled=True)
+            everything = lax.all_gather(jnp.concatenate([total, joint_total], axis=1), "ctx", axis=0)
+            placed = place_pieces(everything, everything, relative, layer, placed)
+
+        placed_query, placed_value = [
+            lax.dynamic_update_slice(jnp.zeros((width,), jnp.float32), part, (here * LANES,))
+            for part in (joint_bias_grad[:LANES], joint_bias_grad[2 * LANES :])
         ]
-        joint_sum = joint_parts[0]
-        for s in range(1, planes):
-            joint_sum = joint_sum + wide(turn(low(joint_parts[s]), s))
-        blocks = [grad_inner_weight[:, j * piece : (j + 1) * piece] for j in range(4)]
-        came = swap(jnp.stack([blocks[1], blocks[3]]), ALONG_X)
-        kept = (wide(blocks[0]) + wide(came[0]), low(wide(blocks[2]) + wide(came[1])))
-        inner_sum = low(kept[0] + wide(swap(kept[1], ALONG_Y)))
-        inner_total = wide(inner_sum[:shard])
-        for r in range(1, planes):
-            inner_total = inner_total + wide(turn(inner_sum[r * shard : (r + 1) * shard], planes - r))
-        blocks = [grad_outer_weight[j * piece : (j + 1) * piece] for j in range(4)]
-        came = swap(jnp.stack([blocks[2], blocks[3]]), ALONG_Y)
-        kept = (wide(blocks[0]) + wide(came[0]), low(wide(blocks[1]) + wide(came[1])))
-        outer_sum = low(kept[0] + wide(swap(kept[1], ALONG_X)))
-        outer_total = wide(outer_sum[:, :shard])
-        for r in range(1, planes):
-            outer_total = outer_total + wide(turn(outer_sum[:, r * shard : (r + 1) * shard], planes - r))
-        joint_near, joint_far = plane_pieces(low(joint_sum), ALONG_X, ALONG_Y)
-        inner_near, inner_far = plane_pieces(low(inner_total), ALONG_X, ALONG_Y)
-        outer_near, outer_far = plane_pieces(low(outer_total), ALONG_Y, ALONG_X)
-        joint_out = place_blocks(joint_near, joint_far, joint_order, layer, 1, (LANES,) * 3, joint_out)
-        inner_out = place_blocks(inner_near, inner_far, inner_place, layer, 1, (piece,), inner_out)
-        outer_out = place_blocks(outer_near, outer_far, outer_place, layer, 0, (shard,), outer_out)
-        out_share = lax.psum_scatter(grad_out_weight, "wsh", scatter_dimension=0, tiled=True)
-        out_grads[layer] = wide(lax.psum(out_share, "ctx"))
-
-        placed_query = lax.dynamic_update_slice(
-            jnp.zeros((width,), jnp.float32), joint_bias_grad[:LANES], (here * LANES,)
-        )
-        placed_value = lax.dynamic_update_slice(
-            jnp.zeros((width,), jnp.float32), joint_bias_grad[2 * LANES :], (here * LANES,)
-        )
         placed_inner = jnp.zeros((hidden,), jnp.float32)
         for j in range(4):
             placed_inner = lax.dynamic_update_slice(
-                placed_inner, grad_inner_bias[j * piece : (j + 1) * piece], (inner_order[j] * piece,)
+                placed_inner, grad_inner_bias[0, j * piece : (j + 1) * piece], (inner_order[layer][j] * piece,)
             )
         small_grads[layer] = jnp.concatenate(
             [
@@ -1137,22 +1493,19 @@
             ],
             axis=1,
         )
-    small_sum = lax.psum(jnp.stack(small_grads), ("ctx", "wsh"))
-    small_mine = lax.dynamic_index_in_dim(small_sum, plane, 1, keepdims=False)
+    small_sent = jnp.concatenate(small_grads, axis=1)
+    small_plane = jnp.sum(lax.all_to_all(small_sent, "wsh", 0, 0, tiled=True), axis=0)
+    small_mine = jnp.sum(lax.all_gather(small_plane, "ctx", axis=0), axis=0).reshape(LAYERS, -1)
     small_outs = [small_mine[:, i * shard : (i + 1) * shard] for i in range(8)]
-    inner_bias_out = small_mine[:, 8 * shard :]
     return (
         outputs[0][None],
         outputs[1][None],
         low(gradient)[None],
-        *joint_out,
-        jnp.stack(out_grads),
-        inner_out[0],
-        outer_out[0],
+        *placed,
         small_outs[0],
         small_outs[1],
         small_outs[2],
-        inner_bias_out,
+        small_mine[:, 8 * shard :],
         small_outs[3],
         small_outs[4],
         small_outs[5],

time: 1310 us -> 836 us (0.64)
  waiting for transfers between devices: 575 us -> 218 us
  matrix products: 120 us -> 31.7 us
  starting transfers between devices: 181 us -> 92.8 us
  Pallas kernels: 170 us -> 229 us
  other arithmetic: 129 us -> 88.9 us
  blocking collectives: 0 us -> 38.4 us
    ppermute x94 -> x41, waiting for transfers between devices: 262 us -> 114 us  [swap(): return lax.ppermute(block, 'ctx', [(i, i ^ mask) for i in devices])]
    ppermute x39 -> x12, waiting for transfers between devices: 213 us -> 77.4 us  [turn(): lax.ppermute(block, 'wsh', [(i, (i + distance) % count) for i in range(co...]
    psum x2 -> x0, waiting for transfers between devices: 99 us -> none  [the longest x1 54.1 us: head_split_body(): out_grads[layer] = wide(lax.psum(out_share, 'ctx'))]
    dot_general x24 -> x10, matrix products: 120 us -> 31.7 us  [mm(): lax.dot_general(left, right, dims, preferred_element_type=jnp.float32)]
    ppermute x94 -> x41, starting transfers between devices: 126 us -> 39.8 us  [swap(): return lax.ppermute(block, 'ctx', [(i, i ^ mask) for i in devices])]
    pallas_call x12 -> x14, Pallas kernels: 170 us -> 229 us  [the longest x2 66.9 us: attention_backward(): pl.pallas_call(attention_backward_kernel, grid_spec=pltpu.PrefetchScalarG...]
    ppermute x39 -> x12, starting transfers between devices: 53.7 us -> 16.3 us  [turn(): lax.ppermute(block, 'wsh', [(i, (i + distance) % count) for i in range(co...]
    concatenate x9 -> x18, other arithmetic: 50.5 us -> 18.5 us  [the longest x2 3.24 us: head_split_body(): jnp.concatenate([hidden_turned, swap(hidden_turned, CORE)], axis=0)]
  transfers between devices with their start and end apart: 139 -> 65, of which waited for: 67 -> 22; matrix products, arithmetic and copies ran while one was open for 20% -> 21% of each run, Pallas kernels for 13% -> 22%
where the time goes in v2:
time: 836 us; the launch traced here: 824 us
  Pallas kernels  229 us (27%)
  waiting for transfers between devices  218 us (26%)
  starting transfers between devices  92.8 us (11%)
  local copies, waits for them, and re-layouts  92.2 us (11%)
  other arithmetic  88.9 us (11%)
  blocking collectives  38.4 us (5%)
  between operations  33.3 us (4%)
  matrix products  31.7 us (4%)
    ppermute x41, waiting for transfers between devices, swap(): return lax.ppermute(block, 'ctx', [(i, i ^ mask) for i in devices])  114 us
    ppermute x12, waiting for transfers between devices, turn(): lax.ppermute(block, 'wsh', [(i, (i + distance) % count) for i in range(co...  77.4 us
    pallas_call x2, Pallas kernels, attention_backward(): pl.pallas_call(attention_backward_kernel, grid_spec=pltpu.PrefetchScalarG...  66.9 us
    pallas_call x2, Pallas kernels, attention_forward(): pl.pallas_call(attention_forward_kernel, grid_spec=pltpu.PrefetchScalarGr...  50.6 us
    unnamed x390, local copies, waits for them, and re-layouts  44.9 us
    ppermute x41, starting transfers between devices, swap(): return lax.ppermute(block, 'ctx', [(i, i ^ mask) for i in devices])  39.8 us
    pallas_call x2, Pallas kernels, feed_forward(): pl.pallas_call(functools.partial(feed_forward_kernel, count), grid=(4,),...  32.1 us
    dot_general x10, matrix products, mm(): lax.dot_general(left, right, dims, preferred_element_type=jnp.float32)  31.7 us
  transfers between devices with their start and end apart: 65, of which 22 were waited for; matrix products, arithmetic and copies ran while one was open for 21% of the time, Pallas kernels for 22%

profile of v2, /device:TPU:9, one launch (start us, length us, event | category | flops | bytes accessed | tf_op | source)
XLA Modules:
  0.0 823.8 jit_solution(6567790493941828008)
XLA Ops:
  62.1 33.8 %collective-permute-done.9 = bf16[256,1152]{1,0:T(8,128)(2,1)S(1)} collective-permute-done((bf16[256,1152]{1,0:T(8,128)(2,1)}, bf16[256,1152]{1,0:T(8,128)(2,1)S(1)}, u32[]{:S(2)}, u32[]{:S(2)}) %collective-permute-start.9) | collective-permute-done | bytes 589856 | tf_op jit(solution)/shard_map/ppermute | solution.py:541
  109.2 14.2 %collective-permute-done.17.refs_6_ = bf16[768,512]{1,0:T(8,128)(2,1)} collective-permute-done((bf16[768,512]{1,0:T(8,128)(2,1)}, bf16[768,512]{1,0:T(8,128)(2,1)}, u32[]{:S(2)}, u32[]{:S(2)}) %collective-permute-start.17) | collective-permute-done | bytes 786464 | tf_op jit(solution)/shard_map/ppermute | solution.py:536
  136.3 25.3 %attention_forward.2 = (bf16[2048,128]{1,0:T(8,128)(2,1)}, f32[2,2048]{1,0:T(2,128)}) custom-call(s32[8]{0:T(128)} %get-tuple-element.352.order_ref, bf16[2048,384]{1,0:T(8,128)(2,1)} %add_convert_fusion.1.query_ref.key_ref.value_ref, bf16[2048,384]{1,0:T(8,128)(2,1)} %add_convert_fusion.1.query_ref.key_ref.value_ref, ...), custom_call_target="tpu_custom_call" | custom-call | flops 8589934592 | bytes 2097152 | tf_op jit(solution)/shard_map/attention_forward/pallas_call | solution.py:596
  189.1 17.4 %feed_forward.2 = (f32[256,1024]{1,0:T(8,128)}, bf16[256,1024]{1,0:T(8,128)(2,1)}, bf16[512,2048]{1,0:T(8,128)(2,1)}, bf16[512,2048]{1,0:T(8,128)(2,1)}) custom-call(bf16[512,1024]{1,0:T(8,128)(2,1)} %pad_maximum_fusion.15.hidden_ref, f32[1,2048]{1,0:T(1,128)} %maximum_convert_fusion.bias_ref, bf16[2,4,256,512]{3,2,1,0:T(8,128)(2,1)} %get-tuple-element.72.own_inner, ...), custom_call_target="tpu_custom_call" | custom-call | flops 4294967296 | bytes 8388608 | tf_op jit(solution)/shard_map/feed_forward/pallas_call | solution.py:961
  211.6 8.3 %collective-permute-done.22 = bf16[256,512]{1,0:T(8,128)(2,1)S(1)} collective-permute-done((bf16[256,512]{1,0:T(8,128)(2,1)S(1)}, bf16[256,512]{1,0:T(8,128)(2,1)S(1)}, u32[]{:S(2)}, u32[]{:S(2)}) %collective-permute-start.22) | collective-permute-done | bytes 262176 | tf_op jit(solution)/shard_map/ppermute | solution.py:536
  221.8 18.5 %collective-permute-done.23 = bf16[2,256,512]{2,1,0:T(8,128)(2,1)S(1)} collective-permute-done((bf16[2,256,512]{2,1,0:T(8,128)(2,1)S(1)}, bf16[2,256,512]{2,1,0:T(8,128)(2,1)S(1)}, u32[]{:S(2)}, u32[]{:S(2)}) %collective-permute-start.23) | collective-permute-done | bytes 524320 | tf_op jit(solution)/shard_map/ppermute | solution.py:536
  257.6 25.3 %attention_forward.3 = (bf16[2048,128]{1,0:T(8,128)(2,1)}, f32[2,2048]{1,0:T(2,128)}) custom-call(s32[8]{0:T(128)} %get-tuple-element.352.order_ref, bf16[2048,384]{1,0:T(8,128)(2,1)} %add_convert_fusion.query_ref.key_ref.value_ref, bf16[2048,384]{1,0:T(8,128)(2,1)} %add_convert_fusion.query_ref.key_ref.value_ref, ...), custom_call_target="tpu_custom_call" | custom-call | flops 8589934592 | bytes 2097152 | tf_op jit(solution)/shard_map/attention_forward/pallas_call | solution.py:596
  286.7 10.1 %reduce-scatter.4.cloned.1.call-start = ((), (), s32[]{:S(2)}) async-start(), calls=%async_computation.10 | async-start | bytes 11796480 | tf_op jit(solution)/shard_map/reduce_scatter | solution.py:1458
  315.8 14.7 %feed_forward.3 = (f32[256,1024]{1,0:T(8,128)}, bf16[256,1024]{1,0:T(8,128)(2,1)}, bf16[512,2048]{1,0:T(8,128)(2,1)}, bf16[512,2048]{1,0:T(8,128)(2,1)}) custom-call(bf16[512,1024]{1,0:T(8,128)(2,1)} %pad_maximum_fusion.16.hidden_ref, f32[1,2048]{1,0:T(1,128)} %maximum_convert_fusion.1.bias_ref, bf16[2,4,256,512]{3,2,1,0:T(8,128)(2,1)} %get-tuple-element.72.own_inner, ...), custom_call_target="tpu_custom_call" | custom-call | flops 4294967296 | bytes 8388608 | tf_op jit(solution)/shard_map/feed_forward/pallas_call | solution.py:961
  339.8 10.2 %feed_backward.2 = (f32[256,1024]{1,0:T(8,128)}, bf16[256,1024]{1,0:T(8,128)(2,1)}, bf16[512,2048]{1,0:T(8,128)(2,1)}, f32[1,2048]{1,0:T(1,128)}) custom-call(bf16[512,1024]{1,0:T(8,128)(2,1)} %pad_maximum_fusion.17.grad_ref, bf16[512,2048]{1,0:T(8,128)(2,1)} %get-tuple-element.80.slope_ref, bf16[2,4,256,512]{3,2,1,0:T(8,128)(2,1)} %get-tuple-element.72.own_inner, ...), custom_call_target="tpu_custom_call" | custom-call | flops 4294967296 | bytes 8388608 | tf_op jit(solution)/shard_map/feed_backward/pallas_call | solution.py:1007
  364.8 12.5 %weight_gradients.3 = bf16[4,1024,1152]{2,1,0:T(8,128)(2,1)} custom-call(s32[4]{0:T(128)} %pad_add_fusion.4.rows_ref, bf16[512,1024]{1,0:T(8,128)(2,1)} %pad_maximum_fusion.16.hidden_ref, bf16[512,1024]{1,0:T(8,128)(2,1)} %pad_maximum_fusion.17.grad_ref, bf16[512,1024]{1,0:T(8,128)(2,1)} %pad_maximum_fusion.20.mixed_ref, ...), custom_call_target="tpu_custom_call" | custom-call | flops 4294967296 | bytes 16777216 | tf_op jit(solution)/shard_map/weight_gradients/pallas_call | solution.py:1097
  380.8 16.2 %all_to_all.39 = bf16[8,256,128]{2,1,0:T(8,128)(2,1)} all-to-all(bf16[8,256,128]{2,1,0:T(8,128)(2,1)S(1)} %constant_dynamic-update-slice_fusion.78), channel_id=1, replica_groups=mesh['ctx'=8,'wsh'=4] {'ctx'}, dimensions={0} | all-to-all | bytes 1048576 | tf_op jit(solution)/shard_map/all_to_all | solution.py:1189
  396.9 33.4 %attention_backward.2 = (bf16[2048,128]{1,0:T(8,128)(2,1)}, bf16[2048,128]{1,0:T(8,128)(2,1)}, bf16[2048,128]{1,0:T(8,128)(2,1)}) custom-call(s32[8]{0:T(128)} %get-tuple-element.352.order_ref, bf16[2048,384]{1,0:T(8,128)(2,1)} %add_convert_fusion.query_ref.key_ref.value_ref, bf16[2048,384]{1,0:T(8,128)(2,1)} %add_convert_fusion.query_ref.key_ref.value_ref, ...), custom_call_target="tpu_custom_call" | custom-call | flops 8589934592 | bytes 4194304 | tf_op jit(solution)/shard_map/attention_backward/pallas_call | solution.py:685
  476.2 23.4 %all-to-all-done.3 = bf16[4,256,1024]{2,1,0:T(8,128)(2,1)} async-done(((bf16[4,256,1024]{2,1,0:T(8,128)(2,1)}), bf16[4,256,1024]{2,1,0:T(8,128)(2,1)}, u32[]{:S(2)}, u32[]{:S(2)}) %all-to-all-start.3) | async-done | bytes 2097184 | tf_op jit(solution)/shard_map/all_to_all | solution.py:1171
  507.8 11.5 %feed_backward.3 = (f32[256,1024]{1,0:T(8,128)}, bf16[256,1024]{1,0:T(8,128)(2,1)}, bf16[512,2048]{1,0:T(8,128)(2,1)}, f32[1,2048]{1,0:T(1,128)}) custom-call(bf16[512,1024]{1,0:T(8,128)(2,1)} %pad_maximum_fusion.18.grad_ref, bf16[512,2048]{1,0:T(8,128)(2,1)} %get-tuple-element.87.slope_ref, bf16[2,4,256,512]{3,2,1,0:T(8,128)(2,1)} %get-tuple-element.72.own_inner, ...), custom_call_target="tpu_custom_call" | custom-call | flops 4294967296 | bytes 8388608 | tf_op jit(solution)/shard_map/feed_backward/pallas_call | solution.py:1007
  541.7 13.1 %weight_gradients.2 = (bf16[2,512,1152]{2,1,0:T(8,128)(2,1)}, bf16[2,512,1152]{2,1,0:T(8,128)(2,1)}, bf16[2,512,1152]{2,1,0:T(8,128)(2,1)}, bf16[2,512,1152]{2,1,0:T(8,128)(2,1)}) custom-call(s32[4]{0:T(128)} %pad_add_fusion.4.rows_ref, bf16[512,1024]{1,0:T(8,128)(2,1)} %pad_maximum_fusion.15.hidden_ref, bf16[512,1024]{1,0:T(8,128)(2,1)} %pad_maximum_fusion.18.grad_ref, ...), custom_call_target="tpu_custom_call" | custom-call | flops 4294967296 | bytes 16777216 | tf_op jit(solution)/shard_map/weight_gradients/pallas_call | solution.py:1097
  558.1 33.4 %attention_backward.3 = (bf16[2048,128]{1,0:T(8,128)(2,1)}, bf16[2048,128]{1,0:T(8,128)(2,1)}, bf16[2048,128]{1,0:T(8,128)(2,1)}) custom-call(s32[8]{0:T(128)} %get-tuple-element.352.order_ref, bf16[2048,384]{1,0:T(8,128)(2,1)} %add_convert_fusion.1.query_ref.key_ref.value_ref, bf16[2048,384]{1,0:T(8,128)(2,1)} %add_convert_fusion.1.query_ref.key_ref.value_ref, ...), custom_call_target="tpu_custom_call" | custom-call | flops 8589934592 | bytes 4194304 | tf_op jit(solution)/shard_map/attention_backward/pallas_call | solution.py:685
  619.5 30.4 %collective-permute-done.40 = bf16[512,1152]{1,0:T(8,128)(2,1)S(1)} collective-permute-done((bf16[512,1152]{1,0:T(8,128)(2,1)S(1)}, bf16[512,1152]{1,0:T(8,128)(2,1)S(1)}, u32[]{:S(2)}, u32[]{:S(2)}) %collective-permute-start.40) | collective-permute-done | bytes 1179680 | tf_op jit(solution)/shard_map/ppermute | solution.py:536
  671.3 38.8 %collective-permute-done.45 = bf16[256,384]{1,0:T(8,128)(2,1)S(1)} collective-permute-done((bf16[256,384]{1,0:T(8,128)(2,1)S(1)}, bf16[256,384]{1,0:T(8,128)(2,1)S(1)}, u32[]{:S(2)}, u32[]{:S(2)}) %collective-permute-start.45) | collective-permute-done | bytes 196640 | tf_op jit(solution)/shard_map/ppermute | solution.py:541
  712.3 8.6 %collective-permute-done.48 = bf16[256,768]{1,0:T(8,128)(2,1)S(1)} collective-permute-done((bf16[256,768]{1,0:T(8,128)(2,1)S(1)}, bf16[256,768]{1,0:T(8,128)(2,1)S(1)}, u32[]{:S(2)}, u32[]{:S(2)}) %collective-permute-start.48) | collective-permute-done | bytes 393248 | tf_op jit(solution)/shard_map/ppermute | solution.py:536
  731.3 7.6 collective-permute-done.49
  760.2 22.3 %all-gather.3 = f32[49152]{0:T(1024)} all-gather(f32[6144]{0:T(1024)S(1)} %reduce_sum.354), channel_id=5, replica_groups=mesh['ctx'=8,'wsh'=4] {'ctx'}, dimensions={0}, use_global_device_ids=true | all-gather | bytes 221184 | tf_op jit(solution)/shard_map/all_gather | solution.py:1498
  795.7 10.4 %place_pieces.2 = (f32[2,256,1024]{2,1,0:T(8,128)}, f32[2,256,1024]{2,1,0:T(8,128)}, f32[2,256,1024]{2,1,0:T(8,128)}, f32[2,256,1024]{2,1,0:T(8,128)}, f32[2,256,4096]{2,1,0:T(8,128)}, /*index=5*/f32[2,4096,256]{2,1,0:T(8,128)}) custom-call(s32[8]{0:T(128)} %iota.32.order_ref, bf16[8,256,1536]{2,1,0:T(8,128)(2,1)} %bitcast.365, bf16[8,256,1536]{2,1,0:T(8,128)(2,1)} %bitcast.366), custom_call_target="tpu_custom_call" | custom-call | bytes 18874368 | tf_op jit(solution)/shard_map/place_pieces/pallas_call | solution.py:843
  806.1 10.4 %place_pieces.3 = (f32[2,256,1024]{2,1,0:T(8,128)}, f32[2,256,1024]{2,1,0:T(8,128)}, f32[2,256,1024]{2,1,0:T(8,128)}, f32[2,256,1024]{2,1,0:T(8,128)}, f32[2,256,4096]{2,1,0:T(8,128)}, /*index=5*/f32[2,4096,256]{2,1,0:T(8,128)}) custom-call(s32[8]{0:T(128)} %pad_add_fusion.3.order_ref, ...), custom_call_target="tpu_custom_call", output_to_operand_aliasing={{0}: (3, {}), {1}: (4, {}), {2}: (5, {}), {3}: (6, {}), {4}... | custom-call | bytes 18874368 | tf_op jit(solution)/shard_map/place_pieces/pallas_call | solution.py:843
  (773 shorter events, 340.6 us)
Async XLA Ops:
  7.2 172.4 %all-gather.8.cloned.1.call-start = ((), (), s32[]{:S(2)}) async-start(), calls=%async_computation.13 | async-start | bytes 3932160 | tf_op jit(solution)/shard_map/all_gather | solution.py:1284
  51.3 44.6 %collective-permute-start.9 = (bf16[256,1152]{1,0:T(8,128)(2,1)}, bf16[256,1152]{1,0:T(8,128)(2,1)S(1)}, u32[]{:S(2)}, u32[]{:S(2)}) collective-permute-start(bf16[256,1152]{1,0:T(8,128)(2,1)} %get-tuple-element.71), channel_id=1, source_target_pairs={{0,2},{1,3},{2,0},{3,1},{4,6},{5,7},{6,4},{7,5},{8,10},{9,11},{10,... | collective-permute-start | bytes 1769480 | tf_op jit(solution)/shard_map/ppermute | solution.py:541
  52.7 48.0 %collective-permute-start.10 = (bf16[256,1152]{1,0:T(8,128)(2,1)}, bf16[256,1152]{1,0:T(8,128)(2,1)S(1)}, u32[]{:S(2)}, u32[]{:S(2)}) collective-permute-start(bf16[256,1152]{1,0:T(8,128)(2,1)} %get-tuple-element.71), channel_id=1, source_target_pairs={{0,3},{1,0},{2,1},{3,2},{4,7},{5,4},{6,5},{7,6},{8,11},{9,8},{10,9... | collective-permute-start | bytes 1769480 | tf_op jit(solution)/shard_map/ppermute | solution.py:541
  57.9 71.7 %collective-permute-start.4 = (bf16[4,256,1024]{2,1,0:T(8,128)(2,1)}, bf16[4,256,1024]{2,1,0:T(8,128)(2,1)}, u32[]{:S(2)}, u32[]{:S(2)}) collective-permute-start(bf16[4,256,1024]{2,1,0:T(8,128)(2,1)} %maximum_maximum_fusion.1), channel_id=1, source_target_pairs={{0,4},{4,0},{8,12},{12,8},{16,20},{20,16},{24,28},{28,24},{1,5},{5... | collective-permute-start | bytes 6291464 | tf_op jit(solution)/shard_map/ppermute | solution.py:536
  108.7 59.4 %collective-permute-start.12 = (bf16[768,640]{1,0:T(8,128)(2,1)}, bf16[768,640]{1,0:T(8,128)(2,1)}, u32[]{:S(2)}, u32[]{:S(2)}) collective-permute-start(bf16[768,640]{1,0:T(8,128)(2,1)} %pad_maximum_fusion.21.refs_0_), channel_id=1, source_target_pairs={{0,16},{4,20},{8,24},{12,28},{16,0},{20,4},{24,8},{28,12},{1,17},{... | collective-permute-start | bytes 2949128 | tf_op jit(solution)/shard_map/ppermute | solution.py:536
  109.0 80.1 %collective-permute-start.16 = (bf16[768,512]{1,0:T(8,128)(2,1)}, bf16[768,512]{1,0:T(8,128)(2,1)}, u32[]{:S(2)}, u32[]{:S(2)}) collective-permute-start(bf16[768,512]{1,0:T(8,128)(2,1)} %get-tuple-element.206.refs_4_), channel_id=1, source_target_pairs={{0,8},{4,12},{8,0},{12,4},{16,24},{20,28},{24,16},{28,20},{1,9},{5... | collective-permute-start | bytes 2359304 | tf_op jit(solution)/shard_map/ppermute | solution.py:536
  123.4 65.7 %collective-permute-start.18 = (bf16[768,512]{1,0:T(8,128)(2,1)}, bf16[768,512]{1,0:T(8,128)(2,1)}, u32[]{:S(2)}, u32[]{:S(2)}) collective-permute-start(bf16[768,512]{1,0:T(8,128)(2,1)} %collective-permute-done.17.refs_6_), channel_id=1, source_target_pairs={{0,8},{4,12},{8,0},{12,4},{16,24},{20,28},{24,16},{28,20},{1,9},{5... | collective-permute-start | bytes 2359304 | tf_op jit(solution)/shard_map/ppermute | solution.py:536
  168.0 129.2 %all-gather.10.cloned.1.call-start = ((), (), s32[]{:S(2)}) async-start(), calls=%async_computation.14 | async-start | bytes 8847360 | tf_op jit(solution)/shard_map/all_gather | solution.py:1287
  286.7 247.7 %reduce-scatter.4.cloned.1.call-start = ((), (), s32[]{:S(2)}) async-start(), calls=%async_computation.10 | async-start | bytes 11796480 | tf_op jit(solution)/shard_map/reduce_scatter | solution.py:1458
  455.3 44.3 %all-to-all-start.3 = ((bf16[4,256,1024]{2,1,0:T(8,128)(2,1)}), bf16[4,256,1024]{2,1,0:T(8,128)(2,1)}, u32[]{:S(2)}, u32[]{:S(2)}) async-start(bf16[4,256,1024]{2,1,0:T(8,128)(2,1)} %pad_maximum_fusion.4), calls=%async_computation.3 | async-start | bytes 4194304 | tf_op jit(solution)/shard_map/all_to_all | solution.py:1171
  460.0 149.1 %reduce-scatter.8.cloned.1.call-start = ((), (), s32[]{:S(2)}) async-start(), calls=%async_computation.12 | async-start | bytes 983040 | tf_op jit(solution)/shard_map/reduce_scatter | solution.py:1466
  525.7 83.4 %reduce-scatter.6.cloned.1.call-start = ((), (), s32[]{:S(2)}) async-start(), calls=%async_computation.11 | async-start | bytes 2949120 | tf_op jit(solution)/shard_map/reduce_scatter | solution.py:1465
  540.6 254.6 %all-gather.12.cloned.1.call-start = ((), (), s32[]{:S(2)}) async-start(), calls=%async_computation.15 | async-start | bytes 7077888 | tf_op jit(solution)/shard_map/all_gather | solution.py:1467
  554.7 62.8 %collective-permute-start.36 = (bf16[2,512,1152]{2,1,0:T(8,128)(2,1)}, bf16[2,512,1152]{2,1,0:T(8,128)(2,1)}, u32[]{:S(2)}, u32[]{:S(2)}) collective-permute-start(bf16[2,512,1152]{2,1,0:T(8,128)(2,1)} %get-tuple-element.97), channel_id=1, source_target_pairs={{0,8},{4,12},{8,0},{12,4},{16,24},{20,28},{24,16},{28,20},{1,9},{5... | collective-permute-start | bytes 7077896 | tf_op jit(solution)/shard_map/ppermute | solution.py:536
  556.1 55.1 %collective-permute-start.39 = (bf16[2,512,1152]{2,1,0:T(8,128)(2,1)}, bf16[2,512,1152]{2,1,0:T(8,128)(2,1)}, u32[]{:S(2)}, u32[]{:S(2)}) collective-permute-start(bf16[2,512,1152]{2,1,0:T(8,128)(2,1)} %get-tuple-element.99), channel_id=1, source_target_pairs={{0,16},{4,20},{8,24},{12,28},{16,0},{20,4},{24,8},{28,12},{1,17},{... | collective-permute-start | bytes 7077896 | tf_op jit(solution)/shard_map/ppermute | solution.py:536
  600.4 64.8 %collective-permute-start.47 = (bf16[256,384]{1,0:T(8,128)(2,1)}, bf16[256,384]{1,0:T(8,128)(2,1)S(1)}, u32[]{:S(2)}, u32[]{:S(2)}) collective-permute-start(bf16[256,384]{1,0:T(8,128)(2,1)} %get-tuple-element.245), channel_id=1, source_target_pairs={{0,1},{1,2},{2,3},{3,0},{4,5},{5,6},{6,7},{7,4},{8,9},{9,10},{10,1... | collective-permute-start | bytes 589832 | tf_op jit(solution)/shard_map/ppermute | solution.py:541
  601.7 66.1 %collective-permute-start.46 = (bf16[256,384]{1,0:T(8,128)(2,1)}, bf16[256,384]{1,0:T(8,128)(2,1)}, u32[]{:S(2)}, u32[]{:S(2)}) collective-permute-start(bf16[256,384]{1,0:T(8,128)(2,1)} %get-tuple-element.246), channel_id=1, source_target_pairs={{0,2},{1,3},{2,0},{3,1},{4,6},{5,7},{6,4},{7,5},{8,10},{9,11},{10,... | collective-permute-start | bytes 589832 | tf_op jit(solution)/shard_map/ppermute | solution.py:541
  619.4 43.9 %collective-permute-start.37 = (bf16[512,1152]{1,0:T(8,128)(2,1)S(1)}, bf16[512,1152]{1,0:T(8,128)(2,1)S(1)}, u32[]{:S(2)}, u32[]{:S(2)}) collective-permute-start(bf16[512,1152]{1,0:T(8,128)(2,1)S(1)} %fusion.18), channel_id=1, source_target_pairs={{0,16},{4,20},{8,24},{12,28},{16,0},{20,4},{24,8},{28,12},{1,17},{... | collective-permute-start | bytes 3538952 | tf_op jit(solution)/shard_map/ppermute | solution.py:536
  651.8 59.5 %collective-permute-start.42 = (bf16[256,1152]{1,0:T(8,128)(2,1)S(1)}, bf16[256,1152]{1,0:T(8,128)(2,1)S(1)}, u32[]{:S(2)}, u32[]{:S(2)}) collective-permute-start(bf16[256,1152]{1,0:T(8,128)(2,1)S(1)} %get-tuple-element.211), channel_id=1, source_target_pairs={{0,1},{1,2},{2,3},{3,0},{4,5},{5,6},{6,7},{7,4},{8,9},{9,10},{10,1... | collective-permute-start | bytes 1769480 | tf_op jit(solution)/shard_map/ppermute | solution.py:541
  651.8 59.4 %collective-permute-start.41 = (bf16[256,1152]{1,0:T(8,128)(2,1)S(1)}, bf16[256,1152]{1,0:T(8,128)(2,1)S(1)}, u32[]{:S(2)}, u32[]{:S(2)}) collective-permute-start(bf16[256,1152]{1,0:T(8,128)(2,1)S(1)} %get-tuple-element.210), channel_id=1, source_target_pairs={{0,2},{1,3},{2,0},{3,1},{4,6},{5,7},{6,4},{7,5},{8,10},{9,11},{10,... | collective-permute-start | bytes 1769480 | tf_op jit(solution)/shard_map/ppermute | solution.py:541
  665.0 46.2 %collective-permute-start.38 = (bf16[256,1152]{1,0:T(8,128)(2,1)S(1)}, bf16[256,1152]{1,0:T(8,128)(2,1)S(1)}, u32[]{:S(2)}, u32[]{:S(2)}) collective-permute-start(bf16[256,1152]{1,0:T(8,128)(2,1)S(1)} %slice.623), channel_id=1, source_target_pairs={{0,3},{1,0},{2,1},{3,2},{4,7},{5,4},{6,5},{7,6},{8,11},{9,8},{10,9... | collective-permute-start | bytes 1769480 | tf_op jit(solution)/shard_map/ppermute | solution.py:541
  665.1 45.0 %collective-permute-start.45 = (bf16[256,384]{1,0:T(8,128)(2,1)S(1)}, bf16[256,384]{1,0:T(8,128)(2,1)S(1)}, u32[]{:S(2)}, u32[]{:S(2)}) collective-permute-start(bf16[256,384]{1,0:T(8,128)(2,1)S(1)} %get-tuple-element.244), channel_id=1, source_target_pairs={{0,3},{1,0},{2,1},{3,2},{4,7},{5,4},{6,5},{7,6},{8,11},{9,8},{10,9... | collective-permute-start | bytes 589832 | tf_op jit(solution)/shard_map/ppermute | solution.py:541
  667.9 59.8 %collective-permute-start.33 = (bf16[4,256,1024]{2,1,0:T(8,128)(2,1)}, bf16[4,256,1024]{2,1,0:T(8,128)(2,1)}, u32[]{:S(2)}, u32[]{:S(2)}) collective-permute-start(bf16[4,256,1024]{2,1,0:T(8,128)(2,1)} %fusion.6), channel_id=1, source_target_pairs={{0,4},{4,0},{8,12},{12,8},{16,20},{20,16},{24,28},{28,24},{1,5},{5... | collective-permute-start | bytes 6291464 | tf_op jit(solution)/shard_map/ppermute | solution.py:536
  741.9 64.2 %collective-permute-start.50 = (bf16[4,256,1536]{2,1,0:T(8,128)(2,1)}, bf16[4,256,1536]{2,1,0:T(8,128)(2,1)}, u32[]{:S(2)}, u32[]{:S(2)}) collective-permute-start(bf16[4,256,1536]{2,1,0:T(8,128)(2,1)} %maximum_maximum_fusion.near_ref), channel_id=1, source_target_pairs={{0,4},{4,0},{8,12},{12,8},{16,20},{20,16},{24,28},{28,24},{1,5},{5... | collective-permute-start | bytes 9437192 | tf_op jit(solution)/shard_map/ppermute | solution.py:536
  (184 other events, 2823.1 us)
Sparse Core Ops, SparseCore 0:
  109.4 61.8 all-gather.7
  183.1 90.4 all-gather.9
  377.4 123.5 reduce-scatter.3
  525.8 20.6 reduce-scatter.7
  548.6 47.0 reduce-scatter.5
  611.3 64.3 all-gather.11

commit v3 on v2

--- a/solution.py
+++ b/solution.py
@@ -525,6 +525,13 @@
 LANES = 128
 QUERY_BLOCK = 256
 CORE, ALONG_X, ALONG_Y = 1, 2, 4
+SMALL_COST = pl.CostEstimate(flops=1000, bytes_accessed=1000, transcendentals=0)
+
+
+def lasting(microseconds):
+    return pl.CostEstimate(
+        flops=int(microseconds * 1.15e9), bytes_accessed=int(microseconds * 3.6e6), transcendentals=0
+    )
 
 
 def mm(left, right, dims=NN):
@@ -618,9 +625,7 @@
             jax.ShapeDtypeStruct((rows, LANES), jnp.bfloat16),
             jax.ShapeDtypeStruct((2, rows), jnp.float32),
         ],
-        cost_estimate=pl.CostEstimate(
-            flops=16 * rows * rows * LANES, bytes_accessed=rows * 1024, transcendentals=2 * rows * rows
-        ),
+        cost_estimate=lasting(25),
         name="attention_forward",
     )(order, packed, packed, packed, labels, labels)
 
@@ -705,24 +710,28 @@
             ],
         ),
         out_shape=[jax.ShapeDtypeStruct((rows, LANES), jnp.bfloat16)] * 3,
-        cost_estimate=pl.CostEstimate(
-            flops=16 * rows * rows * LANES, bytes_accessed=rows * 2048, transcendentals=2 * rows * rows
-        ),
+        cost_estimate=lasting(33),
         name="attention_backward",
     )(order, packed, packed, packed, labels, labels, grad, log_all)
 
 
-def own_pieces(inner_weight, outer_weight, out_weight, joint_weights, here, first_block):
+def own_pieces(inner_weight, outer_weight, out_weight, joint_weights, small_params, here, first_block):
     layers, shard, hidden = inner_weight.shape
     piece = hidden // 8
-    total = 2 * piece + LANES
-
-    def kernel(place_ref, inner_ref, outer_ref, out_ref, query_ref, key_ref, value_ref, wide_ref, joint_ref):
-        wide_ref[0, :, :piece] = low(inner_ref[0])
-        wide_ref[0, :, piece : 2 * piece] = low(outer_ref[0]).T
-        wide_ref[0, :, 2 * piece :] = low(out_ref[0])
+    width = 3 * LANES
+
+    def kernel(place_ref, inner_ref, outer_ref, out_ref, query_ref, key_ref, value_ref, *refs):
+        small_refs, (first_ref, second_ref, joint_ref) = refs[:-3], refs[-3:]
+        first_ref[0, :, :piece] = low(inner_ref[0])
+        first_ref[0, :, piece:] = low(out_ref[0])
+        second_ref[0] = low(outer_ref[0]).T
         for at, ref in enumerate((query_ref, key_ref, value_ref)):
-            joint_ref[0, :, at * LANES : (at + 1) * LANES] = low(ref[0])
+            joint_ref[0, :shard, at * LANES : (at + 1) * LANES] = low(ref[0])
+        rows = [jnp.concatenate([ref[...] for ref in small_refs[:8]], axis=0)]
+        rows += [small_refs[8][:, q * shard : (q + 1) * shard] for q in range(4)]
+        rows += [jnp.zeros((8, shard), jnp.float32)]
+        packed = low(jnp.concatenate(rows, axis=0))
+        joint_ref[0, shard:] = jnp.concatenate([packed, jnp.zeros((32, width - shard), jnp.bfloat16)], axis=1)
 
     column = pl.BlockSpec((1, shard, LANES), lambda layer, place_ref: (layer, 0, place_ref[0]))
     return pl.pallas_call(
@@ -737,29 +746,37 @@
                 column,
                 column,
                 column,
-            ],
+            ]
+            + [pl.BlockSpec(param.shape, lambda layer, place_ref: (0, 0)) for param in small_params],
             out_specs=[
-                pl.BlockSpec((1, shard, total), lambda layer, place_ref: (layer, 0, 0)),
-                pl.BlockSpec((1, shard, 3 * LANES), lambda layer, place_ref: (layer, 0, 0)),
+                pl.BlockSpec((1, shard, piece + LANES), lambda layer, place_ref: (layer, 0, 0)),
+                pl.BlockSpec((1, shard, piece), lambda layer, place_ref: (layer, 0, 0)),
+                pl.BlockSpec((1, shard + 32, width), lambda layer, place_ref: (layer, 0, 0)),
             ],
         ),
         out_shape=[
-            jax.ShapeDtypeStruct((layers, shard, total), jnp.bfloat16),
-            jax.ShapeDtypeStruct((layers, shard, 3 * LANES), jnp.bfloat16),
+            jax.ShapeDtypeStruct((layers, shard, piece + LANES), jnp.bfloat16),
+            jax.ShapeDtypeStruct((layers, shard, piece), jnp.bfloat16),
+            jax.ShapeDtypeStruct((layers, shard + 32, width), jnp.bfloat16),
         ],
-        cost_estimate=pl.CostEstimate(
-            flops=0, bytes_accessed=layers * shard * (total + 3 * LANES) * 6, transcendentals=0
-        ),
+        cost_estimate=lasting(4),
         name="own_pieces",
-    )(jnp.stack([here, first_block]).astype(jnp.int32), inner_weight, outer_weight, out_weight, *joint_weights)
-
-
-def own_blocks(inner_weight, outer_weight, out_weight, inner_order, out_order):
+    )(
+        jnp.stack([here, first_block]).astype(jnp.int32),
+        inner_weight,
+        outer_weight,
+        out_weight,
+        *joint_weights,
+        *small_params,
+    )
+
+
+def own_blocks(inner_weight, outer_weight, out_weight, inner_order, out_order, after):
     layers, shard, hidden = inner_weight.shape
     piece = hidden // 8
 
     def kernel(inner_order_ref, out_order_ref, *refs):
-        ins, (inner_out, outer_out, out_out) = refs[:-3], refs[-3:]
+        ins, (inner_out, outer_out, out_out) = refs[:16], refs[-3:]
         for j in range(4):
             inner_out[0, j] = low(ins[j][0])
             outer_out[0, j] = low(ins[4 + j][0]).T
@@ -783,7 +800,8 @@
             grid=(layers,),
             in_specs=[inner_at(j) for j in range(4)]
             + [outer_at(j) for j in range(4)]
-            + [out_at(j) for j in range(8)],
+            + [out_at(j) for j in range(8)]
+            + [pl.BlockSpec(memory_space=pl.ANY)],
             out_specs=[block, block, pl.BlockSpec((1, shard, 8 * LANES), lambda layer, *_: (layer, 0, 0))],
         ),
         out_shape=[
@@ -791,11 +809,9 @@
             jax.ShapeDtypeStruct((layers, 4, shard, piece), jnp.bfloat16),
             jax.ShapeDtypeStruct((layers, shard, 8 * LANES), jnp.bfloat16),
         ],
-        cost_estimate=pl.CostEstimate(
-            flops=0, bytes_accessed=layers * 8 * shard * (piece + LANES) * 6, transcendentals=0
-        ),
+        cost_estimate=lasting(7),
         name="own_blocks",
-    )(inner_order, out_order, *[inner_weight] * 4, *[outer_weight] * 4, *[out_weight] * 8)
+    )(inner_order, out_order, *[inner_weight] * 4, *[outer_weight] * 4, *[out_weight] * 8, after)
 
 
 def place_pieces(near, far, order, layer, previous):
@@ -815,14 +831,17 @@
     outs = [square] * 4 + [
         jax.ShapeDtypeStruct((LAYERS, shard, 8 * piece), jnp.float32),
         jax.ShapeDtypeStruct((LAYERS, 8 * piece, shard), jnp.float32),
+        jax.ShapeDtypeStruct((8, LANES), jnp.float32),
     ]
     specs = [pl.BlockSpec((1, shard, LANES), column)] * 4 + [
         pl.BlockSpec((1, shard, piece), lambda i, order_ref: (layer, 0, inner_place(i, order_ref))),
         pl.BlockSpec((1, piece, shard), lambda i, order_ref: (layer, inner_place(i, order_ref), 0)),
+        pl.BlockSpec((8, LANES), lambda i, order_ref: (0, 0)),
     ]
 
     def kernel(order_ref, near_ref, far_ref, *refs):
-        query_out, key_out, value_out, out_out, inner_out, outer_out = refs[-6:]
+        query_out, key_out, value_out, out_out, inner_out, outer_out, token_out = refs[-7:]
+        token_out[...] = jnp.zeros_like(token_out)
 
         def write(source):
             inner_out[0] = wide(source[0, :, :piece])
@@ -856,9 +875,7 @@
         ),
         out_shape=outs,
         input_output_aliases={3 + i: i for i in range(len(held))},
-        cost_estimate=pl.CostEstimate(
-            flops=0, bytes_accessed=12 * count * shard * columns, transcendentals=0
-        ),
+        cost_estimate=lasting(10),
         name="place_pieces",
     )(order, near, far, *held)
 
@@ -890,26 +907,28 @@
         inner_now[shard:] = inner_refs[0][0]
         outer_now[shard:] = outer_refs[0][0]
         return
-    for j in range(len(inner_refs)):
+    chunks = len(inner_refs) // 4
+    rows = inner_refs[0].shape[0]
+    for j in range(4):
 
         @pl.when(step == j)
         def _(j=j):
-            inner_now[shard:] = inner_refs[j][...]
-            outer_now[shard:] = outer_refs[j][...]
+            for chunk in range(chunks):
+                begin = shard + chunk * rows
+                inner_now[begin : begin + rows] = inner_refs[j * chunks + chunk][...]
+                outer_now[begin : begin + rows] = outer_refs[j * chunks + chunk][...]
 
 
 def weight_operands(weights, layer):
     own_inner, own_outer, inner_parts, outer_parts = weights
     shard, piece = own_inner.shape[2:]
     own = pl.BlockSpec((1, 1, shard, piece), lambda i: (layer, i, 0, 0))
-    rest = 3 * shard
-    if inner_parts is outer_parts:
-        specs = [
-            pl.BlockSpec((1, rest, piece), lambda i: (i, 0, 0)),
-            pl.BlockSpec((1, rest, piece), lambda i: (i, 0, 1)),
-        ]
-        return ([own_inner, own_outer, inner_parts, outer_parts], [own, own] + specs, 1)
-    fixed = pl.BlockSpec((rest, piece), lambda i: (0, 0), pipeline_mode=pl.Buffered(1))
+    if len(inner_parts) == 1:
+        rest = inner_parts[0].shape[1]
+        part = pl.BlockSpec((1, rest, piece), lambda i: (i, 0, 0))
+        return ([own_inner, own_outer, *inner_parts, *outer_parts], [own, own, part, part], 1)
+    rows = inner_parts[0].shape[0]
+    fixed = pl.BlockSpec((rows, piece), lambda i: (0, 0), pipeline_mode=pl.Buffered(1))
     return (
         [own_inner, own_outer, *inner_parts, *outer_parts],
         [own, own] + [fixed] * (2 * len(inner_parts)),
@@ -978,9 +997,7 @@
             pltpu.VMEM((width, block), jnp.bfloat16),
             pltpu.VMEM((width, block), jnp.bfloat16),
         ],
-        cost_estimate=pl.CostEstimate(
-            flops=4 * rows * width * hidden, bytes_accessed=4 * width * hidden, transcendentals=2 * rows * hidden
-        ),
+        cost_estimate=lasting(16),
         name="feed_forward",
     )(hidden_pair, bias_row, *arrays)
 
@@ -1020,9 +1037,7 @@
             pltpu.VMEM((width, block), jnp.bfloat16),
             pltpu.VMEM((width, block), jnp.bfloat16),
         ],
-        cost_estimate=pl.CostEstimate(
-            flops=4 * rows * width * hidden, bytes_accessed=4 * width * hidden, transcendentals=0
-        ),
+        cost_estimate=lasting(11),
         name="feed_backward",
     )(grad_pair, slope, *arrays)
 
@@ -1036,6 +1051,7 @@
     inner_grad_ref,
     active_ref,
     branch_ref,
+    after_ref,
     *refs,
 ):
     outs, (hidden_t, grad_t, mixed_t) = refs[:-3], refs[-3:]
@@ -1054,13 +1070,15 @@
         store(2 * piece, 2 * piece + LANES, low(mm(mixed_t[...], branch_ref[...])))
 
     if not split:
-        (out_ref,) = outs
+        first_out, second_out = outs
 
         def store(begin, end, value):
             shard = value.shape[0] // 4
+            ref = second_out if begin == piece else first_out
+            column = {0: 0, piece: 0, 2 * piece: piece}[begin]
             for r in range(4):
                 place = pl.multiple_of(rows_ref[r] * shard, shard)
-                out_ref[0, pl.ds(place, shard), begin:end] = value[r * shard : (r + 1) * shard]
+                ref[0, pl.ds(place, shard), column : column + end - begin] = value[r * shard : (r + 1) * shard]
 
         write(store)
         return
@@ -1080,7 +1098,7 @@
             write(store)
 
 
-def weight_gradients(hidden_pair, grad_pair, mixed_pair, inner_grad, active, branch_pair, plane_rows, split):
+def weight_gradients(hidden_pair, grad_pair, mixed_pair, inner_grad, active, branch_pair, plane_rows, split, after):
     rows, width = hidden_pair.shape
     hidden = active.shape[1]
     piece = hidden // 4
@@ -1092,8 +1110,10 @@
         out_specs = [pl.BlockSpec(shape, lambda i, rows_ref: (0, 0, 0), pipeline_mode=pl.Buffered(1))] * 4
         out_shape = [jax.ShapeDtypeStruct(shape, jnp.bfloat16)] * 4
     else:
-        out_specs = [pl.BlockSpec((1, width, total), lambda i, rows_ref: (i, 0, 0))]
-        out_shape = [jax.ShapeDtypeStruct((4, width, total), jnp.bfloat16)]
+        out_specs = [
+            pl.BlockSpec((1, width, columns), lambda i, rows_ref: (i, 0, 0)) for columns in (piece + LANES, piece)
+        ]
+        out_shape = [jax.ShapeDtypeStruct((4, width, columns), jnp.bfloat16) for columns in (piece + LANES, piece)]
     return pl.pallas_call(
         functools.partial(weight_gradient_kernel, split),
         grid_spec=pltpu.PrefetchScalarGridSpec(
@@ -1106,16 +1126,15 @@
                 column,
                 column,
                 pl.BlockSpec((rows, LANES), lambda i, rows_ref: (0, i)),
+                pl.BlockSpec(memory_space=pl.ANY),
             ],
             out_specs=out_specs,
             scratch_shapes=[pltpu.VMEM((width, rows), jnp.bfloat16)] * 3,
         ),
         out_shape=out_shape,
-        cost_estimate=pl.CostEstimate(
-            flops=4 * rows * width * hidden, bytes_accessed=8 * width * hidden, transcendentals=0
-        ),
+        cost_estimate=lasting(13),
         name="weight_gradients",
-    )(plane_rows, hidden_pair, grad_pair, mixed_pair, inner_grad, active, branch_pair)
+    )(plane_rows, hidden_pair, grad_pair, mixed_pair, inner_grad, active, branch_pair, after)
 
 
 def block_columns(values_in, order, width):
@@ -1140,6 +1159,210 @@
         - unit * jnp.mean(grad_unit * unit, axis=-1, keepdims=True)
     )
     return (back, jnp.sum(grad * unit, axis=0), jnp.sum(grad, axis=0))
+
+
+def attention_output_kernel(
+    place_ref,
+    heads_ref,
+    own_ref,
+    near_ref,
+    far_ref,
+    activation_ref,
+    bias_ref,
+    gain_ref,
+    shift_ref,
+    mixed_ref,
+    unit_ref,
+    inverse_ref,
+    hidden_ref,
+    turned_ref,
+    held,
+    held_low,
+):
+    shard = own_ref.shape[0]
+    half = near_ref.shape[1]
+    for p in range(8):
+        mixed_ref[:, p * LANES : (p + 1) * LANES] = heads_ref[place_ref[p]]
+    own, rest = mixed_ref[:, :shard], mixed_ref[:, shard:]
+    held[:, :half] = mm(own, own_ref[:, :half]) + mm(rest, near_ref[...])
+    held[:, half:] = mm(own, own_ref[:, half:]) + mm(rest, far_ref[...])
+    attended = jnp.concatenate(
+        [held[:, pl.ds(pl.multiple_of(place_ref[8 + b] * LANES, LANES), LANES)] for b in range(8)], axis=1
+    )
+    first_pre = wide(activation_ref[...]) + (attended + bias_ref[...])
+    hidden, unit, inverse = norm_forward(first_pre, gain_ref[...], shift_ref[...])
+    unit_ref[...] = unit
+    inverse_ref[...] = inverse
+    hidden_ref[...] = hidden
+    held_low[...] = low(hidden)
+    for r in range(4):
+        turned_ref[:, r * shard : (r + 1) * shard] = held_low[
+            :, pl.ds(pl.multiple_of(place_ref[16 + r] * shard, shard), shard)
+        ]
+
+
+def attention_output(heads, out_weights, activation, bias_row, gain_row, shift_row, places):
+    rows, width = activation.shape
+    wide_rows = jax.ShapeDtypeStruct((rows, width), jnp.float32)
+    low_rows = jax.ShapeDtypeStruct((rows, width), jnp.bfloat16)
+    return pl.pallas_call(
+        attention_output_kernel,
+        grid_spec=pltpu.PrefetchScalarGridSpec(
+            num_scalar_prefetch=1,
+            grid=(1,),
+            in_specs=[
+                pl.BlockSpec(array.shape, lambda i, place_ref, rank=array.ndim: (0,) * rank)
+                for array in (heads, *out_weights, activation, bias_row, gain_row, shift_row)
+            ],
+            out_specs=[
+                pl.BlockSpec((rows, width), lambda i, place_ref: (0, 0)),
+                pl.BlockSpec((rows, width), lambda i, place_ref: (0, 0)),
+                pl.BlockSpec((rows, 1), lambda i, place_ref: (0, 0)),
+                pl.BlockSpec((rows, width), lambda i, place_ref: (0, 0)),
+                pl.BlockSpec((rows, width), lambda i, place_ref: (0, 0)),
+            ],
+            scratch_shapes=[pltpu.VMEM((rows, width), jnp.float32), pltpu.VMEM((rows, width), jnp.bfloat16)],
+        ),
+        out_shape=[low_rows, wide_rows, jax.ShapeDtypeStruct((rows, 1), jnp.float32), wide_rows, low_rows],
+        cost_estimate=lasting(5),
+        name="attention_output",
+    )(places, heads, *out_weights, activation, bias_row, gain_row, shift_row)
+
+
+def attention_output_back_kernel(
+    place_ref,
+    near_back_ref,
+    came_ref,
+    grad_ref,
+    unit_ref,
+    inverse_ref,
+    gain_ref,
+    own_ref,
+    near_ref,
+    far_ref,
+    first_ref,
+    rows_ref,
+    spread_ref,
+    sent_ref,
+    held,
+    held_low,
+):
+    shard = own_ref.shape[0]
+    half = near_ref.shape[1]
+    held[...] = near_back_ref[...] + wide(came_ref[...])
+    back = jnp.concatenate(
+        [held[:, pl.ds(pl.multiple_of(place_ref[16 + r] * shard, shard), shard)] for r in range(4)], axis=1
+    )
+    grad_first, gain_row, shift_row = norm_backward(
+        grad_ref[...] + back, unit_ref[...], inverse_ref[...], gain_ref[...]
+    )
+    first_ref[...] = grad_first
+    branch = low(grad_first)
+    rows_ref[0:1] = gain_row[None]
+    rows_ref[1:2] = shift_row[None]
+    rows_ref[2:3] = jnp.sum(wide(branch), axis=0, keepdims=True)
+    held_low[...] = branch
+    for p in range(8):
+        spread_ref[:, p * LANES : (p + 1) * LANES] = held_low[
+            :, pl.ds(pl.multiple_of(place_ref[24 + p] * LANES, LANES), LANES)
+        ]
+    spread = spread_ref[...]
+    held_low[:, :shard] = low(mm(spread, own_ref[...], NT))
+    held_low[:, shard:] = low(mm(spread[:, :half], near_ref[...], NT) + mm(spread[:, half:], far_ref[...], NT))
+    for head in range(8):
+        begin = place_ref[16 + head // 2] * shard + (head % 2) * LANES
+        sent_ref[head] = held_low[:, pl.ds(pl.multiple_of(begin, LANES), LANES)]
+
+
+def attention_output_back(near_back, came, grad_second, unit, inverse, gain_row, out_weights, places):
+    rows, width = grad_second.shape
+    operands = (near_back, came, grad_second, unit, inverse, gain_row, *out_weights)
+    whole = pl.BlockSpec((rows, width), lambda i, place_ref: (0, 0))
+    return pl.pallas_call(
+        attention_output_back_kernel,
+        grid_spec=pltpu.PrefetchScalarGridSpec(
+            num_scalar_prefetch=1,
+            grid=(1,),
+            in_specs=[pl.BlockSpec(array.shape, lambda i, place_ref: (0, 0)) for array in operands],
+            out_specs=[
+                whole,
+                pl.BlockSpec((3, width), lambda i, place_ref: (0, 0)),
+                whole,
+                pl.BlockSpec((8, rows, LANES), lambda i, place_ref: (0, 0, 0)),
+            ],
+            scratch_shapes=[pltpu.VMEM((rows, width), jnp.float32), pltpu.VMEM((rows, width), jnp.bfloat16)],
+        ),
+        out_shape=[
+            jax.ShapeDtypeStruct((rows, width), jnp.float32),
+            jax.ShapeDtypeStruct((3, width), jnp.float32),
+            jax.ShapeDtypeStruct((rows, width), jnp.bfloat16),
+            jax.ShapeDtypeStruct((8, rows, LANES), jnp.bfloat16),
+        ],
+        cost_estimate=lasting(6),
+        name="attention_output_back",
+    )(places, *operands)
+
+
+def token_gradient_kernel(
+    place_ref, query_ref, key_ref, value_ref, joint_ref, *refs
+):
+    near_ref, far_ref, packed_ref, bias_ref = refs[-4:]
+    step = pl.program_id(0)
+    packed = jnp.concatenate([query_ref[...], key_ref[...], value_ref[...]], axis=1)
+    packed_ref[...] = packed
+    accumulate(step, bias_ref, jnp.sum(wide(packed), axis=0, keepdims=True))
+    part = mm(packed, joint_ref[...], NT)
+
+    @pl.when(step < 4)
+    def _():
+        near_ref[0] = part
+
+    @pl.when(step >= 4)
+    def _():
+        far_ref[0] = low(part)
+
+
+def token_gradients(grads, joint, chips, after):
+    tokens = grads[0].shape[0]
+    rows = tokens // 8
+    width, columns = joint.shape
+    block = pl.BlockSpec((rows, LANES), lambda i, place_ref: (i, 0))
+    return pl.pallas_call(
+        token_gradient_kernel,
+        grid_spec=pltpu.PrefetchScalarGridSpec(
+            num_scalar_prefetch=1,
+            grid=(8,),
+            in_specs=[block, block, block, pl.BlockSpec((width, columns), lambda i, place_ref: (0, 0))]
+            + [pl.BlockSpec(memory_space=pl.ANY)] * len(after),
+            out_specs=[
+                pl.BlockSpec((1, rows, width), lambda i, place_ref: (place_ref[jnp.minimum(i, 3)], 0, 0)),
+                pl.BlockSpec((1, rows, width), lambda i, place_ref: (place_ref[jnp.maximum(i - 4, 0)], 0, 0)),
+                pl.BlockSpec((rows, columns), lambda i, place_ref: (i, 0)),
+                pl.BlockSpec((1, columns), lambda i, place_ref: (0, 0)),
+            ],
+        ),
+        out_shape=[
+            jax.ShapeDtypeStruct((4, rows, width), jnp.float32),
+            jax.ShapeDtypeStruct((4, rows, width), jnp.bfloat16),
+            jax.ShapeDtypeStruct((tokens, columns), jnp.bfloat16),
+            jax.ShapeDtypeStruct((1, columns), jnp.float32),
+        ],
+        cost_estimate=lasting(60 if after else 10),
+        name="token_gradients",
+    )(chips, *grads, joint, *after)
+
+
+def gate(values_in, *points):
+    anywhere = pl.BlockSpec(memory_space=pl.ANY)
+    return pl.pallas_call(
+        lambda *refs: None,
+        in_specs=[anywhere] * (len(values_in) + len(points)),
+        out_specs=[anywhere] * len(values_in),
+        out_shape=[jax.ShapeDtypeStruct(value.shape, value.dtype) for value in values_in],
+        input_output_aliases={i: i for i in range(len(values_in))},
+        cost_estimate=SMALL_COST,
+        name="gate",
+    )(*values_in, *points)
 
 
 def spread_tokens(rows_in):
@@ -1151,10 +1374,8 @@
     right_far = swap(right_pair, ALONG_X)
     left_all = jnp.concatenate([left_pair, left_far])
     right_all = jnp.stack([right_pair[0], right_far[0], right_pair[1], right_far[1]])
-    near = jnp.concatenate([left_all, right_all], axis=2)
-    far = swap(near, CORE)
-    both = jnp.stack([near, far], axis=1)
-    return both.reshape(8 * rows_in.shape[0], rows_in.shape[1])
+    near = jnp.concatenate([left_all, right_all], axis=2).reshape(4 * rows_in.shape[0], rows_in.shape[1])
+    return (near, swap(near, CORE))
 
 
 def plane_groups():
@@ -1162,23 +1383,20 @@
     return [list(range(0, count, 2)), list(range(1, count, 2))]
 
 
-def collect_tokens(partial, chip):
-    rows = partial.shape[0] // 8
-    width = partial.shape[1]
-    blocks = partial.reshape(4, 2, rows, width)
-    near = low(blocks[:, 0] + wide(swap(low(blocks[:, 1]), CORE)))
-    sent = jnp.stack([lax.dynamic_index_in_dim(near, chip ^ j, 0, keepdims=False) for j in range(4)])
+def collect_tokens(near, far_came, *points):
+    sent = low(near + wide(far_came))
+    if points:
+        (sent,) = gate([sent], *points)
     came = lax.all_to_all(sent, "ctx", 0, 0, axis_index_groups=plane_groups(), tiled=True)
     return jnp.sum(wide(came), axis=0)
 
 
-def plane_pieces(piece):
+def plane_pieces(piece, *points):
     half = piece.shape[1] // 2
     left, right = piece[:, :half], piece[:, half:]
     left_pair = jnp.stack([left, swap(left, ALONG_X)])
     right_pair = jnp.stack([right, swap(right, ALONG_Y)])
-    left_far = swap(left_pair, ALONG_Y)
-    right_far = swap(right_pair, ALONG_X)
+    left_far, right_far = gate([swap(left_pair, ALONG_Y), swap(right_pair, ALONG_X)], *points)
     left_all = jnp.concatenate([left_pair, left_far])
     right_all = jnp.stack([right_pair[0], right_far[0], right_pair[1], right_far[1]])
     near = jnp.concatenate([left_all, right_all], axis=2)
@@ -1221,88 +1439,85 @@
     core = here % 2
     chip = here // 2
     relative = jnp.arange(8, dtype=jnp.int32)
+    spread = jnp.array((0, 2, 4, 6, 1, 3, 5, 7), jnp.int32)
     turned = [(plane - r) % planes for r in range(planes)]
     unturned = turned
-    positions = ((here ^ relative)[:, None] * rows + jnp.arange(rows, dtype=jnp.int32)).reshape(-1)
+    positions = ((here ^ spread)[:, None] * rows + jnp.arange(rows, dtype=jnp.int32)).reshape(-1)
     labels = doc_labels(positions, doc_starts[0], doc_lengths[0])[:, None]
 
     four = jnp.arange(4, dtype=jnp.int32)
     chip_order = [chip ^ four, four]
     inner_order = [core * 4 + order for order in chip_order]
     out_order = [jnp.concatenate([2 * order + core, 2 * order + 1 - core]) for order in chip_order]
-    block_order = here ^ relative
+    block_order = here ^ spread
     plane_rows = jnp.stack(turned).astype(jnp.int32)
-    wide_own, joint_own = own_pieces(
+    first_own, second_own, joint_own = own_pieces(
         inner_weight,
         outer_weight,
         out_weight,
         (query_weight, key_weight, value_weight),
+        (
+            query_bias,
+            value_bias,
+            out_bias,
+            outer_bias,
+            first_gain,
+            first_shift,
+            second_gain,
+            second_shift,
+            inner_bias,
+        ),
         here,
         core * 4 + chip,
     )
-    inner_own, outer_own, out_own = own_blocks(
-        inner_weight, outer_weight, out_weight, jnp.concatenate(inner_order), jnp.concatenate(out_order)
-    )
-    small_own = low(
-        jnp.concatenate(
-            [
-                query_bias,
-                value_bias,
-                out_bias,
-                outer_bias,
-                first_gain,
-                first_shift,
-                second_gain,
-                second_shift,
-                inner_bias,
-            ],
-            axis=1,
-        )
-    )
-    wide_piece = 2 * piece + LANES
     joint_width = 3 * LANES
-    small_rows = small_own.size // joint_width
-    first_joint = jnp.concatenate([joint_own[0], small_own.reshape(small_rows, joint_width)], axis=0)
-    joint_turned = jnp.stack([first_joint] + [turn(first_joint, r) for r in range(1, planes)])
-    joint_plain = jnp.stack([lax.dynamic_index_in_dim(joint_turned, i, 0, keepdims=False) for i in unturned])
-    small_all = joint_plain[:, shard:].reshape(planes, LAYERS, -1)
-
-    def small(layer, index):
-        return small_all[:, layer, index * shard : (index + 1) * shard].reshape(width)
-
-    inner_bias_all = small_all[:, :, 8 * shard :].swapaxes(0, 1).reshape(LAYERS, hidden)
 
     def ordered(stack, order):
         return jnp.concatenate([lax.dynamic_index_in_dim(stack, i, 0, keepdims=False) for i in order], axis=0)
 
-    joint_first = joint_plain[:, :shard].reshape(width, joint_width)
-    wide_first, _ = lax.optimization_barrier((wide_own[0], joint_first))
-    others_first = jnp.concatenate([turn(wide_first, r) for r in range(1, planes)], axis=0)
-    second_own, _ = lax.optimization_barrier(
-        (jnp.concatenate([wide_own[1], joint_own[1]], axis=1), others_first)
-    )
-    second_stack = lax.all_gather(second_own, "wsh", axis=0)
-    joint_second = second_stack[:, :, wide_piece:].reshape(width, joint_width)
-    others_second = ordered(second_stack[:, :, :wide_piece], turned[1:])
-    second_parts = lax.all_gather(others_second, "ctx", axis=0, axis_index_groups=plane_groups())
+    first_joint = joint_own[0]
+    joint_turned = jnp.stack([first_joint] + [turn(first_joint, r) for r in range(1, planes)])
+    joint_first = ordered(joint_turned[:, :shard], unturned)
+    small_all = ordered(joint_turned[:, None, shard:, :shard], unturned)
+
+    def small(layer, index):
+        return small_all[:, 2 * index + layer].reshape(width)
+
+    inner_bias_all = small_all[:, 16:24].reshape(planes, 4, LAYERS, shard).transpose(2, 0, 1, 3).reshape(LAYERS, hidden)
+
+    inner_near = ordered(lax.all_gather(first_own[0], "wsh", axis=0), turned[1:])
+    first_tokens = spread_tokens(tokens[0])
+    (outer_sent,) = gate([second_own[0]], first_tokens[0])
+    outer_stack = lax.all_gather(outer_sent, "wsh", axis=0)
+    middle = 3 * shard // 2
+
+    def spread_first(near):
+        left, right = near[:middle], near[middle:]
+        return (left, right, swap(left, ALONG_X), swap(right, ALONG_Y))
+
+    def spread_second(left, right, left_x, right_y):
+        lefts = (left, left_x, swap(left, ALONG_Y), swap(left_x, ALONG_Y))
+        rights = (right, swap(right, ALONG_X), right_y, swap(right_y, ALONG_X))
+        return [part for pair in zip(lefts, rights) for part in pair]
+
+    inner_half = spread_first(inner_near)
+    layer_own = jnp.concatenate([first_own[1], second_own[1], joint_own[1, :shard]], axis=1)
+    wide_piece = 2 * piece + LANES
 
     def layer_weights(layer):
         if layer == 0:
-            first = jnp.concatenate([others_first[:, :piece], others_first[:, 2 * piece :]], axis=1)
-            second = others_first[:, piece : 2 * piece]
-            first_x = swap(first, ALONG_X)
-            second_y = swap(second, ALONG_Y)
-            firsts = (first, first_x, swap(first, ALONG_Y), swap(first_x, ALONG_Y))
-            seconds = (second, swap(second, ALONG_X), second_y, swap(second_y, ALONG_X))
-            near = jnp.concatenate([part[:, piece:] for part in firsts], axis=1)
-            weights = (inner_own, outer_own, firsts, seconds)
+            near = jnp.concatenate(
+                [
+                    jnp.concatenate([inner_first[2 * j][:, piece:], inner_first[2 * j + 1][:, piece:]], axis=0)
+                    for j in range(4)
+                ],
+                axis=1,
+            )
+            weights = (inner_own, outer_own, inner_first, outer_first)
         else:
-            near = jnp.concatenate([second_parts[j, :, 2 * piece :] for j in range(4)], axis=1)
-            weights = (inner_own, outer_own, second_parts, second_parts)
-        out_full = jnp.concatenate(
-            [out_own[layer], jnp.concatenate([near, swap(near, CORE)], axis=1)], axis=0
-        )
-        return (joint_first if layer == 0 else joint_second, weights, out_full)
+            near = jnp.concatenate([inner_second[j, :, piece:] for j in range(4)], axis=1)
+            weights = (inner_own, outer_own, [inner_second])
+        return (weights, (out_own[layer], near, swap(near, CORE)))
 
     def out_place(layer, block):
         at = (block // 2) ^ chip if layer == 0 else block // 2
@@ -1312,30 +1527,56 @@
     stashed = []
     outputs = []
     for layer in range(LAYERS):
-        joint, weights, out_full = layer_weights(layer)
+        joint = joint_first if layer == 0 else joint_second
         first_gain_row, first_shift_row = wide(small(layer, 4)), wide(small(layer, 5))
         second_gain_row, second_shift_row = wide(small(layer, 6)), wide(small(layer, 7))
 
-        everyone = spread_tokens(activation)
+        near_tokens, far_tokens = first_tokens if layer == 0 else spread_tokens(activation)
+        everyone = jnp.concatenate([near_tokens, far_tokens], axis=0)
         query_bias_own = lax.dynamic_slice_in_dim(small(layer, 0), here * LANES, LANES, 0)
         value_bias_own = lax.dynamic_slice_in_dim(small(layer, 1), here * LANES, LANES, 0)
-        joint_bias = jnp.concatenate([query_bias_own, jnp.zeros_like(query_bias_own), value_bias_own])
-        packed = low(mm(everyone, joint) + wide(joint_bias))
+        joint_bias = wide(jnp.concatenate([query_bias_own, jnp.zeros_like(query_bias_own), value_bias_own]))
+        packed = low(mm(everyone, joint) + joint_bias)
+        if layer == 0:
+            (packed,) = gate([packed], inner_near)
+            (layer_own,) = gate([layer_own], packed)
+            second_stack = lax.all_gather(layer_own, "wsh", axis=0)
         mixed, log_all = attention_forward(packed, labels, block_order)
+        if layer == 0:
+            inner_own, outer_own, out_own = own_blocks(
+                inner_weight,
+                outer_weight,
+                out_weight,
+                jnp.concatenate(inner_order),
+                jnp.concatenate(out_order),
+                mixed,
+            )
+            left_x, right_y, outer_stack = gate([*inner_half[2:], outer_stack], mixed)
+            inner_first = spread_second(*inner_half[:2], left_x, right_y)
+            outer_first = spread_second(*spread_first(ordered(outer_stack, turned[1:])))
+        else:
+            (inner_second,) = gate([inner_second], mixed)
+        weights, out_weights = layer_weights(layer)
         mixed_heads = exchange(mixed.reshape(8, rows, LANES))
-        mixed_turned = jnp.concatenate(
-            [
-                lax.dynamic_index_in_dim(mixed_heads, 2 * turned[r] + i, 0, keepdims=False)
-                for r in range(planes)
-                for i in range(2)
-            ],
-            axis=1,
-        )
+        places = jnp.stack(
+            [2 * turned[p // 2] + p % 2 for p in range(8)]
+            + [out_place(layer, b) for b in range(8)]
+            + turned
+            + [jnp.int32(0)] * 4
+            + [out_order[layer][p] for p in range(8)]
+        ).astype(jnp.int32)
+        mixed_turned, first_unit, first_inverse, hidden_rows, hidden_turned = attention_output(
+            mixed_heads,
+            out_weights,
+            activation,
+            wide(small(layer, 2))[None],
+            first_gain_row[None],
+            first_shift_row[None],
+            places,
+        )
+        if layer == 1:
+            weights = (*weights, gate([outer_second], hidden_turned))
         mixed_pair = jnp.concatenate([mixed_turned, swap(mixed_turned, CORE)], axis=0)
-        attended = block_columns(mm(mixed_turned, out_full), [out_place(layer, b) for b in range(8)], LANES)
-        first_pre = wide(activation) + (attended + wide(small(layer, 2)))
-        hidden_rows, first_unit, first_inverse = norm_forward(first_pre, first_gain_row, first_shift_row)
-        hidden_turned = block_columns(low(hidden_rows), turned, shard)
         hidden_pair = jnp.concatenate([hidden_turned, swap(hidden_turned, CORE)], axis=0)
         inner_bias_own = jnp.concatenate(
             [lax.dynamic_slice_in_dim(inner_bias_all[layer], inner_order[layer][j] * piece, piece, 0) for j in range(4)]
@@ -1344,6 +1585,14 @@
             hidden_pair, wide(inner_bias_own)[None], weights, layer
         )
         outer_turned = outer_near + wide(swap(outer_far, CORE))
+        if layer == 0:
+            (second_stack,) = gate([second_stack], active)
+            joint_second = second_stack[:, :, wide_piece:].reshape(width, joint_width)
+            others_second = ordered(second_stack[:, :, :wide_piece], turned[1:])
+            inner_second, outer_second = [
+                lax.all_gather(part, "ctx", axis=0, axis_index_groups=plane_groups())
+                for part in (others_second[:, : piece + LANES], others_second[:, piece + LANES :])
+            ]
         outer_out = block_columns(outer_turned, unturned, shard)
         second_pre = hidden_rows + (outer_out + wide(small(layer, 3)))
         result, second_unit, second_inverse = norm_forward(second_pre, second_gain_row, second_shift_row)
@@ -1361,7 +1610,8 @@
                 second_unit,
                 second_inverse,
                 joint,
-                out_full,
+                out_weights,
+                places,
                 weights,
                 first_gain_row,
                 second_gain_row,
@@ -1372,7 +1622,6 @@
 
     gradient = wide(cotangent[0])
     small_grads = [None] * LAYERS
-    placed = None
     for layer in reversed(range(LAYERS)):
         (
             everyone,
@@ -1387,7 +1636,8 @@
             second_unit,
             second_inverse,
             joint,
-            out_full,
+            out_weights,
+            places,
             weights,
             first_gain_row,
             second_gain_row,
@@ -1400,72 +1650,57 @@
         grad_turned = block_columns(grad_outer, turned, shard)
         grad_pair = jnp.concatenate([grad_turned, swap(grad_turned, CORE)], axis=0)
         hidden_near, hidden_far, grad_inner, grad_inner_bias = feed_backward(grad_pair, slope, weights, layer)
-        hidden_back = hidden_near + wide(swap(hidden_far, CORE))
-        grad_hidden = grad_second + block_columns(hidden_back, unturned, shard)
-        grad_first, grad_first_gain, grad_first_shift = norm_backward(
-            grad_hidden, first_unit, first_inverse, first_gain_row
-        )
-        grad_branch = low(grad_first)
-        grad_out_bias = jnp.sum(wide(grad_branch), axis=0)
-        branch_spread = block_columns(grad_branch, [out_order[layer][p] for p in range(8)], LANES)
-        grad_mixed_turned = low(mm(branch_spread, out_full, NT))
-        grad_mixed = exchange(
-            jnp.stack(
-                [
-                    lax.dynamic_slice_in_dim(grad_mixed_turned, unturned[i // 2] * shard + (i % 2) * LANES, LANES, 1)
-                    for i in range(8)
-                ]
-            )
-        ).reshape(8 * rows, LANES)
+        grad_first, first_rows, branch_spread, grad_sent = attention_output_back(
+            hidden_near,
+            swap(hidden_far, CORE),
+            grad_second,
+            first_unit,
+            first_inverse,
+            first_gain_row[None],
+            out_weights,
+            places,
+        )
+        grad_first_gain, grad_first_shift, grad_out_bias = first_rows[0], first_rows[1], first_rows[2]
+        grad_mixed = exchange(grad_sent).reshape(8 * rows, LANES)
         branch_half = 4 * LANES
         branch_pair = jnp.concatenate(
             [branch_spread[:, :branch_half], swap(branch_spread[:, branch_half:], CORE)], axis=0
         )
         summed = weight_gradients(
-            hidden_pair, grad_pair, mixed_pair, grad_inner, active, branch_pair, plane_rows, layer == 0
-        )
+            hidden_pair, grad_pair, mixed_pair, grad_inner, active, branch_pair, plane_rows, layer == 0, grad_sent
+        )
+        (grad_mixed,) = gate([grad_mixed], summed[0])
         grad_query, grad_key, grad_value = attention_backward(packed, labels, grad_mixed, log_all, block_order)
-        grad_packed = jnp.concatenate([grad_query, grad_key, grad_value], axis=1)
-        gradient = grad_first + collect_tokens(mm(grad_packed, joint, NT), chip)
-        grad_joint = low(mm(everyone, grad_packed, TN))
-        joint_bias_grad = jnp.sum(wide(grad_packed), axis=0)
-
+        first_points = ()
         if layer == 0:
             first_keep, first_send, second_keep, second_send = summed
-            came = swap(first_send, ALONG_X)
-            first_sum = (
-                wide(first_keep[0])
-                + wide(came[0])
-                + wide(swap(low(wide(first_keep[1]) + wide(came[1])), ALONG_Y))
+            first_came = swap(first_send, ALONG_X)
+            second_came = swap(second_send, ALONG_Y)
+            first_came, second_came = gate([first_came, second_came], grad_query)
+            first_next = low(wide(first_keep[1]) + wide(first_came[1]))
+            second_next = low(wide(second_keep[1]) + wide(second_came[1]))
+            first_points = (first_next, second_next)
+        near_part, far_part, grad_packed, joint_bias_grad = token_gradients(
+            (grad_query, grad_key, grad_value), joint, chip_order[0], first_points
+        )
+        joint_bias_grad = joint_bias_grad[0]
+        if layer == 0:
+            first_last = swap(first_next, ALONG_Y)
+            second_last = swap(second_next, ALONG_X)
+            first_sum = wide(first_keep[0]) + wide(first_came[0]) + wide(first_last)
+            second_sum = wide(second_keep[0]) + wide(second_came[0]) + wide(second_last)
+            first_points = (first_last, second_last)
+            (plane_second,) = gate([plane_second], grad_mixed)
+            sum_second = lax.psum_scatter(plane_second, "wsh", scatter_dimension=0, tiled=True)
+            sum_first, sum_second, sum_joint = gate([sum_first, sum_second, sum_joint], near_part, first_last, second_last)
+            everything = lax.all_gather(
+                jnp.concatenate([sum_first[:, :piece], sum_second, sum_first[:, piece:], sum_joint], axis=1),
+                "ctx",
+                axis=0,
             )
-            came = swap(second_send, ALONG_Y)
-            second_sum = (
-                wide(second_keep[0])
-                + wide(came[0])
-                + wide(swap(low(wide(second_keep[1]) + wide(came[1])), ALONG_X))
-            )
-            total = first_sum[:shard]
-            for r, rows_sent in enumerate((first_sum[shard:], second_sum[:shard], second_sum[shard:]), 1):
-                total = total + wide(turn(low(rows_sent), planes - r))
-            joint_total = wide(lax.dynamic_slice_in_dim(grad_joint, plane * shard, shard, 0))
-            for r in range(1, planes):
-                part = lax.dynamic_slice_in_dim(grad_joint, turned[r] * shard, shard, 0)
-                joint_total = joint_total + wide(turn(part, planes - r))
-            near, far = plane_pieces(low(jnp.concatenate([total, joint_total], axis=1)))
-            near_first = here ^ (2 * four)
-            placed = place_pieces(near, far, jnp.concatenate([near_first, near_first ^ 1]), layer, placed)
-        else:
-            plane_sum = lax.psum_scatter(
-                summed[0].reshape(4 * width, wide_piece),
-                "ctx",
-                scatter_dimension=0,
-                axis_index_groups=plane_groups(),
-                tiled=True,
-            )
-            total = lax.psum_scatter(plane_sum, "wsh", scatter_dimension=0, tiled=True)
-            joint_total = lax.psum_scatter(grad_joint, "wsh", scatter_dimension=0, tiled=True)
-            everything = lax.all_gather(jnp.concatenate([total, joint_total], axis=1), "ctx", axis=0)
-            placed = place_pieces(everything, everything, relative, layer, placed)
+        far_came = swap(far_part, CORE)
+        gradient = grad_first + collect_tokens(near_part, far_came, *first_points)
+        grad_joint = low(mm(everyone, grad_packed, TN))
 
         placed_query, placed_value = [
             lax.dynamic_update_slice(jnp.zeros((width,), jnp.float32), part, (here * LANES,))
@@ -1493,9 +1728,47 @@
             ],
             axis=1,
         )
-    small_sent = jnp.concatenate(small_grads, axis=1)
-    small_plane = jnp.sum(lax.all_to_all(small_sent, "wsh", 0, 0, tiled=True), axis=0)
-    small_mine = jnp.sum(lax.all_gather(small_plane, "ctx", axis=0), axis=0).reshape(LAYERS, -1)
+        if layer == 0:
+            small_sent = jnp.concatenate(small_grads, axis=1)
+            small_plane = jnp.sum(lax.all_to_all(small_sent, "wsh", 0, 0, tiled=True), axis=0)
+            small_spread = jnp.broadcast_to(small_plane, (8, small_plane.shape[0]))
+            small_mine = jnp.sum(exchange(small_spread), axis=0).reshape(LAYERS, -1)
+
+        if layer == 0:
+            joint_rows = [
+                lax.dynamic_slice_in_dim(grad_joint, turned[r] * shard, shard, 0) for r in range(planes)
+            ]
+            sent = (first_sum[shard:], second_sum[:shard], second_sum[shard:])
+            came = [
+                turn(jnp.concatenate([low(sent[r - 1]), joint_rows[r]], axis=1), planes - r)
+                for r in range(1, planes)
+            ]
+            came = gate(came, gradient, small_mine)
+            last_total = jnp.concatenate([first_sum[:shard], wide(joint_rows[0])], axis=1)
+            for part in came:
+                last_total = last_total + wide(part)
+            last_total = low(last_total)
+            (everything,) = gate([everything], last_total)
+            *placed, placed_token = place_pieces(everything, everything, relative, 1, None)
+        else:
+            plane_first, plane_second = [
+                lax.psum_scatter(
+                    part.reshape(4 * width, -1),
+                    "ctx",
+                    scatter_dimension=0,
+                    axis_index_groups=plane_groups(),
+                    tiled=True,
+                )
+                for part in (summed[0], *gate([summed[1]], gradient))
+            ]
+            (plane_first,) = gate([plane_first], far_came)
+            sum_first = lax.psum_scatter(plane_first, "wsh", scatter_dimension=0, tiled=True)
+            sum_joint = lax.psum_scatter(grad_joint, "wsh", scatter_dimension=0, tiled=True)
+
+
+    near, far = plane_pieces(last_total, placed_token)
+    near_first = here ^ (2 * four)
+    *placed, _ = place_pieces(near, far, jnp.concatenate([near_first, near_first ^ 1]), 0, placed)
     small_outs = [small_mine[:, i * shard : (i + 1) * shard] for i in range(8)]
     return (
         outputs[0][None],

time: 836 us -> 778 us (0.931)
  Pallas kernels: 229 us -> 271 us
  local copies, waits for them, and re-layouts: 92.2 us -> 60.5 us
  waiting for transfers between devices: 218 us -> 192 us
  other arithmetic: 88.9 us -> 69.6 us
  between operations: 33.3 us -> 20.9 us
  matrix products: 31.7 us -> 21.5 us
    ppermute x12 -> x6, waiting for transfers between devices: 77.4 us -> 33.6 us  [turn(): lax.ppermute(block, 'wsh', [(i, (i + distance) % count) for i in range(co...]
    pallas_call x0 -> x24, Pallas kernels: none -> 42 us  [the longest x2 19.6 us: token_gradients(): pl.pallas_call(token_gradient_kernel, grid_spec=pltpu.PrefetchScalarGridS...]
    all_to_all x0 -> x1, blocking collectives: none -> 27.2 us  [collect_tokens(): lax.all_to_all(sent, 'ctx', 0, 0, axis_index_groups=plane_groups(), tiled...]
    all_gather x1 -> x0, blocking collectives: 22.3 us -> none  [head_split_body(): lax.all_gather(small_plane, 'ctx', axis=0)]
    unnamed x390 -> x249, local copies, waits for them, and re-layouts: 44.9 us -> 22.7 us
    all_gather x3 -> x6, waiting for transfers between devices: 0.04 us -> 15.9 us  [the longest x2 13.3 us: head_split_body(): lax.all_gather(part, 'ctx', axis=0, axis_index_groups=plane_groups())]
    ppermute x41 -> x47, starting transfers between devices: 39.8 us -> 51.5 us  [swap(): return lax.ppermute(block, 'ctx', [(i, i ^ mask) for i in devices])]
    dot_general x10 -> x4, matrix products: 31.7 us -> 21.5 us  [mm(): lax.dot_general(left, right, dims, preferred_element_type=jnp.float32)]
  transfers between devices with their start and end apart: 65 -> 70, of which waited for: 22 -> 30; matrix products, arithmetic and copies ran while one was open for 21% -> 15% of each run, Pallas kernels for 22% -> 29%
where the time goes in v3:
time: 778 us; the launch traced here: 766 us
  Pallas kernels  271 us (35%)
  waiting for transfers between devices  192 us (25%)
  starting transfers between devices  88.9 us (11%)
  other arithmetic  69.6 us (9%)
  local copies, waits for them, and re-layouts  60.5 us (8%)
  blocking collectives  42.4 us (5%)
  matrix products  21.5 us (3%)
  between operations  20.9 us (3%)
    ppermute x47, waiting for transfers between devices, swap(): return lax.ppermute(block, 'ctx', [(i, i ^ mask) for i in devices])  113 us
    pallas_call x2, Pallas kernels, attention_backward(): pl.pallas_call(attention_backward_kernel, grid_spec=pltpu.PrefetchScalarG...  67 us
    ppermute x47, starting transfers between devices, swap(): return lax.ppermute(block, 'ctx', [(i, i ^ mask) for i in devices])  51.5 us
    pallas_call x2, Pallas kernels, attention_forward(): pl.pallas_call(attention_forward_kernel, grid_spec=pltpu.PrefetchScalarGr...  50.6 us
    ppermute x6, waiting for transfers between devices, turn(): lax.ppermute(block, 'wsh', [(i, (i + distance) % count) for i in range(co...  33.6 us
    pallas_call x2, Pallas kernels, feed_forward(): pl.pallas_call(functools.partial(feed_forward_kernel, count), grid=(4,),...  31.2 us
    all_to_all x1, blocking collectives, collect_tokens(): lax.all_to_all(sent, 'ctx', 0, 0, axis_index_groups=plane_groups(), tiled...  27.2 us
    pallas_call x2, Pallas kernels, weight_gradients(): pl.pallas_call(functools.partial(weight_gradient_kernel, split), grid_spe...  25.5 us
  transfers between devices with their start and end apart: 70, of which 30 were waited for; matrix products, arithmetic and copies ran while one was open for 15% of the time, Pallas kernels for 29%

profile of v3, /device:TPU:9, one launch (start us, length us, event | category | flops | bytes accessed | tf_op | source)
XLA Modules:
  0.0 766.1 jit_solution(7688859864066837664)
XLA Ops:
  28.0 8.6 %collective-permute-done.3 = bf16[2,256,512]{2,1,0:T(8,128)(2,1)S(1)} collective-permute-done((bf16[2,256,512]{2,1,0:T(8,128)(2,1)S(1)}, bf16[2,256,512]{2,1,0:T(8,128)(2,1)S(1)}, u32[]{:S(2)}, u32[]{:S(2)}) %collective-permute-start.3) | collective-permute-done | bytes 524320 | tf_op jit(solution)/shard_map/ppermute | solution.py:543
  68.2 25.4 %attention_forward.2 = (bf16[2048,128]{1,0:T(8,128)(2,1)}, f32[2,2048]{1,0:T(2,128)}) custom-call(s32[8]{0:T(128)} %get-tuple-element.359.order_ref, bf16[2048,384]{1,0:T(8,128)(2,1)} %gate.18.query_ref.key_ref.value_ref.refs_1_, bf16[2048,384]{1,0:T(8,128)(2,1)} %gate.18.query_ref.key_ref.value_ref.refs_1_, ...), custom_call_target="tpu_custom_call" | custom-call | flops 28750000128 | bytes 90000000 | tf_op jit(solution)/shard_map/attention_forward/pallas_call | solution.py:603
  151.8 16.5 %feed_forward.2 = (f32[256,1024]{1,0:T(8,128)}, bf16[256,1024]{1,0:T(8,128)(2,1)}, bf16[512,2048]{1,0:T(8,128)(2,1)}, bf16[512,2048]{1,0:T(8,128)(2,1)}) custom-call(bf16[512,1024]{1,0:T(8,128)(2,1)} %copy-done.59, f32[1,2048]{1,0:T(1,128)} %maximum_convert_fusion.bias_ref, bf16[2,4,256,512]{3,2,1,0:T(8,128)(2,1)} %get-tuple-element.117.own_inner, ...), custom_call_target="tpu_custom_call" | custom-call | flops 18400000000 | bytes 57600000 | tf_op jit(solution)/shard_map/feed_forward/pallas_call | solution.py:980
  185.6 20.4 %collective-permute-done.26 = bf16[2,256,512]{2,1,0:T(8,128)(2,1)S(1)} collective-permute-done((bf16[2,256,512]{2,1,0:T(8,128)(2,1)S(1)}, bf16[2,256,512]{2,1,0:T(8,128)(2,1)S(1)}, u32[]{:S(2)}, u32[]{:S(2)}) %collective-permute-start.26) | collective-permute-done | bytes 524320 | tf_op jit(solution)/shard_map/ppermute | solution.py:543
  218.7 25.3 %attention_forward.3 = (bf16[2048,128]{1,0:T(8,128)(2,1)}, f32[2,2048]{1,0:T(2,128)}) custom-call(s32[8]{0:T(128)} %get-tuple-element.359.order_ref, bf16[2048,384]{1,0:T(8,128)(2,1)} %add_convert_fusion.2.query_ref.key_ref.value_ref, bf16[2048,384]{1,0:T(8,128)(2,1)} %add_convert_fusion.2.query_ref.key_ref.value_ref, ...), custom_call_target="tpu_custom_call" | custom-call | flops 28750000128 | bytes 90000000 | tf_op jit(solution)/shard_map/attention_forward/pallas_call | solution.py:603
  272.9 13.3 %all-gather.20.cloned.1.call-done = bf16[3072,512]{1,0:T(8,128)(2,1)} async-done(((bf16[768,512]{1,0:T(8,128)(2,1)}), bf16[3072,512]{1,0:T(8,128)(2,1)}) %all-gather.20.cloned.1.call-update) | async-done | bytes 3145744 | tf_op jit(solution)/shard_map/all_gather | solution.py:1593
  288.3 14.6 %feed_forward.3 = (f32[256,1024]{1,0:T(8,128)}, bf16[256,1024]{1,0:T(8,128)(2,1)}, bf16[512,2048]{1,0:T(8,128)(2,1)}, bf16[512,2048]{1,0:T(8,128)(2,1)}) custom-call(bf16[512,1024]{1,0:T(8,128)(2,1)} %copy-done.60, f32[1,2048]{1,0:T(1,128)} %maximum_convert_fusion.1.bias_ref, bf16[2,4,256,512]{3,2,1,0:T(8,128)(2,1)} %get-tuple-element.117.own_inner, ...), custom_call_target="tpu_custom_call" | custom-call | flops 18400000000 | bytes 57600000 | tf_op jit(solution)/shard_map/feed_forward/pallas_call | solution.py:980
  314.5 10.3 %feed_backward.2 = (f32[256,1024]{1,0:T(8,128)}, bf16[256,1024]{1,0:T(8,128)(2,1)}, bf16[512,2048]{1,0:T(8,128)(2,1)}, f32[1,2048]{1,0:T(1,128)}) custom-call(bf16[512,1024]{1,0:T(8,128)(2,1)} %pad_maximum_fusion.11.grad_ref, bf16[512,2048]{1,0:T(8,128)(2,1)} %get-tuple-element.128.slope_ref, bf16[2,4,256,512]{3,2,1,0:T(8,128)(2,1)} %get-tuple-element.117.own_inner, ...), custom_call_target="tpu_custom_call" | custom-call | flops 12650000384 | bytes 39600000 | tf_op jit(solution)/shard_map/feed_backward/pallas_call | solution.py:1024
  337.5 12.4 %weight_gradients.2 = (bf16[4,1024,640]{2,1,0:T(8,128)(2,1)}, bf16[4,1024,512]{2,1,0:T(8,128)(2,1)}) custom-call(s32[4]{0:T(128)} %pad_add_fusion.3.rows_ref, bf16[512,1024]{1,0:T(8,128)(2,1)} %copy-done.60, bf16[512,1024]{1,0:T(8,128)(2,1)} %pad_maximum_fusion.11.grad_ref, bf16[512,1024]{1,0:T(8,128)(2,1)} %pad_maximum_fusion.12.mixed_ref, ...), custom_call_target="tpu_custom_call" | custom-call | flops 14949999616 | bytes 46800000 | tf_op jit(solution)/shard_map/weight_gradients/pallas_call | solution.py:1117
  350.9 15.2 %all_to_all.45 = bf16[8,256,128]{2,1,0:T(8,128)(2,1)} all-to-all(bf16[8,256,128]{2,1,0:T(8,128)(2,1)S(1)} %copy-done.54), channel_id=1, replica_groups=mesh['ctx'=8,'wsh'=4] {'ctx'}, dimensions={0} | all-to-all | bytes 1048576 | tf_op jit(solution)/shard_map/all_to_all | solution.py:1407
  366.0 33.5 %attention_backward.2 = (bf16[2048,128]{1,0:T(8,128)(2,1)}, bf16[2048,128]{1,0:T(8,128)(2,1)}, bf16[2048,128]{1,0:T(8,128)(2,1)}) custom-call(s32[8]{0:T(128)} %get-tuple-element.359.order_ref, bf16[2048,384]{1,0:T(8,128)(2,1)} %add_convert_fusion.2.query_ref.key_ref.value_ref, bf16[2048,384]{1,0:T(8,128)(2,1)} %add_convert_fusion.2.query_ref.key_ref.value_ref, ...), custom_call_target="tpu_custom_call" | custom-call | flops 37950001152 | bytes 118800000 | tf_op jit(solution)/shard_map/attention_backward/pallas_call | solution.py:690
  399.6 9.8 %token_gradients.2 = (f32[4,256,1024]{2,1,0:T(8,128)}, bf16[4,256,1024]{2,1,0:T(8,128)(2,1)}, bf16[2048,384]{1,0:T(8,128)(2,1)}, f32[1,384]{1,0:T(1,128)}) custom-call(s32[4]{0:T(128)} %get-tuple-element.364.place_ref, bf16[2048,128]{1,0:T(8,128)(2,1)} %get-tuple-element.141.query_ref, bf16[2048,128]{1,0:T(8,128)(2,1)} %get-tuple-element.142.key_ref, ...), custom_call_target="tpu_custom_call" | custom-call | flops 11500000256 | bytes 36000000 | tf_op jit(solution)/shard_map/token_gradients/pallas_call | solution.py:1330
  419.9 27.2 %all_to_all.46 = bf16[4,256,1024]{2,1,0:T(8,128)(2,1)S(1)} all-to-all(bf16[4,256,1024]{2,1,0:T(8,128)(2,1)S(1)} %add_convert_fusion.1), channel_id=1, replica_groups={{0,8,16,24},{4,12,20,28},{1,9,17,25},{5,13,21,29},{2,10,18,26},{6,14,22..., dimensions={0} | all-to-all | bytes 4194304 | tf_op jit(solution)/shard_map/all_to_all | solution.py:1390
  458.4 11.8 %feed_backward.3 = (f32[256,1024]{1,0:T(8,128)}, bf16[256,1024]{1,0:T(8,128)(2,1)}, bf16[512,2048]{1,0:T(8,128)(2,1)}, f32[1,2048]{1,0:T(1,128)}) custom-call(bf16[512,1024]{1,0:T(8,128)(2,1)} %pad_maximum_fusion.13.grad_ref, bf16[512,2048]{1,0:T(8,128)(2,1)} %get-tuple-element.146.slope_ref, bf16[2,4,256,512]{3,2,1,0:T(8,128)(2,1)} %get-tuple-element.117.own_inner, ...), custom_call_target="tpu_custom_call" | custom-call | flops 12650000384 | bytes 39600000 | tf_op jit(solution)/shard_map/feed_backward/pallas_call | solution.py:1024
  491.7 13.1 %weight_gradients.3 = (bf16[2,512,1152]{2,1,0:T(8,128)(2,1)}, bf16[2,512,1152]{2,1,0:T(8,128)(2,1)}, bf16[2,512,1152]{2,1,0:T(8,128)(2,1)}, bf16[2,512,1152]{2,1,0:T(8,128)(2,1)}) custom-call(s32[4]{0:T(128)} %pad_add_fusion.3.rows_ref, bf16[512,1024]{1,0:T(8,128)(2,1)} %copy-done.59, bf16[512,1024]{1,0:T(8,128)(2,1)} %pad_maximum_fusion.13.grad_ref, ...), custom_call_target="tpu_custom_call" | custom-call | flops 14949999616 | bytes 46800000 | tf_op jit(solution)/shard_map/weight_gradients/pallas_call | solution.py:1117
  508.5 33.5 %attention_backward.3 = (bf16[2048,128]{1,0:T(8,128)(2,1)}, bf16[2048,128]{1,0:T(8,128)(2,1)}, bf16[2048,128]{1,0:T(8,128)(2,1)}) custom-call(s32[8]{0:T(128)} %get-tuple-element.359.order_ref, bf16[2048,384]{1,0:T(8,128)(2,1)} %gate.18.query_ref.key_ref.value_ref.refs_1_, bf16[2048,384]{1,0:T(8,128)(2,1)} %gate.18.query_ref.key_ref.value_ref.refs_1_, ...), custom_call_target="tpu_custom_call" | custom-call | flops 37950001152 | bytes 118800000 | tf_op jit(solution)/shard_map/attention_backward/pallas_call | solution.py:690
  542.0 16.7 %collective-permute-done.40.refs_0_ = bf16[2,512,1152]{2,1,0:T(8,128)(2,1)S(1)} collective-permute-done((bf16[2,512,1152]{2,1,0:T(8,128)(2,1)}, bf16[2,512,1152]{2,1,0:T(8,128)(2,1)S(1)}, u32[]{:S(2)}, u32[]{:S(2)}) %collective-permute-start.40) | collective-permute-done | bytes 2359328 | tf_op jit(solution)/shard_map/ppermute | solution.py:543
  567.7 9.8 %token_gradients.3 = (f32[4,256,1024]{2,1,0:T(8,128)}, bf16[4,256,1024]{2,1,0:T(8,128)(2,1)}, bf16[2048,384]{1,0:T(8,128)(2,1)}, f32[1,384]{1,0:T(1,128)}) custom-call(s32[4]{0:T(128)} %get-tuple-element.364.place_ref, bf16[2048,128]{1,0:T(8,128)(2,1)} %get-tuple-element.158.refs_2_.query_ref, bf16[2048,128]{1,0:T(8,128)(2,1)} %get-tuple-element.159.key_ref, ...), custom_call_target="tpu_custom_call" | custom-call | flops 69000003584 | bytes 216000000 | tf_op jit(solution)/shard_map/token_gradients/pallas_call | solution.py:1330
  577.4 13.1 %collective-permute-done.43.refs_1_.refs_4_ = bf16[512,1152]{1,0:T(8,128)(2,1)S(1)} collective-permute-done((bf16[512,1152]{1,0:T(8,128)(2,1)S(1)}, bf16[512,1152]{1,0:T(8,128)(2,1)S(1)}, u32[]{:S(2)}, u32[]{:S(2)}) %collective-permute-start.43) | collective-permute-done | bytes 1179680 | tf_op jit(solution)/shard_map/ppermute | solution.py:543
  646.4 21.1 %all-to-all-done.5 = bf16[4,256,1024]{2,1,0:T(8,128)(2,1)S(1)} async-done(((bf16[4,256,1024]{2,1,0:T(8,128)(2,1)}), bf16[4,256,1024]{2,1,0:T(8,128)(2,1)S(1)}, u32[]{:S(2)}, u32[]{:S(2)}) %all-to-all-start.5) | async-done | bytes 2097184 | tf_op jit(solution)/shard_map/all_to_all | solution.py:1390
  669.2 16.7 %collective-permute-done.46.refs_1_ = bf16[256,1536]{1,0:T(8,128)(2,1)} collective-permute-done((bf16[256,1536]{1,0:T(8,128)(2,1)}, bf16[256,1536]{1,0:T(8,128)(2,1)}, u32[]{:S(2)}, u32[]{:S(2)}) %collective-permute-start.46) | collective-permute-done | bytes 786464 | tf_op jit(solution)/shard_map/ppermute | solution.py:548
  685.9 16.9 %collective-permute-done.47.refs_2_ = bf16[256,1536]{1,0:T(8,128)(2,1)} collective-permute-done((bf16[256,1536]{1,0:T(8,128)(2,1)}, bf16[256,1536]{1,0:T(8,128)(2,1)}, u32[]{:S(2)}, u32[]{:S(2)}) %collective-permute-start.47) | collective-permute-done | bytes 786464 | tf_op jit(solution)/shard_map/ppermute | solution.py:548
  720.9 10.4 %place_pieces.2 = (f32[2,256,1024]{2,1,0:T(8,128)}, f32[2,256,1024]{2,1,0:T(8,128)}, f32[2,256,1024]{2,1,0:T(8,128)}, f32[2,256,1024]{2,1,0:T(8,128)}, f32[2,256...) custom-call(s32[8]{0:T(128)} %iota.27.order_ref, bf16[8,256,1536]{2,1,0:T(8,128)(2,1)} %gate.34.near_ref.far_ref, ...), custom_call_target="tpu_custom_call" | custom-call | flops 11500000256 | bytes 36000000 | tf_op jit(solution)/shard_map/place_pieces/pallas_call | solution.py:862
  749.0 10.4 %place_pieces.3 = (f32[2,256,1024]{2,1,0:T(8,128)}, f32[2,256,1024]{2,1,0:T(8,128)}, f32[2,256,1024]{2,1,0:T(8,128)}, f32[2,256,1024]{2,1,0:T(8,128)}, f32[2,256...) custom-call(s32[8]{0:T(128)} %pad_add_fusion.4.order_ref, ...), custom_call_target="tpu_custom_call", output_to_operand_aliasing={{0}: (3, {}), {1}: (4, {}), {2}: (5, {}), {3}: (6, {}), {4}... | custom-call | flops 11500000256 | bytes 36000000 | tf_op jit(solution)/shard_map/place_pieces/pallas_call | solution.py:862
  (625 shorter events, 339.3 us)
Async XLA Ops:
  7.2 49.5 %all-gather.12.cloned.1.call-start = ((), (), s32[]{:S(2)}) async-start(), calls=%async_computation.13 | async-start | bytes 1638400 | tf_op jit(solution)/shard_map/all_gather | solution.py:1488
  13.3 36.0 %collective-permute-start.7 = (bf16[288,384]{1,0:T(8,128)(2,1)}, bf16[288,384]{1,0:T(8,128)(2,1)}, u32[]{:S(2)}, u32[]{:S(2)}) collective-permute-start(bf16[288,384]{1,0:T(8,128)(2,1)} %get-tuple-element.297), channel_id=1, source_target_pairs={{0,3},{1,0},{2,1},{3,2},{4,7},{5,4},{6,5},{7,6},{8,11},{9,8},{10,9... | collective-permute-start | bytes 663560 | tf_op jit(solution)/shard_map/ppermute | solution.py:548
  13.3 36.0 %collective-permute-start.6 = (bf16[288,384]{1,0:T(8,128)(2,1)}, bf16[288,384]{1,0:T(8,128)(2,1)}, u32[]{:S(2)}, u32[]{:S(2)}) collective-permute-start(bf16[288,384]{1,0:T(8,128)(2,1)} %get-tuple-element.297), channel_id=1, source_target_pairs={{0,2},{1,3},{2,0},{3,1},{4,6},{5,7},{6,4},{7,5},{8,10},{9,11},{10,... | collective-permute-start | bytes 663560 | tf_op jit(solution)/shard_map/ppermute | solution.py:548
  15.8 33.5 %collective-permute-start.5 = (bf16[288,384]{1,0:T(8,128)(2,1)}, bf16[288,384]{1,0:T(8,128)(2,1)}, u32[]{:S(2)}, u32[]{:S(2)}) collective-permute-start(bf16[288,384]{1,0:T(8,128)(2,1)} %get-tuple-element.297), channel_id=1, source_target_pairs={{0,1},{1,2},{2,3},{3,0},{4,5},{5,6},{6,7},{7,4},{8,9},{9,10},{10,1... | collective-permute-start | bytes 663560 | tf_op jit(solution)/shard_map/ppermute | solution.py:548
  21.4 72.2 %all-gather.14.cloned.1.call-start = ((), (), s32[]{:S(2)}) async-start(), calls=%async_computation.19 | async-start | bytes 1310720 | tf_op jit(solution)/shard_map/all_gather | solution.py:1491
  54.0 115.8 %all-gather.16.cloned.1.call-start = ((), (), s32[]{:S(2)}) async-start(), calls=%async_computation.20 | async-start | bytes 3932160 | tf_op jit(solution)/shard_map/all_gather | solution.py:1543
  59.0 34.6 %collective-permute-start.8 = (bf16[384,640]{1,0:T(8,128)(2,1)}, bf16[384,640]{1,0:T(8,128)(2,1)}, u32[]{:S(2)}, u32[]{:S(2)}) collective-permute-start(bf16[384,640]{1,0:T(8,128)(2,1)} %get-tuple-element.299.refs_0_), channel_id=1, source_target_pairs={{0,8},{4,12},{8,0},{12,4},{16,24},{20,28},{24,16},{28,20},{1,9},{5... | collective-permute-start | bytes 1474568 | tf_op jit(solution)/shard_map/ppermute | solution.py:543
  60.2 39.7 %collective-permute-start.11 = (bf16[384,640]{1,0:T(8,128)(2,1)}, bf16[384,640]{1,0:T(8,128)(2,1)}, u32[]{:S(2)}, u32[]{:S(2)}) collective-permute-start(bf16[384,640]{1,0:T(8,128)(2,1)} %get-tuple-element.299.refs_0_), channel_id=1, source_target_pairs={{0,16},{4,20},{8,24},{12,28},{16,0},{20,4},{24,8},{28,12},{1,17},{... | collective-permute-start | bytes 1474568 | tf_op jit(solution)/shard_map/ppermute | solution.py:543
  61.5 32.1 %collective-permute-start.9 = (bf16[384,640]{1,0:T(8,128)(2,1)}, bf16[384,640]{1,0:T(8,128)(2,1)}, u32[]{:S(2)}, u32[]{:S(2)}) collective-permute-start(bf16[384,640]{1,0:T(8,128)(2,1)} %get-tuple-element.298.refs_1_), channel_id=1, source_target_pairs={{0,16},{4,20},{8,24},{12,28},{16,0},{20,4},{24,8},{28,12},{1,17},{... | collective-permute-start | bytes 1474568 | tf_op jit(solution)/shard_map/ppermute | solution.py:543
  67.9 33.0 %collective-permute-start.10 = (bf16[384,640]{1,0:T(8,128)(2,1)}, bf16[384,640]{1,0:T(8,128)(2,1)S(1)}, u32[]{:S(2)}, u32[]{:S(2)}) collective-permute-start(bf16[384,640]{1,0:T(8,128)(2,1)} %get-tuple-element.298.refs_1_), channel_id=1, source_target_pairs={{0,8},{4,12},{8,0},{12,4},{16,24},{20,28},{24,16},{28,20},{1,9},{5... | collective-permute-start | bytes 1474568 | tf_op jit(solution)/shard_map/ppermute | solution.py:543
  108.9 135.1 %all-gather.18.cloned.1.call-start = ((), (), s32[]{:S(2)}) async-start(), calls=%async_computation.21 | async-start | bytes 4915200 | tf_op jit(solution)/shard_map/all_gather | solution.py:1593
  173.1 113.1 %all-gather.20.cloned.1.call-start = ((), (), s32[]{:S(2)}) async-start(), calls=%async_computation.22 | async-start | bytes 3932160 | tf_op jit(solution)/shard_map/all_gather | solution.py:1593
  249.5 258.8 %reduce-scatter.6.cloned.1.call-start = ((), (), s32[]{:S(2)}) async-start(), calls=%async_computation.14 | async-start | bytes 6553600 | tf_op jit(solution)/shard_map/reduce_scatter | solution.py:1755
  349.8 217.7 %reduce-scatter.10.cloned.1.call-start = ((), (), s32[]{:S(2)}) async-start(), calls=%async_computation.16 | async-start | bytes 5242880 | tf_op jit(solution)/shard_map/reduce_scatter | solution.py:1755
  450.7 126.7 %reduce-scatter.14.cloned.1.call-start = ((), (), s32[]{:S(2)}) async-start(), calls=%async_computation.18 | async-start | bytes 983040 | tf_op jit(solution)/shard_map/reduce_scatter | solution.py:1766
  490.9 102.8 %reduce-scatter.8.cloned.1.call-start = ((), (), s32[]{:S(2)}) async-start(), calls=%async_computation.15 | async-start | bytes 1638400 | tf_op jit(solution)/shard_map/reduce_scatter | solution.py:1765
  504.8 53.9 %collective-permute-start.40 = (bf16[2,512,1152]{2,1,0:T(8,128)(2,1)}, bf16[2,512,1152]{2,1,0:T(8,128)(2,1)S(1)}, u32[]{:S(2)}, u32[]{:S(2)}) collective-permute-start(bf16[2,512,1152]{2,1,0:T(8,128)(2,1)} %get-tuple-element.161), channel_id=1, source_target_pairs={{0,8},{4,12},{8,0},{12,4},{16,24},{20,28},{24,16},{28,20},{1,9},{5... | collective-permute-start | bytes 7077896 | tf_op jit(solution)/shard_map/ppermute | solution.py:543
  506.2 52.5 %collective-permute-start.41 = (bf16[2,512,1152]{2,1,0:T(8,128)(2,1)}, bf16[2,512,1152]{2,1,0:T(8,128)(2,1)}, u32[]{:S(2)}, u32[]{:S(2)}) collective-permute-start(bf16[2,512,1152]{2,1,0:T(8,128)(2,1)} %get-tuple-element.162), channel_id=1, source_target_pairs={{0,16},{4,20},{8,24},{12,28},{16,0},{20,4},{24,8},{28,12},{1,17},{... | collective-permute-start | bytes 7077896 | tf_op jit(solution)/shard_map/ppermute | solution.py:543
  508.3 86.3 %reduce-scatter.12.cloned.1.call-start = ((), (), s32[]{:S(2)}) async-start(), calls=%async_computation.17 | async-start | bytes 1310720 | tf_op jit(solution)/shard_map/reduce_scatter | solution.py:1694
  567.6 152.8 %all-gather.22.cloned.1.call-start = ((), (), s32[]{:S(2)}) async-start(), calls=%async_computation.23 | async-start | bytes 7077888 | tf_op jit(solution)/shard_map/all_gather | solution.py:1696
  631.6 37.6 %collective-permute-start.45 = (bf16[256,1536]{1,0:T(8,128)(2,1)}, bf16[256,1536]{1,0:T(8,128)(2,1)}, u32[]{:S(2)}, u32[]{:S(2)}) collective-permute-start(bf16[256,1536]{1,0:T(8,128)(2,1)} %pad_maximum_fusion.21), channel_id=1, source_target_pairs={{0,3},{1,0},{2,1},{3,2},{4,7},{5,4},{6,5},{7,6},{8,11},{9,8},{10,9... | collective-permute-start | bytes 2359304 | tf_op jit(solution)/shard_map/ppermute | solution.py:548
  631.6 35.9 %all-to-all-start.5 = ((bf16[4,256,1024]{2,1,0:T(8,128)(2,1)}), bf16[4,256,1024]{2,1,0:T(8,128)(2,1)S(1)}, u32[]{:S(2)}, u32[]{:S(2)}) async-start(bf16[4,256,1024]{2,1,0:T(8,128)(2,1)} %gate.28), calls=%async_computation.5 | async-start | bytes 4194304 | tf_op jit(solution)/shard_map/all_to_all | solution.py:1390
  639.3 46.6 %collective-permute-start.46 = (bf16[256,1536]{1,0:T(8,128)(2,1)}, bf16[256,1536]{1,0:T(8,128)(2,1)}, u32[]{:S(2)}, u32[]{:S(2)}) collective-permute-start(bf16[256,1536]{1,0:T(8,128)(2,1)} %pad_maximum_fusion.22), channel_id=1, source_target_pairs={{0,2},{1,3},{2,0},{3,1},{4,6},{5,7},{6,4},{7,5},{8,10},{9,11},{10,... | collective-permute-start | bytes 2359304 | tf_op jit(solution)/shard_map/ppermute | solution.py:548
  642.6 60.2 %collective-permute-start.47 = (bf16[256,1536]{1,0:T(8,128)(2,1)}, bf16[256,1536]{1,0:T(8,128)(2,1)}, u32[]{:S(2)}, u32[]{:S(2)}) collective-permute-start(bf16[256,1536]{1,0:T(8,128)(2,1)} %pad_maximum_fusion.23), channel_id=1, source_target_pairs={{0,1},{1,2},{2,3},{3,0},{4,5},{5,6},{6,7},{7,4},{8,9},{9,10},{10,1... | collective-permute-start | bytes 2359304 | tf_op jit(solution)/shard_map/ppermute | solution.py:548
  (159 other events, 1532.7 us)
Sparse Core Ops, SparseCore 0:
  21.5 35.0 all-gather.11
  58.8 29.5 all-gather.13
  97.7 62.6 all-gather.15
  173.2 61.0 all-gather.17
  236.5 49.5 all-gather.19
  350.0 65.1 reduce-scatter.5
  450.9 58.6 reduce-scatter.9
  512.0 21.3 reduce-scatter.13
  535.8 30.5 reduce-scatter.7
  568.6 25.9 reduce-scatter.11
  598.8 66.2 all-gather.21

commit v4 on v3

--- a/solution.py
+++ b/solution.py
@@ -814,12 +814,10 @@
     )(inner_order, out_order, *[inner_weight] * 4, *[outer_weight] * 4, *[out_weight] * 8, after)
 
 
-def place_pieces(near, far, order, layer, previous):
-    count = 4
-    shard, columns = near.shape[1:]
+def place_pieces(pieces, order, layer, previous):
+    count, shard, columns = pieces.shape
     piece = (columns - 4 * LANES) // 2
     width = 8 * LANES
-    offset = far.shape[0] - count
 
     def column(index, order_ref):
         return (layer, 0, order_ref[index])
@@ -839,45 +837,30 @@
         pl.BlockSpec((8, LANES), lambda i, order_ref: (0, 0)),
     ]
 
-    def kernel(order_ref, near_ref, far_ref, *refs):
+    def kernel(order_ref, source, *refs):
         query_out, key_out, value_out, out_out, inner_out, outer_out, token_out = refs[-7:]
         token_out[...] = jnp.zeros_like(token_out)
-
-        def write(source):
-            inner_out[0] = wide(source[0, :, :piece])
-            outer_out[0] = wide(source[0, :, piece : 2 * piece].T)
-            for at, ref in enumerate((out_out, query_out, key_out, value_out)):
-                begin = 2 * piece + at * LANES
-                ref[0] = wide(source[0, :, begin : begin + LANES])
-
-        @pl.when(pl.program_id(0) < count)
-        def _():
-            write(near_ref)
-
-        @pl.when(pl.program_id(0) >= count)
-        def _():
-            write(far_ref)
+        inner_out[0] = wide(source[0, :, :piece])
+        outer_out[0] = wide(source[0, :, piece : 2 * piece].T)
+        for at, ref in enumerate((out_out, query_out, key_out, value_out)):
+            begin = 2 * piece + at * LANES
+            ref[0] = wide(source[0, :, begin : begin + LANES])
 
     held = [] if previous is None else list(previous)
     return pl.pallas_call(
         kernel,
         grid_spec=pltpu.PrefetchScalarGridSpec(
             num_scalar_prefetch=1,
-            grid=(2 * count,),
-            in_specs=[
-                pl.BlockSpec((1, shard, columns), lambda i, order_ref: (jnp.minimum(i, count - 1), 0, 0)),
-                pl.BlockSpec(
-                    (1, shard, columns), lambda i, order_ref: (jnp.maximum(i - count, 0) + offset, 0, 0)
-                ),
-            ]
+            grid=(count,),
+            in_specs=[pl.BlockSpec((1, shard, columns), lambda i, order_ref: (i, 0, 0))]
             + [pl.BlockSpec(memory_space=pl.ANY)] * len(held),
             out_specs=specs,
         ),
         out_shape=outs,
-        input_output_aliases={3 + i: i for i in range(len(held))},
-        cost_estimate=lasting(10),
+        input_output_aliases={2 + i: i for i in range(len(held))},
+        cost_estimate=lasting(count * 5 // 4),
         name="place_pieces",
-    )(order, near, far, *held)
+    )(order, pieces, *held)
 
 
 def half_erfc(values_in):
@@ -1322,7 +1305,7 @@
         far_ref[0] = low(part)
 
 
-def token_gradients(grads, joint, chips, after):
+def token_gradients(grads, joint, chips):
     tokens = grads[0].shape[0]
     rows = tokens // 8
     width, columns = joint.shape
@@ -1332,8 +1315,7 @@
         grid_spec=pltpu.PrefetchScalarGridSpec(
             num_scalar_prefetch=1,
             grid=(8,),
-            in_specs=[block, block, block, pl.BlockSpec((width, columns), lambda i, place_ref: (0, 0))]
-            + [pl.BlockSpec(memory_space=pl.ANY)] * len(after),
+            in_specs=[block, block, block, pl.BlockSpec((width, columns), lambda i, place_ref: (0, 0))],
             out_specs=[
                 pl.BlockSpec((1, rows, width), lambda i, place_ref: (place_ref[jnp.minimum(i, 3)], 0, 0)),
                 pl.BlockSpec((1, rows, width), lambda i, place_ref: (place_ref[jnp.maximum(i - 4, 0)], 0, 0)),
@@ -1347,9 +1329,103 @@
             jax.ShapeDtypeStruct((tokens, columns), jnp.bfloat16),
             jax.ShapeDtypeStruct((1, columns), jnp.float32),
         ],
-        cost_estimate=lasting(60 if after else 10),
+        cost_estimate=lasting(10),
         name="token_gradients",
-    )(chips, *grads, joint, *after)
+    )(chips, *grads, joint)
+
+
+def plane_sum_kernel(first_keep, first_came, first_last, second_keep, second_came, second_last, *outs):
+    shard = outs[0].shape[0]
+    first = wide(first_keep[0]) + wide(first_came[0]) + wide(first_last[...])
+    second = wide(second_keep[0]) + wide(second_came[0]) + wide(second_last[...])
+    outs[0][...] = first[:shard]
+    outs[1][...] = low(first[shard:])
+    outs[2][...] = low(second[:shard])
+    outs[3][...] = low(second[shard:])
+
+
+def plane_sum(first, second):
+    columns = first[0].shape[2]
+    shard = first[0].shape[1] // 2
+    block = pl.BlockSpec((1, 2 * shard, columns), lambda i: (0, 0, 0))
+    last = pl.BlockSpec((2 * shard, columns), lambda i: (0, 0))
+    return pl.pallas_call(
+        plane_sum_kernel,
+        grid=(1,),
+        in_specs=[block, block, last] * 2,
+        out_specs=[pl.BlockSpec((shard, columns), lambda i: (0, 0))] * 4,
+        out_shape=[jax.ShapeDtypeStruct((shard, columns), jnp.float32)]
+        + [jax.ShapeDtypeStruct((shard, columns), jnp.bfloat16)] * 3,
+        cost_estimate=lasting(3),
+        name="plane_sum",
+    )(*first, *second)
+
+
+def final_sum_kernel(*refs):
+    left_ref, right_ref = refs[-2:]
+    half = left_ref.shape[1]
+    whole = jnp.concatenate(
+        [
+            low(wide(refs[at][...]) + wide(refs[at + 1][...]) + wide(refs[at + 2][...]) + wide(refs[at + 3][...]))
+            for at in (0, 4)
+        ],
+        axis=1,
+    )
+    left_ref[...] = whole[:, :half]
+    right_ref[...] = whole[:, half:]
+
+
+def final_sum(plain, joint):
+    shard = plain[0].shape[0]
+    half = (plain[0].shape[1] + joint[0].shape[1]) // 2
+    operands = (*plain, *joint)
+    return pl.pallas_call(
+        final_sum_kernel,
+        grid=(1,),
+        in_specs=[pl.BlockSpec(array.shape, lambda i: (0, 0)) for array in operands],
+        out_specs=[pl.BlockSpec((shard, half), lambda i: (0, 0))] * 2,
+        out_shape=[jax.ShapeDtypeStruct((shard, half), jnp.bfloat16)] * 2,
+        cost_estimate=lasting(3),
+        name="final_sum",
+    )(*operands)
+
+
+def small_rows_kernel(place_ref, joint_ref, first_ref, outer_ref, gain_ref, shift_ref, inner_ref, out_ref):
+    shard = out_ref.shape[1] // 4
+    out_ref[...] = jnp.zeros_like(out_ref)
+    at = pl.ds(pl.multiple_of(place_ref[0] * LANES, LANES), LANES)
+    out_ref[0:1, at] = joint_ref[:, :LANES]
+    out_ref[1:2, at] = joint_ref[:, 2 * LANES :]
+    out_ref[2:3] = first_ref[2:3]
+    out_ref[3:4] = outer_ref[...]
+    out_ref[4:6] = first_ref[0:2]
+    out_ref[6:7] = gain_ref[...]
+    out_ref[7:8] = shift_ref[...]
+    count = inner_ref.shape[1] // shard // 4
+    for j in range(4):
+        block = place_ref[1 + j]
+        columns = pl.ds(pl.multiple_of((block // 2) * shard, shard), shard)
+        for part in range(count):
+            begin = (j * count + part) * shard
+            row = 8 + (block % 2) * count + part
+            out_ref[pl.ds(row, 1), columns] = inner_ref[:, begin : begin + shard]
+
+
+def small_rows(places, joint, first, outer, gain, shift, inner):
+    width = first.shape[1]
+    operands = (joint, first, outer[None], gain[None], shift[None], inner)
+    return pl.pallas_call(
+        small_rows_kernel,
+        grid_spec=pltpu.PrefetchScalarGridSpec(
+            num_scalar_prefetch=1,
+            grid=(1,),
+            in_specs=[pl.BlockSpec(array.shape, lambda i, place_ref: (0, 0)) for array in operands],
+            out_specs=pl.BlockSpec((16, width), lambda i, place_ref: (0, 0)),
+        ),
+        out_shape=jax.ShapeDtypeStruct((16, width), jnp.float32),
+        cost_estimate=lasting(2),
+        name="small_rows",
+    )(places, *operands)
 
 
 def gate(values_in, *points):
@@ -1383,17 +1459,16 @@
     return [list(range(0, count, 2)), list(range(1, count, 2))]
 
 
-def collect_tokens(near, far_came, *points):
-    sent = low(near + wide(far_came))
+def collect_tokens(sent, points, late_points):
     if points:
         (sent,) = gate([sent], *points)
     came = lax.all_to_all(sent, "ctx", 0, 0, axis_index_groups=plane_groups(), tiled=True)
+    if late_points:
+        (came,) = gate([came], *late_points)
     return jnp.sum(wide(came), axis=0)
 
 
-def plane_pieces(piece, *points):
-    half = piece.shape[1] // 2
-    left, right = piece[:, :half], piece[:, half:]
+def plane_pieces(left, right, *points):
     left_pair = jnp.stack([left, swap(left, ALONG_X)])
     right_pair = jnp.stack([right, swap(right, ALONG_Y)])
     left_far, right_far = gate([swap(left_pair, ALONG_Y), swap(right_pair, ALONG_X)], *points)
@@ -1538,8 +1613,7 @@
         joint_bias = wide(jnp.concatenate([query_bias_own, jnp.zeros_like(query_bias_own), value_bias_own]))
         packed = low(mm(everyone, joint) + joint_bias)
         if layer == 0:
-            (packed,) = gate([packed], inner_near)
-            (layer_own,) = gate([layer_own], packed)
+            packed, layer_own = gate([packed, layer_own], inner_near)
             second_stack = lax.all_gather(layer_own, "wsh", axis=0)
         mixed, log_all = attention_forward(packed, labels, block_order)
         if layer == 0:
@@ -1589,9 +1663,9 @@
             (second_stack,) = gate([second_stack], active)
             joint_second = second_stack[:, :, wide_piece:].reshape(width, joint_width)
             others_second = ordered(second_stack[:, :, :wide_piece], turned[1:])
+            sent_second = (others_second[:, : piece + LANES], others_second[:, piece + LANES :])
             inner_second, outer_second = [
-                lax.all_gather(part, "ctx", axis=0, axis_index_groups=plane_groups())
-                for part in (others_second[:, : piece + LANES], others_second[:, piece + LANES :])
+                lax.all_gather(part, "ctx", axis=0, axis_index_groups=plane_groups()) for part in sent_second
             ]
         outer_out = block_columns(outer_turned, unturned, shard)
         second_pre = hidden_rows + (outer_out + wide(small(layer, 3)))
@@ -1660,7 +1734,6 @@
             out_weights,
             places,
         )
-        grad_first_gain, grad_first_shift, grad_out_bias = first_rows[0], first_rows[1], first_rows[2]
         grad_mixed = exchange(grad_sent).reshape(8 * rows, LANES)
         branch_half = 4 * LANES
         branch_pair = jnp.concatenate(
@@ -1669,107 +1742,95 @@
         summed = weight_gradients(
             hidden_pair, grad_pair, mixed_pair, grad_inner, active, branch_pair, plane_rows, layer == 0, grad_sent
         )
-        (grad_mixed,) = gate([grad_mixed], summed[0])
+        if layer == 0:
+            (grad_mixed,) = gate([grad_mixed], summed[0], plane_first)
+        else:
+            grad_mixed, first_sum = gate([grad_mixed, summed[0]])
         grad_query, grad_key, grad_value = attention_backward(packed, labels, grad_mixed, log_all, block_order)
-        first_points = ()
         if layer == 0:
             first_keep, first_send, second_keep, second_send = summed
             first_came = swap(first_send, ALONG_X)
             second_came = swap(second_send, ALONG_Y)
-            first_came, second_came = gate([first_came, second_came], grad_query)
-            first_next = low(wide(first_keep[1]) + wide(first_came[1]))
-            second_next = low(wide(second_keep[1]) + wide(second_came[1]))
-            first_points = (first_next, second_next)
         near_part, far_part, grad_packed, joint_bias_grad = token_gradients(
-            (grad_query, grad_key, grad_value), joint, chip_order[0], first_points
-        )
-        joint_bias_grad = joint_bias_grad[0]
-        if layer == 0:
-            first_last = swap(first_next, ALONG_Y)
-            second_last = swap(second_next, ALONG_X)
-            first_sum = wide(first_keep[0]) + wide(first_came[0]) + wide(first_last)
-            second_sum = wide(second_keep[0]) + wide(second_came[0]) + wide(second_last)
-            first_points = (first_last, second_last)
-            (plane_second,) = gate([plane_second], grad_mixed)
-            sum_second = lax.psum_scatter(plane_second, "wsh", scatter_dimension=0, tiled=True)
-            sum_first, sum_second, sum_joint = gate([sum_first, sum_second, sum_joint], near_part, first_last, second_last)
-            everything = lax.all_gather(
-                jnp.concatenate([sum_first[:, :piece], sum_second, sum_first[:, piece:], sum_joint], axis=1),
-                "ctx",
-                axis=0,
-            )
+            (grad_query, grad_key, grad_value), joint, chip_order[0]
+        )
+        grad_joint = low(mm(everyone, grad_packed, TN))
         far_came = swap(far_part, CORE)
-        gradient = grad_first + collect_tokens(near_part, far_came, *first_points)
-        grad_joint = low(mm(everyone, grad_packed, TN))
-
-        placed_query, placed_value = [
-            lax.dynamic_update_slice(jnp.zeros((width,), jnp.float32), part, (here * LANES,))
-            for part in (joint_bias_grad[:LANES], joint_bias_grad[2 * LANES :])
-        ]
-        placed_inner = jnp.zeros((hidden,), jnp.float32)
-        for j in range(4):
-            placed_inner = lax.dynamic_update_slice(
-                placed_inner, grad_inner_bias[0, j * piece : (j + 1) * piece], (inner_order[layer][j] * piece,)
-            )
-        small_grads[layer] = jnp.concatenate(
-            [
-                row.reshape(planes, -1)
-                for row in (
-                    placed_query,
-                    placed_value,
-                    grad_out_bias,
-                    grad_outer_bias,
-                    grad_first_gain,
-                    grad_first_shift,
-                    grad_second_gain,
-                    grad_second_shift,
-                    placed_inner,
-                )
-            ],
-            axis=1,
-        )
-        if layer == 0:
-            small_sent = jnp.concatenate(small_grads, axis=1)
-            small_plane = jnp.sum(lax.all_to_all(small_sent, "wsh", 0, 0, tiled=True), axis=0)
-            small_spread = jnp.broadcast_to(small_plane, (8, small_plane.shape[0]))
-            small_mine = jnp.sum(exchange(small_spread), axis=0).reshape(LAYERS, -1)
-
-        if layer == 0:
-            joint_rows = [
-                lax.dynamic_slice_in_dim(grad_joint, turned[r] * shard, shard, 0) for r in range(planes)
-            ]
-            sent = (first_sum[shard:], second_sum[:shard], second_sum[shard:])
-            came = [
-                turn(jnp.concatenate([low(sent[r - 1]), joint_rows[r]], axis=1), planes - r)
-                for r in range(1, planes)
-            ]
-            came = gate(came, gradient, small_mine)
-            last_total = jnp.concatenate([first_sum[:shard], wide(joint_rows[0])], axis=1)
-            for part in came:
-                last_total = last_total + wide(part)
-            last_total = low(last_total)
-            (everything,) = gate([everything], last_total)
-            *placed, placed_token = place_pieces(everything, everything, relative, 1, None)
-        else:
-            plane_first, plane_second = [
+        tokens_sent = low(near_part + wide(far_came))
+        small_grads[layer] = small_rows(
+            jnp.concatenate([here[None], inner_order[layer]]).astype(jnp.int32),
+            joint_bias_grad,
+            first_rows,
+            grad_outer_bias,
+            grad_second_gain,
+            grad_second_shift,
+            grad_inner_bias,
+        )
+        if layer == 1:
+            (plane_first,) = [
                 lax.psum_scatter(
-                    part.reshape(4 * width, -1),
+                    first_sum.reshape(4 * width, -1),
                     "ctx",
                     scatter_dimension=0,
                     axis_index_groups=plane_groups(),
                     tiled=True,
                 )
-                for part in (summed[0], *gate([summed[1]], gradient))
             ]
             (plane_first,) = gate([plane_first], far_came)
             sum_first = lax.psum_scatter(plane_first, "wsh", scatter_dimension=0, tiled=True)
+            gradient = grad_first + collect_tokens(tokens_sent, (), (grad_joint,))
+            (second_sum,) = gate([summed[1]], gradient)
+            plane_second = lax.psum_scatter(
+                second_sum.reshape(4 * width, -1),
+                "ctx",
+                scatter_dimension=0,
+                axis_index_groups=plane_groups(),
+                tiled=True,
+            )
             sum_joint = lax.psum_scatter(grad_joint, "wsh", scatter_dimension=0, tiled=True)
-
-
-    near, far = plane_pieces(last_total, placed_token)
+            continue
+        small_sent = jnp.concatenate(small_grads, axis=0)
+        small_plane = jnp.sum(
+            lax.all_to_all(
+                jnp.stack([small_sent[:, p * shard : (p + 1) * shard] for p in range(planes)]), "wsh", 0, 0, tiled=True
+            ),
+            axis=0,
+        )
+        small_spread = jnp.broadcast_to(small_plane, (8, *small_plane.shape))
+        first_came, second_came = gate([first_came, second_came], near_part, grad_joint)
+        first_next = low(wide(first_keep[1]) + wide(first_came[1]))
+        second_next = low(wide(second_keep[1]) + wide(second_came[1]))
+        joint_rows = [lax.dynamic_slice_in_dim(grad_joint, turned[r] * shard, shard, 0) for r in range(planes)]
+        came_joint = [turn(joint_rows[r], planes - r) for r in range(1, planes)]
+        first_last, second_last = gate(
+            [swap(first_next, ALONG_Y), swap(second_next, ALONG_X)], small_plane, tokens_sent, *came_joint
+        )
+        own_total, *sent = plane_sum(
+            (first_keep, first_came, first_last), (second_keep, second_came, second_last)
+        )
+        came = [turn(sent[r - 1], planes - r) for r in range(1, planes)]
+        (plane_second,) = gate([plane_second], grad_mixed)
+        sum_second = lax.psum_scatter(plane_second, "wsh", scatter_dimension=0, tiled=True)
+        sum_first, sum_second, sum_joint = gate([sum_first, sum_second, sum_joint], own_total)
+        everything = lax.all_gather(
+            jnp.concatenate([sum_first[:, :piece], sum_second, sum_first[:, piece:], sum_joint], axis=1),
+            "ctx",
+            axis=0,
+        )
+        gradient = grad_first + collect_tokens(tokens_sent, (own_total,), ())
+        came = gate(came, gradient)
+        left_total, right_total = final_sum((own_total, *came), (joint_rows[0], *came_joint))
+        (everything,) = gate([everything], left_total)
+        *placed, placed_token = place_pieces(everything, relative, 1, None)
+        (small_spread,) = gate([small_spread], left_total)
+        small_mine = jnp.sum(exchange(small_spread), axis=0).reshape(LAYERS, 16, shard)
+
+    near, far = plane_pieces(left_total, right_total, placed_token, small_mine)
     near_first = here ^ (2 * four)
-    *placed, _ = place_pieces(near, far, jnp.concatenate([near_first, near_first ^ 1]), 0, placed)
-    small_outs = [small_mine[:, i * shard : (i + 1) * shard] for i in range(8)]
+    *placed, placed_token = place_pieces(near, near_first, 0, placed)
+    (far,) = gate([far], placed_token)
+    *placed, _ = place_pieces(far, near_first ^ 1, 0, placed)
+    small_outs = [small_mine[:, i] for i in range(8)]
     return (
         outputs[0][None],
         outputs[1][None],
@@ -1778,7 +1839,7 @@
         small_outs[0],
         small_outs[1],
         small_outs[2],
-        small_mine[:, 8 * shard :],
+        small_mine[:, 8:12].reshape(LAYERS, 4 * shard),
         small_outs[3],
         small_outs[4],
         small_outs[5],

time: 778 us -> 754 us (0.969)
  blocking collectives: 42.4 us -> 11.1 us
  Pallas kernels: 271 us -> 284 us
    ppermute x47, waiting for transfers between devices: 113 us -> 76.9 us  [swap(): return lax.ppermute(block, 'ctx', [(i, i ^ mask) for i in devices])]
    all_to_all x1 -> x0, blocking collectives: 27.2 us -> none  [collect_tokens(): lax.all_to_all(sent, 'ctx', 0, 0, axis_index_groups=plane_groups(), tiled...]
    all_to_all x1 -> x2, waiting for transfers between devices: 21.1 us -> 47.7 us  [collect_tokens(): lax.all_to_all(sent, 'ctx', 0, 0, axis_index_groups=plane_groups(), tiled...]
    pallas_call x0 -> x4, Pallas kernels: none -> 12.3 us  [the longest x1 4.85 us: plane_sum(): pl.pallas_call(plane_sum_kernel, grid=(1,), in_specs=[block, block, last]...]
    ppermute x47, starting transfers between devices: 51.5 us -> 42.2 us  [swap(): return lax.ppermute(block, 'ctx', [(i, i ^ mask) for i in devices])]
    ppermute x6 -> x9, waiting for transfers between devices: 33.6 us -> 41.5 us  [turn(): lax.ppermute(block, 'wsh', [(i, (i + distance) % count) for i in range(co...]
    unnamed x249 -> x206, local copies, waits for them, and re-layouts: 22.7 us -> 26.9 us
    pallas_call x2 -> x3, Pallas kernels: 20.8 us -> 21 us  [place_pieces(): pl.pallas_call(kernel, grid_spec=pltpu.PrefetchScalarGridSpec(num_scalar_...]
  transfers between devices with their start and end apart: 70 -> 74, of which waited for: 30 -> 30; matrix products, arithmetic and copies ran while one was open for 15% -> 15% of each run, Pallas kernels for 29% -> 34%
where the time goes in v4:
time: 754 us; the launch traced here: 742 us
  Pallas kernels  284 us (38%)
  waiting for transfers between devices  189 us (25%)
  starting transfers between devices  84.4 us (11%)
  other arithmetic  70.5 us (9%)
  local copies, waits for them, and re-layouts  59.5 us (8%)
  matrix products  22.1 us (3%)
  between operations  21 us (3%)
  blocking collectives  11.1 us (1%)
    ppermute x47, waiting for transfers between devices, swap(): return lax.ppermute(block, 'ctx', [(i, i ^ mask) for i in devices])  76.9 us
    pallas_call x2, Pallas kernels, attention_backward(): pl.pallas_call(attention_backward_kernel, grid_spec=pltpu.PrefetchScalarG...  66.9 us
    pallas_call x2, Pallas kernels, attention_forward(): pl.pallas_call(attention_forward_kernel, grid_spec=pltpu.PrefetchScalarGr...  50.6 us
    all_to_all x2, waiting for transfers between devices, collect_tokens(): lax.all_to_all(sent, 'ctx', 0, 0, axis_index_groups=plane_groups(), tiled...  47.7 us
    ppermute x47, starting transfers between devices, swap(): return lax.ppermute(block, 'ctx', [(i, i ^ mask) for i in devices])  42.2 us
    ppermute x9, waiting for transfers between devices, turn(): lax.ppermute(block, 'wsh', [(i, (i + distance) % count) for i in range(co...  41.5 us
    pallas_call x2, Pallas kernels, feed_forward(): pl.pallas_call(functools.partial(feed_forward_kernel, count), grid=(4,),...  31.1 us
    unnamed x206, local copies, waits for them, and re-layouts  26.9 us
  transfers between devices with their start and end apart: 74, of which 30 were waited for; matrix products, arithmetic and copies ran while one was open for 15% of the time, Pallas kernels for 34%

profile of v4, /device:TPU:9, one launch (start us, length us, event | category | flops | bytes accessed | tf_op | source)
XLA Modules:
  0.0 741.8 jit_solution(11953990169308227003)
XLA Ops:
  27.1 8.5 %collective-permute-done.3 = bf16[2,256,512]{2,1,0:T(8,128)(2,1)S(1)} collective-permute-done((bf16[2,256,512]{2,1,0:T(8,128)(2,1)S(1)}, bf16[2,256,512]{2,1,0:T(8,128)(2,1)S(1)}, u32[]{:S(2)}, u32[]{:S(2)}) %collective-permute-start.3) | collective-permute-done | bytes 524320 | tf_op jit(solution)/shard_map/ppermute | solution.py:543
  67.2 25.4 %attention_forward.2 = (bf16[2048,128]{1,0:T(8,128)(2,1)}, f32[2,2048]{1,0:T(2,128)}) custom-call(s32[8]{0:T(128)} %get-tuple-element.381.order_ref, bf16[2048,384]{1,0:T(8,128)(2,1)} %get-tuple-element.130.query_ref.key_ref.value_ref, bf16[2048,384]{1,0:T(8,128)(2,1)} %get-tuple-element.130.query_ref.key_ref.value_ref, ...), custom_call_target="tpu_custom_call" | custom-call | flops 28750000128 | bytes 90000000 | tf_op jit(solution)/shard_map/attention_forward/pallas_call | solution.py:603
  103.4 7.2 all-to-all-start
  112.9 7.5 %own_blocks.1 = (bf16[2,4,256,512]{3,2,1,0:T(8,128)(2,1)}, bf16[2,4,256,512]{3,2,1,0:T(8,128)(2,1)}, bf16[2,256,1024]{2,1,0:T(8,128)(2,1)}) custom-call(s32[8]{0:T(128)} %pad_add_fusion.1.inner_order_ref, s32[16]{0:T(128)} %pad_add_fusion.2.out_order_ref, f32[2,256,4096]{2,1,0:T(8,128)} %refs_3_.3, f32[2,256,4096]{2,1,0:T(8,128)} %refs_3_.3, ...), custom_call_target="tpu_custom_call" | custom-call | flops 8049999872 | bytes 25200000 | tf_op jit(solution)/shard_map/own_blocks/pallas_call | solution.py:796
  141.2 8.4 %collective-permute-done.20.refs_14_ = bf16[384,512]{1,0:T(8,128)(2,1)S(1)} collective-permute-done((bf16[384,512]{1,0:T(8,128)(2,1)}, bf16[384,512]{1,0:T(8,128)(2,1)S(1)}, u32[]{:S(2)}, u32[]{:S(2)}) %collective-permute-start.20) | collective-permute-done | bytes 393248 | tf_op jit(solution)/shard_map/ppermute | solution.py:543
  150.6 16.5 %feed_forward.2 = (f32[256,1024]{1,0:T(8,128)}, bf16[256,1024]{1,0:T(8,128)(2,1)}, bf16[512,2048]{1,0:T(8,128)(2,1)}, bf16[512,2048]{1,0:T(8,128)(2,1)}) custom-call(bf16[512,1024]{1,0:T(8,128)(2,1)} %copy-done.51, f32[1,2048]{1,0:T(1,128)} %maximum_convert_fusion.bias_ref, bf16[2,4,256,512]{3,2,1,0:T(8,128)(2,1)} %get-tuple-element.137.own_inner, ...), custom_call_target="tpu_custom_call" | custom-call | flops 18400000000 | bytes 57600000 | tf_op jit(solution)/shard_map/feed_forward/pallas_call | solution.py:963
  184.9 20.7 %collective-permute-done.26 = bf16[2,256,512]{2,1,0:T(8,128)(2,1)S(1)} collective-permute-done((bf16[2,256,512]{2,1,0:T(8,128)(2,1)S(1)}, bf16[2,256,512]{2,1,0:T(8,128)(2,1)S(1)}, u32[]{:S(2)}, u32[]{:S(2)}) %collective-permute-start.26) | collective-permute-done | bytes 524320 | tf_op jit(solution)/shard_map/ppermute | solution.py:543
  217.9 25.3 %attention_forward.3 = (bf16[2048,128]{1,0:T(8,128)(2,1)}, f32[2,2048]{1,0:T(2,128)}) custom-call(s32[8]{0:T(128)} %get-tuple-element.381.order_ref, bf16[2048,384]{1,0:T(8,128)(2,1)} %add_convert_fusion.2.query_ref.key_ref.value_ref, bf16[2048,384]{1,0:T(8,128)(2,1)} %add_convert_fusion.2.query_ref.key_ref.value_ref, ...), custom_call_target="tpu_custom_call" | custom-call | flops 28750000128 | bytes 90000000 | tf_op jit(solution)/shard_map/attention_forward/pallas_call | solution.py:603
  269.9 11.6 %all-gather.20.cloned.1.call-done = bf16[3072,512]{1,0:T(8,128)(2,1)} async-done(((bf16[768,512]{1,0:T(8,128)(2,1)}), bf16[3072,512]{1,0:T(8,128)(2,1)}) %all-gather.20.cloned.1.call-update) | async-done | bytes 3145744 | tf_op jit(solution)/shard_map/all_gather | solution.py:1668
  283.7 14.6 %feed_forward.3 = (f32[256,1024]{1,0:T(8,128)}, bf16[256,1024]{1,0:T(8,128)(2,1)}, bf16[512,2048]{1,0:T(8,128)(2,1)}, bf16[512,2048]{1,0:T(8,128)(2,1)}) custom-call(bf16[512,1024]{1,0:T(8,128)(2,1)} %copy-done.52, f32[1,2048]{1,0:T(1,128)} %maximum_convert_fusion.1.bias_ref, bf16[2,4,256,512]{3,2,1,0:T(8,128)(2,1)} %get-tuple-element.137.own_inner, ...), custom_call_target="tpu_custom_call" | custom-call | flops 18400000000 | bytes 57600000 | tf_op jit(solution)/shard_map/feed_forward/pallas_call | solution.py:963
  309.9 10.2 %feed_backward.2 = (f32[256,1024]{1,0:T(8,128)}, bf16[256,1024]{1,0:T(8,128)(2,1)}, bf16[512,2048]{1,0:T(8,128)(2,1)}, f32[1,2048]{1,0:T(1,128)}) custom-call(bf16[512,1024]{1,0:T(8,128)(2,1)} %pad_maximum_fusion.11.grad_ref, bf16[512,2048]{1,0:T(8,128)(2,1)} %get-tuple-element.149.slope_ref, bf16[2,4,256,512]{3,2,1,0:T(8,128)(2,1)} %get-tuple-element.137.own_inner, ...), custom_call_target="tpu_custom_call" | custom-call | flops 12650000384 | bytes 39600000 | tf_op jit(solution)/shard_map/feed_backward/pallas_call | solution.py:1007
  336.6 12.4 %weight_gradients.2 = (bf16[4,1024,640]{2,1,0:T(8,128)(2,1)}, bf16[4,1024,512]{2,1,0:T(8,128)(2,1)}) custom-call(s32[4]{0:T(128)} %pad_add_fusion.3.rows_ref, bf16[512,1024]{1,0:T(8,128)(2,1)} %copy-done.52, bf16[512,1024]{1,0:T(8,128)(2,1)} %pad_maximum_fusion.11.grad_ref, bf16[512,1024]{1,0:T(8,128)(2,1)} %pad_maximum_fusion.12.mixed_ref, ...), custom_call_target="tpu_custom_call" | custom-call | flops 14949999616 | bytes 46800000 | tf_op jit(solution)/shard_map/weight_gradients/pallas_call | solution.py:1100
  350.3 33.4 %attention_backward.2 = (bf16[2048,128]{1,0:T(8,128)(2,1)}, bf16[2048,128]{1,0:T(8,128)(2,1)}, bf16[2048,128]{1,0:T(8,128)(2,1)}) custom-call(s32[8]{0:T(128)} %get-tuple-element.381.order_ref, bf16[2048,384]{1,0:T(8,128)(2,1)} %add_convert_fusion.2.query_ref.key_ref.value_ref, bf16[2048,384]{1,0:T(8,128)(2,1)} %add_convert_fusion.2.query_ref.key_ref.value_ref, ...), custom_call_target="tpu_custom_call" | custom-call | flops 37950001152 | bytes 118800000 | tf_op jit(solution)/shard_map/attention_backward/pallas_call | solution.py:690
  383.8 9.8 %token_gradients.2 = (f32[4,256,1024]{2,1,0:T(8,128)}, bf16[4,256,1024]{2,1,0:T(8,128)(2,1)}, bf16[2048,384]{1,0:T(8,128)(2,1)}, f32[1,384]{1,0:T(1,128)}) custom-call(s32[4]{0:T(128)} %iota_xor_fusion.place_ref, bf16[2048,128]{1,0:T(8,128)(2,1)} %get-tuple-element.163.query_ref, bf16[2048,128]{1,0:T(8,128)(2,1)} %get-tuple-element.164.key_ref, ...), custom_call_target="tpu_custom_call" | custom-call | flops 11500000256 | bytes 36000000 | tf_op jit(solution)/shard_map/token_gradients/pallas_call | solution.py:1313
  413.4 19.3 %all-to-all-done.3.refs_0_ = bf16[4,256,1024]{2,1,0:T(8,128)(2,1)S(1)} async-done(((bf16[4,256,1024]{2,1,0:T(8,128)(2,1)}), bf16[4,256,1024]{2,1,0:T(8,128)(2,1)S(1)}, u32[]{:S(2)}, u32[]{:S(2)}) %all-to-all-start.3) | async-done | bytes 2097184 | tf_op jit(solution)/shard_map/all_to_all | solution.py:1465
  445.2 12.2 %feed_backward.3 = (f32[256,1024]{1,0:T(8,128)}, bf16[256,1024]{1,0:T(8,128)(2,1)}, bf16[512,2048]{1,0:T(8,128)(2,1)}, f32[1,2048]{1,0:T(1,128)}) custom-call(bf16[512,1024]{1,0:T(8,128)(2,1)} %pad_maximum_fusion.13.grad_ref, bf16[512,2048]{1,0:T(8,128)(2,1)} %get-tuple-element.169.slope_ref, bf16[2,4,256,512]{3,2,1,0:T(8,128)(2,1)} %get-tuple-element.137.own_inner, ...), custom_call_target="tpu_custom_call" | custom-call | flops 12650000384 | bytes 39600000 | tf_op jit(solution)/shard_map/feed_backward/pallas_call | solution.py:1007
  475.7 13.8 %weight_gradients.3 = (bf16[2,512,1152]{2,1,0:T(8,128)(2,1)}, bf16[2,512,1152]{2,1,0:T(8,128)(2,1)}, bf16[2,512,1152]{2,1,0:T(8,128)(2,1)}, bf16[2,512,1152]{2,1,0:T(8,128)(2,1)}) custom-call(s32[4]{0:T(128)} %pad_add_fusion.3.rows_ref, bf16[512,1024]{1,0:T(8,128)(2,1)} %copy-done.51, bf16[512,1024]{1,0:T(8,128)(2,1)} %pad_maximum_fusion.13.grad_ref, ...), custom_call_target="tpu_custom_call" | custom-call | flops 14949999616 | bytes 46800000 | tf_op jit(solution)/shard_map/weight_gradients/pallas_call | solution.py:1100
  493.2 33.4 %attention_backward.3 = (bf16[2048,128]{1,0:T(8,128)(2,1)}, bf16[2048,128]{1,0:T(8,128)(2,1)}, bf16[2048,128]{1,0:T(8,128)(2,1)}) custom-call(s32[8]{0:T(128)} %get-tuple-element.381.order_ref, bf16[2048,384]{1,0:T(8,128)(2,1)} %get-tuple-element.130.query_ref.key_ref.value_ref, bf16[2048,384]{1,0:T(8,128)(2,1)} %get-tuple-element.130.query_ref.key_ref.value_ref, ...), custom_call_target="tpu_custom_call" | custom-call | flops 37950001152 | bytes 118800000 | tf_op jit(solution)/shard_map/attention_backward/pallas_call | solution.py:690
  526.6 9.9 %token_gradients.3 = (f32[4,256,1024]{2,1,0:T(8,128)}, bf16[4,256,1024]{2,1,0:T(8,128)(2,1)}, bf16[2048,384]{1,0:T(8,128)(2,1)}, f32[1,384]{1,0:T(1,128)}) custom-call(s32[4]{0:T(128)} %iota_xor_fusion.place_ref, bf16[2048,128]{1,0:T(8,128)(2,1)} %get-tuple-element.182.query_ref, bf16[2048,128]{1,0:T(8,128)(2,1)} %get-tuple-element.183.key_ref, ...), custom_call_target="tpu_custom_call" | custom-call | flops 11500000256 | bytes 36000000 | tf_op jit(solution)/shard_map/token_gradients/pallas_call | solution.py:1313
  577.8 9.1 %collective-permute-done.45.refs_4_.refs_5_ = bf16[256,384]{1,0:T(8,128)(2,1)S(1)} collective-permute-done((bf16[256,384]{1,0:T(8,128)(2,1)}, bf16[256,384]{1,0:T(8,128)(2,1)S(1)}, u32[]{:S(2)}, u32[]{:S(2)}) %collective-permute-start.45) | collective-permute-done | bytes 196640 | tf_op jit(solution)/shard_map/ppermute | solution.py:548
  618.4 28.4 %all-to-all-done.6 = bf16[4,256,1024]{2,1,0:T(8,128)(2,1)S(1)} async-done(((bf16[4,256,1024]{2,1,0:T(8,128)(2,1)}), bf16[4,256,1024]{2,1,0:T(8,128)(2,1)S(1)}, u32[]{:S(2)}, u32[]{:S(2)}) %all-to-all-start.6) | async-done | bytes 2097184 | tf_op jit(solution)/shard_map/all_to_all | solution.py:1465
  655.6 12.6 %collective-permute-done.50.refs_2_ = bf16[256,1152]{1,0:T(8,128)(2,1)} collective-permute-done((bf16[256,1152]{1,0:T(8,128)(2,1)}, bf16[256,1152]{1,0:T(8,128)(2,1)}, u32[]{:S(2)}, u32[]{:S(2)}) %collective-permute-start.50) | collective-permute-done | bytes 589856 | tf_op jit(solution)/shard_map/ppermute | solution.py:548
  674.6 11.1 %all_to_all.40 = f32[8,32,256]{2,1,0:T(8,128)S(1)} all-to-all(f32[8,32,256]{2,1,0:T(8,128)} %gate.39), channel_id=1, replica_groups=mesh['ctx'=8,'wsh'=4] {'ctx'}, dimensions={0} | all-to-all | bytes 524288 | tf_op jit(solution)/shard_map/all_to_all | solution.py:1482
  691.8 9.7 %place_pieces.3 = (f32[2,256,1024]{2,1,0:T(8,128)}, f32[2,256,1024]{2,1,0:T(8,128)}, f32[2,256,1024]{2,1,0:T(8,128)}, f32[2,256,1024]{2,1,0:T(8,128)}, f32[2,256...) custom-call(s32[8]{0:T(128)} %iota.27.order_ref, bf16[8,256,1536]{2,1,0:T(8,128)(2,1)} %gate.38.source), custom_call_target="tpu_custom_call" | custom-call | flops 11500000256 | bytes 36000000 | tf_op jit(solution)/shard_map/place_pieces/pallas_call | solution.py:850
  (547 shorter events, 349.7 us)
Async XLA Ops:
  7.2 48.4 %all-gather.12.cloned.1.call-start = ((), (), s32[]{:S(2)}) async-start(), calls=%async_computation.13 | async-start | bytes 1638400 | tf_op jit(solution)/shard_map/all_gather | solution.py:1563
  13.3 35.1 %collective-permute-start.5 = (bf16[288,384]{1,0:T(8,128)(2,1)}, bf16[288,384]{1,0:T(8,128)(2,1)}, u32[]{:S(2)}, u32[]{:S(2)}) collective-permute-start(bf16[288,384]{1,0:T(8,128)(2,1)} %get-tuple-element.323), channel_id=1, source_target_pairs={{0,1},{1,2},{2,3},{3,0},{4,5},{5,6},{6,7},{7,4},{8,9},{9,10},{10,1... | collective-permute-start | bytes 663560 | tf_op jit(solution)/shard_map/ppermute | solution.py:548
  14.6 33.8 %collective-permute-start.6 = (bf16[288,384]{1,0:T(8,128)(2,1)}, bf16[288,384]{1,0:T(8,128)(2,1)}, u32[]{:S(2)}, u32[]{:S(2)}) collective-permute-start(bf16[288,384]{1,0:T(8,128)(2,1)} %get-tuple-element.323), channel_id=1, source_target_pairs={{0,2},{1,3},{2,0},{3,1},{4,6},{5,7},{6,4},{7,5},{8,10},{9,11},{10,... | collective-permute-start | bytes 663560 | tf_op jit(solution)/shard_map/ppermute | solution.py:548
  20.5 72.1 %all-gather.14.cloned.1.call-start = ((), (), s32[]{:S(2)}) async-start(), calls=%async_computation.19 | async-start | bytes 1310720 | tf_op jit(solution)/shard_map/all_gather | solution.py:1566
  53.7 115.0 %all-gather.16.cloned.1.call-start = ((), (), s32[]{:S(2)}) async-start(), calls=%async_computation.20 | async-start | bytes 3932160 | tf_op jit(solution)/shard_map/all_gather | solution.py:1617
  58.0 34.7 %collective-permute-start.9 = (bf16[384,640]{1,0:T(8,128)(2,1)}, bf16[384,640]{1,0:T(8,128)(2,1)}, u32[]{:S(2)}, u32[]{:S(2)}) collective-permute-start(bf16[384,640]{1,0:T(8,128)(2,1)} %get-tuple-element.324.refs_1_), channel_id=1, source_target_pairs={{0,16},{4,20},{8,24},{12,28},{16,0},{20,4},{24,8},{28,12},{1,17},{... | collective-permute-start | bytes 1474568 | tf_op jit(solution)/shard_map/ppermute | solution.py:543
  59.5 39.6 %collective-permute-start.10 = (bf16[384,640]{1,0:T(8,128)(2,1)}, bf16[384,640]{1,0:T(8,128)(2,1)}, u32[]{:S(2)}, u32[]{:S(2)}) collective-permute-start(bf16[384,640]{1,0:T(8,128)(2,1)} %get-tuple-element.324.refs_1_), channel_id=1, source_target_pairs={{0,8},{4,12},{8,0},{12,4},{16,24},{20,28},{24,16},{28,20},{1,9},{5... | collective-permute-start | bytes 1474568 | tf_op jit(solution)/shard_map/ppermute | solution.py:543
  110.6 132.5 %all-gather.18.cloned.1.call-start = ((), (), s32[]{:S(2)}) async-start(), calls=%async_computation.21 | async-start | bytes 4915200 | tf_op jit(solution)/shard_map/all_gather | solution.py:1668
  171.8 109.7 %all-gather.20.cloned.1.call-start = ((), (), s32[]{:S(2)}) async-start(), calls=%async_computation.22 | async-start | bytes 3932160 | tf_op jit(solution)/shard_map/all_gather | solution.py:1668
  335.6 156.4 %reduce-scatter.6.cloned.1.call-start = ((), (), s32[]{:S(2)}) async-start(), calls=%async_computation.14 | async-start | bytes 6553600 | tf_op jit(solution)/shard_map/reduce_scatter | solution.py:1771
  407.3 143.0 %reduce-scatter.10.cloned.1.call-start = ((), (), s32[]{:S(2)}) async-start(), calls=%async_computation.16 | async-start | bytes 5242880 | tf_op jit(solution)/shard_map/reduce_scatter | solution.py:1783
  438.3 168.1 %reduce-scatter.14.cloned.1.call-start = ((), (), s32[]{:S(2)}) async-start(), calls=%async_computation.18 | async-start | bytes 983040 | tf_op jit(solution)/shard_map/reduce_scatter | solution.py:1790
  474.8 131.6 %reduce-scatter.8.cloned.1.call-start = ((), (), s32[]{:S(2)}) async-start(), calls=%async_computation.15 | async-start | bytes 1638400 | tf_op jit(solution)/shard_map/reduce_scatter | solution.py:1780
  489.5 55.5 %collective-permute-start.41 = (bf16[2,512,1152]{2,1,0:T(8,128)(2,1)}, bf16[2,512,1152]{2,1,0:T(8,128)(2,1)}, u32[]{:S(2)}, u32[]{:S(2)}) collective-permute-start(bf16[2,512,1152]{2,1,0:T(8,128)(2,1)} %get-tuple-element.187), channel_id=1, source_target_pairs={{0,8},{4,12},{8,0},{12,4},{16,24},{20,28},{24,16},{28,20},{1,9},{5... | collective-permute-start | bytes 7077896 | tf_op jit(solution)/shard_map/ppermute | solution.py:543
  490.8 54.2 %collective-permute-start.42 = (bf16[2,512,1152]{2,1,0:T(8,128)(2,1)}, bf16[2,512,1152]{2,1,0:T(8,128)(2,1)}, u32[]{:S(2)}, u32[]{:S(2)}) collective-permute-start(bf16[2,512,1152]{2,1,0:T(8,128)(2,1)} %get-tuple-element.188), channel_id=1, source_target_pairs={{0,16},{4,20},{8,24},{12,28},{16,0},{20,4},{24,8},{28,12},{1,17},{... | collective-permute-start | bytes 7077896 | tf_op jit(solution)/shard_map/ppermute | solution.py:543
  492.1 114.4 %reduce-scatter.12.cloned.1.call-start = ((), (), s32[]{:S(2)}) async-start(), calls=%async_computation.17 | async-start | bytes 1310720 | tf_op jit(solution)/shard_map/reduce_scatter | solution.py:1813
  536.5 36.3 %collective-permute-start.40 = (bf16[4,256,1024]{2,1,0:T(8,128)(2,1)}, bf16[4,256,1024]{2,1,0:T(8,128)(2,1)}, u32[]{:S(2)}, u32[]{:S(2)}) collective-permute-start(bf16[4,256,1024]{2,1,0:T(8,128)(2,1)} %get-tuple-element.186), channel_id=1, source_target_pairs={{0,4},{4,0},{8,12},{12,8},{16,20},{20,16},{24,28},{28,24},{1,5},{5... | collective-permute-start | bytes 6291464 | tf_op jit(solution)/shard_map/ppermute | solution.py:543
  549.2 50.7 %collective-permute-start.44 = (bf16[512,1152]{1,0:T(8,128)(2,1)}, bf16[512,1152]{1,0:T(8,128)(2,1)}, u32[]{:S(2)}, u32[]{:S(2)}) collective-permute-start(bf16[512,1152]{1,0:T(8,128)(2,1)} %fusion.16), channel_id=1, source_target_pairs={{0,8},{4,12},{8,0},{12,4},{16,24},{20,28},{24,16},{28,20},{1,9},{5... | collective-permute-start | bytes 3538952 | tf_op jit(solution)/shard_map/ppermute | solution.py:543
  553.5 46.4 %collective-permute-start.43 = (bf16[512,1152]{1,0:T(8,128)(2,1)}, bf16[512,1152]{1,0:T(8,128)(2,1)S(1)}, u32[]{:S(2)}, u32[]{:S(2)}) collective-permute-start(bf16[512,1152]{1,0:T(8,128)(2,1)} %fusion.15), channel_id=1, source_target_pairs={{0,16},{4,20},{8,24},{12,28},{16,0},{20,4},{24,8},{28,12},{1,17},{... | collective-permute-start | bytes 3538952 | tf_op jit(solution)/shard_map/ppermute | solution.py:543
  564.9 126.3 %all-gather.22.cloned.1.call-start = ((), (), s32[]{:S(2)}) async-start(), calls=%async_computation.23 | async-start | bytes 7077888 | tf_op jit(solution)/shard_map/all_gather | solution.py:1815
  610.3 36.5 %all-to-all-start.6 = ((bf16[4,256,1024]{2,1,0:T(8,128)(2,1)}), bf16[4,256,1024]{2,1,0:T(8,128)(2,1)S(1)}, u32[]{:S(2)}, u32[]{:S(2)}) async-start(bf16[4,256,1024]{2,1,0:T(8,128)(2,1)} %gate.33), calls=%async_computation.7 | async-start | bytes 4194304 | tf_op jit(solution)/shard_map/all_to_all | solution.py:1465
  613.9 35.4 %collective-permute-start.48 = (bf16[256,1152]{1,0:T(8,128)(2,1)}, bf16[256,1152]{1,0:T(8,128)(2,1)}, u32[]{:S(2)}, u32[]{:S(2)}) collective-permute-start(bf16[256,1152]{1,0:T(8,128)(2,1)} %get-tuple-element.202), channel_id=1, source_target_pairs={{0,3},{1,0},{2,1},{3,2},{4,7},{5,4},{6,5},{7,6},{8,11},{9,8},{10,9... | collective-permute-start | bytes 1769480 | tf_op jit(solution)/shard_map/ppermute | solution.py:548
  617.1 38.4 %collective-permute-start.49 = (bf16[256,1152]{1,0:T(8,128)(2,1)}, bf16[256,1152]{1,0:T(8,128)(2,1)}, u32[]{:S(2)}, u32[]{:S(2)}) collective-permute-start(bf16[256,1152]{1,0:T(8,128)(2,1)} %get-tuple-element.203), channel_id=1, source_target_pairs={{0,2},{1,3},{2,0},{3,1},{4,6},{5,7},{6,4},{7,5},{8,10},{9,11},{10,... | collective-permute-start | bytes 1769480 | tf_op jit(solution)/shard_map/ppermute | solution.py:548
  617.3 50.9 %collective-permute-start.50 = (bf16[256,1152]{1,0:T(8,128)(2,1)}, bf16[256,1152]{1,0:T(8,128)(2,1)}, u32[]{:S(2)}, u32[]{:S(2)}) collective-permute-start(bf16[256,1152]{1,0:T(8,128)(2,1)} %get-tuple-element.204), channel_id=1, source_target_pairs={{0,1},{1,2},{2,3},{3,0},{4,5},{5,6},{6,7},{7,4},{8,9},{9,10},{10,1... | collective-permute-start | bytes 1769480 | tf_op jit(solution)/shard_map/ppermute | solution.py:548
  (144 other events, 1520.4 us)
Sparse Core Ops, SparseCore 0:
  20.6 34.9 all-gather.11
  57.8 29.6 all-gather.13
  96.9 62.4 all-gather.15
  171.9 59.2 all-gather.17
  233.5 47.9 all-gather.19
  349.9 62.3 reduce-scatter.5
  438.4 59.3 reduce-scatter.9
  500.2 20.7 reduce-scatter.13
  523.4 30.6 reduce-scatter.7
  556.4 44.0 reduce-scatter.11
  610.4 63.7 all-gather.21

commit v5 on v4

--- a/solution.py
+++ b/solution.py
@@ -523,7 +523,7 @@
 NT = (((1,), (1,)), ((), ()))
 TN = (((0,), (0,)), ((), ()))
 LANES = 128
-QUERY_BLOCK = 256
+QUERY_BLOCK = 1024
 CORE, ALONG_X, ALONG_Y = 1, 2, 4
 SMALL_COST = pl.CostEstimate(flops=1000, bytes_accessed=1000, transcendentals=0)
 
@@ -594,7 +594,12 @@
         mixed = mm(value_t[pl.ds(HDIM * head, HDIM), :], low(exponent))
         parts.append(mixed / total)
         log_ref[pl.ds(head, 1), :] = peak + jnp.log(total)
-    mixed_ref[...] = low(jnp.concatenate(parts, axis=0).T)
+    mixed_all = low(jnp.concatenate(parts, axis=0).T)
+    block_rows = mixed_ref.shape[1]
+    count = mixed_all.shape[0] // block_rows
+    for at in range(count):
+        place = order_ref[pl.program_id(0) * count + at]
+        mixed_ref[place] = mixed_all[at * block_rows : (at + 1) * block_rows]
 
 
 def attention_forward(packed, labels, order):
@@ -613,7 +618,7 @@
                 pl.BlockSpec((QUERY_BLOCK, 1), lambda i, order_ref: (i, 0)),
             ],
             out_specs=[
-                pl.BlockSpec((QUERY_BLOCK, LANES), lambda i, order_ref: (order_ref[i], 0)),
+                pl.BlockSpec((8, rows // 8, LANES), lambda i, order_ref: (0, 0, 0)),
                 pl.BlockSpec((2, QUERY_BLOCK), lambda i, order_ref: (0, i)),
             ],
             scratch_shapes=[
@@ -622,10 +627,10 @@
             ],
         ),
         out_shape=[
-            jax.ShapeDtypeStruct((rows, LANES), jnp.bfloat16),
+            jax.ShapeDtypeStruct((8, rows // 8, LANES), jnp.bfloat16),
             jax.ShapeDtypeStruct((2, rows), jnp.float32),
         ],
-        cost_estimate=lasting(25),
+        cost_estimate=lasting(17),
         name="attention_forward",
     )(order, packed, packed, packed, labels, labels)
 
@@ -657,7 +662,8 @@
         value_sum[...] = jnp.zeros_like(value_sum)
 
     scaled = low(wide(query_ref[...]) * HDIM ** (-0.5))
-    grad = grad_ref[...]
+    count = scaled.shape[0] // grad_ref.shape[1]
+    grad = jnp.concatenate([grad_ref[order_ref[step * count + at]] for at in range(count)], axis=0)
     value_rows = value_ref[...]
     lane = lax.broadcasted_iota(jnp.int32, scaled.shape, 1)
     features, _ = mask_features(query_label_ref[...])
@@ -698,7 +704,7 @@
                 pl.BlockSpec((rows, LANES), lambda i, order_ref: (0, 2)),
                 pl.BlockSpec((rows, 1), lambda i, order_ref: (0, 0)),
                 pl.BlockSpec((QUERY_BLOCK, 1), lambda i, order_ref: (i, 0)),
-                pl.BlockSpec((QUERY_BLOCK, LANES), lambda i, order_ref: (order_ref[i], 0)),
+                pl.BlockSpec((8, rows // 8, LANES), lambda i, order_ref: (0, 0, 0)),
                 pl.BlockSpec((2, QUERY_BLOCK), lambda i, order_ref: (0, i)),
             ],
             out_specs=[mine, whole, whole],
@@ -710,7 +716,7 @@
             ],
         ),
         out_shape=[jax.ShapeDtypeStruct((rows, LANES), jnp.bfloat16)] * 3,
-        cost_estimate=lasting(33),
+        cost_estimate=lasting(29),
         name="attention_backward",
     )(order, packed, packed, packed, labels, labels, grad, log_all)
 
@@ -908,8 +914,8 @@
     own = pl.BlockSpec((1, 1, shard, piece), lambda i: (layer, i, 0, 0))
     if len(inner_parts) == 1:
         rest = inner_parts[0].shape[1]
-        part = pl.BlockSpec((1, rest, piece), lambda i: (i, 0, 0))
-        return ([own_inner, own_outer, *inner_parts, *outer_parts], [own, own, part, part], 1)
+        parts = [pl.BlockSpec((1, rest, piece), lambda i, at=at: (i, 0, at)) for at in range(2)]
+        return ([own_inner, own_outer, *inner_parts, *outer_parts], [own, own, *parts], 1)
     rows = inner_parts[0].shape[0]
     fixed = pl.BlockSpec((rows, piece), lambda i: (0, 0), pipeline_mode=pl.Buffered(1))
     return (
@@ -1576,7 +1582,9 @@
         return [part for pair in zip(lefts, rights) for part in pair]
 
     inner_half = spread_first(inner_near)
-    layer_own = jnp.concatenate([first_own[1], second_own[1], joint_own[1, :shard]], axis=1)
+    layer_own = jnp.concatenate(
+        [first_own[1, :, :piece], second_own[1], first_own[1, :, piece:], joint_own[1, :shard]], axis=1
+    )
     wide_piece = 2 * piece + LANES
 
     def layer_weights(layer):
@@ -1590,8 +1598,8 @@
             )
             weights = (inner_own, outer_own, inner_first, outer_first)
         else:
-            near = jnp.concatenate([inner_second[j, :, piece:] for j in range(4)], axis=1)
-            weights = (inner_own, outer_own, [inner_second])
+            near = jnp.concatenate([out_parts[j] for j in range(4)], axis=1)
+            weights = (inner_own, outer_own)
         return (weights, (out_own[layer], near, swap(near, CORE)))
 
     def out_place(layer, block):
@@ -1629,9 +1637,17 @@
             inner_first = spread_second(*inner_half[:2], left_x, right_y)
             outer_first = spread_second(*spread_first(ordered(outer_stack, turned[1:])))
         else:
-            (inner_second,) = gate([inner_second], mixed)
+            out_parts = lax.all_to_all(
+                jnp.broadcast_to(out_second, (4, *out_second.shape)),
+                "ctx",
+                0,
+                0,
+                axis_index_groups=plane_groups(),
+                tiled=True,
+            )
+            (out_parts,) = gate([out_parts], mixed)
         weights, out_weights = layer_weights(layer)
-        mixed_heads = exchange(mixed.reshape(8, rows, LANES))
+        mixed_heads = exchange(mixed)
         places = jnp.stack(
             [2 * turned[p // 2] + p % 2 for p in range(8)]
             + [out_place(layer, b) for b in range(8)]
@@ -1649,7 +1665,8 @@
             places,
         )
         if layer == 1:
-            weights = (*weights, gate([outer_second], hidden_turned))
+            second_parts = gate([second_parts], hidden_turned)
+            weights = (*weights, second_parts, second_parts)
         mixed_pair = jnp.concatenate([mixed_turned, swap(mixed_turned, CORE)], axis=0)
         hidden_pair = jnp.concatenate([hidden_turned, swap(hidden_turned, CORE)], axis=0)
         inner_bias_own = jnp.concatenate(
@@ -1664,9 +1681,10 @@
             joint_second = second_stack[:, :, wide_piece:].reshape(width, joint_width)
             others_second = ordered(second_stack[:, :, :wide_piece], turned[1:])
             sent_second = (others_second[:, : piece + LANES], others_second[:, piece + LANES :])
-            inner_second, outer_second = [
-                lax.all_gather(part, "ctx", axis=0, axis_index_groups=plane_groups()) for part in sent_second
-            ]
+            second_parts = lax.all_gather(
+                others_second[:, : 2 * piece], "ctx", axis=0, axis_index_groups=plane_groups()
+            )
+            out_second = others_second[:, 2 * piece :]
         outer_out = block_columns(outer_turned, unturned, shard)
         second_pre = hidden_rows + (outer_out + wide(small(layer, 3)))
         result, second_unit, second_inverse = norm_forward(second_pre, second_gain_row, second_shift_row)
@@ -1734,7 +1752,7 @@
             out_weights,
             places,
         )
-        grad_mixed = exchange(grad_sent).reshape(8 * rows, LANES)
+        grad_mixed = exchange(grad_sent)
         branch_half = 4 * LANES
         branch_pair = jnp.concatenate(
             [branch_spread[:, :branch_half], swap(branch_spread[:, branch_half:], CORE)], axis=0
@@ -1777,9 +1795,12 @@
                 )
             ]
             (plane_first,) = gate([plane_first], far_came)
-            sum_first = lax.psum_scatter(plane_first, "wsh", scatter_dimension=0, tiled=True)
+            plane_rows_first = [
+                lax.dynamic_slice_in_dim(plane_first, turned[r] * shard, shard, 0) for r in range(planes)
+            ]
+            came_first = [turn(plane_rows_first[r], planes - r) for r in range(1, planes)]
             gradient = grad_first + collect_tokens(tokens_sent, (), (grad_joint,))
-            (second_sum,) = gate([summed[1]], gradient)
+            (second_sum,) = gate([summed[1]], gradient, plane_first)
             plane_second = lax.psum_scatter(
                 second_sum.reshape(4 * width, -1),
                 "ctx",
@@ -1797,7 +1818,11 @@
             axis=0,
         )
         small_spread = jnp.broadcast_to(small_plane, (8, *small_plane.shape))
-        first_came, second_came = gate([first_came, second_came], near_part, grad_joint)
+        first_came, second_came = gate([first_came, second_came], near_part, grad_joint, *came_first)
+        sum_first = wide(plane_rows_first[0])
+        for part in came_first:
+            sum_first = sum_first + wide(part)
+        sum_first = low(sum_first)
         first_next = low(wide(first_keep[1]) + wide(first_came[1]))
         second_next = low(wide(second_keep[1]) + wide(second_came[1]))
         joint_rows = [lax.dynamic_slice_in_dim(grad_joint, turned[r] * shard, shard, 0) for r in range(planes)]

time: 754 us -> 737 us (0.977)
  Pallas kernels: 284 us -> 257 us
  starting transfers between devices: 84.4 us -> 95.3 us
    pallas_call x2, Pallas kernels: 50.6 us -> 30.6 us  [attention_forward(): pl.pallas_call(attention_forward_kernel, grid_spec=pltpu.PrefetchScalarGr...]
    all_gather x2 -> x1, waiting for transfers between devices: 11.6 us -> 0.02 us  [head_split_body(): lax.all_gather(others_second[:, :2 * piece], 'ctx', axis=0, axis_index_gr...]
    pallas_call x2, Pallas kernels: 66.9 us -> 59.1 us  [attention_backward(): pl.pallas_call(attention_backward_kernel, grid_spec=pltpu.PrefetchScalarG...]
    ppermute x9 -> x12, waiting for transfers between devices: 41.5 us -> 34.4 us  [turn(): lax.ppermute(block, 'wsh', [(i, (i + distance) % count) for i in range(co...]
    convert_element_type x5 -> x6, other arithmetic: 14.7 us -> 17.1 us  [low(): return values_in.astype(jnp.bfloat16)]
    unnamed x206 -> x204, local copies, waits for them, and re-layouts: 26.9 us -> 25.5 us
  transfers between devices with their start and end apart: 74 -> 76, of which waited for: 30 -> 30; matrix products, arithmetic and copies ran while one was open for 15% -> 16% of each run, Pallas kernels for 34% -> 31%
where the time goes in v5:
time: 737 us; the launch traced here: 723 us
  Pallas kernels  257 us (35%)
  waiting for transfers between devices  182 us (25%)
  starting transfers between devices  95.3 us (13%)
  other arithmetic  73.7 us (10%)
  local copies, waits for them, and re-layouts  61.3 us (8%)
  matrix products  22.1 us (3%)
  between operations  20.7 us (3%)
  blocking collectives  11.1 us (2%)
    ppermute x47, waiting for transfers between devices, swap(): return lax.ppermute(block, 'ctx', [(i, i ^ mask) for i in devices])  76.2 us
    pallas_call x2, Pallas kernels, attention_backward(): pl.pallas_call(attention_backward_kernel, grid_spec=pltpu.PrefetchScalarG...  59.1 us
    all_to_all x2, waiting for transfers between devices, collect_tokens(): lax.all_to_all(sent, 'ctx', 0, 0, axis_index_groups=plane_groups(), tiled...  50.6 us
    ppermute x47, starting transfers between devices, swap(): return lax.ppermute(block, 'ctx', [(i, i ^ mask) for i in devices])  46.6 us
    ppermute x12, waiting for transfers between devices, turn(): lax.ppermute(block, 'wsh', [(i, (i + distance) % count) for i in range(co...  34.4 us
    pallas_call x2, Pallas kernels, feed_forward(): pl.pallas_call(functools.partial(feed_forward_kernel, count), grid=(4,),...  31.1 us
    pallas_call x2, Pallas kernels, attention_forward(): pl.pallas_call(attention_forward_kernel, grid_spec=pltpu.PrefetchScalarGr...  30.6 us
    pallas_call x2, Pallas kernels, weight_gradients(): pl.pallas_call(functools.partial(weight_gradient_kernel, split), grid_spe...  26.3 us
  transfers between devices with their start and end apart: 76, of which 30 were waited for; matrix products, arithmetic and copies ran while one was open for 16% of the time, Pallas kernels for 31%

profile of v5, /device:TPU:9, one launch (start us, length us, event | category | flops | bytes accessed | tf_op | source)
XLA Modules:
  0.0 723.4 jit_solution(8922419886900332461)
XLA Ops:
  28.6 7.1 collective-permute-done.3
  67.2 15.3 %attention_forward.2 = (bf16[8,256,128]{2,1,0:T(8,128)(2,1)}, f32[2,2048]{1,0:T(2,128)}) custom-call(s32[8]{0:T(128)} %get-tuple-element.382.order_ref, bf16[2048,384]{1,0:T(8,128)(2,1)} %get-tuple-element.130.query_ref.key_ref.value_ref, bf16[2048,384]{1,0:T(8,128)(2,1)} %get-tuple-element.130.query_ref.key_ref.value_ref, ...), custom_call_target="tpu_custom_call" | custom-call | flops 19549999104 | bytes 61200000 | tf_op jit(solution)/shard_map/attention_forward/pallas_call | solution.py:608
  109.2 8.3 %own_blocks.1 = (bf16[2,4,256,512]{3,2,1,0:T(8,128)(2,1)}, bf16[2,4,256,512]{3,2,1,0:T(8,128)(2,1)}, bf16[2,256,1024]{2,1,0:T(8,128)(2,1)}) custom-call(s32[8]{0:T(128)} %pad_add_fusion.1.inner_order_ref, s32[16]{0:T(128)} %pad_add_fusion.2.out_order_ref, f32[2,256,4096]{2,1,0:T(8,128)} %refs_3_.3, f32[2,256,4096]{2,1,0:T(8,128)} %refs_3_.3, ...), custom_call_target="tpu_custom_call" | custom-call | flops 8049999872 | bytes 25200000 | tf_op jit(solution)/shard_map/own_blocks/pallas_call | solution.py:802
  136.5 8.3 %collective-permute-done.20.refs_14_ = bf16[384,512]{1,0:T(8,128)(2,1)S(1)} collective-permute-done((bf16[384,512]{1,0:T(8,128)(2,1)}, bf16[384,512]{1,0:T(8,128)(2,1)S(1)}, u32[]{:S(2)}, u32[]{:S(2)}) %collective-permute-start.20) | collective-permute-done | bytes 393248 | tf_op jit(solution)/shard_map/ppermute | solution.py:543
  145.7 16.5 %feed_forward.2 = (f32[256,1024]{1,0:T(8,128)}, bf16[256,1024]{1,0:T(8,128)(2,1)}, bf16[512,2048]{1,0:T(8,128)(2,1)}, bf16[512,2048]{1,0:T(8,128)(2,1)}) custom-call(bf16[512,1024]{1,0:T(8,128)(2,1)} %copy-done.51, f32[1,2048]{1,0:T(1,128)} %maximum_convert_fusion.bias_ref, bf16[2,4,256,512]{3,2,1,0:T(8,128)(2,1)} %get-tuple-element.137.own_inner, ...), custom_call_target="tpu_custom_call" | custom-call | flops 18400000000 | bytes 57600000 | tf_op jit(solution)/shard_map/feed_forward/pallas_call | solution.py:969
  175.0 6.1 collective-permute-done.25
  182.8 23.2 %collective-permute-done.26 = bf16[2,256,512]{2,1,0:T(8,128)(2,1)S(1)} collective-permute-done((bf16[2,256,512]{2,1,0:T(8,128)(2,1)S(1)}, bf16[2,256,512]{2,1,0:T(8,128)(2,1)S(1)}, u32[]{:S(2)}, u32[]{:S(2)}) %collective-permute-start.26) | collective-permute-done | bytes 524320 | tf_op jit(solution)/shard_map/ppermute | solution.py:543
  223.5 15.3 %attention_forward.3 = (bf16[8,256,128]{2,1,0:T(8,128)(2,1)}, f32[2,2048]{1,0:T(2,128)}) custom-call(s32[8]{0:T(128)} %get-tuple-element.382.order_ref, bf16[2048,384]{1,0:T(8,128)(2,1)} %add_convert_fusion.2.query_ref.key_ref.value_ref, bf16[2048,384]{1,0:T(8,128)(2,1)} %add_convert_fusion.2.query_ref.key_ref.value_ref, ...), custom_call_target="tpu_custom_call" | custom-call | flops 19549999104 | bytes 61200000 | tf_op jit(solution)/shard_map/attention_forward/pallas_call | solution.py:608
  248.2 9.5 %all-to-all-done.1.heads_ref = bf16[8,256,128]{2,1,0:T(8,128)(2,1)S(1)} async-done(((bf16[8,256,128]{2,1,0:T(8,128)(2,1)}), bf16[8,256,128]{2,1,0:T(8,128)(2,1)S(1)}, u32[]{:S(2)}, u32[]{:S(2)}) %all-to-all-start.1) | async-done | bytes 524320 | tf_op jit(solution)/shard_map/all_to_all | solution.py:1488
  274.0 14.6 %feed_forward.3 = (f32[256,1024]{1,0:T(8,128)}, bf16[256,1024]{1,0:T(8,128)(2,1)}, bf16[512,2048]{1,0:T(8,128)(2,1)}, bf16[512,2048]{1,0:T(8,128)(2,1)}) custom-call(bf16[512,1024]{1,0:T(8,128)(2,1)} %copy-done.52, f32[1,2048]{1,0:T(1,128)} %maximum_convert_fusion.1.bias_ref, bf16[2,4,256,512]{3,2,1,0:T(8,128)(2,1)} %get-tuple-element.137.own_inner, ...), custom_call_target="tpu_custom_call" | custom-call | flops 18400000000 | bytes 57600000 | tf_op jit(solution)/shard_map/feed_forward/pallas_call | solution.py:969
  299.9 10.3 %feed_backward.2 = (f32[256,1024]{1,0:T(8,128)}, bf16[256,1024]{1,0:T(8,128)(2,1)}, bf16[512,2048]{1,0:T(8,128)(2,1)}, f32[1,2048]{1,0:T(1,128)}) custom-call(bf16[512,1024]{1,0:T(8,128)(2,1)} %pad_maximum_fusion.12.grad_ref, bf16[512,2048]{1,0:T(8,128)(2,1)} %get-tuple-element.149.slope_ref, bf16[2,4,256,512]{3,2,1,0:T(8,128)(2,1)} %get-tuple-element.137.own_inner, ...), custom_call_target="tpu_custom_call" | custom-call | flops 12650000384 | bytes 39600000 | tf_op jit(solution)/shard_map/feed_backward/pallas_call | solution.py:1013
  326.4 12.4 %weight_gradients.2 = (bf16[4,1024,640]{2,1,0:T(8,128)(2,1)}, bf16[4,1024,512]{2,1,0:T(8,128)(2,1)}) custom-call(s32[4]{0:T(128)} %pad_add_fusion.3.rows_ref, bf16[512,1024]{1,0:T(8,128)(2,1)} %copy-done.52, bf16[512,1024]{1,0:T(8,128)(2,1)} %pad_maximum_fusion.12.grad_ref, bf16[512,1024]{1,0:T(8,128)(2,1)} %pad_maximum_fusion.13.mixed_ref, ...), custom_call_target="tpu_custom_call" | custom-call | flops 14949999616 | bytes 46800000 | tf_op jit(solution)/shard_map/weight_gradients/pallas_call | solution.py:1106
  340.1 29.6 %attention_backward.2 = (bf16[2048,128]{1,0:T(8,128)(2,1)}, bf16[2048,128]{1,0:T(8,128)(2,1)}, bf16[2048,128]{1,0:T(8,128)(2,1)}) custom-call(s32[8]{0:T(128)} %get-tuple-element.382.order_ref, bf16[2048,384]{1,0:T(8,128)(2,1)} %add_convert_fusion.2.query_ref.key_ref.value_ref, bf16[2048,384]{1,0:T(8,128)(2,1)} %add_convert_fusion.2.query_ref.key_ref.value_ref, ...), custom_call_target="tpu_custom_call" | custom-call | flops 33350000640 | bytes 104400000 | tf_op jit(solution)/shard_map/attention_backward/pallas_call | solution.py:696
  369.8 9.9 %token_gradients.2 = (f32[4,256,1024]{2,1,0:T(8,128)}, bf16[4,256,1024]{2,1,0:T(8,128)(2,1)}, bf16[2048,384]{1,0:T(8,128)(2,1)}, f32[1,384]{1,0:T(1,128)}) custom-call(s32[4]{0:T(128)} %iota_xor_fusion.place_ref, bf16[2048,128]{1,0:T(8,128)(2,1)} %get-tuple-element.163.query_ref, bf16[2048,128]{1,0:T(8,128)(2,1)} %get-tuple-element.164.key_ref, ...), custom_call_target="tpu_custom_call" | custom-call | flops 11500000256 | bytes 36000000 | tf_op jit(solution)/shard_map/token_gradients/pallas_call | solution.py:1319
  399.3 22.0 %all-to-all-done.4.refs_0_ = bf16[4,256,1024]{2,1,0:T(8,128)(2,1)S(1)} async-done(((bf16[4,256,1024]{2,1,0:T(8,128)(2,1)}), bf16[4,256,1024]{2,1,0:T(8,128)(2,1)S(1)}, u32[]{:S(2)}, u32[]{:S(2)}) %all-to-all-start.4) | async-done | bytes 2097184 | tf_op jit(solution)/shard_map/all_to_all | solution.py:1471
  433.8 12.2 %feed_backward.3 = (f32[256,1024]{1,0:T(8,128)}, bf16[256,1024]{1,0:T(8,128)(2,1)}, bf16[512,2048]{1,0:T(8,128)(2,1)}, f32[1,2048]{1,0:T(1,128)}) custom-call(bf16[512,1024]{1,0:T(8,128)(2,1)} %pad_maximum_fusion.14.grad_ref, bf16[512,2048]{1,0:T(8,128)(2,1)} %get-tuple-element.169.slope_ref, bf16[2,4,256,512]{3,2,1,0:T(8,128)(2,1)} %get-tuple-element.137.own_inner, ...), custom_call_target="tpu_custom_call" | custom-call | flops 12650000384 | bytes 39600000 | tf_op jit(solution)/shard_map/feed_backward/pallas_call | solution.py:1013
  464.4 13.9 %weight_gradients.3 = (bf16[2,512,1152]{2,1,0:T(8,128)(2,1)}, bf16[2,512,1152]{2,1,0:T(8,128)(2,1)}, bf16[2,512,1152]{2,1,0:T(8,128)(2,1)}, bf16[2,512,1152]{2,1,0:T(8,128)(2,1)}) custom-call(s32[4]{0:T(128)} %pad_add_fusion.3.rows_ref, bf16[512,1024]{1,0:T(8,128)(2,1)} %copy-done.51, bf16[512,1024]{1,0:T(8,128)(2,1)} %pad_maximum_fusion.14.grad_ref, ...), custom_call_target="tpu_custom_call" | custom-call | flops 14949999616 | bytes 46800000 | tf_op jit(solution)/shard_map/weight_gradients/pallas_call | solution.py:1106
  487.1 29.5 %attention_backward.3 = (bf16[2048,128]{1,0:T(8,128)(2,1)}, bf16[2048,128]{1,0:T(8,128)(2,1)}, bf16[2048,128]{1,0:T(8,128)(2,1)}) custom-call(s32[8]{0:T(128)} %get-tuple-element.382.order_ref, bf16[2048,384]{1,0:T(8,128)(2,1)} %get-tuple-element.130.query_ref.key_ref.value_ref, bf16[2048,384]{1,0:T(8,128)(2,1)} %get-tuple-element.130.query_ref.key_ref.value_ref, ...), custom_call_target="tpu_custom_call" | custom-call | flops 33350000640 | bytes 104400000 | tf_op jit(solution)/shard_map/attention_backward/pallas_call | solution.py:696
  516.6 9.9 %token_gradients.3 = (f32[4,256,1024]{2,1,0:T(8,128)}, bf16[4,256,1024]{2,1,0:T(8,128)(2,1)}, bf16[2048,384]{1,0:T(8,128)(2,1)}, f32[1,384]{1,0:T(1,128)}) custom-call(s32[4]{0:T(128)} %iota_xor_fusion.place_ref, bf16[2048,128]{1,0:T(8,128)(2,1)} %get-tuple-element.182.query_ref, bf16[2048,128]{1,0:T(8,128)(2,1)} %get-tuple-element.183.key_ref, ...), custom_call_target="tpu_custom_call" | custom-call | flops 11500000256 | bytes 36000000 | tf_op jit(solution)/shard_map/token_gradients/pallas_call | solution.py:1319
  566.9 6.5 collective-permute-done.48.refs_4_.refs_5_
  600.1 28.6 %all-to-all-done.7 = bf16[4,256,1024]{2,1,0:T(8,128)(2,1)S(1)} async-done(((bf16[4,256,1024]{2,1,0:T(8,128)(2,1)}), bf16[4,256,1024]{2,1,0:T(8,128)(2,1)S(1)}, u32[]{:S(2)}, u32[]{:S(2)}) %all-to-all-start.7) | async-done | bytes 2097184 | tf_op jit(solution)/shard_map/all_to_all | solution.py:1471
  637.3 12.6 %collective-permute-done.53.refs_2_ = bf16[256,1152]{1,0:T(8,128)(2,1)} collective-permute-done((bf16[256,1152]{1,0:T(8,128)(2,1)}, bf16[256,1152]{1,0:T(8,128)(2,1)}, u32[]{:S(2)}, u32[]{:S(2)}) %collective-permute-start.53) | collective-permute-done | bytes 589856 | tf_op jit(solution)/shard_map/ppermute | solution.py:548
  656.4 11.1 %all_to_all.45 = f32[8,32,256]{2,1,0:T(8,128)S(1)} all-to-all(f32[8,32,256]{2,1,0:T(8,128)} %gate.39), channel_id=1, replica_groups=mesh['ctx'=8,'wsh'=4] {'ctx'}, dimensions={0} | all-to-all | bytes 524288 | tf_op jit(solution)/shard_map/all_to_all | solution.py:1488
  673.5 9.7 %place_pieces.3 = (f32[2,256,1024]{2,1,0:T(8,128)}, f32[2,256,1024]{2,1,0:T(8,128)}, f32[2,256,1024]{2,1,0:T(8,128)}, f32[2,256,1024]{2,1,0:T(8,128)}, f32[2,256...) custom-call(s32[8]{0:T(128)} %iota.27.order_ref, bf16[8,256,1536]{2,1,0:T(8,128)(2,1)} %gate.38.source), custom_call_target="tpu_custom_call" | custom-call | flops 11500000256 | bytes 36000000 | tf_op jit(solution)/shard_map/place_pieces/pallas_call | solution.py:856
  (551 shorter events, 360.3 us)
Async XLA Ops:
  7.2 48.4 %all-gather.10.cloned.1.call-start = ((), (), s32[]{:S(2)}) async-start(), calls=%async_computation.13 | async-start | bytes 1638400 | tf_op jit(solution)/shard_map/all_gather | solution.py:1569
  13.3 34.8 %collective-permute-start.5 = (bf16[288,384]{1,0:T(8,128)(2,1)}, bf16[288,384]{1,0:T(8,128)(2,1)}, u32[]{:S(2)}, u32[]{:S(2)}) collective-permute-start(bf16[288,384]{1,0:T(8,128)(2,1)} %get-tuple-element.324), channel_id=1, source_target_pairs={{0,1},{1,2},{2,3},{3,0},{4,5},{5,6},{6,7},{7,4},{8,9},{9,10},{10,1... | collective-permute-start | bytes 663560 | tf_op jit(solution)/shard_map/ppermute | solution.py:548
  14.6 33.5 %collective-permute-start.6 = (bf16[288,384]{1,0:T(8,128)(2,1)}, bf16[288,384]{1,0:T(8,128)(2,1)}, u32[]{:S(2)}, u32[]{:S(2)}) collective-permute-start(bf16[288,384]{1,0:T(8,128)(2,1)} %get-tuple-element.324), channel_id=1, source_target_pairs={{0,2},{1,3},{2,0},{3,1},{4,6},{5,7},{6,4},{7,5},{8,10},{9,11},{10,... | collective-permute-start | bytes 663560 | tf_op jit(solution)/shard_map/ppermute | solution.py:548
  15.6 33.4 %collective-permute-start.7 = (bf16[288,384]{1,0:T(8,128)(2,1)}, bf16[288,384]{1,0:T(8,128)(2,1)}, u32[]{:S(2)}, u32[]{:S(2)}) collective-permute-start(bf16[288,384]{1,0:T(8,128)(2,1)} %get-tuple-element.324), channel_id=1, source_target_pairs={{0,3},{1,0},{2,1},{3,2},{4,7},{5,4},{6,5},{7,6},{8,11},{9,8},{10,9... | collective-permute-start | bytes 663560 | tf_op jit(solution)/shard_map/ppermute | solution.py:548
  20.5 66.9 %all-gather.12.cloned.1.call-start = ((), (), s32[]{:S(2)}) async-start(), calls=%async_computation.18 | async-start | bytes 1310720 | tf_op jit(solution)/shard_map/all_gather | solution.py:1572
  59.5 34.2 %collective-permute-start.10 = (bf16[384,640]{1,0:T(8,128)(2,1)}, bf16[384,640]{1,0:T(8,128)(2,1)}, u32[]{:S(2)}, u32[]{:S(2)}) collective-permute-start(bf16[384,640]{1,0:T(8,128)(2,1)} %get-tuple-element.325.refs_1_), channel_id=1, source_target_pairs={{0,8},{4,12},{8,0},{12,4},{16,24},{20,28},{24,16},{28,20},{1,9},{5... | collective-permute-start | bytes 1474568 | tf_op jit(solution)/shard_map/ppermute | solution.py:543
  102.0 65.9 %all-gather.14.cloned.1.call-start = ((), (), s32[]{:S(2)}) async-start(), calls=%async_computation.19 | async-start | bytes 3932160 | tf_op jit(solution)/shard_map/all_gather | solution.py:1625
  105.7 167.3 %all-gather.16.cloned.1.call-start = ((), (), s32[]{:S(2)}) async-start(), calls=%async_computation.20 | async-start | bytes 7864320 | tf_op jit(solution)/shard_map/all_gather | solution.py:1684
  325.6 101.4 %reduce-scatter.5.cloned.1.call-start = ((), (), s32[]{:S(2)}) async-start(), calls=%async_computation.14 | async-start | bytes 6553600 | tf_op jit(solution)/shard_map/reduce_scatter | solution.py:1789
  393.3 145.1 %reduce-scatter.7.cloned.1.call-start = ((), (), s32[]{:S(2)}) async-start(), calls=%async_computation.15 | async-start | bytes 5242880 | tf_op jit(solution)/shard_map/reduce_scatter | solution.py:1804
  427.0 161.3 %reduce-scatter.11.cloned.1.call-start = ((), (), s32[]{:S(2)}) async-start(), calls=%async_computation.17 | async-start | bytes 983040 | tf_op jit(solution)/shard_map/reduce_scatter | solution.py:1811
  463.5 124.8 %reduce-scatter.9.cloned.1.call-start = ((), (), s32[]{:S(2)}) async-start(), calls=%async_computation.16 | async-start | bytes 1310720 | tf_op jit(solution)/shard_map/reduce_scatter | solution.py:1838
  478.3 55.4 %collective-permute-start.41 = (bf16[2,512,1152]{2,1,0:T(8,128)(2,1)}, bf16[2,512,1152]{2,1,0:T(8,128)(2,1)}, u32[]{:S(2)}, u32[]{:S(2)}) collective-permute-start(bf16[2,512,1152]{2,1,0:T(8,128)(2,1)} %get-tuple-element.187), channel_id=1, source_target_pairs={{0,8},{4,12},{8,0},{12,4},{16,24},{20,28},{24,16},{28,20},{1,9},{5... | collective-permute-start | bytes 7077896 | tf_op jit(solution)/shard_map/ppermute | solution.py:543
  479.5 54.8 %collective-permute-start.42 = (bf16[2,512,1152]{2,1,0:T(8,128)(2,1)}, bf16[2,512,1152]{2,1,0:T(8,128)(2,1)}, u32[]{:S(2)}, u32[]{:S(2)}) collective-permute-start(bf16[2,512,1152]{2,1,0:T(8,128)(2,1)} %get-tuple-element.188), channel_id=1, source_target_pairs={{0,16},{4,20},{8,24},{12,28},{16,0},{20,4},{24,8},{28,12},{1,17},{... | collective-permute-start | bytes 7077896 | tf_op jit(solution)/shard_map/ppermute | solution.py:543
  481.8 52.5 %collective-permute-start.43 = (bf16[256,640]{1,0:T(8,128)(2,1)}, bf16[256,640]{1,0:T(8,128)(2,1)S(1)}, u32[]{:S(2)}, u32[]{:S(2)}) collective-permute-start(bf16[256,640]{1,0:T(8,128)(2,1)} %get-tuple-element.265), channel_id=1, source_target_pairs={{0,3},{1,0},{2,1},{3,2},{4,7},{5,4},{6,5},{7,6},{8,11},{9,8},{10,9... | collective-permute-start | bytes 983048 | tf_op jit(solution)/shard_map/ppermute | solution.py:548
  482.0 52.3 %collective-permute-start.44 = (bf16[256,640]{1,0:T(8,128)(2,1)}, bf16[256,640]{1,0:T(8,128)(2,1)}, u32[]{:S(2)}, u32[]{:S(2)}) collective-permute-start(bf16[256,640]{1,0:T(8,128)(2,1)} %get-tuple-element.264), channel_id=1, source_target_pairs={{0,2},{1,3},{2,0},{3,1},{4,6},{5,7},{6,4},{7,5},{8,10},{9,11},{10,... | collective-permute-start | bytes 983048 | tf_op jit(solution)/shard_map/ppermute | solution.py:548
  484.2 50.1 %collective-permute-start.45 = (bf16[256,640]{1,0:T(8,128)(2,1)}, bf16[256,640]{1,0:T(8,128)(2,1)}, u32[]{:S(2)}, u32[]{:S(2)}) collective-permute-start(bf16[256,640]{1,0:T(8,128)(2,1)} %get-tuple-element.263), channel_id=1, source_target_pairs={{0,1},{1,2},{2,3},{3,0},{4,5},{5,6},{6,7},{7,4},{8,9},{9,10},{10,1... | collective-permute-start | bytes 983048 | tf_op jit(solution)/shard_map/ppermute | solution.py:548
  537.9 43.8 %collective-permute-start.47 = (bf16[512,1152]{1,0:T(8,128)(2,1)}, bf16[512,1152]{1,0:T(8,128)(2,1)}, u32[]{:S(2)}, u32[]{:S(2)}) collective-permute-start(bf16[512,1152]{1,0:T(8,128)(2,1)} %fusion.16), channel_id=1, source_target_pairs={{0,8},{4,12},{8,0},{12,4},{16,24},{20,28},{24,16},{28,20},{1,9},{5... | collective-permute-start | bytes 3538952 | tf_op jit(solution)/shard_map/ppermute | solution.py:543
  542.2 39.6 %collective-permute-start.46 = (bf16[512,1152]{1,0:T(8,128)(2,1)}, bf16[512,1152]{1,0:T(8,128)(2,1)S(1)}, u32[]{:S(2)}, u32[]{:S(2)}) collective-permute-start(bf16[512,1152]{1,0:T(8,128)(2,1)} %fusion.15), channel_id=1, source_target_pairs={{0,16},{4,20},{8,24},{12,28},{16,0},{20,4},{24,8},{28,12},{1,17},{... | collective-permute-start | bytes 3538952 | tf_op jit(solution)/shard_map/ppermute | solution.py:543
  551.7 121.4 %all-gather.18.cloned.1.call-start = ((), (), s32[]{:S(2)}) async-start(), calls=%async_computation.21 | async-start | bytes 7077888 | tf_op jit(solution)/shard_map/all_gather | solution.py:1840
  592.2 36.6 %all-to-all-start.7 = ((bf16[4,256,1024]{2,1,0:T(8,128)(2,1)}), bf16[4,256,1024]{2,1,0:T(8,128)(2,1)S(1)}, u32[]{:S(2)}, u32[]{:S(2)}) async-start(bf16[4,256,1024]{2,1,0:T(8,128)(2,1)} %gate.33), calls=%async_computation.8 | async-start | bytes 4194304 | tf_op jit(solution)/shard_map/all_to_all | solution.py:1471
  595.8 35.5 %collective-permute-start.51 = (bf16[256,1152]{1,0:T(8,128)(2,1)}, bf16[256,1152]{1,0:T(8,128)(2,1)}, u32[]{:S(2)}, u32[]{:S(2)}) collective-permute-start(bf16[256,1152]{1,0:T(8,128)(2,1)} %get-tuple-element.202), channel_id=1, source_target_pairs={{0,3},{1,0},{2,1},{3,2},{4,7},{5,4},{6,5},{7,6},{8,11},{9,8},{10,9... | collective-permute-start | bytes 1769480 | tf_op jit(solution)/shard_map/ppermute | solution.py:548
  598.9 38.4 %collective-permute-start.52 = (bf16[256,1152]{1,0:T(8,128)(2,1)}, bf16[256,1152]{1,0:T(8,128)(2,1)}, u32[]{:S(2)}, u32[]{:S(2)}) collective-permute-start(bf16[256,1152]{1,0:T(8,128)(2,1)} %get-tuple-element.203), channel_id=1, source_target_pairs={{0,2},{1,3},{2,0},{3,1},{4,6},{5,7},{6,4},{7,5},{8,10},{9,11},{10,... | collective-permute-start | bytes 1769480 | tf_op jit(solution)/shard_map/ppermute | solution.py:548
  599.1 50.8 %collective-permute-start.53 = (bf16[256,1152]{1,0:T(8,128)(2,1)}, bf16[256,1152]{1,0:T(8,128)(2,1)}, u32[]{:S(2)}, u32[]{:S(2)}) collective-permute-start(bf16[256,1152]{1,0:T(8,128)(2,1)} %get-tuple-element.204), channel_id=1, source_target_pairs={{0,1},{1,2},{2,3},{3,0},{4,5},{5,6},{6,7},{7,4},{8,9},{9,10},{10,1... | collective-permute-start | bytes 1769480 | tf_op jit(solution)/shard_map/ppermute | solution.py:548
  (145 other events, 1624.5 us)
Sparse Core Ops, SparseCore 0:
  20.6 34.9 all-gather.9
  57.8 29.6 all-gather.11
  105.8 59.0 all-gather.13
  171.5 93.8 all-gather.15
  339.8 74.2 reduce-scatter.4
  427.1 59.2 reduce-scatter.6
  488.8 36.9 reduce-scatter.10
  538.6 38.3 reduce-scatter.8
  592.3 63.7 all-gather.17

commit v6 on v5

--- a/solution.py
+++ b/solution.py
@@ -1836,20 +1836,19 @@
         came = [turn(sent[r - 1], planes - r) for r in range(1, planes)]
         (plane_second,) = gate([plane_second], grad_mixed)
         sum_second = lax.psum_scatter(plane_second, "wsh", scatter_dimension=0, tiled=True)
-        sum_first, sum_second, sum_joint = gate([sum_first, sum_second, sum_joint], own_total)
+        sum_first, sum_second, sum_joint = gate([sum_first, sum_second, sum_joint], own_total, tokens_sent)
         everything = lax.all_gather(
             jnp.concatenate([sum_first[:, :piece], sum_second, sum_first[:, piece:], sum_joint], axis=1),
             "ctx",
             axis=0,
         )
         gradient = grad_first + collect_tokens(tokens_sent, (own_total,), ())
-        came = gate(came, gradient)
+        (small_spread,) = gate([small_spread], gradient)
+        small_mine = jnp.sum(exchange(small_spread), axis=0).reshape(LAYERS, 16, shard)
+        came = gate(came, small_mine)
         left_total, right_total = final_sum((own_total, *came), (joint_rows[0], *came_joint))
         (everything,) = gate([everything], left_total)
         *placed, placed_token = place_pieces(everything, relative, 1, None)
-        (small_spread,) = gate([small_spread], left_total)
-        small_mine = jnp.sum(exchange(small_spread), axis=0).reshape(LAYERS, 16, shard)
-
     near, far = plane_pieces(left_total, right_total, placed_token, small_mine)
     near_first = here ^ (2 * four)
     *placed, placed_token = place_pieces(near, near_first, 0, placed)

time: 737 us -> 734 us (level)
    ppermute x12, waiting for transfers between devices: 34.4 us -> 21.8 us  [turn(): lax.ppermute(block, 'wsh', [(i, (i + distance) % count) for i in range(co...]
    ppermute x47, waiting for transfers between devices: 76.2 us -> 86.4 us  [swap(): return lax.ppermute(block, 'ctx', [(i, i ^ mask) for i in devices])]
    unnamed x204 -> x202, local copies, waits for them, and re-layouts: 25.5 us -> 24.7 us
  transfers between devices with their start and end apart: 76 -> 76, of which waited for: 30 -> 30; matrix products, arithmetic and copies ran while one was open for 16% -> 17% of each run, Pallas kernels for 31% -> 31%
where the time goes in v6:
time: 734 us; the launch traced here: 721 us
  Pallas kernels  257 us (35%)
  waiting for transfers between devices  180 us (25%)
  starting transfers between devices  94.1 us (13%)
  other arithmetic  75.8 us (10%)
  local copies, waits for them, and re-layouts  60.5 us (8%)
  matrix products  22.1 us (3%)
  between operations  20.6 us (3%)
  blocking collectives  11.4 us (2%)
    ppermute x47, waiting for transfers between devices, swap(): return lax.ppermute(block, 'ctx', [(i, i ^ mask) for i in devices])  86.4 us
    pallas_call x2, Pallas kernels, attention_backward(): pl.pallas_call(attention_backward_kernel, grid_spec=pltpu.PrefetchScalarG...  59.1 us
    all_to_all x2, waiting for transfers between devices, collect_tokens(): lax.all_to_all(sent, 'ctx', 0, 0, axis_index_groups=plane_groups(), tiled...  50.5 us
    ppermute x47, starting transfers between devices, swap(): return lax.ppermute(block, 'ctx', [(i, i ^ mask) for i in devices])  45.4 us
    pallas_call x2, Pallas kernels, feed_forward(): pl.pallas_call(functools.partial(feed_forward_kernel, count), grid=(4,),...  31.2 us
    pallas_call x2, Pallas kernels, attention_forward(): pl.pallas_call(attention_forward_kernel, grid_spec=pltpu.PrefetchScalarGr...  30.6 us
    pallas_call x2, Pallas kernels, weight_gradients(): pl.pallas_call(functools.partial(weight_gradient_kernel, split), grid_spe...  26.3 us
    unnamed x202, local copies, waits for them, and re-layouts  24.7 us
  transfers between devices with their start and end apart: 76, of which 30 were waited for; matrix products, arithmetic and copies ran while one was open for 17% of the time, Pallas kernels for 31%

profile of v6, /device:TPU:9, one launch (start us, length us, event | category | flops | bytes accessed | tf_op | source)
XLA Modules:
  0.0 721.0 jit_solution(7717345506762785351)
XLA Ops:
  28.5 7.1 collective-permute-done.3
  67.2 15.3 %attention_forward.2 = (bf16[8,256,128]{2,1,0:T(8,128)(2,1)}, f32[2,2048]{1,0:T(2,128)}) custom-call(s32[8]{0:T(128)} %get-tuple-element.382.order_ref, bf16[2048,384]{1,0:T(8,128)(2,1)} %get-tuple-element.130.query_ref.key_ref.value_ref, bf16[2048,384]{1,0:T(8,128)(2,1)} %get-tuple-element.130.query_ref.key_ref.value_ref, ...), custom_call_target="tpu_custom_call" | custom-call | flops 19549999104 | bytes 61200000 | tf_op jit(solution)/shard_map/attention_forward/pallas_call | solution.py:608
  109.1 8.3 %own_blocks.1 = (bf16[2,4,256,512]{3,2,1,0:T(8,128)(2,1)}, bf16[2,4,256,512]{3,2,1,0:T(8,128)(2,1)}, bf16[2,256,1024]{2,1,0:T(8,128)(2,1)}) custom-call(s32[8]{0:T(128)} %pad_add_fusion.1.inner_order_ref, s32[16]{0:T(128)} %pad_add_fusion.2.out_order_ref, f32[2,256,4096]{2,1,0:T(8,128)} %refs_3_.3, f32[2,256,4096]{2,1,0:T(8,128)} %refs_3_.3, ...), custom_call_target="tpu_custom_call" | custom-call | flops 8049999872 | bytes 25200000 | tf_op jit(solution)/shard_map/own_blocks/pallas_call | solution.py:802
  136.4 8.3 %collective-permute-done.20.refs_14_ = bf16[384,512]{1,0:T(8,128)(2,1)S(1)} collective-permute-done((bf16[384,512]{1,0:T(8,128)(2,1)}, bf16[384,512]{1,0:T(8,128)(2,1)S(1)}, u32[]{:S(2)}, u32[]{:S(2)}) %collective-permute-start.20) | collective-permute-done | bytes 393248 | tf_op jit(solution)/shard_map/ppermute | solution.py:543
  145.6 16.5 %feed_forward.2 = (f32[256,1024]{1,0:T(8,128)}, bf16[256,1024]{1,0:T(8,128)(2,1)}, bf16[512,2048]{1,0:T(8,128)(2,1)}, bf16[512,2048]{1,0:T(8,128)(2,1)}) custom-call(bf16[512,1024]{1,0:T(8,128)(2,1)} %copy-done.51, f32[1,2048]{1,0:T(1,128)} %maximum_convert_fusion.bias_ref, bf16[2,4,256,512]{3,2,1,0:T(8,128)(2,1)} %get-tuple-element.137.own_inner, ...), custom_call_target="tpu_custom_call" | custom-call | flops 18400000000 | bytes 57600000 | tf_op jit(solution)/shard_map/feed_forward/pallas_call | solution.py:969
  175.0 6.1 collective-permute-done.25
  182.8 23.2 %collective-permute-done.26 = bf16[2,256,512]{2,1,0:T(8,128)(2,1)S(1)} collective-permute-done((bf16[2,256,512]{2,1,0:T(8,128)(2,1)S(1)}, bf16[2,256,512]{2,1,0:T(8,128)(2,1)S(1)}, u32[]{:S(2)}, u32[]{:S(2)}) %collective-permute-start.26) | collective-permute-done | bytes 524320 | tf_op jit(solution)/shard_map/ppermute | solution.py:543
  223.4 15.3 %attention_forward.3 = (bf16[8,256,128]{2,1,0:T(8,128)(2,1)}, f32[2,2048]{1,0:T(2,128)}) custom-call(s32[8]{0:T(128)} %get-tuple-element.382.order_ref, bf16[2048,384]{1,0:T(8,128)(2,1)} %add_convert_fusion.2.query_ref.key_ref.value_ref, bf16[2048,384]{1,0:T(8,128)(2,1)} %add_convert_fusion.2.query_ref.key_ref.value_ref, ...), custom_call_target="tpu_custom_call" | custom-call | flops 19549999104 | bytes 61200000 | tf_op jit(solution)/shard_map/attention_forward/pallas_call | solution.py:608
  248.2 9.5 %all-to-all-done.1.heads_ref = bf16[8,256,128]{2,1,0:T(8,128)(2,1)S(1)} async-done(((bf16[8,256,128]{2,1,0:T(8,128)(2,1)}), bf16[8,256,128]{2,1,0:T(8,128)(2,1)S(1)}, u32[]{:S(2)}, u32[]{:S(2)}) %all-to-all-start.1) | async-done | bytes 524320 | tf_op jit(solution)/shard_map/all_to_all | solution.py:1488
  273.9 14.6 %feed_forward.3 = (f32[256,1024]{1,0:T(8,128)}, bf16[256,1024]{1,0:T(8,128)(2,1)}, bf16[512,2048]{1,0:T(8,128)(2,1)}, bf16[512,2048]{1,0:T(8,128)(2,1)}) custom-call(bf16[512,1024]{1,0:T(8,128)(2,1)} %copy-done.52, f32[1,2048]{1,0:T(1,128)} %maximum_convert_fusion.1.bias_ref, bf16[2,4,256,512]{3,2,1,0:T(8,128)(2,1)} %get-tuple-element.137.own_inner, ...), custom_call_target="tpu_custom_call" | custom-call | flops 18400000000 | bytes 57600000 | tf_op jit(solution)/shard_map/feed_forward/pallas_call | solution.py:969
  299.8 10.2 %feed_backward.2 = (f32[256,1024]{1,0:T(8,128)}, bf16[256,1024]{1,0:T(8,128)(2,1)}, bf16[512,2048]{1,0:T(8,128)(2,1)}, f32[1,2048]{1,0:T(1,128)}) custom-call(bf16[512,1024]{1,0:T(8,128)(2,1)} %pad_maximum_fusion.12.grad_ref, bf16[512,2048]{1,0:T(8,128)(2,1)} %get-tuple-element.149.slope_ref, bf16[2,4,256,512]{3,2,1,0:T(8,128)(2,1)} %get-tuple-element.137.own_inner, ...), custom_call_target="tpu_custom_call" | custom-call | flops 12650000384 | bytes 39600000 | tf_op jit(solution)/shard_map/feed_backward/pallas_call | solution.py:1013
  326.3 12.4 %weight_gradients.2 = (bf16[4,1024,640]{2,1,0:T(8,128)(2,1)}, bf16[4,1024,512]{2,1,0:T(8,128)(2,1)}) custom-call(s32[4]{0:T(128)} %pad_add_fusion.3.rows_ref, bf16[512,1024]{1,0:T(8,128)(2,1)} %copy-done.52, bf16[512,1024]{1,0:T(8,128)(2,1)} %pad_maximum_fusion.12.grad_ref, bf16[512,1024]{1,0:T(8,128)(2,1)} %pad_maximum_fusion.13.mixed_ref, ...), custom_call_target="tpu_custom_call" | custom-call | flops 14949999616 | bytes 46800000 | tf_op jit(solution)/shard_map/weight_gradients/pallas_call | solution.py:1106
  340.0 29.6 %attention_backward.2 = (bf16[2048,128]{1,0:T(8,128)(2,1)}, bf16[2048,128]{1,0:T(8,128)(2,1)}, bf16[2048,128]{1,0:T(8,128)(2,1)}) custom-call(s32[8]{0:T(128)} %get-tuple-element.382.order_ref, bf16[2048,384]{1,0:T(8,128)(2,1)} %add_convert_fusion.2.query_ref.key_ref.value_ref, bf16[2048,384]{1,0:T(8,128)(2,1)} %add_convert_fusion.2.query_ref.key_ref.value_ref, ...), custom_call_target="tpu_custom_call" | custom-call | flops 33350000640 | bytes 104400000 | tf_op jit(solution)/shard_map/attention_backward/pallas_call | solution.py:696
  369.7 9.9 %token_gradients.2 = (f32[4,256,1024]{2,1,0:T(8,128)}, bf16[4,256,1024]{2,1,0:T(8,128)(2,1)}, bf16[2048,384]{1,0:T(8,128)(2,1)}, f32[1,384]{1,0:T(1,128)}) custom-call(s32[4]{0:T(128)} %iota_xor_fusion.place_ref, bf16[2048,128]{1,0:T(8,128)(2,1)} %get-tuple-element.163.query_ref, bf16[2048,128]{1,0:T(8,128)(2,1)} %get-tuple-element.164.key_ref, ...), custom_call_target="tpu_custom_call" | custom-call | flops 11500000256 | bytes 36000000 | tf_op jit(solution)/shard_map/token_gradients/pallas_call | solution.py:1319
  399.2 22.0 %all-to-all-done.4.refs_0_ = bf16[4,256,1024]{2,1,0:T(8,128)(2,1)S(1)} async-done(((bf16[4,256,1024]{2,1,0:T(8,128)(2,1)}), bf16[4,256,1024]{2,1,0:T(8,128)(2,1)S(1)}, u32[]{:S(2)}, u32[]{:S(2)}) %all-to-all-start.4) | async-done | bytes 2097184 | tf_op jit(solution)/shard_map/all_to_all | solution.py:1471
  433.7 12.2 %feed_backward.3 = (f32[256,1024]{1,0:T(8,128)}, bf16[256,1024]{1,0:T(8,128)(2,1)}, bf16[512,2048]{1,0:T(8,128)(2,1)}, f32[1,2048]{1,0:T(1,128)}) custom-call(bf16[512,1024]{1,0:T(8,128)(2,1)} %pad_maximum_fusion.14.grad_ref, bf16[512,2048]{1,0:T(8,128)(2,1)} %get-tuple-element.169.slope_ref, bf16[2,4,256,512]{3,2,1,0:T(8,128)(2,1)} %get-tuple-element.137.own_inner, ...), custom_call_target="tpu_custom_call" | custom-call | flops 12650000384 | bytes 39600000 | tf_op jit(solution)/shard_map/feed_backward/pallas_call | solution.py:1013
  464.2 13.9 %weight_gradients.3 = (bf16[2,512,1152]{2,1,0:T(8,128)(2,1)}, bf16[2,512,1152]{2,1,0:T(8,128)(2,1)}, bf16[2,512,1152]{2,1,0:T(8,128)(2,1)}, bf16[2,512,1152]{2,1,0:T(8,128)(2,1)}) custom-call(s32[4]{0:T(128)} %pad_add_fusion.3.rows_ref, bf16[512,1024]{1,0:T(8,128)(2,1)} %copy-done.51, bf16[512,1024]{1,0:T(8,128)(2,1)} %pad_maximum_fusion.14.grad_ref, ...), custom_call_target="tpu_custom_call" | custom-call | flops 14949999616 | bytes 46800000 | tf_op jit(solution)/shard_map/weight_gradients/pallas_call | solution.py:1106
  487.0 29.5 %attention_backward.3 = (bf16[2048,128]{1,0:T(8,128)(2,1)}, bf16[2048,128]{1,0:T(8,128)(2,1)}, bf16[2048,128]{1,0:T(8,128)(2,1)}) custom-call(s32[8]{0:T(128)} %get-tuple-element.382.order_ref, bf16[2048,384]{1,0:T(8,128)(2,1)} %get-tuple-element.130.query_ref.key_ref.value_ref, bf16[2048,384]{1,0:T(8,128)(2,1)} %get-tuple-element.130.query_ref.key_ref.value_ref, ...), custom_call_target="tpu_custom_call" | custom-call | flops 33350000640 | bytes 104400000 | tf_op jit(solution)/shard_map/attention_backward/pallas_call | solution.py:696
  516.5 9.9 %token_gradients.3 = (f32[4,256,1024]{2,1,0:T(8,128)}, bf16[4,256,1024]{2,1,0:T(8,128)(2,1)}, bf16[2048,384]{1,0:T(8,128)(2,1)}, f32[1,384]{1,0:T(1,128)}) custom-call(s32[4]{0:T(128)} %iota_xor_fusion.place_ref, bf16[2048,128]{1,0:T(8,128)(2,1)} %get-tuple-element.182.query_ref, bf16[2048,128]{1,0:T(8,128)(2,1)} %get-tuple-element.183.key_ref, ...), custom_call_target="tpu_custom_call" | custom-call | flops 11500000256 | bytes 36000000 | tf_op jit(solution)/shard_map/token_gradients/pallas_call | solution.py:1319
  566.8 6.5 collective-permute-done.48.refs_4_.refs_5_
  600.0 28.6 %all-to-all-done.7 = bf16[4,256,1024]{2,1,0:T(8,128)(2,1)S(1)} async-done(((bf16[4,256,1024]{2,1,0:T(8,128)(2,1)}), bf16[4,256,1024]{2,1,0:T(8,128)(2,1)S(1)}, u32[]{:S(2)}, u32[]{:S(2)}) %all-to-all-start.7) | async-done | bytes 2097184 | tf_op jit(solution)/shard_map/all_to_all | solution.py:1471
  631.9 11.4 %all_to_all.45 = f32[8,32,256]{2,1,0:T(8,128)S(1)} all-to-all(f32[8,32,256]{2,1,0:T(8,128)} %gate.34), channel_id=1, replica_groups=mesh['ctx'=8,'wsh'=4] {'ctx'}, dimensions={0} | all-to-all | bytes 524288 | tf_op jit(solution)/shard_map/all_to_all | solution.py:1488
  655.5 9.3 %collective-permute-done.56 = bf16[256,768]{1,0:T(8,128)(2,1)S(1)} collective-permute-done((bf16[256,768]{1,0:T(8,128)(2,1)}, bf16[256,768]{1,0:T(8,128)(2,1)S(1)}, u32[]{:S(2)}, u32[]{:S(2)}) %collective-permute-start.56) | collective-permute-done | bytes 393248 | tf_op jit(solution)/shard_map/ppermute | solution.py:543
  670.7 9.7 %place_pieces.3 = (f32[2,256,1024]{2,1,0:T(8,128)}, f32[2,256,1024]{2,1,0:T(8,128)}, f32[2,256,1024]{2,1,0:T(8,128)}, f32[2,256,1024]{2,1,0:T(8,128)}, f32[2,256...) custom-call(s32[8]{0:T(128)} %iota.27.order_ref, bf16[8,256,1536]{2,1,0:T(8,128)(2,1)} %gate.39.source), custom_call_target="tpu_custom_call" | custom-call | flops 11500000256 | bytes 36000000 | tf_op jit(solution)/shard_map/place_pieces/pallas_call | solution.py:856
  (549 shorter events, 361.1 us)
Async XLA Ops:
  7.2 48.4 %all-gather.10.cloned.1.call-start = ((), (), s32[]{:S(2)}) async-start(), calls=%async_computation.13 | async-start | bytes 1638400 | tf_op jit(solution)/shard_map/all_gather | solution.py:1569
  13.3 34.7 %collective-permute-start.5 = (bf16[288,384]{1,0:T(8,128)(2,1)}, bf16[288,384]{1,0:T(8,128)(2,1)}, u32[]{:S(2)}, u32[]{:S(2)}) collective-permute-start(bf16[288,384]{1,0:T(8,128)(2,1)} %get-tuple-element.324), channel_id=1, source_target_pairs={{0,1},{1,2},{2,3},{3,0},{4,5},{5,6},{6,7},{7,4},{8,9},{9,10},{10,1... | collective-permute-start | bytes 663560 | tf_op jit(solution)/shard_map/ppermute | solution.py:548
  14.6 33.4 %collective-permute-start.6 = (bf16[288,384]{1,0:T(8,128)(2,1)}, bf16[288,384]{1,0:T(8,128)(2,1)}, u32[]{:S(2)}, u32[]{:S(2)}) collective-permute-start(bf16[288,384]{1,0:T(8,128)(2,1)} %get-tuple-element.324), channel_id=1, source_target_pairs={{0,2},{1,3},{2,0},{3,1},{4,6},{5,7},{6,4},{7,5},{8,10},{9,11},{10,... | collective-permute-start | bytes 663560 | tf_op jit(solution)/shard_map/ppermute | solution.py:548
  15.6 33.4 %collective-permute-start.7 = (bf16[288,384]{1,0:T(8,128)(2,1)}, bf16[288,384]{1,0:T(8,128)(2,1)}, u32[]{:S(2)}, u32[]{:S(2)}) collective-permute-start(bf16[288,384]{1,0:T(8,128)(2,1)} %get-tuple-element.324), channel_id=1, source_target_pairs={{0,3},{1,0},{2,1},{3,2},{4,7},{5,4},{6,5},{7,6},{8,11},{9,8},{10,9... | collective-permute-start | bytes 663560 | tf_op jit(solution)/shard_map/ppermute | solution.py:548
  20.5 66.9 %all-gather.12.cloned.1.call-start = ((), (), s32[]{:S(2)}) async-start(), calls=%async_computation.18 | async-start | bytes 1310720 | tf_op jit(solution)/shard_map/all_gather | solution.py:1572
  59.5 34.1 %collective-permute-start.10 = (bf16[384,640]{1,0:T(8,128)(2,1)}, bf16[384,640]{1,0:T(8,128)(2,1)}, u32[]{:S(2)}, u32[]{:S(2)}) collective-permute-start(bf16[384,640]{1,0:T(8,128)(2,1)} %get-tuple-element.325.refs_1_), channel_id=1, source_target_pairs={{0,8},{4,12},{8,0},{12,4},{16,24},{20,28},{24,16},{28,20},{1,9},{5... | collective-permute-start | bytes 1474568 | tf_op jit(solution)/shard_map/ppermute | solution.py:543
  102.0 65.9 %all-gather.14.cloned.1.call-start = ((), (), s32[]{:S(2)}) async-start(), calls=%async_computation.19 | async-start | bytes 3932160 | tf_op jit(solution)/shard_map/all_gather | solution.py:1625
  105.7 167.3 %all-gather.16.cloned.1.call-start = ((), (), s32[]{:S(2)}) async-start(), calls=%async_computation.20 | async-start | bytes 7864320 | tf_op jit(solution)/shard_map/all_gather | solution.py:1684
  325.5 101.4 %reduce-scatter.5.cloned.1.call-start = ((), (), s32[]{:S(2)}) async-start(), calls=%async_computation.14 | async-start | bytes 6553600 | tf_op jit(solution)/shard_map/reduce_scatter | solution.py:1789
  393.2 145.1 %reduce-scatter.7.cloned.1.call-start = ((), (), s32[]{:S(2)}) async-start(), calls=%async_computation.15 | async-start | bytes 5242880 | tf_op jit(solution)/shard_map/reduce_scatter | solution.py:1804
  426.9 161.3 %reduce-scatter.11.cloned.1.call-start = ((), (), s32[]{:S(2)}) async-start(), calls=%async_computation.17 | async-start | bytes 983040 | tf_op jit(solution)/shard_map/reduce_scatter | solution.py:1811
  463.4 124.8 %reduce-scatter.9.cloned.1.call-start = ((), (), s32[]{:S(2)}) async-start(), calls=%async_computation.16 | async-start | bytes 1310720 | tf_op jit(solution)/shard_map/reduce_scatter | solution.py:1838
  478.2 55.4 %collective-permute-start.41 = (bf16[2,512,1152]{2,1,0:T(8,128)(2,1)}, bf16[2,512,1152]{2,1,0:T(8,128)(2,1)}, u32[]{:S(2)}, u32[]{:S(2)}) collective-permute-start(bf16[2,512,1152]{2,1,0:T(8,128)(2,1)} %get-tuple-element.187), channel_id=1, source_target_pairs={{0,8},{4,12},{8,0},{12,4},{16,24},{20,28},{24,16},{28,20},{1,9},{5... | collective-permute-start | bytes 7077896 | tf_op jit(solution)/shard_map/ppermute | solution.py:543
  479.4 54.8 %collective-permute-start.42 = (bf16[2,512,1152]{2,1,0:T(8,128)(2,1)}, bf16[2,512,1152]{2,1,0:T(8,128)(2,1)}, u32[]{:S(2)}, u32[]{:S(2)}) collective-permute-start(bf16[2,512,1152]{2,1,0:T(8,128)(2,1)} %get-tuple-element.188), channel_id=1, source_target_pairs={{0,16},{4,20},{8,24},{12,28},{16,0},{20,4},{24,8},{28,12},{1,17},{... | collective-permute-start | bytes 7077896 | tf_op jit(solution)/shard_map/ppermute | solution.py:543
  481.7 52.5 %collective-permute-start.43 = (bf16[256,640]{1,0:T(8,128)(2,1)}, bf16[256,640]{1,0:T(8,128)(2,1)S(1)}, u32[]{:S(2)}, u32[]{:S(2)}) collective-permute-start(bf16[256,640]{1,0:T(8,128)(2,1)} %get-tuple-element.265), channel_id=1, source_target_pairs={{0,3},{1,0},{2,1},{3,2},{4,7},{5,4},{6,5},{7,6},{8,11},{9,8},{10,9... | collective-permute-start | bytes 983048 | tf_op jit(solution)/shard_map/ppermute | solution.py:548
  481.9 52.3 %collective-permute-start.44 = (bf16[256,640]{1,0:T(8,128)(2,1)}, bf16[256,640]{1,0:T(8,128)(2,1)}, u32[]{:S(2)}, u32[]{:S(2)}) collective-permute-start(bf16[256,640]{1,0:T(8,128)(2,1)} %get-tuple-element.264), channel_id=1, source_target_pairs={{0,2},{1,3},{2,0},{3,1},{4,6},{5,7},{6,4},{7,5},{8,10},{9,11},{10,... | collective-permute-start | bytes 983048 | tf_op jit(solution)/shard_map/ppermute | solution.py:548
  484.1 50.1 %collective-permute-start.45 = (bf16[256,640]{1,0:T(8,128)(2,1)}, bf16[256,640]{1,0:T(8,128)(2,1)}, u32[]{:S(2)}, u32[]{:S(2)}) collective-permute-start(bf16[256,640]{1,0:T(8,128)(2,1)} %get-tuple-element.263), channel_id=1, source_target_pairs={{0,1},{1,2},{2,3},{3,0},{4,5},{5,6},{6,7},{7,4},{8,9},{9,10},{10,1... | collective-permute-start | bytes 983048 | tf_op jit(solution)/shard_map/ppermute | solution.py:548
  537.8 43.8 %collective-permute-start.47 = (bf16[512,1152]{1,0:T(8,128)(2,1)}, bf16[512,1152]{1,0:T(8,128)(2,1)}, u32[]{:S(2)}, u32[]{:S(2)}) collective-permute-start(bf16[512,1152]{1,0:T(8,128)(2,1)} %fusion.16), channel_id=1, source_target_pairs={{0,8},{4,12},{8,0},{12,4},{16,24},{20,28},{24,16},{28,20},{1,9},{5... | collective-permute-start | bytes 3538952 | tf_op jit(solution)/shard_map/ppermute | solution.py:543
  542.0 39.6 %collective-permute-start.46 = (bf16[512,1152]{1,0:T(8,128)(2,1)}, bf16[512,1152]{1,0:T(8,128)(2,1)S(1)}, u32[]{:S(2)}, u32[]{:S(2)}) collective-permute-start(bf16[512,1152]{1,0:T(8,128)(2,1)} %fusion.15), channel_id=1, source_target_pairs={{0,16},{4,20},{8,24},{12,28},{16,0},{20,4},{24,8},{28,12},{1,17},{... | collective-permute-start | bytes 3538952 | tf_op jit(solution)/shard_map/ppermute | solution.py:543
  551.5 118.6 %all-gather.18.cloned.1.call-start = ((), (), s32[]{:S(2)}) async-start(), calls=%async_computation.21 | async-start | bytes 7077888 | tf_op jit(solution)/shard_map/all_gather | solution.py:1840
  592.0 36.6 %all-to-all-start.7 = ((bf16[4,256,1024]{2,1,0:T(8,128)(2,1)}), bf16[4,256,1024]{2,1,0:T(8,128)(2,1)S(1)}, u32[]{:S(2)}, u32[]{:S(2)}) async-start(bf16[4,256,1024]{2,1,0:T(8,128)(2,1)} %gate.33), calls=%async_computation.8 | async-start | bytes 4194304 | tf_op jit(solution)/shard_map/all_to_all | solution.py:1471
  595.6 48.2 %collective-permute-start.51 = (bf16[256,1152]{1,0:T(8,128)(2,1)}, bf16[256,1152]{1,0:T(8,128)(2,1)}, u32[]{:S(2)}, u32[]{:S(2)}) collective-permute-start(bf16[256,1152]{1,0:T(8,128)(2,1)} %get-tuple-element.202), channel_id=1, source_target_pairs={{0,3},{1,0},{2,1},{3,2},{4,7},{5,4},{6,5},{7,6},{8,11},{9,8},{10,9... | collective-permute-start | bytes 1769480 | tf_op jit(solution)/shard_map/ppermute | solution.py:548
  598.8 45.1 %collective-permute-start.52 = (bf16[256,1152]{1,0:T(8,128)(2,1)}, bf16[256,1152]{1,0:T(8,128)(2,1)}, u32[]{:S(2)}, u32[]{:S(2)}) collective-permute-start(bf16[256,1152]{1,0:T(8,128)(2,1)} %get-tuple-element.203), channel_id=1, source_target_pairs={{0,2},{1,3},{2,0},{3,1},{4,6},{5,7},{6,4},{7,5},{8,10},{9,11},{10,... | collective-permute-start | bytes 1769480 | tf_op jit(solution)/shard_map/ppermute | solution.py:548
  599.0 50.8 %collective-permute-start.53 = (bf16[256,1152]{1,0:T(8,128)(2,1)}, bf16[256,1152]{1,0:T(8,128)(2,1)}, u32[]{:S(2)}, u32[]{:S(2)}) collective-permute-start(bf16[256,1152]{1,0:T(8,128)(2,1)} %get-tuple-element.204), channel_id=1, source_target_pairs={{0,1},{1,2},{2,3},{3,0},{4,5},{5,6},{6,7},{7,4},{8,9},{9,10},{10,1... | collective-permute-start | bytes 1769480 | tf_op jit(solution)/shard_map/ppermute | solution.py:548
  (144 other events, 1593.3 us)
Sparse Core Ops, SparseCore 0:
  20.6 34.9 all-gather.9
  57.8 29.6 all-gather.11
  105.8 59.0 all-gather.13
  171.4 93.8 all-gather.15
  339.6 74.2 reduce-scatter.4
  427.0 59.2 reduce-scatter.6
  488.7 37.0 reduce-scatter.10
  538.4 38.3 reduce-scatter.8
  592.1 67.3 all-gather.17

commit v7 on v6

--- a/solution.py
+++ b/solution.py
@@ -777,47 +777,62 @@
     )
 
 
-def own_blocks(inner_weight, outer_weight, out_weight, inner_order, out_order, after):
+def own_blocks(inner_weight, outer_weight, inner_order, after):
     layers, shard, hidden = inner_weight.shape
     piece = hidden // 8
 
-    def kernel(inner_order_ref, out_order_ref, *refs):
-        ins, (inner_out, outer_out, out_out) = refs[:16], refs[-3:]
+    def kernel(inner_order_ref, *refs):
+        ins, (inner_out, outer_out) = refs[:8], refs[-2:]
         for j in range(4):
             inner_out[0, j] = low(ins[j][0])
             outer_out[0, j] = low(ins[4 + j][0]).T
-        for j in range(8):
-            out_out[0, :, j * LANES : (j + 1) * LANES] = low(ins[8 + j][0])
 
     def inner_at(j):
-        return pl.BlockSpec((1, shard, piece), lambda layer, inner_ref, out_ref: (layer, 0, inner_ref[layer * 4 + j]))
+        return pl.BlockSpec((1, shard, piece), lambda layer, inner_ref: (layer, 0, inner_ref[layer * 4 + j]))
 
     def outer_at(j):
-        return pl.BlockSpec((1, piece, shard), lambda layer, inner_ref, out_ref: (layer, inner_ref[layer * 4 + j], 0))
-
-    def out_at(j):
-        return pl.BlockSpec((1, shard, LANES), lambda layer, inner_ref, out_ref: (layer, 0, out_ref[layer * 8 + j]))
+        return pl.BlockSpec((1, piece, shard), lambda layer, inner_ref: (layer, inner_ref[layer * 4 + j], 0))
 
     block = pl.BlockSpec((1, 4, shard, piece), lambda layer, *_: (layer, 0, 0, 0))
     return pl.pallas_call(
         kernel,
         grid_spec=pltpu.PrefetchScalarGridSpec(
-            num_scalar_prefetch=2,
+            num_scalar_prefetch=1,
             grid=(layers,),
             in_specs=[inner_at(j) for j in range(4)]
             + [outer_at(j) for j in range(4)]
-            + [out_at(j) for j in range(8)]
             + [pl.BlockSpec(memory_space=pl.ANY)],
-            out_specs=[block, block, pl.BlockSpec((1, shard, 8 * LANES), lambda layer, *_: (layer, 0, 0))],
+            out_specs=[block, block],
         ),
-        out_shape=[
-            jax.ShapeDtypeStruct((layers, 4, shard, piece), jnp.bfloat16),
-            jax.ShapeDtypeStruct((layers, 4, shard, piece), jnp.bfloat16),
-            jax.ShapeDtypeStruct((layers, shard, 8 * LANES), jnp.bfloat16),
-        ],
-        cost_estimate=lasting(7),
+        out_shape=[jax.ShapeDtypeStruct((layers, 4, shard, piece), jnp.bfloat16)] * 2,
+        cost_estimate=lasting(6),
         name="own_blocks",
-    )(inner_order, out_order, *[inner_weight] * 4, *[outer_weight] * 4, *[out_weight] * 8, after)
+    )(inner_order, *[inner_weight] * 4, *[outer_weight] * 4, after)
+
+
+def own_out_blocks(out_weight, out_order):
+    layers, shard, width = out_weight.shape
+
+    def kernel_layers(out_order_ref, *refs):
+        for layer in range(layers):
+            for j in range(8):
+                refs[8 * layers + layer][:, j * LANES : (j + 1) * LANES] = low(refs[8 * layer + j][0])
+
+    def at_layer(layer, j):
+        return pl.BlockSpec((1, shard, LANES), lambda i, out_ref: (layer, 0, out_ref[8 * layer + j]))
+
+    return pl.pallas_call(
+        kernel_layers,
+        grid_spec=pltpu.PrefetchScalarGridSpec(
+            num_scalar_prefetch=1,
+            grid=(1,),
+            in_specs=[at_layer(layer, j) for layer in range(layers) for j in range(8)],
+            out_specs=[pl.BlockSpec((shard, width), lambda i, out_ref: (0, 0))] * layers,
+        ),
+        out_shape=[jax.ShapeDtypeStruct((shard, width), jnp.bfloat16)] * layers,
+        cost_estimate=lasting(2),
+        name="own_out_blocks",
+    )(out_order, *[out_weight] * (8 * layers))
 
 
 def place_pieces(pieces, order, layer, previous):
@@ -1596,10 +1611,10 @@
                 ],
                 axis=1,
             )
-            weights = (inner_own, outer_own, inner_first, outer_first)
+            weights = (inner_first, outer_first)
         else:
             near = jnp.concatenate([out_parts[j] for j in range(4)], axis=1)
-            weights = (inner_own, outer_own)
+            weights = ()
         return (weights, (out_own[layer], near, swap(near, CORE)))
 
     def out_place(layer, block):
@@ -1621,18 +1636,11 @@
         joint_bias = wide(jnp.concatenate([query_bias_own, jnp.zeros_like(query_bias_own), value_bias_own]))
         packed = low(mm(everyone, joint) + joint_bias)
         if layer == 0:
-            packed, layer_own = gate([packed, layer_own], inner_near)
+            out_own = own_out_blocks(out_weight, jnp.concatenate(out_order))
+            packed, layer_own = gate([packed, layer_own], inner_near, out_own[0])
             second_stack = lax.all_gather(layer_own, "wsh", axis=0)
         mixed, log_all = attention_forward(packed, labels, block_order)
         if layer == 0:
-            inner_own, outer_own, out_own = own_blocks(
-                inner_weight,
-                outer_weight,
-                out_weight,
-                jnp.concatenate(inner_order),
-                jnp.concatenate(out_order),
-                mixed,
-            )
             left_x, right_y, outer_stack = gate([*inner_half[2:], outer_stack], mixed)
             inner_first = spread_second(*inner_half[:2], left_x, right_y)
             outer_first = spread_second(*spread_first(ordered(outer_stack, turned[1:])))
@@ -1664,9 +1672,14 @@
             first_shift_row[None],
             places,
         )
-        if layer == 1:
+        if layer == 0:
+            inner_own, outer_own = own_blocks(
+                inner_weight, outer_weight, jnp.concatenate(inner_order), hidden_turned
+            )
+        else:
             second_parts = gate([second_parts], hidden_turned)
-            weights = (*weights, second_parts, second_parts)
+            weights = (second_parts, second_parts)
+        weights = (inner_own, outer_own, *weights)
         mixed_pair = jnp.concatenate([mixed_turned, swap(mixed_turned, CORE)], axis=0)
         hidden_pair = jnp.concatenate([hidden_turned, swap(hidden_turned, CORE)], axis=0)
         inner_bias_own = jnp.concatenate(
@@ -1762,6 +1775,7 @@
         )
         if layer == 0:
             (grad_mixed,) = gate([grad_mixed], summed[0], plane_first)
+            (plane_second,) = gate([plane_second], grad_mixed)
         else:
             grad_mixed, first_sum = gate([grad_mixed, summed[0]])
         grad_query, grad_key, grad_value = attention_backward(packed, labels, grad_mixed, log_all, block_order)
@@ -1834,7 +1848,6 @@
             (first_keep, first_came, first_last), (second_keep, second_came, second_last)
         )
         came = [turn(sent[r - 1], planes - r) for r in range(1, planes)]
-        (plane_second,) = gate([plane_second], grad_mixed)
         sum_second = lax.psum_scatter(plane_second, "wsh", scatter_dimension=0, tiled=True)
         sum_first, sum_second, sum_joint = gate([sum_first, sum_second, sum_joint], own_total, tokens_sent)
         everything = lax.all_gather(

time: 734 us -> 734 us (level)
    all_gather x1, waiting for transfers between devices: 0.01 us -> 7.47 us  [head_split_body(): second_stack = lax.all_gather(layer_own, 'wsh', axis=0)]
    unnamed x202 -> x210, local copies, waits for them, and re-layouts: 24.7 us -> 23.8 us
  transfers between devices with their start and end apart: 76 -> 76, of which waited for: 30 -> 30; matrix products, arithmetic and copies ran while one was open for 17% -> 16% of each run, Pallas kernels for 31% -> 31%
where the time goes in v7:
time: 734 us; the launch traced here: 722 us
  Pallas kernels  257 us (35%)
  waiting for transfers between devices  185 us (25%)
  starting transfers between devices  95.6 us (13%)
  other arithmetic  75.1 us (10%)
  local copies, waits for them, and re-layouts  54.6 us (7%)
  matrix products  22.4 us (3%)
  between operations  20.5 us (3%)
  blocking collectives  11.4 us (2%)
    ppermute x47, waiting for transfers between devices, swap(): return lax.ppermute(block, 'ctx', [(i, i ^ mask) for i in devices])  79.7 us
    pallas_call x2, Pallas kernels, attention_backward(): pl.pallas_call(attention_backward_kernel, grid_spec=pltpu.PrefetchScalarG...  59.1 us
    all_to_all x2, waiting for transfers between devices, collect_tokens(): lax.all_to_all(sent, 'ctx', 0, 0, axis_index_groups=plane_groups(), tiled...  52.3 us
    ppermute x47, starting transfers between devices, swap(): return lax.ppermute(block, 'ctx', [(i, i ^ mask) for i in devices])  46.6 us
    pallas_call x2, Pallas kernels, feed_forward(): pl.pallas_call(functools.partial(feed_forward_kernel, count), grid=(4,),...  31.1 us
    pallas_call x2, Pallas kernels, attention_forward(): pl.pallas_call(attention_forward_kernel, grid_spec=pltpu.PrefetchScalarGr...  30.6 us
    pallas_call x2, Pallas kernels, weight_gradients(): pl.pallas_call(functools.partial(weight_gradient_kernel, split), grid_spe...  25.9 us
    unnamed x210, local copies, waits for them, and re-layouts  23.8 us
  transfers between devices with their start and end apart: 76, of which 30 were waited for; matrix products, arithmetic and copies ran while one was open for 16% of the time, Pallas kernels for 31%

profile of v7, /device:TPU:9, one launch (start us, length us, event | category | flops | bytes accessed | tf_op | source)
XLA Modules:
  0.0 721.6 jit_solution(5743629527434255769)
XLA Ops:
  27.1 8.5 %collective-permute-done.3 = bf16[2,256,512]{2,1,0:T(8,128)(2,1)S(1)} collective-permute-done((bf16[2,256,512]{2,1,0:T(8,128)(2,1)S(1)}, bf16[2,256,512]{2,1,0:T(8,128)(2,1)S(1)}, u32[]{:S(2)}, u32[]{:S(2)}) %collective-permute-start.3) | collective-permute-done | bytes 524320 | tf_op jit(solution)/shard_map/ppermute | solution.py:543
  67.2 15.3 %attention_forward.2 = (bf16[8,256,128]{2,1,0:T(8,128)(2,1)}, f32[2,2048]{1,0:T(2,128)}) custom-call(s32[8]{0:T(128)} %get-tuple-element.382.order_ref, bf16[2048,384]{1,0:T(8,128)(2,1)} %get-tuple-element.132.query_ref.key_ref.value_ref, bf16[2048,384]{1,0:T(8,128)(2,1)} %get-tuple-element.132.query_ref.key_ref.value_ref, ...), custom_call_target="tpu_custom_call" | custom-call | flops 19549999104 | bytes 61200000 | tf_op jit(solution)/shard_map/attention_forward/pallas_call | solution.py:608
  112.7 7.3 %collective-permute-done.16.refs_10_ = bf16[384,512]{1,0:T(8,128)(2,1)S(1)} collective-permute-done((bf16[384,512]{1,0:T(8,128)(2,1)S(1)}, bf16[384,512]{1,0:T(8,128)(2,1)S(1)}, u32[]{:S(2)}, u32[]{:S(2)}) %collective-permute-start.16) | collective-permute-done | bytes 393248 | tf_op jit(solution)/shard_map/ppermute | solution.py:543
  137.5 16.5 %feed_forward.2 = (f32[256,1024]{1,0:T(8,128)}, bf16[256,1024]{1,0:T(8,128)(2,1)}, bf16[512,2048]{1,0:T(8,128)(2,1)}, bf16[512,2048]{1,0:T(8,128)(2,1)}) custom-call(bf16[512,1024]{1,0:T(8,128)(2,1)} %copy-done.53, f32[1,2048]{1,0:T(1,128)} %maximum_convert_fusion.bias_ref, bf16[2,4,256,512]{3,2,1,0:T(8,128)(2,1)} %get-tuple-element.138.own_inner, ...), custom_call_target="tpu_custom_call" | custom-call | flops 18400000000 | bytes 57600000 | tf_op jit(solution)/shard_map/feed_forward/pallas_call | solution.py:984
  158.9 7.5 %all-gather.14.cloned.1.call-done = bf16[1024,1536]{1,0:T(8,128)(2,1)} async-done(((bf16[256,1536]{1,0:T(8,128)(2,1)}), bf16[1024,1536]{1,0:T(8,128)(2,1)}) %all-gather.14.cloned.1.call-update) | async-done | bytes 3145744 | tf_op jit(solution)/shard_map/all_gather | solution.py:1641
  181.9 20.8 %collective-permute-done.26 = bf16[2,256,512]{2,1,0:T(8,128)(2,1)S(1)} collective-permute-done((bf16[2,256,512]{2,1,0:T(8,128)(2,1)S(1)}, bf16[2,256,512]{2,1,0:T(8,128)(2,1)S(1)}, u32[]{:S(2)}, u32[]{:S(2)}) %collective-permute-start.26) | collective-permute-done | bytes 524320 | tf_op jit(solution)/shard_map/ppermute | solution.py:543
  221.4 15.3 %attention_forward.3 = (bf16[8,256,128]{2,1,0:T(8,128)(2,1)}, f32[2,2048]{1,0:T(2,128)}) custom-call(s32[8]{0:T(128)} %get-tuple-element.382.order_ref, bf16[2048,384]{1,0:T(8,128)(2,1)} %add_convert_fusion.2.query_ref.key_ref.value_ref, bf16[2048,384]{1,0:T(8,128)(2,1)} %add_convert_fusion.2.query_ref.key_ref.value_ref, ...), custom_call_target="tpu_custom_call" | custom-call | flops 19549999104 | bytes 61200000 | tf_op jit(solution)/shard_map/attention_forward/pallas_call | solution.py:608
  246.4 9.5 %all-to-all-done.1.heads_ref = bf16[8,256,128]{2,1,0:T(8,128)(2,1)S(1)} async-done(((bf16[8,256,128]{2,1,0:T(8,128)(2,1)}), bf16[8,256,128]{2,1,0:T(8,128)(2,1)S(1)}, u32[]{:S(2)}, u32[]{:S(2)}) %all-to-all-start.1) | async-done | bytes 524320 | tf_op jit(solution)/shard_map/all_to_all | solution.py:1503
  271.9 14.6 %feed_forward.3 = (f32[256,1024]{1,0:T(8,128)}, bf16[256,1024]{1,0:T(8,128)(2,1)}, bf16[512,2048]{1,0:T(8,128)(2,1)}, bf16[512,2048]{1,0:T(8,128)(2,1)}) custom-call(bf16[512,1024]{1,0:T(8,128)(2,1)} %copy-done.54, f32[1,2048]{1,0:T(1,128)} %maximum_convert_fusion.1.bias_ref, bf16[2,4,256,512]{3,2,1,0:T(8,128)(2,1)} %get-tuple-element.138.own_inner, ...), custom_call_target="tpu_custom_call" | custom-call | flops 18400000000 | bytes 57600000 | tf_op jit(solution)/shard_map/feed_forward/pallas_call | solution.py:984
  297.8 10.2 %feed_backward.2 = (f32[256,1024]{1,0:T(8,128)}, bf16[256,1024]{1,0:T(8,128)(2,1)}, bf16[512,2048]{1,0:T(8,128)(2,1)}, f32[1,2048]{1,0:T(1,128)}) custom-call(bf16[512,1024]{1,0:T(8,128)(2,1)} %pad_maximum_fusion.12.grad_ref, bf16[512,2048]{1,0:T(8,128)(2,1)} %get-tuple-element.151.slope_ref, bf16[2,4,256,512]{3,2,1,0:T(8,128)(2,1)} %get-tuple-element.138.own_inner, ...), custom_call_target="tpu_custom_call" | custom-call | flops 12650000384 | bytes 39600000 | tf_op jit(solution)/shard_map/feed_backward/pallas_call | solution.py:1028
  324.3 12.4 %weight_gradients.2 = (bf16[4,1024,640]{2,1,0:T(8,128)(2,1)}, bf16[4,1024,512]{2,1,0:T(8,128)(2,1)}) custom-call(s32[4]{0:T(128)} %pad_add_fusion.3.rows_ref, bf16[512,1024]{1,0:T(8,128)(2,1)} %copy-done.54, bf16[512,1024]{1,0:T(8,128)(2,1)} %pad_maximum_fusion.12.grad_ref, bf16[512,1024]{1,0:T(8,128)(2,1)} %pad_maximum_fusion.13.mixed_ref, ...), custom_call_target="tpu_custom_call" | custom-call | flops 14949999616 | bytes 46800000 | tf_op jit(solution)/shard_map/weight_gradients/pallas_call | solution.py:1121
  338.0 29.6 %attention_backward.2 = (bf16[2048,128]{1,0:T(8,128)(2,1)}, bf16[2048,128]{1,0:T(8,128)(2,1)}, bf16[2048,128]{1,0:T(8,128)(2,1)}) custom-call(s32[8]{0:T(128)} %get-tuple-element.382.order_ref, bf16[2048,384]{1,0:T(8,128)(2,1)} %add_convert_fusion.2.query_ref.key_ref.value_ref, bf16[2048,384]{1,0:T(8,128)(2,1)} %add_convert_fusion.2.query_ref.key_ref.value_ref, ...), custom_call_target="tpu_custom_call" | custom-call | flops 33350000640 | bytes 104400000 | tf_op jit(solution)/shard_map/attention_backward/pallas_call | solution.py:696
  367.7 9.9 %token_gradients.2 = (f32[4,256,1024]{2,1,0:T(8,128)}, bf16[4,256,1024]{2,1,0:T(8,128)(2,1)}, bf16[2048,384]{1,0:T(8,128)(2,1)}, f32[1,384]{1,0:T(1,128)}) custom-call(s32[4]{0:T(128)} %iota_xor_fusion.place_ref, bf16[2048,128]{1,0:T(8,128)(2,1)} %get-tuple-element.165.query_ref, bf16[2048,128]{1,0:T(8,128)(2,1)} %get-tuple-element.166.key_ref, ...), custom_call_target="tpu_custom_call" | custom-call | flops 11500000256 | bytes 36000000 | tf_op jit(solution)/shard_map/token_gradients/pallas_call | solution.py:1334
  392.0 6.0 fusion.9.refs_1_
  398.0 23.7 %all-to-all-done.4.refs_0_ = bf16[4,256,1024]{2,1,0:T(8,128)(2,1)S(1)} async-done(((bf16[4,256,1024]{2,1,0:T(8,128)(2,1)}), bf16[4,256,1024]{2,1,0:T(8,128)(2,1)S(1)}, u32[]{:S(2)}, u32[]{:S(2)}) %all-to-all-start.4) | async-done | bytes 2097184 | tf_op jit(solution)/shard_map/all_to_all | solution.py:1486
  434.2 12.2 %feed_backward.3 = (f32[256,1024]{1,0:T(8,128)}, bf16[256,1024]{1,0:T(8,128)(2,1)}, bf16[512,2048]{1,0:T(8,128)(2,1)}, f32[1,2048]{1,0:T(1,128)}) custom-call(bf16[512,1024]{1,0:T(8,128)(2,1)} %pad_maximum_fusion.14.grad_ref, bf16[512,2048]{1,0:T(8,128)(2,1)} %get-tuple-element.171.slope_ref, bf16[2,4,256,512]{3,2,1,0:T(8,128)(2,1)} %get-tuple-element.138.own_inner, ...), custom_call_target="tpu_custom_call" | custom-call | flops 12650000384 | bytes 39600000 | tf_op jit(solution)/shard_map/feed_backward/pallas_call | solution.py:1028
  464.8 13.6 %weight_gradients.3 = (bf16[2,512,1152]{2,1,0:T(8,128)(2,1)}, bf16[2,512,1152]{2,1,0:T(8,128)(2,1)}, bf16[2,512,1152]{2,1,0:T(8,128)(2,1)}, bf16[2,512,1152]{2,1,0:T(8,128)(2,1)}) custom-call(s32[4]{0:T(128)} %pad_add_fusion.3.rows_ref, bf16[512,1024]{1,0:T(8,128)(2,1)} %copy-done.53, bf16[512,1024]{1,0:T(8,128)(2,1)} %pad_maximum_fusion.14.grad_ref, ...), custom_call_target="tpu_custom_call" | custom-call | flops 14949999616 | bytes 46800000 | tf_op jit(solution)/shard_map/weight_gradients/pallas_call | solution.py:1121
  487.2 29.5 %attention_backward.3 = (bf16[2048,128]{1,0:T(8,128)(2,1)}, bf16[2048,128]{1,0:T(8,128)(2,1)}, bf16[2048,128]{1,0:T(8,128)(2,1)}) custom-call(s32[8]{0:T(128)} %get-tuple-element.382.order_ref, bf16[2048,384]{1,0:T(8,128)(2,1)} %get-tuple-element.132.query_ref.key_ref.value_ref, bf16[2048,384]{1,0:T(8,128)(2,1)} %get-tuple-element.132.query_ref.key_ref.value_ref, ...), custom_call_target="tpu_custom_call" | custom-call | flops 33350000640 | bytes 104400000 | tf_op jit(solution)/shard_map/attention_backward/pallas_call | solution.py:696
  516.7 9.9 %token_gradients.3 = (f32[4,256,1024]{2,1,0:T(8,128)}, bf16[4,256,1024]{2,1,0:T(8,128)(2,1)}, bf16[2048,384]{1,0:T(8,128)(2,1)}, f32[1,384]{1,0:T(1,128)}) custom-call(s32[4]{0:T(128)} %iota_xor_fusion.place_ref, bf16[2048,128]{1,0:T(8,128)(2,1)} %get-tuple-element.184.query_ref, bf16[2048,128]{1,0:T(8,128)(2,1)} %get-tuple-element.185.key_ref, ...), custom_call_target="tpu_custom_call" | custom-call | flops 11500000256 | bytes 36000000 | tf_op jit(solution)/shard_map/token_gradients/pallas_call | solution.py:1334
  567.3 6.5 collective-permute-done.48.refs_4_.refs_5_
  600.6 28.6 %all-to-all-done.7 = bf16[4,256,1024]{2,1,0:T(8,128)(2,1)S(1)} async-done(((bf16[4,256,1024]{2,1,0:T(8,128)(2,1)}), bf16[4,256,1024]{2,1,0:T(8,128)(2,1)S(1)}, u32[]{:S(2)}, u32[]{:S(2)}) %all-to-all-start.7) | async-done | bytes 2097184 | tf_op jit(solution)/shard_map/all_to_all | solution.py:1486
  632.4 11.4 %all_to_all.45 = f32[8,32,256]{2,1,0:T(8,128)S(1)} all-to-all(f32[8,32,256]{2,1,0:T(8,128)} %gate.34), channel_id=1, replica_groups=mesh['ctx'=8,'wsh'=4] {'ctx'}, dimensions={0} | all-to-all | bytes 524288 | tf_op jit(solution)/shard_map/all_to_all | solution.py:1503
  656.0 9.4 %collective-permute-done.56 = bf16[256,768]{1,0:T(8,128)(2,1)S(1)} collective-permute-done((bf16[256,768]{1,0:T(8,128)(2,1)}, bf16[256,768]{1,0:T(8,128)(2,1)S(1)}, u32[]{:S(2)}, u32[]{:S(2)}) %collective-permute-start.56) | collective-permute-done | bytes 393248 | tf_op jit(solution)/shard_map/ppermute | solution.py:543
  671.3 9.7 %place_pieces.3 = (f32[2,256,1024]{2,1,0:T(8,128)}, f32[2,256,1024]{2,1,0:T(8,128)}, f32[2,256,1024]{2,1,0:T(8,128)}, f32[2,256,1024]{2,1,0:T(8,128)}, f32[2,256...) custom-call(s32[8]{0:T(128)} %iota.27.order_ref, bf16[8,256,1536]{2,1,0:T(8,128)(2,1)} %gate.39.source), custom_call_target="tpu_custom_call" | custom-call | flops 11500000256 | bytes 36000000 | tf_op jit(solution)/shard_map/place_pieces/pallas_call | solution.py:871
  (556 shorter events, 363.2 us)
Async XLA Ops:
  7.2 48.4 %all-gather.10.cloned.1.call-start = ((), (), s32[]{:S(2)}) async-start(), calls=%async_computation.13 | async-start | bytes 1638400 | tf_op jit(solution)/shard_map/all_gather | solution.py:1584
  15.6 33.4 %collective-permute-start.7 = (bf16[288,384]{1,0:T(8,128)(2,1)}, bf16[288,384]{1,0:T(8,128)(2,1)}, u32[]{:S(2)}, u32[]{:S(2)}) collective-permute-start(bf16[288,384]{1,0:T(8,128)(2,1)} %get-tuple-element.324), channel_id=1, source_target_pairs={{0,3},{1,0},{2,1},{3,2},{4,7},{5,4},{6,5},{7,6},{8,11},{9,8},{10,9... | collective-permute-start | bytes 663560 | tf_op jit(solution)/shard_map/ppermute | solution.py:548
  20.5 66.9 %all-gather.12.cloned.1.call-start = ((), (), s32[]{:S(2)}) async-start(), calls=%async_computation.18 | async-start | bytes 1310720 | tf_op jit(solution)/shard_map/all_gather | solution.py:1587
  59.5 34.7 %collective-permute-start.10 = (bf16[384,640]{1,0:T(8,128)(2,1)}, bf16[384,640]{1,0:T(8,128)(2,1)}, u32[]{:S(2)}, u32[]{:S(2)}) collective-permute-start(bf16[384,640]{1,0:T(8,128)(2,1)} %get-tuple-element.325.refs_1_), channel_id=1, source_target_pairs={{0,8},{4,12},{8,0},{12,4},{16,24},{20,28},{24,16},{28,20},{1,9},{5... | collective-permute-start | bytes 1474568 | tf_op jit(solution)/shard_map/ppermute | solution.py:543
  61.0 34.2 %collective-permute-start.11 = (bf16[384,640]{1,0:T(8,128)(2,1)}, bf16[384,640]{1,0:T(8,128)(2,1)}, u32[]{:S(2)}, u32[]{:S(2)}) collective-permute-start(bf16[384,640]{1,0:T(8,128)(2,1)} %get-tuple-element.326.refs_0_), channel_id=1, source_target_pairs={{0,16},{4,20},{8,24},{12,28},{16,0},{20,4},{24,8},{28,12},{1,17},{... | collective-permute-start | bytes 1474568 | tf_op jit(solution)/shard_map/ppermute | solution.py:543
  103.5 62.9 %all-gather.14.cloned.1.call-start = ((), (), s32[]{:S(2)}) async-start(), calls=%async_computation.19 | async-start | bytes 3932160 | tf_op jit(solution)/shard_map/all_gather | solution.py:1641
  104.2 166.8 %all-gather.16.cloned.1.call-start = ((), (), s32[]{:S(2)}) async-start(), calls=%async_computation.20 | async-start | bytes 7864320 | tf_op jit(solution)/shard_map/all_gather | solution.py:1697
  323.5 103.9 %reduce-scatter.5.cloned.1.call-start = ((), (), s32[]{:S(2)}) async-start(), calls=%async_computation.14 | async-start | bytes 6553600 | tf_op jit(solution)/shard_map/reduce_scatter | solution.py:1803
  388.3 33.4 %all-to-all-start.4 = ((bf16[4,256,1024]{2,1,0:T(8,128)(2,1)}), bf16[4,256,1024]{2,1,0:T(8,128)(2,1)S(1)}, u32[]{:S(2)}, u32[]{:S(2)}) async-start(bf16[4,256,1024]{2,1,0:T(8,128)(2,1)} %add_convert_fusion.1), calls=%async_computation.4 | async-start | bytes 4194304 | tf_op jit(solution)/shard_map/all_to_all | solution.py:1486
  391.9 146.9 %reduce-scatter.7.cloned.1.call-start = ((), (), s32[]{:S(2)}) async-start(), calls=%async_computation.15 | async-start | bytes 5242880 | tf_op jit(solution)/shard_map/reduce_scatter | solution.py:1818
  427.4 161.3 %reduce-scatter.11.cloned.1.call-start = ((), (), s32[]{:S(2)}) async-start(), calls=%async_computation.17 | async-start | bytes 983040 | tf_op jit(solution)/shard_map/reduce_scatter | solution.py:1825
  463.9 124.8 %reduce-scatter.9.cloned.1.call-start = ((), (), s32[]{:S(2)}) async-start(), calls=%async_computation.16 | async-start | bytes 1310720 | tf_op jit(solution)/shard_map/reduce_scatter | solution.py:1851
  478.3 55.7 %collective-permute-start.41 = (bf16[2,512,1152]{2,1,0:T(8,128)(2,1)}, bf16[2,512,1152]{2,1,0:T(8,128)(2,1)}, u32[]{:S(2)}, u32[]{:S(2)}) collective-permute-start(bf16[2,512,1152]{2,1,0:T(8,128)(2,1)} %get-tuple-element.189), channel_id=1, source_target_pairs={{0,8},{4,12},{8,0},{12,4},{16,24},{20,28},{24,16},{28,20},{1,9},{5... | collective-permute-start | bytes 7077896 | tf_op jit(solution)/shard_map/ppermute | solution.py:543
  479.7 55.0 %collective-permute-start.42 = (bf16[2,512,1152]{2,1,0:T(8,128)(2,1)}, bf16[2,512,1152]{2,1,0:T(8,128)(2,1)}, u32[]{:S(2)}, u32[]{:S(2)}) collective-permute-start(bf16[2,512,1152]{2,1,0:T(8,128)(2,1)} %get-tuple-element.190), channel_id=1, source_target_pairs={{0,16},{4,20},{8,24},{12,28},{16,0},{20,4},{24,8},{28,12},{1,17},{... | collective-permute-start | bytes 7077896 | tf_op jit(solution)/shard_map/ppermute | solution.py:543
  481.9 52.8 %collective-permute-start.43 = (bf16[256,640]{1,0:T(8,128)(2,1)}, bf16[256,640]{1,0:T(8,128)(2,1)S(1)}, u32[]{:S(2)}, u32[]{:S(2)}) collective-permute-start(bf16[256,640]{1,0:T(8,128)(2,1)} %get-tuple-element.267), channel_id=1, source_target_pairs={{0,3},{1,0},{2,1},{3,2},{4,7},{5,4},{6,5},{7,6},{8,11},{9,8},{10,9... | collective-permute-start | bytes 983048 | tf_op jit(solution)/shard_map/ppermute | solution.py:548
  482.1 52.6 %collective-permute-start.44 = (bf16[256,640]{1,0:T(8,128)(2,1)}, bf16[256,640]{1,0:T(8,128)(2,1)}, u32[]{:S(2)}, u32[]{:S(2)}) collective-permute-start(bf16[256,640]{1,0:T(8,128)(2,1)} %get-tuple-element.266), channel_id=1, source_target_pairs={{0,2},{1,3},{2,0},{3,1},{4,6},{5,7},{6,4},{7,5},{8,10},{9,11},{10,... | collective-permute-start | bytes 983048 | tf_op jit(solution)/shard_map/ppermute | solution.py:548
  484.3 50.4 %collective-permute-start.45 = (bf16[256,640]{1,0:T(8,128)(2,1)}, bf16[256,640]{1,0:T(8,128)(2,1)}, u32[]{:S(2)}, u32[]{:S(2)}) collective-permute-start(bf16[256,640]{1,0:T(8,128)(2,1)} %get-tuple-element.265), channel_id=1, source_target_pairs={{0,1},{1,2},{2,3},{3,0},{4,5},{5,6},{6,7},{7,4},{8,9},{9,10},{10,1... | collective-permute-start | bytes 983048 | tf_op jit(solution)/shard_map/ppermute | solution.py:548
  538.3 43.8 %collective-permute-start.47 = (bf16[512,1152]{1,0:T(8,128)(2,1)}, bf16[512,1152]{1,0:T(8,128)(2,1)}, u32[]{:S(2)}, u32[]{:S(2)}) collective-permute-start(bf16[512,1152]{1,0:T(8,128)(2,1)} %fusion.16), channel_id=1, source_target_pairs={{0,8},{4,12},{8,0},{12,4},{16,24},{20,28},{24,16},{28,20},{1,9},{5... | collective-permute-start | bytes 3538952 | tf_op jit(solution)/shard_map/ppermute | solution.py:543
  542.5 39.6 %collective-permute-start.46 = (bf16[512,1152]{1,0:T(8,128)(2,1)}, bf16[512,1152]{1,0:T(8,128)(2,1)S(1)}, u32[]{:S(2)}, u32[]{:S(2)}) collective-permute-start(bf16[512,1152]{1,0:T(8,128)(2,1)} %fusion.15), channel_id=1, source_target_pairs={{0,16},{4,20},{8,24},{12,28},{16,0},{20,4},{24,8},{28,12},{1,17},{... | collective-permute-start | bytes 3538952 | tf_op jit(solution)/shard_map/ppermute | solution.py:543
  552.0 118.7 %all-gather.18.cloned.1.call-start = ((), (), s32[]{:S(2)}) async-start(), calls=%async_computation.21 | async-start | bytes 7077888 | tf_op jit(solution)/shard_map/all_gather | solution.py:1853
  592.6 36.6 %all-to-all-start.7 = ((bf16[4,256,1024]{2,1,0:T(8,128)(2,1)}), bf16[4,256,1024]{2,1,0:T(8,128)(2,1)S(1)}, u32[]{:S(2)}, u32[]{:S(2)}) async-start(bf16[4,256,1024]{2,1,0:T(8,128)(2,1)} %gate.33), calls=%async_computation.8 | async-start | bytes 4194304 | tf_op jit(solution)/shard_map/all_to_all | solution.py:1486
  596.2 48.2 %collective-permute-start.51 = (bf16[256,1152]{1,0:T(8,128)(2,1)}, bf16[256,1152]{1,0:T(8,128)(2,1)}, u32[]{:S(2)}, u32[]{:S(2)}) collective-permute-start(bf16[256,1152]{1,0:T(8,128)(2,1)} %get-tuple-element.204), channel_id=1, source_target_pairs={{0,3},{1,0},{2,1},{3,2},{4,7},{5,4},{6,5},{7,6},{8,11},{9,8},{10,9... | collective-permute-start | bytes 1769480 | tf_op jit(solution)/shard_map/ppermute | solution.py:548
  599.3 45.1 %collective-permute-start.52 = (bf16[256,1152]{1,0:T(8,128)(2,1)}, bf16[256,1152]{1,0:T(8,128)(2,1)}, u32[]{:S(2)}, u32[]{:S(2)}) collective-permute-start(bf16[256,1152]{1,0:T(8,128)(2,1)} %get-tuple-element.205), channel_id=1, source_target_pairs={{0,2},{1,3},{2,0},{3,1},{4,6},{5,7},{6,4},{7,5},{8,10},{9,11},{10,... | collective-permute-start | bytes 1769480 | tf_op jit(solution)/shard_map/ppermute | solution.py:548
  599.5 50.8 %collective-permute-start.53 = (bf16[256,1152]{1,0:T(8,128)(2,1)}, bf16[256,1152]{1,0:T(8,128)(2,1)}, u32[]{:S(2)}, u32[]{:S(2)}) collective-permute-start(bf16[256,1152]{1,0:T(8,128)(2,1)} %get-tuple-element.206), channel_id=1, source_target_pairs={{0,1},{1,2},{2,3},{3,0},{4,5},{5,6},{6,7},{7,4},{8,9},{9,10},{10,1... | collective-permute-start | bytes 1769480 | tf_op jit(solution)/shard_map/ppermute | solution.py:548
  (147 other events, 1636.9 us)
Sparse Core Ops, SparseCore 0:
  20.6 34.9 all-gather.9
  57.8 29.5 all-gather.11
  105.9 60.4 all-gather.13
  170.0 96.2 all-gather.15
  337.6 78.5 reduce-scatter.4
  427.6 59.5 reduce-scatter.6
  489.5 36.4 reduce-scatter.10
  538.9 38.3 reduce-scatter.8
  592.7 67.3 all-gather.17
